TPU v7x, 32 devices: a whole 2x2x4 slice. The times are simulated.
32 devices in a mesh: blk: 4 (over x, core), docs: 8 (over z, y).
Axes of the slice: x: 2, y: 2, z: 4, core: 2. Of those that a mesh axis runs over, the one named last changes fastest.
Arguments:
- tokens: bfloat16 [8, 512, 1024], P('docs', 'blk'), may hold values from -6 to 6
- lengths: int32 [8], P('docs'), may hold values from 51 to 512, as said below
- positions: int32 [8, 512], P('docs', 'blk'), may hold values from 0 to 1022, as said below
- token_boxes: int32 [4, 8, 512], P(None, 'docs', 'blk'), may hold values from 0 to 1000, as said below
- ln1_gain: float32 [1024], replicated, may hold values from 0.5 to 1.5
- ln1_bias: float32 [1024], replicated, may hold values from -1.75 to 1.75
- w_query: bfloat16 [1024, 1024], replicated, may hold values from -0.1875 to 0.1875
- w_key: bfloat16 [1024, 1024], replicated, may hold values from -0.1875 to 0.1875
- w_value: bfloat16 [1024, 1024], replicated, may hold values from -0.1875 to 0.1875
- w_out: bfloat16 [1024, 1024], replicated, may hold values from -0.75 to 0.75
- rel_table: bfloat16 [128, 1024], replicated, may hold values from -6 to 6
- xbias_table: bfloat16 [64, 16], replicated, may hold values from -3 to 3
- ybias_table: bfloat16 [64, 16], replicated, may hold values from -3 to 3
- ln2_gain: float32 [1024], replicated, may hold values from 0.5 to 1.5
- ln2_bias: float32 [1024], replicated, may hold values from -1.75 to 1.75
- w_in: bfloat16 [1024, 4096], replicated, may hold values from -0.1875 to 0.1875
- b_in: float32 [4096], replicated, may hold values from -3 to 3
- w_down: bfloat16 [4096, 1024], replicated, may hold values from -0.09375 to 0.09375
- cotangent: bfloat16 [8, 512, 1024], P('docs', 'blk'), may hold values from -6 to 6
Outputs:
- block_out: bfloat16 [8, 512, 1024], P('docs', 'blk')
- grad_tokens: float32 [8, 512, 1024], P('docs', 'blk')
- grad_ln1_gain: float32 [1024], P('docs')
- grad_ln1_bias: float32 [1024], P('docs')
- grad_w_query: float32 [1024, 1024], P('docs')
- grad_w_key: float32 [1024, 1024], P('docs')
- grad_w_value: float32 [1024, 1024], P('docs')
- grad_w_out: float32 [1024, 1024], P('docs')
- grad_rel_table: float32 [128, 1024], P('docs')
- grad_xbias_table: float32 [64, 16], P('docs')
- grad_ybias_table: float32 [64, 16], P('docs')
- grad_ln2_gain: float32 [1024], P('docs')
- grad_ln2_bias: float32 [1024], P('docs')
- grad_w_in: float32 [1024, 4096], P('docs')
- grad_b_in: float32 [4096], P('docs')
- grad_w_down: float32 [4096, 1024], P('docs')
Inputs may be any that keep to these rules, and one draw needn't show every extreme that they name: `lengths`: each document's count of text slots; its later slots are padding, never attended to as keys. `positions`: a document's first slot has position 0 and each next slot 0, 1 or 2 more. `token_boxes`: each box has x0 < x1 and y0 < y1.
All inputs are finite; a program needn't handle non-finite values.
Results may differ from a plain program's by a relative error of at most 0.035.
Values may be sent and summed in bfloat16 or wider, within the bound.
No kernel may reach another device: no remote copies, remote signals or barrier semaphores. Data moves between devices by JAX's collectives and lax.ppermute only.
A program may use at most 192 MiB of HBM per device.

v0:
```python
import math

import jax
import jax.numpy as jnp
from jax import lax
from jax.experimental import pallas as pl
from jax.experimental.pallas import tpu as pltpu
from jax.sharding import PartitionSpec as P

norm_eps = 1e-05
mask_value = -1e30
f32 = jnp.float32
bf16 = jnp.bfloat16
lanes = 128


def dot(a, b, contract=((1,), (0,))):
    return lax.dot_general(a, b, (contract, ((), ())), preferred_element_type=f32)


def pick(table, index):
    return jnp.take_along_axis(table, index, axis=1, mode="promise_in_bounds")


def ahead_of(first, second):
    return jnp.clip(first - second, -64, 63) + 64


def attn_fwd_kernel(
    place, x_ref, wq_ref, wk_ref, wv_ref, rel_ref, tab_ref, row_ref, col_ref,
    att_ref, probs_ref, qkv_ref, relkq_ref, key_rel,
):
    scale = 1.0 / math.sqrt(192.0)
    step = pl.program_id(0)
    rows = x_ref.shape[0]
    width = wq_ref.shape[1]
    heads = tab_ref.shape[1]
    size = width // heads
    tiles = rows // lanes

    @pl.when(step == 0)
    def _():
        for at, w_ref in enumerate((wq_ref, wk_ref, wv_ref)):
            for t in range(tiles):
                qkv_ref[t * lanes : (t + 1) * lanes, at * width : (at + 1) * width] = dot(
                    x_ref[t * lanes : (t + 1) * lanes, :], w_ref[...]
                ).astype(bf16)
        relkq_ref[:, :width] = dot(rel_ref[...], wk_ref[...]).astype(bf16)
        relkq_ref[:, width:] = dot(rel_ref[...], wq_ref[...]).astype(bf16)
        for h in range(heads):
            key_rel[h] = (
                dot(
                    qkv_ref[:, width + h * size : width + (h + 1) * size],
                    relkq_ref[:, width + h * size : width + (h + 1) * size],
                    ((1,), (1,)),
                )
                .astype(bf16)
                .astype(f32)
            )

    here = pl.ds(pl.multiple_of(step * lanes, lanes), lanes)
    pos_i = col_ref[here, 0:1]
    cx_i = col_ref[here, 1:2]
    cy_i = col_ref[here, 2:3]
    own_row = row_ref[0:1, here]
    ahead, mirror, across, vertical = [], [], [], []
    for t in range(tiles):
        span = slice(t * lanes, (t + 1) * lanes)
        ahead.append(ahead_of(pos_i, row_ref[0:1, span]))
        mirror.append(ahead_of(col_ref[span, 0:1], own_row))
        across.append(jnp.clip(jnp.right_shift(cx_i - row_ref[1:2, span], 5), -32, 31) + 32)
        vertical.append(jnp.clip(jnp.right_shift(cy_i - row_ref[2:3, span], 5), -32, 31) + 96)
    valid = row_ref[3:4, :] > 0
    for h in range(heads):
        cols = slice(h * size, (h + 1) * size)
        query = qkv_ref[here, cols]
        rel_scores = (
            dot(query, relkq_ref[:, cols], ((1,), (1,))).astype(bf16).astype(f32)
        )
        table = jnp.broadcast_to(tab_ref[0, h : h + 1, :], (lanes, lanes))
        pieces = []
        for t in range(tiles):
            span = slice(t * lanes, (t + 1) * lanes)
            content = dot(
                query, qkv_ref[span, width + h * size : width + (h + 1) * size], ((1,), (1,))
            )
            mirrored = pick(key_rel[h, span, :], mirror[t]).T
            bias = pick(table, across[t]) + pick(table, vertical[t])
            pieces.append(
                scale * (content + pick(rel_scores, ahead[t]) + mirrored) + bias
            )
        scores = jnp.where(valid, jnp.concatenate(pieces, axis=1), mask_value)
        top = jnp.max(scores, axis=1, keepdims=True)
        raised = jnp.exp(scores - top)
        probs = (raised * (1.0 / jnp.sum(raised, axis=1, keepdims=True))).astype(bf16)
        probs_ref[h] = probs
        att_ref[:, cols] = dot(
            probs, qkv_ref[:, 2 * width + h * size : 2 * width + (h + 1) * size]
        ).astype(bf16)


def attn_fwd(place, x_all, w_query, w_key, w_value, rel_table, tables, ints_row, ints_col):
    rows, model = x_all.shape
    parts, heads, _ = tables.shape
    width = w_query.shape[1] // parts
    tiles = rows // lanes
    buckets = rel_table.shape[0]
    whole = lambda *shape: pl.BlockSpec(shape, lambda i, at: (0,) * len(shape))
    column = pl.BlockSpec((model, width), lambda i, at: (0, at[0]))
    return pl.pallas_call(
        attn_fwd_kernel,
        out_shape=(
            jax.ShapeDtypeStruct((rows, width), bf16),
            jax.ShapeDtypeStruct((heads, rows, rows), bf16),
            jax.ShapeDtypeStruct((rows, 3 * width), bf16),
            jax.ShapeDtypeStruct((buckets, 2 * width), bf16),
        ),
        grid_spec=pltpu.PrefetchScalarGridSpec(
            num_scalar_prefetch=1,
            grid=(tiles,),
            in_specs=[
                whole(rows, model),
                column,
                column,
                column,
                whole(buckets, model),
                pl.BlockSpec((1, heads, lanes), lambda i, at: (at[0], 0, 0)),
                whole(8, rows),
                whole(rows, 8),
            ],
            out_specs=[
                pl.BlockSpec((lanes, width), lambda i, at: (i, 0)),
                pl.BlockSpec((heads, lanes, rows), lambda i, at: (0, i, 0)),
                whole(rows, 3 * width),
                whole(buckets, 2 * width),
            ],
            scratch_shapes=[pltpu.VMEM((heads, rows, lanes), f32)],
        ),
        compiler_params=pltpu.CompilerParams(vmem_limit_bytes=40 << 20),
        cost_estimate=pl.CostEstimate(
            flops=6 * 10**9, transcendentals=10**6, bytes_accessed=8 << 20
        ),
        name="attn_fwd",
    )(place, x_all, w_query, w_key, w_value, rel_table, tables, ints_row, ints_col)


def attn_bwd_kernel(
    ga_ref, qkv_ref, probs_ref, relkq_ref, row_ref, col_ref,
    dqkv_ref, drel_ref, boxes_ref, ds_ref,
):
    scale = 1.0 / math.sqrt(192.0)
    rows = ga_ref.shape[0]
    heads = probs_ref.shape[0]
    width = ga_ref.shape[1]
    size = width // heads
    tiles = rows // lanes
    span_width = 3 * lanes
    drel_ref[...] = jnp.zeros_like(drel_ref)
    boxes_ref[...] = jnp.zeros_like(boxes_ref)
    window = lax.broadcasted_iota(jnp.int32, (rows, span_width), 1)
    bucket = lax.broadcasted_iota(jnp.int32, (lanes, lanes), 1)
    label = lax.broadcasted_iota(jnp.int32, (rows, lanes), 1)
    all_pos = col_ref[:, 0:1]
    all_x, all_y = col_ref[:, 1:2], col_ref[:, 2:3]
    sector_x, sector_y = jnp.right_shift(all_x, 5), jnp.right_shift(all_y, 5)
    hot_x = (label == sector_x).astype(bf16)
    hot_y = (label == sector_y + 64).astype(bf16)
    hot_both = ((label == sector_x) | (label == sector_y + 64)).astype(bf16)

    def histogram(sums, total, at, base_row):
        first = at - base_row + (2 * lanes // 2 - 1) - bucket
        low = jnp.bitwise_and(first, lanes - 1)
        group = jnp.right_shift(first, 7)
        found = jnp.where(
            group == 0,
            pick(sums[:, :lanes], low),
            jnp.where(
                group == 1,
                pick(sums[:, lanes : 2 * lanes], low),
                pick(sums[:, 2 * lanes :], low),
            ),
        )
        found = jnp.where(bucket == 0, total, found)
        later = jnp.where(bucket == lanes - 1, 0.0, pltpu.roll(found, lanes - 1, 1))
        return found - later

    def by_rows(ib, carry):
        here = pl.ds(pl.multiple_of(ib * lanes, lanes), lanes)
        pos_i = col_ref[here, 0:1]
        cx_i, cy_i = col_ref[here, 1:2], col_ref[here, 2:3]
        base = jnp.min(pos_i, axis=0, keepdims=True)
        below = (all_pos <= base - 63 + window).astype(bf16)
        short_x = jnp.bitwise_and(cx_i, 31) < jnp.bitwise_and(row_ref[1:2, :], 31)
        short_y = jnp.bitwise_and(cy_i, 31) < jnp.bitwise_and(row_ref[2:3, :], 31)
        step_x = jnp.right_shift(cx_i, 5) + 32 - bucket
        step_y = jnp.right_shift(cy_i, 5) + 32 - (bucket - 64)
        in_x = (bucket < 64) & (step_x >= 0) & (step_x < 32)
        in_y = (bucket >= 64) & (step_y >= 0) & (step_y < 32)
        seek = jnp.where(in_x, step_x, jnp.where(in_y, step_y + 64, 0))
        inside = in_x | in_y
        for h in range(heads):
            cols = slice(h * size, (h + 1) * size)
            kcols = slice(width + h * size, width + (h + 1) * size)
            vcols = slice(2 * width + h * size, 2 * width + (h + 1) * size)
            probs = probs_ref[h, here, :].astype(f32)
            gained = dot(ga_ref[here, cols], qkv_ref[:, vcols], ((1,), (1,)))
            row_dots = jnp.sum(probs * gained, axis=1, keepdims=True)
            grad32 = probs * (gained - row_dots)
            grad = grad32.astype(bf16)
            ds_ref[h, here, :] = grad
            exact = grad.astype(f32)
            total = jnp.sum(exact, axis=1, keepdims=True)
            rel = histogram(dot(grad, below), total, pos_i, base)
            rel = (scale * rel).astype(bf16)
            query = qkv_ref[here, cols]
            dqkv_ref[here, cols] = (
                scale * dot(grad, qkv_ref[:, kcols]) + dot(rel, relkq_ref[:, cols])
            ).astype(bf16)
            drel_ref[:, cols] += dot(rel, query, ((0,), (0,)))
            grad_x = jnp.where(short_x, exact, 0.0).astype(bf16)
            grad_y = jnp.where(short_y, exact, 0.0).astype(bf16)
            plain = dot(grad, hot_both)
            less = dot(grad_x, hot_x) + dot(grad_y, hot_y)
            plain = jnp.where(inside, pick(plain, seek), 0.0)
            less = jnp.where(inside, pick(less, seek), 0.0)
            boxes_ref[2 * h : 2 * h + 1, :] += jnp.sum(plain, axis=0, keepdims=True)
            boxes_ref[2 * h + 1 : 2 * h + 2, :] += jnp.sum(less, axis=0, keepdims=True)
        return carry

    lax.fori_loop(0, tiles, by_rows, 0)

    def by_columns(jb, carry):
        here = pl.ds(pl.multiple_of(jb * lanes, lanes), lanes)
        pos_j = col_ref[here, 0:1]
        base = jnp.min(pos_j, axis=0, keepdims=True)
        below = (all_pos <= base - 63 + window).astype(bf16)
        for h in range(heads):
            cols = slice(h * size, (h + 1) * size)
            kcols = slice(width + h * size, width + (h + 1) * size)
            vcols = slice(2 * width + h * size, 2 * width + (h + 1) * size)
            grad = ds_ref[h, :, here]
            total = dot(grad, jnp.ones((rows, lanes), bf16), ((0,), (0,)))
            sums = dot(grad, below, ((0,), (0,)))
            mirror = (scale * histogram(sums, total, pos_j, base)).astype(bf16)
            dqkv_ref[here, kcols] = (
                scale * dot(grad, qkv_ref[:, cols], ((0,), (0,)))
                + dot(mirror, relkq_ref[:, kcols])
            ).astype(bf16)
            drel_ref[:, kcols] += dot(mirror, qkv_ref[here, kcols], ((0,), (0,)))
            dqkv_ref[here, vcols] = dot(
                probs_ref[h, :, here], ga_ref[:, cols], ((0,), (0,))
            ).astype(bf16)
        return carry

    lax.fori_loop(0, tiles, by_columns, 0)


def attn_bwd(grad_att, qkv, probs, relkq, ints_row, ints_col):
    rows, width = grad_att.shape
    heads = probs.shape[0]
    buckets = relkq.shape[0]
    inside = pl.BlockSpec(memory_space=pltpu.VMEM)
    return pl.pallas_call(
        attn_bwd_kernel,
        out_shape=(
            jax.ShapeDtypeStruct((rows, 3 * width), bf16),
            jax.ShapeDtypeStruct((buckets, 2 * width), f32),
            jax.ShapeDtypeStruct((2 * heads, lanes), f32),
        ),
        in_specs=[inside] * 6,
        out_specs=[inside] * 3,
        scratch_shapes=[pltpu.VMEM((heads, rows, rows), bf16)],
        compiler_params=pltpu.CompilerParams(vmem_limit_bytes=40 << 20),
        cost_estimate=pl.CostEstimate(
            flops=12 * 10**9, transcendentals=0, bytes_accessed=6 << 20
        ),
        name="attn_bwd",
    )(grad_att, qkv, probs, relkq, ints_row, ints_col)


def layer_norm(inputs, gain_vec, bias_vec):
    row_mean = jnp.mean(inputs, axis=-1, keepdims=True)
    centered = inputs - row_mean
    inverse = lax.rsqrt(jnp.mean(centered * centered, axis=-1, keepdims=True) + norm_eps)
    normed = centered * inverse
    return (normed * gain_vec + bias_vec, normed, inverse)


def norm_backward(grad_in, normed, inverse, gain_vec):
    grad_gain = jnp.sum(grad_in * normed, axis=0)
    grad_shift = jnp.sum(grad_in, axis=0)
    scaled = grad_in * gain_vec
    grad_input = inverse * (
        scaled
        - jnp.mean(scaled, axis=-1, keepdims=True)
        - normed * jnp.mean(scaled * normed, axis=-1, keepdims=True)
    )
    return (grad_input, grad_gain, grad_shift)


def bits_of(count):
    assert count & (count - 1) == 0
    return [1 << at for at in range(count.bit_length() - 1)]


def swap(array, axis, by):
    count = lax.axis_size(axis)
    return lax.ppermute(array, axis, [(i, i ^ by) for i in range(count)])


def offsets(count):
    order = [0]
    for bit in reversed(bits_of(count)):
        order = order + [at ^ bit for at in order]
    return order


def spread(shared, pieces):
    count = lax.axis_size("blk")
    got = {0: shared} if shared is not None else {}
    held = {(0, at): piece for at, piece in pieces.items()} if pieces else {}
    for bit in reversed(bits_of(count)):
        out_keys = [key for key in sorted(held) if key[1] & bit]
        out_shared = sorted(got)
        parts = [got[at] for at in out_shared] + [held[key] for key in out_keys]
        if bit == 1:
            came = [swap(part, "blk", bit) for part in parts]
        else:
            came = swap(jnp.concatenate(parts, axis=1), "blk", bit)
            edges = [0]
            for part in parts:
                edges.append(edges[-1] + part.shape[1])
            came = [came[:, a:b] for a, b in zip(edges[:-1], edges[1:])]
        for at, part in zip(out_shared, came):
            got[at ^ bit] = part
        for key, part in zip(out_keys, came[len(out_shared) :]):
            del held[key]
            held[(key[0] ^ bit, key[1] ^ bit)] = part
    return got, {key[0]: part for key, part in held.items()}


def by_place(stacked, place):
    count = len(stacked)
    for bit in bits_of(count):
        turned = (place & bit) != 0
        stacked = [jnp.where(turned, stacked[at ^ bit], stacked[at]) for at in range(count)]
    return stacked


def chunk_order(count):
    order = [0]
    for bit in reversed(bits_of(count)):
        order = order + [at | bit for at in order]
    return order


def for_docs(chunks, doc_place):
    moved = by_place(chunks, doc_place)
    return [moved[at] for at in chunk_order(len(chunks))]


def halve(keep, send, bits):
    count = lax.axis_size("docs")
    first = True
    current = keep
    for bit in bits:
        if not first:
            half = current.shape[0] // 2
            current, send = current[:half], current[half:]
        first = False
        came = swap(send, "docs", bit)
        current = (current.astype(f32) + came.astype(f32)).astype(bf16)
    return current


def shards(
    tokens, lengths, positions, token_boxes, ln1_gain, ln1_bias, w_query, w_key, w_value, w_out,
    rel_table, xbias_table, ybias_table, ln2_gain, ln2_bias, w_in, b_in, w_down, cotangent,
):
    doc_count, row_count, model = tokens.shape
    assert doc_count == 1 and row_count == lanes
    parts = lax.axis_size("blk")
    docs = lax.axis_size("docs")
    place = lax.axis_index("blk")
    doc_place = lax.axis_index("docs")
    heads = xbias_table.shape[1]
    own_heads = heads // parts
    width = model // parts
    buckets = rel_table.shape[0]
    boxes = xbias_table.shape[0]
    hidden_units = w_in.shape[1]
    order = offsets(parts)
    x_own = tokens[0]

    centers_x = jnp.right_shift(token_boxes[0] + token_boxes[2], 1)
    centers_y = jnp.right_shift(token_boxes[1] + token_boxes[3], 1)
    own_ints = jnp.concatenate([positions, centers_x, centers_y], axis=0)
    coded = jnp.concatenate(
        [jnp.right_shift(own_ints, 5), jnp.bitwise_and(own_ints, 31)], axis=0
    ).astype(bf16)
    coded = jnp.pad(coded.reshape(1, -1), ((0, 7), (0, model - coded.size)))
    got, _ = spread(jnp.concatenate([x_own, coded], axis=0), None)
    x_all = jnp.concatenate([got[at][:row_count] for at in order], axis=0)
    decoded = jnp.concatenate(
        [got[at][row_count : row_count + 1, : 6 * row_count].reshape(6, row_count) for at in order], axis=1
    ).astype(jnp.int32)
    ints = decoded[:3] * 32 + decoded[3:]
    slot_ids = jnp.concatenate(
        [
            (place ^ at) * row_count + lax.broadcasted_iota(jnp.int32, (1, row_count), 1)
            for at in order
        ],
        axis=1,
    )
    ints = jnp.concatenate(
        [ints, (slot_ids < lengths[0]).astype(jnp.int32), jnp.zeros((4, ints.shape[1]), jnp.int32)],
        axis=0,
    )
    ints_col = ints.T
    tables = jnp.concatenate([xbias_table.T, ybias_table.T], axis=1).astype(f32)
    tables = tables.reshape(parts, own_heads, 2 * boxes)

    attended_own, probs, qkv, relkq = attn_fwd(
        place.reshape(1), x_all, w_query, w_key, w_value, rel_table, tables, ints, ints_col
    )

    def row_block(array, at):
        t = order.index(at)
        return array[t * row_count : (t + 1) * row_count]

    _, came = spread(None, {at: row_block(attended_own, at) for at in order})
    attended = jnp.concatenate(by_place([came[at] for at in range(parts)], place), axis=1)
    attn_out = jnp.dot(attended, w_out, preferred_element_type=f32)
    hidden, normed1, inverse1 = layer_norm(x_own.astype(f32) + attn_out, ln1_gain, ln1_bias)
    hidden_low = hidden.astype(bf16)
    up_proj = jnp.dot(hidden_low, w_in, preferred_element_type=f32) + b_in
    activated, gelu_back = jax.vjp(lambda inputs: jax.nn.gelu(inputs, approximate=True), up_proj)
    activated_low = activated.astype(bf16)
    ffn_out = jnp.dot(activated_low, w_down, preferred_element_type=f32)
    normed_out, normed2, inverse2 = layer_norm(hidden + ffn_out, ln2_gain, ln2_bias)
    block_out = normed_out.astype(bf16)[None]
    grad_output = cotangent[0].astype(f32)
    grad_mix, grad_ln2_gain, grad_ln2_bias = norm_backward(grad_output, normed2, inverse2, ln2_gain)
    grad_ffn = grad_mix.astype(bf16)
    grad_act = jnp.dot(grad_ffn, w_down.T, preferred_element_type=f32)
    grad_up = gelu_back(grad_act)[0].astype(bf16)
    grad_b_in = jnp.sum(grad_up, axis=0, dtype=f32)
    grad_hidden = grad_mix + jnp.dot(grad_up, w_in.T, preferred_element_type=f32)
    grad_resid, grad_ln1_gain, grad_ln1_bias = norm_backward(
        grad_hidden, normed1, inverse1, ln1_gain
    )
    grad_attn = grad_resid.astype(bf16)
    grad_att = jnp.dot(grad_attn, w_out.T, preferred_element_type=f32).astype(bf16)

    def column_block(array, at, count):
        size = array.shape[1] // count
        return lax.dynamic_slice_in_dim(array, at * size, size, axis=1)

    _, came = spread(None, {at: column_block(grad_att, place ^ at, parts) for at in order})
    grad_att_own = jnp.concatenate([came[at] for at in order], axis=0)
    dqkv, drel, box_sums = attn_bwd(grad_att_own, qkv, probs, relkq, ints, ints_col)

    def docs_columns(array):
        size = array.shape[1] // docs
        chunks = [array[:, at * size : (at + 1) * size] for at in range(docs)]
        return jnp.concatenate(for_docs(chunks, doc_place), axis=1)

    strips = activated_low.reshape(row_count, docs, parts, -1)
    strips = [
        docs_columns(
            lax.dynamic_index_in_dim(strips, place ^ at, axis=2, keepdims=False).reshape(row_count, -1)
        )
        for at in range(parts)
    ]
    got, came = spread(docs_columns(hidden_low), dict(enumerate(strips)))
    hidden_all = jnp.concatenate([got[at] for at in order], axis=0)
    activated_all = jnp.concatenate([came[at] for at in order], axis=0)
    got, came = spread(grad_ffn, {at: column_block(grad_up, place ^ at, parts) for at in order})
    grad_ffn_all = jnp.concatenate([got[at] for at in order], axis=0)
    grad_up_all = jnp.concatenate([came[at] for at in order], axis=0)
    got, came = spread(
        docs_columns(attended), {at: column_block(grad_attn, place ^ at, parts) for at in order}
    )
    attended_all = jnp.concatenate([got[at] for at in order], axis=0)
    grad_attn_all = jnp.concatenate([came[at] for at in order], axis=0)

    def halves(left, right):
        middle = left.shape[1] // 2
        send = dot(left[:, middle:], right, ((0,), (0,))).astype(bf16)
        keep = dot(left[:, :middle], right, ((0,), (0,))).astype(bf16)
        return keep, send

    bits = bits_of(docs)
    down_part = halve(*halves(activated_all, grad_ffn_all), bits)
    in_part = halve(*halves(hidden_all, grad_up_all), bits)
    out_part = halve(*halves(attended_all, grad_attn_all), bits)

    drel_low = drel.astype(bf16)
    left = docs_columns(jnp.concatenate([x_all, rel_table], axis=0))
    right = jnp.concatenate(
        [
            dqkv,
            jnp.concatenate(
                [drel_low[:, width:], drel_low[:, :width], jnp.zeros((buckets, width), bf16)], axis=1
            ),
        ],
        axis=0,
    )
    grad_rel_table = dot(
        drel_low[:, :width], column_block(w_key, place, parts), ((1,), (1,))
    ) + dot(drel_low[:, width:], column_block(w_query, place, parts), ((1,), (1,)))
    plain, less = box_sums[0::2], box_sums[1::2]

    def box_grad(at):
        plain_here, less_here = plain[:, at : at + boxes], less[:, at : at + boxes]
        later = jnp.pad(less_here[:, 1:], ((0, 0), (0, 1)))
        grad = (plain_here - less_here + later).T
        return lax.dynamic_update_slice(jnp.zeros((boxes, heads), f32), grad, (0, place * own_heads))

    small = jnp.concatenate(
        [
            grad_rel_table.reshape(docs, -1),
            grad_ln1_gain.reshape(docs, -1),
            grad_ln1_bias.reshape(docs, -1),
            grad_ln2_gain.reshape(docs, -1),
            grad_ln2_bias.reshape(docs, -1),
            grad_b_in.reshape(docs, -1),
            box_grad(0).reshape(docs, -1),
            box_grad(boxes).reshape(docs, -1),
        ],
        axis=1,
    ).astype(bf16)
    small_width = small.shape[1]
    across = 3 * width
    small = jnp.pad(small, ((0, 0), (0, -small_width % (8 * across))))
    small = for_docs([small[at] for at in range(docs)], doc_place)
    small = jnp.stack(small).reshape(docs, -1, across)
    keep, send = halves(left, right)
    middle = docs // 2
    chunk_rows = model // docs

    def with_small(main, extra):
        main = main.reshape(middle, chunk_rows, across)
        return jnp.concatenate([main, extra], axis=1).reshape(-1, across)

    qkv_part = halve(with_small(keep, small[:middle]), with_small(send, small[middle:]), bits)

    _, came = spread(None, {at: row_block(dqkv, at) for at in order})
    came = by_place([came[at] for at in range(parts)], place)
    grad_tokens = grad_resid
    for at, weight in enumerate((w_query, w_key, w_value)):
        grad = jnp.concatenate([rows[:, at * width : (at + 1) * width] for rows in came], axis=1)
        grad_tokens = grad_tokens + dot(grad, weight, ((1,), (1,)))

    def whole(part):
        got, _ = spread(part, None)
        return by_place([got[at] for at in range(parts)], place)

    grad_w_down = jnp.concatenate(whole(down_part), axis=0).astype(f32)
    grad_w_in = jnp.concatenate(whole(in_part), axis=1).astype(f32)
    grad_w_out = jnp.concatenate(whole(out_part), axis=1).astype(f32)
    pieces = whole(qkv_part)
    grads = [
        jnp.concatenate(
            [piece[:chunk_rows, at * width : (at + 1) * width] for piece in pieces], axis=1
        ).astype(f32)
        for at in range(3)
    ]
    total = sum(piece[chunk_rows:].astype(f32) for piece in pieces).reshape(-1)
    sizes = [
        (buckets // docs, model),
        (model // docs,),
        (model // docs,),
        (model // docs,),
        (model // docs,),
        (hidden_units // docs,),
        (boxes // docs, heads),
        (boxes // docs, heads),
    ]
    small_out = []
    start = 0
    for size in sizes:
        small_out.append(total[start : start + math.prod(size)].reshape(size))
        start += math.prod(size)
    rel_out, ln1g, ln1b, ln2g, ln2b, b_in_out, xb, yb = small_out
    return (
        block_out, grad_tokens[None], ln1g, ln1b, grads[0], grads[1], grads[2], grad_w_out,
        rel_out, xb, yb, ln2g, ln2b, grad_w_in, b_in_out, grad_w_down,
    )


blocks = 4
slots = (0, 2, 1, 3)


def rows_of(handle, tile=None, column=None):
    array, lead = handle if isinstance(handle, tuple) else (handle, None)
    shape = array.shape[-2:] if tile is None else tile
    column = column or (lambda *grid: 0)
    if lead is None:
        return pl.BlockSpec(shape, lambda *grid: (0, column(*grid)))
    return pl.BlockSpec((None,) + shape, lambda *grid: (lead, 0, column(*grid)))


def array_of(handle):
    return handle[0] if isinstance(handle, tuple) else handle


def full(shape):
    return pl.BlockSpec(shape, lambda *grid: (0,) * len(shape))


def params(limit):
    return pltpu.CompilerParams(vmem_limit_bytes=limit << 20)


def gelu_parts(u):
    root = math.sqrt(2.0 / math.pi)
    inner = jnp.tanh(root * (u + 0.044715 * u * u * u))
    value = 0.5 * u * (1.0 + inner)
    slope = 0.5 * (1.0 + inner) + 0.5 * u * (1.0 - inner * inner) * root * (
        1.0 + 3.0 * 0.044715 * u * u
    )
    return value, slope


def scores_kernel(
    at_ref, x0, x1, x2, x3, i0, i1, i2, i3, wq_ref, wk_ref, wv_ref, rel_ref, tab_ref,
    own_ref, core_ref, far_ref, probs_ref, qkv_ref, relkq_ref, row_ref, col_ref, key_rel,
):
    scale = 1.0 / math.sqrt(192.0)
    step = pl.program_id(0)
    rows = blocks * lanes
    width = wq_ref.shape[1]
    heads = tab_ref.shape[1]
    size = width // heads

    @pl.when(step == 0)
    def _():
        for t, (x_ref, i_ref) in enumerate(zip((x0, x1, x2, x3), (i0, i1, i2, i3))):
            span = slice(t * lanes, (t + 1) * lanes)
            for at, w_ref in enumerate((wq_ref, wk_ref, wv_ref)):
                qkv_ref[span, at * width : (at + 1) * width] = dot(
                    x_ref[...], w_ref[...]
                ).astype(bf16)
            first = jnp.bitwise_xor(at_ref[0], slots[t]) * lanes
            slot = first + lax.broadcasted_iota(jnp.int32, (8, lanes), 1)
            kind = lax.broadcasted_iota(jnp.int32, (8, lanes), 0)
            ints = jnp.where(kind == 3, (slot < at_ref[1]).astype(jnp.int32), i_ref[...])
            row_ref[:, span] = ints
            col_ref[span, :] = ints.astype(f32).T.astype(jnp.int32)
        relkq_ref[:, :width] = dot(rel_ref[...], wk_ref[...]).astype(bf16)
        relkq_ref[:, width:] = dot(rel_ref[...], wq_ref[...]).astype(bf16)
        for h in range(heads):
            cols = slice(width + h * size, width + (h + 1) * size)
            key_rel[h] = (
                dot(qkv_ref[:, cols], relkq_ref[:, cols], ((1,), (1,))).astype(bf16).astype(f32)
            )

    here = pl.ds(pl.multiple_of(step * lanes, lanes), lanes)
    pos_i = col_ref[here, 0:1]
    cx_i = col_ref[here, 1:2]
    cy_i = col_ref[here, 2:3]
    own_row = row_ref[0:1, here]
    ahead, mirror, across, vertical = [], [], [], []
    for t in range(blocks):
        span = slice(t * lanes, (t + 1) * lanes)
        ahead.append(ahead_of(pos_i, row_ref[0:1, span]))
        mirror.append(ahead_of(col_ref[span, 0:1], own_row))
        across.append(jnp.clip(jnp.right_shift(cx_i - row_ref[1:2, span], 5), -32, 31) + 32)
        vertical.append(jnp.clip(jnp.right_shift(cy_i - row_ref[2:3, span], 5), -32, 31) + 96)
    valid = row_ref[3:4, :] > 0
    attended = []
    for h in range(heads):
        cols = slice(h * size, (h + 1) * size)
        query = qkv_ref[here, cols]
        rel_scores = (
            dot(query, relkq_ref[:, cols], ((1,), (1,))).astype(bf16).astype(f32)
        )
        table = jnp.broadcast_to(tab_ref[0, h : h + 1, :], (lanes, lanes))
        pieces = []
        for t in range(blocks):
            span = slice(t * lanes, (t + 1) * lanes)
            content = dot(
                query, qkv_ref[span, width + h * size : width + (h + 1) * size], ((1,), (1,))
            )
            mirrored = pick(key_rel[h, span, :], mirror[t]).T
            bias = pick(table, across[t]) + pick(table, vertical[t])
            pieces.append(
                scale * (content + pick(rel_scores, ahead[t]) + mirrored) + bias
            )
        scores = jnp.where(valid, jnp.concatenate(pieces, axis=1), mask_value)
        top = jnp.max(scores, axis=1, keepdims=True)
        raised = jnp.exp(scores - top)
        probs = (raised * (1.0 / jnp.sum(raised, axis=1, keepdims=True))).astype(bf16)
        probs_ref[h] = probs
        attended.append(
            dot(
                probs, qkv_ref[:, 2 * width + h * size : 2 * width + (h + 1) * size]
            ).astype(bf16)
        )
    attended = jnp.concatenate(attended, axis=1)
    for t, target in enumerate((own_ref, far_ref.at[0], core_ref, far_ref.at[1])):

        @pl.when(step == t)
        def _(target=target):
            target[...] = attended


def scores_call(at, xs, ints, w_query, w_key, w_value, rel_table, tables):
    rows, model = blocks * lanes, w_query.shape[0]
    parts, heads, _ = tables.shape
    width = w_query.shape[1] // parts
    buckets = rel_table.shape[0]
    column = pl.BlockSpec((model, width), lambda i, at: (0, at[0]))
    return pl.pallas_call(
        scores_kernel,
        out_shape=(
            jax.ShapeDtypeStruct((lanes, width), bf16),
            jax.ShapeDtypeStruct((lanes, width), bf16),
            jax.ShapeDtypeStruct((2, lanes, width), bf16),
            jax.ShapeDtypeStruct((heads, rows, rows), bf16),
            jax.ShapeDtypeStruct((rows, 3 * width), bf16),
            jax.ShapeDtypeStruct((buckets, 2 * width), bf16),
            jax.ShapeDtypeStruct((8, rows), jnp.int32),
            jax.ShapeDtypeStruct((rows, 8), jnp.int32),
        ),
        grid_spec=pltpu.PrefetchScalarGridSpec(
            num_scalar_prefetch=1,
            grid=(blocks,),
            in_specs=[rows_of(x) for x in xs]
            + [rows_of(i) for i in ints]
            + [
                column,
                column,
                column,
                full((buckets, model)),
                pl.BlockSpec((1, heads, lanes), lambda i, at: (at[0], 0, 0)),
            ],
            out_specs=[
                full((lanes, width)),
                full((lanes, width)),
                full((2, lanes, width)),
                pl.BlockSpec((heads, lanes, rows), lambda i, at: (0, i, 0)),
                full((rows, 3 * width)),
                full((buckets, 2 * width)),
                full((8, rows)),
                full((rows, 8)),
            ],
            scratch_shapes=[pltpu.VMEM((heads, rows, lanes), f32)],
        ),
        compiler_params=params(56),
        cost_estimate=pl.CostEstimate(
            flops=10**10, transcendentals=10**6, bytes_accessed=8 << 20
        ),
        name="scores",
    )(
        at, *map(array_of, xs), *map(array_of, ints), w_query, w_key, w_value, rel_table, tables
    )


def up_kernel(
    at_ref, a0, a1, a2, a3, x_ref, wout_ref, gain_ref, bias_ref, win_ref, bin_ref,
    far_ref, core_ref, own_ref, act_ref, slope_ref, normed_ref, inverse_ref, attended_ref,
    hidden_low,
):
    step = pl.program_id(0)
    width = a0.shape[1]
    tile = win_ref.shape[1]

    @pl.when(step == 0)
    def _():
        total = x_ref[...].astype(f32)
        for t, piece in enumerate((a0, a1, a2, a3)):
            first = pl.multiple_of(jnp.bitwise_xor(at_ref[0], slots[t]) * width, width)
            total = total + dot(piece[...], wout_ref[pl.ds(first, width), :])
            attended_ref[:, pl.ds(first, width)] = piece[...]
        centered = total - jnp.mean(total, axis=1, keepdims=True)
        inverse = lax.rsqrt(jnp.mean(centered * centered, axis=1, keepdims=True) + norm_eps)
        normed = centered * inverse
        normed_ref[...] = normed
        inverse_ref[...] = jnp.broadcast_to(inverse, inverse_ref.shape)
        hidden = (normed * gain_ref[...] + bias_ref[...]).astype(bf16)
        hidden_low[...] = hidden
        far_ref[0] = hidden
        core_ref[0] = hidden

    value, slope = gelu_parts(dot(hidden_low[...], win_ref[...]) + bin_ref[...])
    value = value.astype(bf16)
    act_ref[...] = value
    slope_ref[...] = slope.astype(bf16)
    strip = tile // blocks
    here = pl.ds(pl.multiple_of(step * strip, strip), strip)
    for t, target in enumerate((own_ref, far_ref.at[1], core_ref.at[1], far_ref.at[2])):
        first = pl.multiple_of(jnp.bitwise_xor(at_ref[0], slots[t]) * strip, strip)
        target[:, here] = act_ref[:, pl.ds(first, strip)]


def up_call(at, pieces, x_own, w_out, gain, bias, w_in, b_in, docs):
    rows, model = x_own.shape
    units = w_in.shape[1]
    tile = units // docs
    quarter = units // blocks
    column = lambda i, at: (0, i)
    return pl.pallas_call(
        up_kernel,
        out_shape=(
            jax.ShapeDtypeStruct((3, rows, model), bf16),
            jax.ShapeDtypeStruct((2, rows, model), bf16),
            jax.ShapeDtypeStruct((rows, quarter), bf16),
            jax.ShapeDtypeStruct((rows, units), bf16),
            jax.ShapeDtypeStruct((rows, units), bf16),
            jax.ShapeDtypeStruct((rows, model), f32),
            jax.ShapeDtypeStruct((rows, lanes), f32),
            jax.ShapeDtypeStruct((rows, model), bf16),
        ),
        grid_spec=pltpu.PrefetchScalarGridSpec(
            num_scalar_prefetch=1,
            grid=(docs,),
            in_specs=[rows_of(piece) for piece in pieces]
            + [
                full((rows, model)),
                full((model, model)),
                full((1, model)),
                full((1, model)),
                pl.BlockSpec((model, tile), column),
                pl.BlockSpec((1, tile), column),
            ],
            out_specs=[
                full((3, rows, model)),
                full((2, rows, model)),
                full((rows, quarter)),
                pl.BlockSpec((rows, tile), column),
                pl.BlockSpec((rows, tile), column),
                full((rows, model)),
                full((rows, lanes)),
                full((rows, model)),
            ],
            scratch_shapes=[pltpu.VMEM((rows, model), bf16)],
        ),
        compiler_params=params(40),
        cost_estimate=pl.CostEstimate(
            flops=4 * 10**9, transcendentals=10**6, bytes_accessed=12 << 20
        ),
        name="up",
    )(at, *map(array_of, pieces), x_own, w_out, gain, bias, w_in, b_in)


def down_kernel(
    at_ref, act_ref, wdown_ref, slope_ref, win_ref, wout_ref, normed_ref, inverse_ref,
    cot_ref, attended_ref, gain1_ref, bias1_ref, gain2_ref, bias2_ref,
    block_ref, own_ref, core_ref, far_ref, resid_ref, upfar_ref, upcore_ref, upown_ref,
    outfar_ref, outcore_ref, outown_ref, sums_ref,
    total, grad_ffn, grad_up,
):
    step = pl.program_id(0)
    steps = pl.num_programs(0) // 2
    rows, tile = slope_ref.shape
    model = block_ref.shape[1]
    width = model // blocks

    @pl.when(step == 0)
    def _():
        total[...] = normed_ref[...] * gain1_ref[...] + bias1_ref[...]

    @pl.when(step < steps)
    def _():
        total[...] += dot(act_ref[...], wdown_ref[...])

    def back(grad, normed, inverse, gain):
        scaled = grad * gain
        return inverse * (
            scaled
            - jnp.mean(scaled, axis=1, keepdims=True)
            - normed * jnp.mean(scaled * normed, axis=1, keepdims=True)
        )

    @pl.when(step == steps - 1)
    def _():
        mixed = total[...]
        centered = mixed - jnp.mean(mixed, axis=1, keepdims=True)
        inverse = lax.rsqrt(jnp.mean(centered * centered, axis=1, keepdims=True) + norm_eps)
        normed = centered * inverse
        block_ref[...] = (normed * gain2_ref[...] + bias2_ref[...]).astype(bf16)
        grad = cot_ref[...].astype(f32)
        sums_ref[2:3, :] = jnp.sum(grad * normed, axis=0, keepdims=True)
        sums_ref[3:4, :] = jnp.sum(grad, axis=0, keepdims=True)
        mix = back(grad, normed, inverse, gain2_ref[...])
        total[...] = mix
        grad_ffn[...] = mix.astype(bf16)
        upfar_ref[0] = mix.astype(bf16)
        upcore_ref[0] = mix.astype(bf16)

    @pl.when(step >= steps)
    def _():
        at = step - steps
        grad = dot(grad_ffn[...], wdown_ref[...], ((1,), (1,))) * slope_ref[...].astype(f32)
        low = grad.astype(bf16)
        total[...] += dot(low, win_ref[...], ((1,), (1,)))
        per = model // tile
        part = at // per
        here = pl.ds(pl.multiple_of((at - part * per) * tile, tile), tile)
        grad_up[jnp.bitwise_xor(part, at_ref[0]), :, here] = low
        sums_ref[pl.ds(4 + part, 1), here] = jnp.sum(low.astype(f32), axis=0, keepdims=True)

    @pl.when(step == 2 * steps - 1)
    def _():
        upown_ref[...] = grad_up[0]
        upcore_ref[1] = grad_up[1]
        upfar_ref[1] = grad_up[2]
        upfar_ref[2] = grad_up[3]
        grad = total[...]
        normed = normed_ref[...]
        sums_ref[0:1, :] = jnp.sum(grad * normed, axis=0, keepdims=True)
        sums_ref[1:2, :] = jnp.sum(grad, axis=0, keepdims=True)
        resid = back(grad, normed, inverse_ref[:, 0:1], gain1_ref[...])
        resid_ref[...] = resid
        low = resid.astype(bf16)
        total[...] = low.astype(f32)
        outfar_ref[:, :model] = attended_ref[...]
        outcore_ref[:, :model] = attended_ref[...]
        targets = (own_ref, core_ref, far_ref.at[0], far_ref.at[1])
        wides = (
            outown_ref, outcore_ref.at[:, pl.ds(model, width)],
            outfar_ref.at[:, pl.ds(model, width)], outfar_ref.at[:, pl.ds(model + width, width)],
        )
        for at, (target, wide) in enumerate(zip(targets, wides)):
            first = pl.multiple_of(jnp.bitwise_xor(at_ref[0], at) * width, width)
            target[...] = dot(low, wout_ref[pl.ds(first, width), :], ((1,), (1,))).astype(bf16)
            wide[...] = total[:, pl.ds(first, width)].astype(bf16)


def down_call(
    at, act, w_down, slope, w_in, w_out, normed, inverse, cotangent, attended,
    gain1, bias1, gain2, bias2, tile,
):
    rows, units = act.shape
    model = w_out.shape[0]
    width = model // blocks
    steps = units // tile
    first = lambda i, at: (0, jnp.minimum(i, steps - 1))
    second = lambda i, at: (0, jnp.maximum(i - steps, 0))
    return pl.pallas_call(
        down_kernel,
        out_shape=(
            jax.ShapeDtypeStruct((rows, model), bf16),
            jax.ShapeDtypeStruct((rows, width), bf16),
            jax.ShapeDtypeStruct((rows, width), bf16),
            jax.ShapeDtypeStruct((2, rows, width), bf16),
            jax.ShapeDtypeStruct((rows, model), f32),
            jax.ShapeDtypeStruct((3, rows, model), bf16),
            jax.ShapeDtypeStruct((2, rows, model), bf16),
            jax.ShapeDtypeStruct((rows, model), bf16),
            jax.ShapeDtypeStruct((rows, model + 2 * width), bf16),
            jax.ShapeDtypeStruct((rows, model + width), bf16),
            jax.ShapeDtypeStruct((rows, width), bf16),
            jax.ShapeDtypeStruct((8, model), f32),
        ),
        grid_spec=pltpu.PrefetchScalarGridSpec(
            num_scalar_prefetch=1,
            grid=(2 * steps,),
            in_specs=[
                pl.BlockSpec((rows, tile), first),
                pl.BlockSpec((tile, model), lambda i, at: (lax.rem(i, steps), 0)),
                pl.BlockSpec((rows, tile), second),
                pl.BlockSpec((model, tile), second),
                full((model, model)),
                full((rows, model)),
                full((rows, lanes)),
                full((rows, model)),
                full((rows, model)),
                full((1, model)),
                full((1, model)),
                full((1, model)),
                full((1, model)),
            ],
            out_specs=[
                full((rows, model)),
                full((rows, width)),
                full((rows, width)),
                full((2, rows, width)),
                full((rows, model)),
                full((3, rows, model)),
                full((2, rows, model)),
                full((rows, model)),
                full((rows, model + 2 * width)),
                full((rows, model + width)),
                full((rows, width)),
                full((8, model)),
            ],
            scratch_shapes=[
                pltpu.VMEM((rows, model), f32),
                pltpu.VMEM((rows, model), bf16),
                pltpu.VMEM((blocks, rows, model), bf16),
            ],
        ),
        compiler_params=params(40),
        cost_estimate=pl.CostEstimate(
            flops=8 * 10**9, transcendentals=0, bytes_accessed=28 << 20
        ),
        name="down",
    )(
        at, act, w_down, slope, w_in, w_out, normed, inverse, cotangent, attended,
        gain1, bias1, gain2, bias2,
    )


def scores_grad_kernel(
    at_ref, g0, g1, g2, g3, qkv_ref, probs_ref, relkq_ref, row_ref, col_ref, wq_ref, wk_ref,
    sums_ref,
    dqkv_ref, core_ref, far_ref, small_ref,
    ga_ref, ds_ref, drel, box_sums,
):
    scale = 1.0 / math.sqrt(192.0)
    rows = blocks * lanes
    heads = probs_ref.shape[0]
    width = g0.shape[1]
    size = width // heads
    span_width = 3 * lanes
    for t, piece in enumerate((g0, g1, g2, g3)):
        ga_ref[t * lanes : (t + 1) * lanes, :] = piece[...]
    drel[...] = jnp.zeros_like(drel)
    box_sums[...] = jnp.zeros_like(box_sums)
    window = lax.broadcasted_iota(jnp.int32, (rows, span_width), 1)
    bucket = lax.broadcasted_iota(jnp.int32, (lanes, lanes), 1)
    label = lax.broadcasted_iota(jnp.int32, (rows, lanes), 1)
    all_pos = col_ref[:, 0:1]
    all_x, all_y = col_ref[:, 1:2], col_ref[:, 2:3]
    sector_x, sector_y = jnp.right_shift(all_x, 5), jnp.right_shift(all_y, 5)
    hot_x = (label == sector_x).astype(bf16)
    hot_y = (label == sector_y + 64).astype(bf16)
    hot_both = ((label == sector_x) | (label == sector_y + 64)).astype(bf16)

    def histogram(sums, total, at, base_row):
        first = at - base_row + (lanes - 1) - bucket
        low = jnp.bitwise_and(first, lanes - 1)
        group = jnp.right_shift(first, 7)
        found = jnp.where(
            group == 0,
            pick(sums[:, :lanes], low),
            jnp.where(
                group == 1,
                pick(sums[:, lanes : 2 * lanes], low),
                pick(sums[:, 2 * lanes :], low),
            ),
        )
        found = jnp.where(bucket == 0, total, found)
        later = jnp.where(bucket == lanes - 1, 0.0, pltpu.roll(found, lanes - 1, 1))
        return found - later

    def by_rows(ib, carry):
        here = pl.ds(pl.multiple_of(ib * lanes, lanes), lanes)
        pos_i = col_ref[here, 0:1]
        cx_i, cy_i = col_ref[here, 1:2], col_ref[here, 2:3]
        base = jnp.min(pos_i, axis=0, keepdims=True)
        below = (all_pos <= base - 63 + window).astype(bf16)
        short_x = jnp.bitwise_and(cx_i, 31) < jnp.bitwise_and(row_ref[1:2, :], 31)
        short_y = jnp.bitwise_and(cy_i, 31) < jnp.bitwise_and(row_ref[2:3, :], 31)
        step_x = jnp.right_shift(cx_i, 5) + 32 - bucket
        step_y = jnp.right_shift(cy_i, 5) + 32 - (bucket - 64)
        in_x = (bucket < 64) & (step_x >= 0) & (step_x < 32)
        in_y = (bucket >= 64) & (step_y >= 0) & (step_y < 32)
        seek = jnp.where(in_x, step_x, jnp.where(in_y, step_y + 64, 0))
        inside = in_x | in_y
        for h in range(heads):
            cols = slice(h * size, (h + 1) * size)
            kcols = slice(width + h * size, width + (h + 1) * size)
            vcols = slice(2 * width + h * size, 2 * width + (h + 1) * size)
            probs = probs_ref[h, here, :].astype(f32)
            gained = dot(ga_ref[here, cols], qkv_ref[:, vcols], ((1,), (1,)))
            row_dots = jnp.sum(probs * gained, axis=1, keepdims=True)
            grad = (probs * (gained - row_dots)).astype(bf16)
            ds_ref[h, here, :] = grad
            exact = grad.astype(f32)
            total = jnp.sum(exact, axis=1, keepdims=True)
            rel = histogram(dot(grad, below), total, pos_i, base)
            rel = (scale * rel).astype(bf16)
            dqkv_ref[here, cols] = (
                scale * dot(grad, qkv_ref[:, kcols]) + dot(rel, relkq_ref[:, cols])
            ).astype(bf16)
            drel[:, cols] += dot(rel, qkv_ref[here, cols], ((0,), (0,)))
            grad_x = jnp.where(short_x, exact, 0.0).astype(bf16)
            grad_y = jnp.where(short_y, exact, 0.0).astype(bf16)
            plain = dot(grad, hot_both)
            less = dot(grad_x, hot_x) + dot(grad_y, hot_y)
            plain = jnp.where(inside, pick(plain, seek), 0.0)
            less = jnp.where(inside, pick(less, seek), 0.0)
            box_sums[h : h + 1, :] += jnp.sum(plain, axis=0, keepdims=True)
            box_sums[8 + h : 9 + h, :] += jnp.sum(less, axis=0, keepdims=True)
        return carry

    lax.fori_loop(0, blocks, by_rows, 0)

    def by_columns(jb, carry):
        here = pl.ds(pl.multiple_of(jb * lanes, lanes), lanes)
        pos_j = col_ref[here, 0:1]
        base = jnp.min(pos_j, axis=0, keepdims=True)
        below = (all_pos <= base - 63 + window).astype(bf16)
        for h in range(heads):
            cols = slice(h * size, (h + 1) * size)
            kcols = slice(width + h * size, width + (h + 1) * size)
            vcols = slice(2 * width + h * size, 2 * width + (h + 1) * size)
            grad = ds_ref[h, :, here]
            total = dot(grad, jnp.ones((rows, lanes), bf16), ((0,), (0,)))
            sums = dot(grad, below, ((0,), (0,)))
            mirror = (scale * histogram(sums, total, pos_j, base)).astype(bf16)
            dqkv_ref[here, kcols] = (
                scale * dot(grad, qkv_ref[:, cols], ((0,), (0,)))
                + dot(mirror, relkq_ref[:, kcols])
            ).astype(bf16)
            drel[:, kcols] += dot(mirror, qkv_ref[here, kcols], ((0,), (0,)))
            dqkv_ref[here, vcols] = dot(
                probs_ref[h, :, here], ga_ref[:, cols], ((0,), (0,))
            ).astype(bf16)
        return carry

    lax.fori_loop(0, blocks, by_columns, 0)
    far_ref[0] = dqkv_ref[lanes : 2 * lanes, :]
    core_ref[...] = dqkv_ref[2 * lanes : 3 * lanes, :]
    far_ref[1] = dqkv_ref[3 * lanes : 4 * lanes, :]
    keys, queries = drel[:, :width].astype(bf16), drel[:, width:].astype(bf16)
    dqkv_ref[rows:, :width] = queries
    dqkv_ref[rows:, width : 2 * width] = keys
    dqkv_ref[rows:, 2 * width :] = jnp.zeros((lanes, width), bf16)

    docs, small_rows, small_width = small_ref.shape
    per = lanes // docs
    table = (
        dot(keys, wk_ref[...], ((1,), (1,))) + dot(queries, wq_ref[...], ((1,), (1,)))
    ).astype(bf16)
    plain, less = box_sums[0:8, :], box_sums[8:16, :]
    place_lane = lax.broadcasted_iota(jnp.int32, (8, lanes), 1)
    later = jnp.where(
        jnp.bitwise_and(place_lane, 63) == 63, 0.0, pltpu.roll(less, lanes - 1, 1)
    )
    boxes = (plain - less + later).astype(bf16)
    row_at = lax.broadcasted_iota(jnp.int32, (8, lanes), 0)
    chosen = ((place_lane == at_ref[0] * heads + row_at) & (row_at < heads)).astype(bf16)
    boxes = dot(boxes, chosen, ((0,), (0,)))
    small_ref[...] = jnp.zeros_like(small_ref)
    model = table.shape[1]
    rest = model - small_width
    sums = sums_ref[...]
    share = model // docs
    for chunk in range(docs):
        small_ref[chunk, 0:per, :] = table[chunk * per : (chunk + 1) * per, :small_width].astype(f32)
        small_ref[chunk, per : 2 * per, 0:rest] = (
            table[chunk * per : (chunk + 1) * per, small_width:].astype(f32)
        )
        for at in range(4):
            small_ref[chunk, per + at : per + at + 1, rest : rest + share] = (
                sums[at : at + 1, chunk * share : (chunk + 1) * share]
            )
        bin_at = chunk * blocks * share
        for at in range(blocks):
            first = bin_at + at * share
            line, first = first // model, first % model
            small_ref[chunk, per + at : per + at + 1, rest + share : rest + 2 * share] = (
                sums[4 + line : 5 + line, first : first + share]
            )
        count = lanes // 2 // docs
        for axis in range(2):
            begin = axis * 64 + chunk * count
            lane = rest + (2 + axis) * share
            small_ref[chunk, per : per + count, lane : lane + lanes] = boxes[begin : begin + count, :]


def scores_grad_call(at, pieces, qkv, probs, relkq, row, col, w_query, w_key, sums, docs):
    rows = blocks * lanes
    heads = probs.shape[0]
    model = w_query.shape[0]
    width = model // blocks
    buckets = relkq.shape[0]
    column = pl.BlockSpec((model, width), lambda i, at: (0, at[0]))
    return pl.pallas_call(
        scores_grad_kernel,
        out_shape=(
            jax.ShapeDtypeStruct((rows + buckets, 3 * width), bf16),
            jax.ShapeDtypeStruct((lanes, 3 * width), bf16),
            jax.ShapeDtypeStruct((2, lanes, 3 * width), bf16),
            jax.ShapeDtypeStruct((docs, 2 * buckets // docs, 3 * width), f32),
        ),
        grid_spec=pltpu.PrefetchScalarGridSpec(
            num_scalar_prefetch=1,
            grid=(1,),
            in_specs=[rows_of(piece) for piece in pieces]
            + [
                full((rows, 3 * width)),
                full((heads, rows, rows)),
                full((buckets, 2 * width)),
                full((8, rows)),
                full((rows, 8)),
                column,
                column,
                full((8, model)),
            ],
            out_specs=[
                full((rows + buckets, 3 * width)),
                full((lanes, 3 * width)),
                full((2, lanes, 3 * width)),
                full((docs, 2 * buckets // docs, 3 * width)),
            ],
            scratch_shapes=[
                pltpu.VMEM((rows, width), bf16),
                pltpu.VMEM((heads, rows, rows), bf16),
                pltpu.VMEM((buckets, 2 * width), f32),
                pltpu.VMEM((16, lanes), f32),
            ],
        ),
        compiler_params=params(56),
        cost_estimate=pl.CostEstimate(
            flops=2 * 10**10, transcendentals=0, bytes_accessed=8 << 20
        ),
        name="scores_grad",
    )(at, *map(array_of, pieces), qkv, probs, relkq, row, col, w_query, w_key, sums)


def weight_grad_call(at, lefts, rights, bits, extra=None, right_column=0, right_width=None, name="weight_grad"):
    count = 1 << len(bits)
    model = array_of(lefts[0]).shape[-1]
    chunk = lanes
    width = right_width or array_of(rights[0]).shape[-1]
    pieces = len(lefts)
    tail = 0 if extra is None else extra.shape[1]
    per = 2
    steps = count // per
    half = steps // 2

    def offset(p):
        total = 0
        for place, bit in enumerate(bits):
            total = total + jnp.bitwise_and(jnp.right_shift(p, len(bits) - 1 - place), 1) * bit
        return total

    def chunk_of(i, at, which):
        p = lax.rem(i + half, steps) * per + which
        return jnp.bitwise_xor(at[1], offset(p))

    def kernel(at_ref, *refs):
        left_refs, refs = refs[: pieces * per], refs[pieces * per :]
        right_refs, refs = refs[:pieces], refs[pieces:]
        if extra is not None:
            extra_refs, refs = refs[:per], refs[per:]
        keep_ref, send_ref, right_all = refs
        step = pl.program_id(0)

        @pl.when(step == 0)
        def _():
            for at, ref in enumerate(right_refs):
                right_all[at * lanes : (at + 1) * lanes, :] = ref[...]

        left = jnp.concatenate(
            [
                jnp.concatenate([left_refs[at * per + which][...] for which in range(per)], axis=1)
                for at in range(pieces)
            ],
            axis=0,
        )
        result = dot(left, right_all[...], ((0,), (0,))).astype(bf16)
        for target, mine in ((send_ref, step < half), (keep_ref, step >= half)):

            @pl.when(mine)
            def _(target=target):
                for which in range(per):
                    target[which, :chunk, :] = result[which * chunk : (which + 1) * chunk, :]
                    if extra is not None:
                        target[which, chunk:, :] = extra_refs[which][...].astype(bf16)

    in_specs, operands = [], []
    for handle in lefts:
        for which in range(per):
            in_specs.append(
                rows_of(handle, (lanes, chunk), lambda i, at, which=which: chunk_of(i, at, which))
            )
            operands.append(array_of(handle))
    for handle in rights:
        column = handle[2] if isinstance(handle, tuple) and len(handle) == 3 else right_column
        handle = handle[:2] if isinstance(handle, tuple) and handle[1] is not None else array_of(handle)
        in_specs.append(rows_of(handle, (lanes, width), lambda i, at, column=column: column))
        operands.append(array_of(handle))
    if extra is not None:
        for which in range(per):
            in_specs.append(
                pl.BlockSpec(
                    (None, tail, width), lambda i, at, which=which: (chunk_of(i, at, which), 0, 0)
                )
            )
            operands.append(extra)
    shape = jax.ShapeDtypeStruct((count // 2, chunk + tail, width), bf16)
    block = (per, chunk + tail, width)
    return pl.pallas_call(
        kernel,
        out_shape=(shape, shape),
        grid_spec=pltpu.PrefetchScalarGridSpec(
            num_scalar_prefetch=1,
            grid=(steps,),
            in_specs=in_specs,
            out_specs=[
                pl.BlockSpec(block, lambda i, at: (jnp.maximum(i - half, 0), 0, 0)),
                pl.BlockSpec(block, lambda i, at: (jnp.minimum(i, half - 1), 0, 0)),
            ],
            scratch_shapes=[pltpu.VMEM((pieces * lanes, width), bf16)],
        ),
        compiler_params=params(40),
        cost_estimate=pl.CostEstimate(
            flops=2 * pieces * lanes * model * width,
            transcendentals=0,
            bytes_accessed=2 * (pieces * lanes + model) * (model + width),
        ),
        name=name,
    )(at, *operands)


def tokens_grad_kernel(at_ref, d0, d1, d2, d3, resid_ref, wq_ref, wk_ref, wv_ref, out_ref):
    step = pl.program_id(0)
    width = wq_ref.shape[1]

    @pl.when(step == 0)
    def _():
        out_ref[...] = resid_ref[...]

    for t, piece in enumerate((d0, d1, d2, d3)):

        @pl.when(step == t)
        def _(piece=piece):
            total = out_ref[...]
            for at, w_ref in enumerate((wq_ref, wk_ref, wv_ref)):
                total = total + dot(
                    piece[:, at * width : (at + 1) * width], w_ref[...], ((1,), (1,))
                )
            out_ref[...] = total


def tokens_grad_call(at, pieces, resid, w_query, w_key, w_value):
    rows, model = resid.shape
    width = model // blocks
    tile = (rows, 3 * width)

    def column(i, at):
        offset = jnp.where(i == 1, 2, jnp.where(i == 2, 1, i))
        return (0, jnp.bitwise_xor(at[0], offset))

    weight = pl.BlockSpec((model, width), column)
    return pl.pallas_call(
        tokens_grad_kernel,
        out_shape=jax.ShapeDtypeStruct((rows, model), f32),
        grid_spec=pltpu.PrefetchScalarGridSpec(
            num_scalar_prefetch=1,
            grid=(blocks,),
            in_specs=[rows_of(piece, tile) for piece in pieces]
            + [full((rows, model)), weight, weight, weight],
            out_specs=full((rows, model)),
        ),
        compiler_params=params(40),
        cost_estimate=pl.CostEstimate(
            flops=8 * 10**8, transcendentals=0, bytes_accessed=8 << 20
        ),
        name="tokens_grad",
    )(at, *map(array_of, pieces), resid, w_query, w_key, w_value)


def halve_chunks(keep, send, bits):
    for place, bit in enumerate(bits):
        came = swap(send, "docs", bit)
        total = lambda part: (keep[part].astype(f32) + came[part].astype(f32)).astype(bf16)
        middle = keep.shape[0] // 2
        if place + 1 < len(bits):
            send = total(slice(middle, None))
            keep = total(slice(0, middle))
        else:
            keep = total(slice(None))
    return keep[0]


def across_core(own, core, far):
    came_far = swap(far, "blk", 2)
    return came_far


def shards_tiles(
    tokens, lengths, positions, token_boxes, ln1_gain, ln1_bias, w_query, w_key, w_value, w_out,
    rel_table, xbias_table, ybias_table, ln2_gain, ln2_bias, w_in, b_in, w_down, cotangent,
):
    row_count, model = tokens.shape[1:]
    docs = lax.axis_size("docs")
    place = lax.axis_index("blk")
    doc_place = lax.axis_index("docs")
    heads = xbias_table.shape[1]
    boxes = xbias_table.shape[0]
    units = w_in.shape[1]
    width = model // blocks
    bits = bits_of(docs)
    other = [bits[1], bits[0]] + bits[2:]
    x_own = tokens[0]

    x_far = swap(x_own, "blk", 2)
    own_ints = jnp.concatenate(
        [
            positions,
            jnp.right_shift(token_boxes[0] + token_boxes[2], 1),
            jnp.right_shift(token_boxes[1] + token_boxes[3], 1),
            jnp.zeros((5, row_count), jnp.int32),
        ],
        axis=0,
    )
    ints_far = swap(own_ints, "blk", 2)
    x_core, ints_core = swap(x_own, "blk", 1), swap(own_ints, "blk", 1)
    x_both, ints_both = swap(x_far, "blk", 1), swap(ints_far, "blk", 1)
    xs = (x_own, x_far, x_core, x_both)
    tables = jnp.concatenate([xbias_table.T, ybias_table.T], axis=1).astype(f32)
    tables = tables.reshape(blocks, heads // blocks, 2 * boxes)
    at = jnp.stack([place.astype(jnp.int32), lengths[0]])
    spot = jnp.stack([place, doc_place]).astype(jnp.int32)
    att_own, att_core, att_far, probs, qkv, relkq, row, col = scores_call(
        at, xs, (own_ints, ints_far, ints_core, ints_both), w_query, w_key, w_value, rel_table, tables
    )

    came_far = swap(att_far, "blk", 2)
    came_core = swap(att_core, "blk", 1)
    came_both = swap(came_far, "blk", 1)
    line = lambda vector: vector.reshape(1, -1)
    far1, core1, act_own, act, slope, normed1, inverse1, attended = up_call(
        spot, (att_own, (came_far, 0), came_core, (came_both, 1)), x_own, w_out,
        line(ln1_gain), line(ln1_bias), w_in, line(b_in), docs,
    )
    got_far1 = swap(far1, "blk", 2)
    (
        block_out, ga_own, ga_core, ga_far, grad_resid, far2, core2, up_own,
        far3, core3, gattn_own, sums,
    ) = down_call(
        spot, act, w_down, slope, w_in, w_out, normed1, inverse1, cotangent[0], attended,
        line(ln1_gain), line(ln1_bias), line(ln2_gain), line(ln2_bias), units // docs,
    )
    came_far = swap(ga_far, "blk", 2)
    got_far2 = swap(far2, "blk", 2)
    got_core1, got_both1 = swap(core1, "blk", 1), swap(got_far1, "blk", 1)
    came_core = swap(ga_core, "blk", 1)
    came_both = swap(came_far, "blk", 1)
    dqkv, dq_core, dq_far, small = scores_grad_call(
        spot, (ga_own, (came_far, 0), came_core, (came_both, 1)), qkv, probs, relkq, row, col,
        w_query, w_key, sums, docs,
    )
    got_core2, got_both2 = swap(core2, "blk", 1), swap(got_far2, "blk", 1)
    got_far3 = swap(far3, "blk", 2)
    got_core3, got_both3 = swap(core3, "blk", 1), swap(got_far3, "blk", 1)

    hidden_all = [(far1, 0), (got_far1, 0), (got_core1, 0), (got_both1, 0)]
    act_all = [act_own, (got_far1, 1), (got_core1, 1), (got_both1, 2)]
    gffn_all = [(far2, 0), (got_far2, 0), (got_core2, 0), (got_both2, 0)]
    up_all = [up_own, (got_far2, 1), (got_core2, 1), (got_both2, 2)]
    att_all = [far3, got_far3, got_core3, got_both3]
    per = model // width
    gattn_all = [
        gattn_own, (got_far3, None, per), (got_core3, None, per), (got_both3, None, per + 1),
    ]

    down_part = halve_chunks(*weight_grad_call(spot, act_all, gffn_all, bits, name="grad_down"), bits)
    in_part = halve_chunks(*weight_grad_call(spot, hidden_all, up_all, other, name="grad_in"), other)
    out_part = halve_chunks(
        *weight_grad_call(spot, att_all, gattn_all, bits, right_width=width, name="grad_out"), bits
    )
    dq_rows = dqkv.reshape(blocks + 1, lanes, 3 * width)
    rights = [(dq_rows, t) for t in range(blocks + 1)]
    qkv_part = halve_chunks(
        *weight_grad_call(spot, list(xs) + [rel_table], rights, bits, extra=small, name="grad_qkv"), bits
    )

    came_far = swap(dq_far, "blk", 2)
    came_core = swap(dq_core, "blk", 1)
    came_both = swap(came_far, "blk", 1)
    grad_tokens = tokens_grad_call(
        spot, ((dq_rows, 0), (came_far, 0), came_core, (came_both, 1)), grad_resid, w_query, w_key, w_value
    )

    def whole(part):
        far = swap(part, "blk", 2)
        parts = [part, swap(part, "blk", 1), far, swap(far, "blk", 1)]
        return by_place(parts, place)

    grad_w_down = jnp.concatenate(whole(down_part), axis=0).astype(f32)
    grad_w_in = jnp.concatenate(whole(in_part), axis=1).astype(f32)
    grad_w_out = jnp.concatenate(whole(out_part), axis=1).astype(f32)
    pieces = whole(qkv_part)
    grads = [
        jnp.concatenate(
            [piece[:lanes, at * width : (at + 1) * width] for piece in pieces], axis=1
        ).astype(f32)
        for at in range(3)
    ]
    total = sum(piece[lanes:].astype(f32) for piece in pieces)
    buckets = rel_table.shape[0] // docs
    rest = model - 3 * width
    rel_out = jnp.concatenate([total[:buckets], total[buckets:, :rest]], axis=1)
    norms = [total[buckets + k, rest : rest + lanes] for k in range(4)]
    b_in_out = total[buckets : buckets + blocks, rest + lanes : rest + 2 * lanes].reshape(-1)
    box_rows = boxes // docs
    xb = total[buckets : buckets + box_rows, rest + 2 * lanes : rest + 2 * lanes + heads]
    yb = total[buckets : buckets + box_rows, rest + 3 * lanes : rest + 3 * lanes + heads]
    return (
        block_out[None], grad_tokens[None], norms[0], norms[1], grads[0], grads[1], grads[2], grad_w_out,
        rel_out, xb, yb, norms[2], norms[3], grad_w_in, b_in_out, grad_w_down,
    )


def choose(*args):
    docs, parts = lax.axis_size("docs"), lax.axis_size("blk")
    tokens, w_in = args[0], args[15]
    model, units = w_in.shape
    fits = (
        parts == blocks
        and tokens.shape[1] == lanes
        and model // docs == lanes
        and units // docs == parts * lanes
        and docs & (docs - 1) == 0
        and docs > 2
        and units == blocks * model
    )
    return (shards_tiles if fits else shards)(*args)


def solution(mesh):
    rows = P("docs", "blk", None)
    placed = (
        rows, P("docs"), P("docs", "blk"), P(None, "docs", "blk"),
        *([P()] * 14), rows,
    )
    over_docs, over_docs2 = P("docs"), P("docs", None)
    return jax.shard_map(
        choose,
        mesh=mesh,
        in_specs=placed,
        out_specs=(
            rows, rows, over_docs, over_docs, over_docs2, over_docs2, over_docs2, over_docs2,
            over_docs2, over_docs2, over_docs2, over_docs, over_docs, over_docs2, over_docs, over_docs2,
        ),
        check_vma=False,
    )
```

profile of v0, /device:TPU:0, one launch (start us, length us, event | category | flops | bytes accessed | tf_op | source)
XLA Modules:
  0.0 313.2 jit_solution(4404873965480382188)
XLA Ops:
  0.6 3.0 collective-permute-start
  4.4 5.7 %collective-permute-done.x1.refs_2_.refs_3_ = bf16[128,1024]{1,0:T(8,128)(2,1)S(1)} collective-permute-done((bf16[128,1024]{1,0:T(8,128)(2,1)}, bf16[128,1024]{1,0:T(8,128)(2,1)S(1)}, u32[]{:S(2)}, u32[]{:S(2)}) %collective-permute-start) | collective-permute-done | bytes 262176 | tf_op jit(solution)/shard_map/ppermute | solution.py:308
  17.6 26.5 %scores.1 = (bf16[128,256]{1,0:T(8,128)(2,1)}, bf16[128,256]{1,0:T(8,128)(2,1)}, bf16[2,128,256]{2,1,0:T(8,128)(2,1)}, bf16[4,512,512]{2,1,0:T(8,128)(2,1)}, bf1...) custom-call(s32[2]{0:T(128)} %pad_add_fusion.1.at_ref, ...), custom_call_target="tpu_custom_call" | custom-call | flops 10000000000 | bytes 8388608 | tf_op jit(solution)/shard_map/scores/pallas_call | solution.py:716
  45.4 4.6 %collective-permute-done.6.a1 = bf16[2,128,256]{2,1,0:T(8,128)(2,1)S(1)} collective-permute-done((bf16[2,128,256]{2,1,0:T(8,128)(2,1)}, bf16[2,128,256]{2,1,0:T(8,128)(2,1)S(1)}, u32[]{:S(2)}, u32[]{:S(2)}) %collective-permute-start.6) | collective-permute-done | bytes 131104 | tf_op jit(solution)/shard_map/ppermute | solution.py:308
  54.1 9.3 %up.1 = (bf16[3,128,1024]{2,1,0:T(8,128)(2,1)S(1)}, bf16[2,128,1024]{2,1,0:T(8,128)(2,1)S(1)}, bf16[128,1024]{1,0:T(8,128)(2,1)S(1)}, bf16[128,4096]{1,0:T(8,128...) custom-call(s32[2]{0:T(128)S(1)} %pad_add_fusion.at_ref, ...), custom_call_target="tpu_custom_call" | custom-call | flops 4000000000 | bytes 12582912 | tf_op jit(solution)/shard_map/up/pallas_call | solution.py:805
  65.0 20.3 %down.1 = (bf16[128,1024]{1,0:T(8,128)(2,1)}, bf16[128,256]{1,0:T(8,128)(2,1)S(1)}, bf16[128,256]{1,0:T(8,128)(2,1)S(1)}, bf16[2,128,256]{2,1,0:T(8,128)(2,1)S(1...) custom-call(s32[2]{0:T(128)S(1)} %pad_add_fusion.at_ref, ...), custom_call_target="tpu_custom_call" | custom-call | flops 8000000000 | bytes 29360128 | tf_op jit(solution)/shard_map/down/pallas_call | solution.py:943
  90.0 4.6 %collective-permute-done.9.g1 = bf16[2,128,256]{2,1,0:T(8,128)(2,1)S(1)} collective-permute-done((bf16[2,128,256]{2,1,0:T(8,128)(2,1)S(1)}, bf16[2,128,256]{2,1,0:T(8,128)(2,1)S(1)}, u32[]{:S(2)}, u32[]{:S(2)}) %collective-permute-start.9) | collective-permute-done | bytes 131104 | tf_op jit(solution)/shard_map/ppermute | solution.py:308
  96.8 30.2 %scores_grad.1 = (bf16[640,768]{1,0:T(8,128)(2,1)}, bf16[128,768]{1,0:T(8,128)(2,1)}, bf16[2,128,768]{2,1,0:T(8,128)(2,1)}, f32[8,32,768]{2,1,0:T(8,128)}) custom-call(s32[2]{0:T(128)} %copy-done.26, bf16[128,256]{1,0:T(8,128)(2,1)} %copy-done.39, bf16[2,128,256]{2,1,0:T(8,128)(2,1)} %copy-done.46, bf16[128,256]{1,0:T(8,128)(2,1)} %copy-done.48, ...), custom_call_target="tpu_custom_call" | custom-call | flops 20000000000 | bytes 8388608 | tf_op jit(solution)/shard_map/scores_grad/pallas_call | solution.py:1175
  129.4 3.9 %grad_qkv.1 = (bf16[4,160,768]{2,1,0:T(8,128)(2,1)S(1)}, bf16[4,160,768]{2,1,0:T(8,128)(2,1)S(1)}) custom-call(s32[2]{0:T(128)S(1)} %copy-done.27, bf16[128,1024]{1,0:T(8,128)(2,1)S(1)} %bitcast.50, bf16[128,1024]{1,0:T(8,128)(2,1)S(1)} %bitcast.51, bf16[128,1024]{1,0:T(8,128)(2,1)S(1)} %copy-done.11, bf16[128,1024]{1,0:T(8,128)(2,1)S(1)} %copy-done.11, ...), custom_call_target="tpu_custom_call" | custom-call | flops 1006632960 | bytes 5963776 | tf_op jit(solution)/shard_map/grad_qkv/pallas_call | solution.py:1291
  136.0 9.9 %collective-permute-done.21.refs_2_.refs_3_.refs_9_ = bf16[128,1536]{1,0:T(8,128)(2,1)S(1)} collective-permute-done((bf16[128,1536]{1,0:T(8,128)(2,1)S(1)}, bf16[128,1536]{1,0:T(8,128)(2,1)S(1)}, u32[]{:S(2)}, u32[]{:S(2)}) %collective-permute-start.21) | collective-permute-done | bytes 393248 | tf_op jit(solution)/shard_map/ppermute | solution.py:308
  152.7 5.2 %collective-permute-done.15 = bf16[4,160,768]{2,1,0:T(8,128)(2,1)S(1)} collective-permute-done((bf16[4,160,768]{2,1,0:T(8,128)(2,1)S(1)}, bf16[4,160,768]{2,1,0:T(8,128)(2,1)S(1)}, u32[]{:S(2)}, u32[]{:S(2)}) %collective-permute-start.15) | collective-permute-done | bytes 983072 | tf_op jit(solution)/shard_map/ppermute | solution.py:308
  159.8 3.1 collective-permute-done.24
  164.6 26.5 %collective-permute-done.12.d1 = bf16[2,128,768]{2,1,0:T(8,128)(2,1)S(1)} collective-permute-done((bf16[2,128,768]{2,1,0:T(8,128)(2,1)S(1)}, bf16[2,128,768]{2,1,0:T(8,128)(2,1)S(1)}, u32[]{:S(2)}, u32[]{:S(2)}) %collective-permute-start.12) | collective-permute-done | bytes 393248 | tf_op jit(solution)/shard_map/ppermute | solution.py:308
  196.4 3.2 %collective-permute-done.26 = bf16[1,128,256]{2,1,0:T(8,128)(2,1)S(1)} collective-permute-done((bf16[1,128,256]{2,1,0:T(8,128)(2,1)S(1)}, bf16[1,128,256]{2,1,0:T(8,128)(2,1)S(1)}, u32[]{:S(2)}, u32[]{:S(2)}) %collective-permute-start.26) | collective-permute-done | bytes 65568 | tf_op jit(solution)/shard_map/ppermute | solution.py:308
  206.6 5.3 %collective-permute-done.17 = bf16[1,160,768]{2,1,0:T(8,128)(2,1)} collective-permute-done((bf16[1,160,768]{2,1,0:T(8,128)(2,1)}, bf16[1,160,768]{2,1,0:T(8,128)(2,1)}, u32[]{:S(2)}, u32[]{:S(2)}) %collective-permute-start.17) | collective-permute-done | bytes 245792 | tf_op jit(solution)/shard_map/ppermute | solution.py:308
  222.4 4.9 %tokens_grad.1 = f32[128,1024]{1,0:T(8,128)} custom-call(s32[2]{0:T(128)S(1)} %copy-done.27, bf16[5,128,768]{2,1,0:T(8,128)(2,1)S(1)} %bitcast.45, bf16[2,128,768]{2,1,0:T(8,128)(2,1)S(1)} %copy-done.21, bf16[128,768]{1,0:T(8,128)(2,1)S(1)} %collective-permute-done.13.d2, bf16[2,128,768]{2,1,0:T(8,128)(2,1)S(1)} %copy-done.23, f32[128,1024]{1,0:T(8,128)S(1)} %copy-done.19, ...), custom_call_target="tpu_custom_call" | custom-call | flops 800000000 | bytes 8388608 | tf_op jit(solution)/shard_map/tokens_grad/pallas_call | solution.py:1344
  229.7 4.4 %grad_down.1 = (bf16[4,128,1024]{2,1,0:T(8,128)(2,1)S(1)}, bf16[4,128,1024]{2,1,0:T(8,128)(2,1)S(1)}) custom-call(s32[2]{0:T(128)S(1)} %copy-done.27, bf16[128,1024]{1,0:T(8,128)(2,1)S(1)} %copy-done.9, bf16[128,1024]{1,0:T(8,128)(2,1)S(1)} %copy-done.9, bf16[3,128,1024]{2,1,0:T(8,128)(2,1)S(1)} %collective-permute-done.30.refs_2_.refs_3_, ...), custom_call_target="tpu_custom_call" | custom-call | flops 1073741824 | bytes 6291456 | tf_op jit(solution)/shard_map/grad_down/pallas_call | solution.py:1291
  234.7 4.6 %grad_in.1 = (bf16[4,128,1024]{2,1,0:T(8,128)(2,1)S(1)}, bf16[4,128,1024]{2,1,0:T(8,128)(2,1)S(1)}) custom-call(s32[2]{0:T(128)S(1)} %copy-done.27, bf16[3,128,1024]{2,1,0:T(8,128)(2,1)S(1)} %get-tuple-element.86.refs_0_.refs_1_, bf16[3,128,1024]{2,1,0:T(8,128)(2,1)S(1)} %get-tuple-element.86.refs_0_.refs_1_, ...), custom_call_target="tpu_custom_call" | custom-call | flops 1073741824 | bytes 6291456 | tf_op jit(solution)/shard_map/grad_in/pallas_call | solution.py:1291
  239.9 19.4 %collective-permute-done.42 = bf16[4,128,1024]{2,1,0:T(8,128)(2,1)S(1)} collective-permute-done((bf16[4,128,1024]{2,1,0:T(8,128)(2,1)S(1)}, bf16[4,128,1024]{2,1,0:T(8,128)(2,1)S(1)}, u32[]{:S(2)}, u32[]{:S(2)}) %collective-permute-start.42) | collective-permute-done | bytes 1048608 | tf_op jit(solution)/shard_map/ppermute | solution.py:308
  260.1 5.3 %collective-permute-done.36 = bf16[4,128,1024]{2,1,0:T(8,128)(2,1)S(1)} collective-permute-done((bf16[4,128,1024]{2,1,0:T(8,128)(2,1)S(1)}, bf16[4,128,1024]{2,1,0:T(8,128)(2,1)S(1)}, u32[]{:S(2)}, u32[]{:S(2)}) %collective-permute-start.36) | collective-permute-done | bytes 1048608 | tf_op jit(solution)/shard_map/ppermute | solution.py:308
  268.8 6.7 %collective-permute-done.43 = bf16[2,128,1024]{2,1,0:T(8,128)(2,1)S(1)} collective-permute-done((bf16[2,128,1024]{2,1,0:T(8,128)(2,1)S(1)}, bf16[2,128,1024]{2,1,0:T(8,128)(2,1)S(1)}, u32[]{:S(2)}, u32[]{:S(2)}) %collective-permute-start.43) | collective-permute-done | bytes 524320 | tf_op jit(solution)/shard_map/ppermute | solution.py:308
  280.7 14.8 %collective-permute-done.44 = bf16[1,128,1024]{2,1,0:T(8,128)(2,1)S(1)} collective-permute-done((bf16[1,128,1024]{2,1,0:T(8,128)(2,1)S(1)}, bf16[1,128,1024]{2,1,0:T(8,128)(2,1)S(1)}, u32[]{:S(2)}, u32[]{:S(2)}) %collective-permute-start.44) | collective-permute-done | bytes 262176 | tf_op jit(solution)/shard_map/ppermute | solution.py:308
  296.6 3.9 %collective-permute-done.38 = bf16[1,128,1024]{2,1,0:T(8,128)(2,1)S(1)} collective-permute-done((bf16[1,128,1024]{2,1,0:T(8,128)(2,1)S(1)}, bf16[1,128,1024]{2,1,0:T(8,128)(2,1)S(1)}, u32[]{:S(2)}, u32[]{:S(2)}) %collective-permute-start.38) | collective-permute-done | bytes 262176 | tf_op jit(solution)/shard_map/ppermute | solution.py:308
  303.5 4.8 %collective-permute-done.39 = bf16[128,1024]{1,0:T(8,128)(2,1)S(1)} collective-permute-done((bf16[128,1024]{1,0:T(8,128)(2,1)S(1)}, bf16[128,1024]{1,0:T(8,128)(2,1)S(1)}, u32[]{:S(2)}, u32[]{:S(2)}) %collective-permute-start.39) | collective-permute-done | bytes 262176 | tf_op jit(solution)/shard_map/ppermute | solution.py:308
  (222 shorter events, 80.9 us)
Async XLA Ops:
  3.6 12.5 %collective-permute-start.1 = (bf16[128,1024]{1,0:T(8,128)(2,1)}, bf16[128,1024]{1,0:T(8,128)(2,1)S(1)}, u32[]{:S(2)}, u32[]{:S(2)}) collective-permute-start(bf16[128,1024]{1,0:T(8,128)(2,1)} %bitcast.47), channel_id=1, source_target_pairs={{0,8},{8,0},{16,24},{24,16},{1,9},{9,1},{17,25},{25,17},{2,10},{10... | collective-permute-start | bytes 786440 | tf_op jit(solution)/shard_map/ppermute | solution.py:308
  133.3 24.6 %collective-permute-start.15 = (bf16[4,160,768]{2,1,0:T(8,128)(2,1)S(1)}, bf16[4,160,768]{2,1,0:T(8,128)(2,1)S(1)}, u32[]{:S(2)}, u32[]{:S(2)}) collective-permute-start(bf16[4,160,768]{2,1,0:T(8,128)(2,1)S(1)} %get-tuple-element.80), channel_id=1, source_target_pairs={{0,1},{1,0},{2,3},{3,2},{4,5},{5,4},{6,7},{7,6},{8,9},{9,8},{10,11... | collective-permute-start | bytes 2949128 | tf_op jit(solution)/shard_map/ppermute | solution.py:308
  134.9 11.1 %collective-permute-start.21 = (bf16[128,1536]{1,0:T(8,128)(2,1)S(1)}, bf16[128,1536]{1,0:T(8,128)(2,1)S(1)}, u32[]{:S(2)}, u32[]{:S(2)}) collective-permute-start(bf16[128,1536]{1,0:T(8,128)(2,1)S(1)} %get-tuple-element.81.refs_0_.refs_1_), channel_id=1, source_target_pairs={{0,16},{8,24},{16,0},{24,8},{1,17},{9,25},{17,1},{25,9},{2,18},{10... | collective-permute-start | bytes 1179656 | tf_op jit(solution)/shard_map/ppermute | solution.py:308
  146.4 44.7 %collective-permute-start.30 = (bf16[3,128,1024]{2,1,0:T(8,128)(2,1)S(1)}, bf16[3,128,1024]{2,1,0:T(8,128)(2,1)S(1)}, u32[]{:S(2)}, u32[]{:S(2)}) collective-permute-start(bf16[3,128,1024]{2,1,0:T(8,128)(2,1)S(1)} %get-tuple-element.86.refs_0_.refs_1_), channel_id=1, source_target_pairs={{0,16},{8,24},{16,0},{24,8},{1,17},{9,25},{17,1},{25,9},{2,18},{10... | collective-permute-start | bytes 2359304 | tf_op jit(solution)/shard_map/ppermute | solution.py:308
  147.6 44.8 %collective-permute-start.33 = (bf16[3,128,1024]{2,1,0:T(8,128)(2,1)S(1)}, bf16[3,128,1024]{2,1,0:T(8,128)(2,1)}, u32[]{:S(2)}, u32[]{:S(2)}) collective-permute-start(bf16[3,128,1024]{2,1,0:T(8,128)(2,1)S(1)} %get-tuple-element.89.refs_8_), channel_id=1, source_target_pairs={{0,16},{8,24},{16,0},{24,8},{1,17},{9,25},{17,1},{25,9},{2,18},{10... | collective-permute-start | bytes 2359304 | tf_op jit(solution)/shard_map/ppermute | solution.py:308
  148.5 42.7 %collective-permute-start.12 = (bf16[2,128,768]{2,1,0:T(8,128)(2,1)S(1)}, bf16[2,128,768]{2,1,0:T(8,128)(2,1)S(1)}, u32[]{:S(2)}, u32[]{:S(2)}) collective-permute-start(bf16[2,128,768]{2,1,0:T(8,128)(2,1)S(1)} %copy-done.44), channel_id=1, source_target_pairs={{0,16},{8,24},{16,0},{24,8},{1,17},{9,25},{17,1},{25,9},{2,18},{10... | collective-permute-start | bytes 1179656 | tf_op jit(solution)/shard_map/ppermute | solution.py:308
  152.2 10.8 %collective-permute-start.24 = (bf16[4,128,256]{2,1,0:T(8,128)(2,1)S(1)}, bf16[4,128,256]{2,1,0:T(8,128)(2,1)S(1)}, u32[]{:S(2)}, u32[]{:S(2)}) collective-permute-start(bf16[4,128,256]{2,1,0:T(8,128)(2,1)S(1)} %get-tuple-element.85), channel_id=1, source_target_pairs={{0,1},{1,0},{2,3},{3,2},{4,5},{5,4},{6,7},{7,6},{8,9},{9,8},{10,11... | collective-permute-start | bytes 786440 | tf_op jit(solution)/shard_map/ppermute | solution.py:308
  158.2 34.8 %collective-permute-start.16 = (bf16[2,160,768]{2,1,0:T(8,128)(2,1)S(1)}, bf16[2,160,768]{2,1,0:T(8,128)(2,1)S(1)}, u32[]{:S(2)}, u32[]{:S(2)}) collective-permute-start(bf16[2,160,768]{2,1,0:T(8,128)(2,1)S(1)} %get-tuple-element.101), channel_id=1, source_target_pairs={{0,2},{1,3},{2,0},{3,1},{4,6},{5,7},{6,4},{7,5},{8,10},{9,11},{10,... | collective-permute-start | bytes 1474568 | tf_op jit(solution)/shard_map/ppermute | solution.py:308
  163.0 29.5 %collective-permute-start.25 = (bf16[2,128,256]{2,1,0:T(8,128)(2,1)S(1)}, bf16[2,128,256]{2,1,0:T(8,128)(2,1)S(1)}, u32[]{:S(2)}, u32[]{:S(2)}) collective-permute-start(bf16[2,128,256]{2,1,0:T(8,128)(2,1)S(1)} %get-tuple-element.115), channel_id=1, source_target_pairs={{0,2},{1,3},{2,0},{3,1},{4,6},{5,7},{6,4},{7,5},{8,10},{9,11},{10,... | collective-permute-start | bytes 393224 | tf_op jit(solution)/shard_map/ppermute | solution.py:308
  191.2 11.4 %collective-permute-start.14 = (bf16[2,128,768]{2,1,0:T(8,128)(2,1)S(1)}, bf16[2,128,768]{2,1,0:T(8,128)(2,1)S(1)}, u32[]{:S(2)}, u32[]{:S(2)}) collective-permute-start(bf16[2,128,768]{2,1,0:T(8,128)(2,1)S(1)} %collective-permute-done.12.d1), channel_id=1, source_target_pairs={{0,8},{8,0},{16,24},{24,16},{1,9},{9,1},{17,25},{25,17},{2,10},{10... | collective-permute-start | bytes 1179656 | tf_op jit(solution)/shard_map/ppermute | solution.py:308
  192.4 37.2 %collective-permute-start.32 = (bf16[3,128,1024]{2,1,0:T(8,128)(2,1)S(1)}, bf16[3,128,1024]{2,1,0:T(8,128)(2,1)S(1)}, u32[]{:S(2)}, u32[]{:S(2)}) collective-permute-start(bf16[3,128,1024]{2,1,0:T(8,128)(2,1)S(1)} %collective-permute-done.30.refs_2_.refs_3_), channel_id=1, source_target_pairs={{0,8},{8,0},{16,24},{24,16},{1,9},{9,1},{17,25},{25,17},{2,10},{10... | collective-permute-start | bytes 2359304 | tf_op jit(solution)/shard_map/ppermute | solution.py:308
  192.5 37.2 %collective-permute-start.35 = (bf16[3,128,1024]{2,1,0:T(8,128)(2,1)}, bf16[3,128,1024]{2,1,0:T(8,128)(2,1)}, u32[]{:S(2)}, u32[]{:S(2)}) collective-permute-start(bf16[3,128,1024]{2,1,0:T(8,128)(2,1)} %collective-permute-done.33.refs_9_), channel_id=1, source_target_pairs={{0,8},{8,0},{16,24},{24,16},{1,9},{9,1},{17,25},{25,17},{2,10},{10... | collective-permute-start | bytes 2359304 | tf_op jit(solution)/shard_map/ppermute | solution.py:308
  199.6 12.3 %collective-permute-start.17 = (bf16[1,160,768]{2,1,0:T(8,128)(2,1)}, bf16[1,160,768]{2,1,0:T(8,128)(2,1)}, u32[]{:S(2)}, u32[]{:S(2)}) collective-permute-start(bf16[1,160,768]{2,1,0:T(8,128)(2,1)} %add_convert_fusion.13), channel_id=1, source_target_pairs={{0,4},{1,5},{2,6},{3,7},{4,0},{5,1},{6,2},{7,3},{8,12},{9,13},{10,... | collective-permute-start | bytes 737288 | tf_op jit(solution)/shard_map/ppermute | solution.py:308
  206.1 22.2 %collective-permute-start.31 = (bf16[2,128,1024]{2,1,0:T(8,128)(2,1)}, bf16[2,128,1024]{2,1,0:T(8,128)(2,1)S(1)}, u32[]{:S(2)}, u32[]{:S(2)}) collective-permute-start(bf16[2,128,1024]{2,1,0:T(8,128)(2,1)} %copy-done.31), channel_id=1, source_target_pairs={{0,8},{8,0},{16,24},{24,16},{1,9},{9,1},{17,25},{25,17},{2,10},{10... | collective-permute-start | bytes 1572872 | tf_op jit(solution)/shard_map/ppermute | solution.py:308
  206.1 23.6 %collective-permute-start.34 = (bf16[2,128,1024]{2,1,0:T(8,128)(2,1)}, bf16[2,128,1024]{2,1,0:T(8,128)(2,1)S(1)}, u32[]{:S(2)}, u32[]{:S(2)}) collective-permute-start(bf16[2,128,1024]{2,1,0:T(8,128)(2,1)} %copy-done.30), channel_id=1, source_target_pairs={{0,8},{8,0},{16,24},{24,16},{1,9},{9,1},{17,25},{25,17},{2,10},{10... | collective-permute-start | bytes 1572872 | tf_op jit(solution)/shard_map/ppermute | solution.py:308
  213.4 15.0 %collective-permute-start.18 = (bf16[160,768]{1,0:T(8,128)(2,1)S(1)}, bf16[160,768]{1,0:T(8,128)(2,1)S(1)}, u32[]{:S(2)}, u32[]{:S(2)}) collective-permute-start(bf16[160,768]{1,0:T(8,128)(2,1)S(1)} %fusion.2), channel_id=1, source_target_pairs={{0,16},{8,24},{16,0},{24,8},{1,17},{9,25},{17,1},{25,9},{2,18},{10... | collective-permute-start | bytes 737288 | tf_op jit(solution)/shard_map/ppermute | solution.py:308
  228.2 11.5 %collective-permute-start.20 = (bf16[160,768]{1,0:T(8,128)(2,1)S(1)}, bf16[160,768]{1,0:T(8,128)(2,1)S(1)}, u32[]{:S(2)}, u32[]{:S(2)}) collective-permute-start(bf16[160,768]{1,0:T(8,128)(2,1)S(1)} %fusion.2), channel_id=1, source_target_pairs={{0,8},{8,0},{16,24},{24,16},{1,9},{9,1},{17,25},{25,17},{2,10},{10... | collective-permute-start | bytes 737288 | tf_op jit(solution)/shard_map/ppermute | solution.py:308
  228.4 11.3 %collective-permute-start.19 = (bf16[160,768]{1,0:T(8,128)(2,1)S(1)}, bf16[160,768]{1,0:T(8,128)(2,1)S(1)}, u32[]{:S(2)}, u32[]{:S(2)}) collective-permute-start(bf16[160,768]{1,0:T(8,128)(2,1)S(1)} %collective-permute-done.18), channel_id=1, source_target_pairs={{0,8},{8,0},{16,24},{24,16},{1,9},{9,1},{17,25},{25,17},{2,10},{10... | collective-permute-start | bytes 737288 | tf_op jit(solution)/shard_map/ppermute | solution.py:308
  234.1 25.2 %collective-permute-start.42 = (bf16[4,128,1024]{2,1,0:T(8,128)(2,1)S(1)}, bf16[4,128,1024]{2,1,0:T(8,128)(2,1)S(1)}, u32[]{:S(2)}, u32[]{:S(2)}) collective-permute-start(bf16[4,128,1024]{2,1,0:T(8,128)(2,1)S(1)} %get-tuple-element.95), channel_id=1, source_target_pairs={{0,1},{1,0},{2,3},{3,2},{4,5},{5,4},{6,7},{7,6},{8,9},{9,8},{10,11... | collective-permute-start | bytes 3145736 | tf_op jit(solution)/shard_map/ppermute | solution.py:308
  239.3 26.1 %collective-permute-start.36 = (bf16[4,128,1024]{2,1,0:T(8,128)(2,1)S(1)}, bf16[4,128,1024]{2,1,0:T(8,128)(2,1)S(1)}, u32[]{:S(2)}, u32[]{:S(2)}) collective-permute-start(bf16[4,128,1024]{2,1,0:T(8,128)(2,1)S(1)} %get-tuple-element.92), channel_id=1, source_target_pairs={{0,2},{1,3},{2,0},{3,1},{4,6},{5,7},{6,4},{7,5},{8,10},{9,11},{10,... | collective-permute-start | bytes 3145736 | tf_op jit(solution)/shard_map/ppermute | solution.py:308
  259.7 15.8 %collective-permute-start.43 = (bf16[2,128,1024]{2,1,0:T(8,128)(2,1)S(1)}, bf16[2,128,1024]{2,1,0:T(8,128)(2,1)S(1)}, u32[]{:S(2)}, u32[]{:S(2)}) collective-permute-start(bf16[2,128,1024]{2,1,0:T(8,128)(2,1)S(1)} %get-tuple-element.97), channel_id=1, source_target_pairs={{0,2},{1,3},{2,0},{3,1},{4,6},{5,7},{6,4},{7,5},{8,10},{9,11},{10,... | collective-permute-start | bytes 1572872 | tf_op jit(solution)/shard_map/ppermute | solution.py:308
  265.8 11.8 %collective-permute-start.37 = (bf16[2,128,1024]{2,1,0:T(8,128)(2,1)S(1)}, bf16[2,128,1024]{2,1,0:T(8,128)(2,1)S(1)}, u32[]{:S(2)}, u32[]{:S(2)}) collective-permute-start(bf16[2,128,1024]{2,1,0:T(8,128)(2,1)S(1)} %get-tuple-element.99), channel_id=1, source_target_pairs={{0,1},{1,0},{2,3},{3,2},{4,5},{5,4},{6,7},{7,6},{8,9},{9,8},{10,11... | collective-permute-start | bytes 1572872 | tf_op jit(solution)/shard_map/ppermute | solution.py:308
  275.6 20.0 %collective-permute-start.44 = (bf16[1,128,1024]{2,1,0:T(8,128)(2,1)S(1)}, bf16[1,128,1024]{2,1,0:T(8,128)(2,1)S(1)}, u32[]{:S(2)}, u32[]{:S(2)}) collective-permute-start(bf16[1,128,1024]{2,1,0:T(8,128)(2,1)S(1)} %add_convert_fusion.7), channel_id=1, source_target_pairs={{0,4},{1,5},{2,6},{3,7},{4,0},{5,1},{6,2},{7,3},{8,12},{9,13},{10,... | collective-permute-start | bytes 786440 | tf_op jit(solution)/shard_map/ppermute | solution.py:308
  277.7 22.8 %collective-permute-start.38 = (bf16[1,128,1024]{2,1,0:T(8,128)(2,1)S(1)}, bf16[1,128,1024]{2,1,0:T(8,128)(2,1)S(1)}, u32[]{:S(2)}, u32[]{:S(2)}) collective-permute-start(bf16[1,128,1024]{2,1,0:T(8,128)(2,1)S(1)} %add_convert_fusion.10), channel_id=1, source_target_pairs={{0,4},{1,5},{2,6},{3,7},{4,0},{5,1},{6,2},{7,3},{8,12},{9,13},{10,... | collective-permute-start | bytes 786440 | tf_op jit(solution)/shard_map/ppermute | solution.py:308
  (76 other events, 746.5 us)
where the time goes:
time: 314 us; the launch traced here: 313 us
  waiting for transfers between devices  129 us (41%)
  Pallas kernels  107 us (34%)
  starting transfers between devices  37 us (12%)
  local copies, waits for them, and re-layouts  23.1 us (7%)
  other arithmetic  15.9 us (5%)
    ppermute x48, waiting for transfers between devices, swap(): return lax.ppermute(array, axis, [(i, i ^ by) for i in range(count)])  129 us
    ppermute x48, starting transfers between devices, swap(): return lax.ppermute(array, axis, [(i, i ^ by) for i in range(count)])  37 us
    pallas_call x1, Pallas kernels, scores_grad_call(): pl.pallas_call(scores_grad_kernel, out_shape=(jax.ShapeDtypeStruct((rows...  30.2 us
    pallas_call x1, Pallas kernels, scores_call(): pl.pallas_call(scores_kernel, out_shape=(jax.ShapeDtypeStruct((lanes, wid...  26.5 us
    unnamed x104, local copies, waits for them, and re-layouts  21.2 us
    pallas_call x1, Pallas kernels, down_call(): pl.pallas_call(down_kernel, out_shape=(jax.ShapeDtypeStruct((rows, model)...  20.3 us
    pallas_call x4, Pallas kernels, weight_grad_call(): pl.pallas_call(kernel, out_shape=(shape, shape), grid_spec=pltpu.Prefetch...  15.4 us
    pallas_call x1, Pallas kernels, up_call(): pl.pallas_call(up_kernel, out_shape=(jax.ShapeDtypeStruct((3, rows, model...  9.31 us
  transfers between devices with their start and end apart: 48, of which 21 were waited for; matrix products, arithmetic and copies ran while one was open for 5% of the time, Pallas kernels for 5%

commit v1 on v0

--- a/solution.py
+++ b/solution.py
@@ -1,3 +1,4 @@
+import functools
 import math
 
 import jax
@@ -608,6 +609,14 @@
 
 def full(shape):
     return pl.BlockSpec(shape, lambda *grid: (0,) * len(shape))
+
+
+def cost(us):
+    return pl.CostEstimate(flops=int(us * 3 * 10**8), transcendentals=0, bytes_accessed=0)
+
+
+def ordered(array, *before):
+    return lax.optimization_barrier((array,) + before)[0]
 
 
 def params(limit):
@@ -750,9 +759,7 @@
             scratch_shapes=[pltpu.VMEM((heads, rows, lanes), f32)],
         ),
         compiler_params=params(56),
-        cost_estimate=pl.CostEstimate(
-            flops=10**10, transcendentals=10**6, bytes_accessed=8 << 20
-        ),
+        cost_estimate=cost(25),
         name="scores",
     )(
         at, *map(array_of, xs), *map(array_of, ints), w_query, w_key, w_value, rel_table, tables
@@ -839,81 +846,111 @@
             scratch_shapes=[pltpu.VMEM((rows, model), bf16)],
         ),
         compiler_params=params(40),
-        cost_estimate=pl.CostEstimate(
-            flops=4 * 10**9, transcendentals=10**6, bytes_accessed=12 << 20
-        ),
+        cost_estimate=cost(9),
         name="up",
     )(at, *map(array_of, pieces), x_own, w_out, gain, bias, w_in, b_in)
 
 
+def norm_back(grad, normed, inverse, gain):
+    scaled = grad * gain
+    return inverse * (
+        scaled
+        - jnp.mean(scaled, axis=1, keepdims=True)
+        - normed * jnp.mean(scaled * normed, axis=1, keepdims=True)
+    )
+
+
 def down_kernel(
-    at_ref, act_ref, wdown_ref, slope_ref, win_ref, wout_ref, normed_ref, inverse_ref,
-    cot_ref, attended_ref, gain1_ref, bias1_ref, gain2_ref, bias2_ref,
-    block_ref, own_ref, core_ref, far_ref, resid_ref, upfar_ref, upcore_ref, upown_ref,
-    outfar_ref, outcore_ref, outown_ref, sums_ref,
-    total, grad_ffn, grad_up,
+    act_ref, wdown_ref, normed_ref, cot_ref, gain1_ref, bias1_ref, gain2_ref, bias2_ref,
+    block_ref, mix_ref, low_ref, sums_ref,
 ):
     step = pl.program_id(0)
-    steps = pl.num_programs(0) // 2
-    rows, tile = slope_ref.shape
-    model = block_ref.shape[1]
-    width = model // blocks
 
     @pl.when(step == 0)
     def _():
-        total[...] = normed_ref[...] * gain1_ref[...] + bias1_ref[...]
-
-    @pl.when(step < steps)
+        mix_ref[...] = normed_ref[...] * gain1_ref[...] + bias1_ref[...]
+
+    mix_ref[...] += dot(act_ref[...], wdown_ref[...])
+
+    @pl.when(step == pl.num_programs(0) - 1)
     def _():
-        total[...] += dot(act_ref[...], wdown_ref[...])
-
-    def back(grad, normed, inverse, gain):
-        scaled = grad * gain
-        return inverse * (
-            scaled
-            - jnp.mean(scaled, axis=1, keepdims=True)
-            - normed * jnp.mean(scaled * normed, axis=1, keepdims=True)
-        )
-
-    @pl.when(step == steps - 1)
-    def _():
-        mixed = total[...]
+        mixed = mix_ref[...]
         centered = mixed - jnp.mean(mixed, axis=1, keepdims=True)
         inverse = lax.rsqrt(jnp.mean(centered * centered, axis=1, keepdims=True) + norm_eps)
         normed = centered * inverse
         block_ref[...] = (normed * gain2_ref[...] + bias2_ref[...]).astype(bf16)
         grad = cot_ref[...].astype(f32)
-        sums_ref[2:3, :] = jnp.sum(grad * normed, axis=0, keepdims=True)
-        sums_ref[3:4, :] = jnp.sum(grad, axis=0, keepdims=True)
-        mix = back(grad, normed, inverse, gain2_ref[...])
-        total[...] = mix
-        grad_ffn[...] = mix.astype(bf16)
-        upfar_ref[0] = mix.astype(bf16)
-        upcore_ref[0] = mix.astype(bf16)
-
-    @pl.when(step >= steps)
+        sums_ref[0:1, :] = jnp.sum(grad * normed, axis=0, keepdims=True)
+        sums_ref[1:2, :] = jnp.sum(grad, axis=0, keepdims=True)
+        mix = norm_back(grad, normed, inverse, gain2_ref[...])
+        mix_ref[...] = mix
+        low_ref[...] = mix.astype(bf16)
+
+
+def down_call(act, w_down, normed, cotangent, gain1, bias1, gain2, bias2, tile):
+    rows, units = act.shape
+    model = w_down.shape[1]
+    return pl.pallas_call(
+        down_kernel,
+        out_shape=(
+            jax.ShapeDtypeStruct((rows, model), bf16),
+            jax.ShapeDtypeStruct((rows, model), f32),
+            jax.ShapeDtypeStruct((rows, model), bf16),
+            jax.ShapeDtypeStruct((8, model), f32),
+        ),
+        grid=(units // tile,),
+        in_specs=[
+            pl.BlockSpec((rows, tile), lambda i: (0, i)),
+            pl.BlockSpec((tile, model), lambda i: (i, 0)),
+            full((rows, model)),
+            full((rows, model)),
+        ]
+        + [full((1, model))] * 4,
+        out_specs=[full((rows, model))] * 3 + [full((8, model))],
+        compiler_params=params(40),
+        cost_estimate=cost(8),
+        name="down",
+    )(act, w_down, normed, cotangent, gain1, bias1, gain2, bias2)
+
+
+def back_kernel(
+    at_ref, wdown_ref, slope_ref, win_ref, wout_ref, normed_ref, inverse_ref, mix_ref, ffn_ref,
+    attended_ref, gain1_ref, above_ref,
+    own_ref, core_ref, far_ref, resid_ref, upfar_ref, upcore_ref, upown_ref,
+    outfar_ref, outcore_ref, outown_ref, sums_ref,
+    total, grad_up,
+):
+    step = pl.program_id(0)
+    steps = pl.num_programs(0)
+    rows, tile = slope_ref.shape
+    model = mix_ref.shape[1]
+    width = model // blocks
+
+    @pl.when(step == 0)
     def _():
-        at = step - steps
-        grad = dot(grad_ffn[...], wdown_ref[...], ((1,), (1,))) * slope_ref[...].astype(f32)
-        low = grad.astype(bf16)
-        total[...] += dot(low, win_ref[...], ((1,), (1,)))
-        per = model // tile
-        part = at // per
-        here = pl.ds(pl.multiple_of((at - part * per) * tile, tile), tile)
-        grad_up[jnp.bitwise_xor(part, at_ref[0]), :, here] = low
-        sums_ref[pl.ds(4 + part, 1), here] = jnp.sum(low.astype(f32), axis=0, keepdims=True)
-
-    @pl.when(step == 2 * steps - 1)
+        total[...] = mix_ref[...]
+
+    grad = dot(ffn_ref[...], wdown_ref[...], ((1,), (1,))) * slope_ref[...].astype(f32)
+    low = grad.astype(bf16)
+    total[...] += dot(low, win_ref[...], ((1,), (1,)))
+    per = model // tile
+    part = step // per
+    here = pl.ds(pl.multiple_of((step - part * per) * tile, tile), tile)
+    grad_up[jnp.bitwise_xor(part, at_ref[0]), :, here] = low
+    sums_ref[pl.ds(4 + part, 1), here] = jnp.sum(low.astype(f32), axis=0, keepdims=True)
+
+    @pl.when(step == steps - 1)
     def _():
         upown_ref[...] = grad_up[0]
-        upcore_ref[1] = grad_up[1]
-        upfar_ref[1] = grad_up[2]
-        upfar_ref[2] = grad_up[3]
+        upcore_ref[...] = grad_up[1]
+        upfar_ref[0] = grad_up[2]
+        upfar_ref[1] = grad_up[3]
         grad = total[...]
         normed = normed_ref[...]
         sums_ref[0:1, :] = jnp.sum(grad * normed, axis=0, keepdims=True)
         sums_ref[1:2, :] = jnp.sum(grad, axis=0, keepdims=True)
-        resid = back(grad, normed, inverse_ref[:, 0:1], gain1_ref[...])
+        sums_ref[2:4, :] = above_ref[0:2, :]
+        resid = norm_back(grad, normed, inverse_ref[:, 0:1], gain1_ref[...])
         resid_ref[...] = resid
         low = resid.astype(bf16)
         total[...] = low.astype(f32)
@@ -930,26 +967,21 @@
             wide[...] = total[:, pl.ds(first, width)].astype(bf16)
 
 
-def down_call(
-    at, act, w_down, slope, w_in, w_out, normed, inverse, cotangent, attended,
-    gain1, bias1, gain2, bias2, tile,
+def back_call(
+    at, w_down, slope, w_in, w_out, normed, inverse, mix, grad_ffn, attended, gain1, above, tile,
 ):
-    rows, units = act.shape
+    rows, units = slope.shape
     model = w_out.shape[0]
     width = model // blocks
-    steps = units // tile
-    first = lambda i, at: (0, jnp.minimum(i, steps - 1))
-    second = lambda i, at: (0, jnp.maximum(i - steps, 0))
     return pl.pallas_call(
-        down_kernel,
+        back_kernel,
         out_shape=(
-            jax.ShapeDtypeStruct((rows, model), bf16),
             jax.ShapeDtypeStruct((rows, width), bf16),
             jax.ShapeDtypeStruct((rows, width), bf16),
             jax.ShapeDtypeStruct((2, rows, width), bf16),
             jax.ShapeDtypeStruct((rows, model), f32),
-            jax.ShapeDtypeStruct((3, rows, model), bf16),
             jax.ShapeDtypeStruct((2, rows, model), bf16),
+            jax.ShapeDtypeStruct((rows, model), bf16),
             jax.ShapeDtypeStruct((rows, model), bf16),
             jax.ShapeDtypeStruct((rows, model + 2 * width), bf16),
             jax.ShapeDtypeStruct((rows, model + width), bf16),
@@ -958,30 +990,27 @@
         ),
         grid_spec=pltpu.PrefetchScalarGridSpec(
             num_scalar_prefetch=1,
-            grid=(2 * steps,),
+            grid=(units // tile,),
             in_specs=[
-                pl.BlockSpec((rows, tile), first),
-                pl.BlockSpec((tile, model), lambda i, at: (lax.rem(i, steps), 0)),
-                pl.BlockSpec((rows, tile), second),
-                pl.BlockSpec((model, tile), second),
+                pl.BlockSpec((tile, model), lambda i, at: (i, 0)),
+                pl.BlockSpec((rows, tile), lambda i, at: (0, i)),
+                pl.BlockSpec((model, tile), lambda i, at: (0, i)),
                 full((model, model)),
                 full((rows, model)),
                 full((rows, lanes)),
                 full((rows, model)),
                 full((rows, model)),
+                full((rows, model)),
                 full((1, model)),
-                full((1, model)),
-                full((1, model)),
-                full((1, model)),
+                full((8, model)),
             ],
             out_specs=[
-                full((rows, model)),
                 full((rows, width)),
                 full((rows, width)),
                 full((2, rows, width)),
                 full((rows, model)),
-                full((3, rows, model)),
                 full((2, rows, model)),
+                full((rows, model)),
                 full((rows, model)),
                 full((rows, model + 2 * width)),
                 full((rows, model + width)),
@@ -990,32 +1019,33 @@
             ],
             scratch_shapes=[
                 pltpu.VMEM((rows, model), f32),
-                pltpu.VMEM((rows, model), bf16),
                 pltpu.VMEM((blocks, rows, model), bf16),
             ],
         ),
         compiler_params=params(40),
-        cost_estimate=pl.CostEstimate(
-            flops=8 * 10**9, transcendentals=0, bytes_accessed=28 << 20
-        ),
-        name="down",
-    )(
-        at, act, w_down, slope, w_in, w_out, normed, inverse, cotangent, attended,
-        gain1, bias1, gain2, bias2,
-    )
-
-
-def scores_grad_kernel(
-    at_ref, g0, g1, g2, g3, qkv_ref, probs_ref, relkq_ref, row_ref, col_ref, wq_ref, wk_ref,
-    sums_ref,
-    dqkv_ref, core_ref, far_ref, small_ref,
-    ga_ref, ds_ref, drel, box_sums,
-):
+        cost_estimate=cost(12),
+        name="back",
+    )(at, w_down, slope, w_in, w_out, normed, inverse, mix, grad_ffn, attended, gain1, above)
+
+
+def scores_grad_kernel(half, held, *refs):
+    at_ref, g0, g1, g2, g3, qkv_ref, probs_ref, relkq_ref, row_ref, col_ref = refs[:10]
+    refs = refs[10:]
+    last = half == 1
+    if last:
+        wq_ref, wk_ref, sums_ref, before_ref, boxes_before = refs[:5]
+        refs = refs[5:]
+    refs = refs[held:]
+    if last:
+        dqkv_ref, own_ref, core_ref, far_ref, small_ref, ga_ref, ds_ref, drel, box_sums = refs
+    else:
+        dqkv_ref, box_sums, ga_ref, ds_ref, drel = refs
     scale = 1.0 / math.sqrt(192.0)
     rows = blocks * lanes
+    width = qkv_ref.shape[1] // 3
+    part = width // 2
     heads = probs_ref.shape[0]
-    width = g0.shape[1]
-    size = width // heads
+    size = part // heads
     span_width = 3 * lanes
     for t, piece in enumerate((g0, g1, g2, g3)):
         ga_ref[t * lanes : (t + 1) * lanes, :] = piece[...]
@@ -1063,11 +1093,15 @@
         seek = jnp.where(in_x, step_x, jnp.where(in_y, step_y + 64, 0))
         inside = in_x | in_y
         for h in range(heads):
-            cols = slice(h * size, (h + 1) * size)
-            kcols = slice(width + h * size, width + (h + 1) * size)
-            vcols = slice(2 * width + h * size, 2 * width + (h + 1) * size)
+            gcols = slice(h * size, (h + 1) * size)
+            kgcols = slice(part + h * size, part + (h + 1) * size)
+            vgcols = slice(2 * part + h * size, 2 * part + (h + 1) * size)
+            cols, kcols, vcols = (
+                slice(k * width + half * part + h * size, k * width + half * part + (h + 1) * size)
+                for k in range(3)
+            )
             probs = probs_ref[h, here, :].astype(f32)
-            gained = dot(ga_ref[here, cols], qkv_ref[:, vcols], ((1,), (1,)))
+            gained = dot(ga_ref[here, gcols], qkv_ref[:, vcols], ((1,), (1,)))
             row_dots = jnp.sum(probs * gained, axis=1, keepdims=True)
             grad = (probs * (gained - row_dots)).astype(bf16)
             ds_ref[h, here, :] = grad
@@ -1075,10 +1109,10 @@
             total = jnp.sum(exact, axis=1, keepdims=True)
             rel = histogram(dot(grad, below), total, pos_i, base)
             rel = (scale * rel).astype(bf16)
-            dqkv_ref[here, cols] = (
+            dqkv_ref[here, gcols] = (
                 scale * dot(grad, qkv_ref[:, kcols]) + dot(rel, relkq_ref[:, cols])
             ).astype(bf16)
-            drel[:, cols] += dot(rel, qkv_ref[here, cols], ((0,), (0,)))
+            drel[:, gcols] += dot(rel, qkv_ref[here, cols], ((0,), (0,)))
             grad_x = jnp.where(short_x, exact, 0.0).astype(bf16)
             grad_y = jnp.where(short_y, exact, 0.0).astype(bf16)
             plain = dot(grad, hot_both)
@@ -1097,125 +1131,143 @@
         base = jnp.min(pos_j, axis=0, keepdims=True)
         below = (all_pos <= base - 63 + window).astype(bf16)
         for h in range(heads):
-            cols = slice(h * size, (h + 1) * size)
-            kcols = slice(width + h * size, width + (h + 1) * size)
-            vcols = slice(2 * width + h * size, 2 * width + (h + 1) * size)
+            gcols = slice(h * size, (h + 1) * size)
+            kgcols = slice(part + h * size, part + (h + 1) * size)
+            vgcols = slice(2 * part + h * size, 2 * part + (h + 1) * size)
+            cols, kcols, vcols = (
+                slice(k * width + half * part + h * size, k * width + half * part + (h + 1) * size)
+                for k in range(3)
+            )
             grad = ds_ref[h, :, here]
             total = dot(grad, jnp.ones((rows, lanes), bf16), ((0,), (0,)))
             sums = dot(grad, below, ((0,), (0,)))
             mirror = (scale * histogram(sums, total, pos_j, base)).astype(bf16)
-            dqkv_ref[here, kcols] = (
+            dqkv_ref[here, kgcols] = (
                 scale * dot(grad, qkv_ref[:, cols], ((0,), (0,)))
                 + dot(mirror, relkq_ref[:, kcols])
             ).astype(bf16)
-            drel[:, kcols] += dot(mirror, qkv_ref[here, kcols], ((0,), (0,)))
-            dqkv_ref[here, vcols] = dot(
-                probs_ref[h, :, here], ga_ref[:, cols], ((0,), (0,))
+            drel[:, kgcols] += dot(mirror, qkv_ref[here, kcols], ((0,), (0,)))
+            dqkv_ref[here, vgcols] = dot(
+                probs_ref[h, :, here], ga_ref[:, gcols], ((0,), (0,))
             ).astype(bf16)
         return carry
 
     lax.fori_loop(0, blocks, by_columns, 0)
-    far_ref[0] = dqkv_ref[lanes : 2 * lanes, :]
-    core_ref[...] = dqkv_ref[2 * lanes : 3 * lanes, :]
-    far_ref[1] = dqkv_ref[3 * lanes : 4 * lanes, :]
-    keys, queries = drel[:, :width].astype(bf16), drel[:, width:].astype(bf16)
-    dqkv_ref[rows:, :width] = queries
-    dqkv_ref[rows:, width : 2 * width] = keys
-    dqkv_ref[rows:, 2 * width :] = jnp.zeros((lanes, width), bf16)
+    keys, queries = drel[:, :part].astype(bf16), drel[:, part:].astype(bf16)
+    dqkv_ref[rows:, :part] = queries
+    dqkv_ref[rows:, part : 2 * part] = keys
+    dqkv_ref[rows:, 2 * part :] = jnp.zeros((lanes, part), bf16)
+    if not last:
+        return
+    for t, target in enumerate((own_ref, far_ref.at[0], core_ref, far_ref.at[1])):
+        span = slice(t * lanes, (t + 1) * lanes)
+        for k in range(3):
+            first = k * width
+            target[:, first : first + part] = before_ref[span, k * part : (k + 1) * part]
+            target[:, first + part : first + width] = dqkv_ref[span, k * part : (k + 1) * part]
+    queries = jnp.concatenate([before_ref[rows:, :part], queries], axis=1)
+    keys = jnp.concatenate([before_ref[rows:, part : 2 * part], keys], axis=1)
 
     docs, small_rows, small_width = small_ref.shape
     per = lanes // docs
     table = (
         dot(keys, wk_ref[...], ((1,), (1,))) + dot(queries, wq_ref[...], ((1,), (1,)))
     ).astype(bf16)
-    plain, less = box_sums[0:8, :], box_sums[8:16, :]
+    plain = jnp.concatenate([boxes_before[0:heads], box_sums[0:heads], box_sums[heads + heads : 8]], axis=0)
+    less = jnp.concatenate(
+        [boxes_before[8 : 8 + heads], box_sums[8 : 8 + heads], box_sums[8 + 2 * heads : 16]], axis=0
+    )
+    heads = 2 * heads
     place_lane = lax.broadcasted_iota(jnp.int32, (8, lanes), 1)
     later = jnp.where(
         jnp.bitwise_and(place_lane, 63) == 63, 0.0, pltpu.roll(less, lanes - 1, 1)
     )
     boxes = (plain - less + later).astype(bf16)
     row_at = lax.broadcasted_iota(jnp.int32, (8, lanes), 0)
-    chosen = ((place_lane == at_ref[0] * heads + row_at) & (row_at < heads)).astype(bf16)
-    boxes = dot(boxes, chosen, ((0,), (0,)))
-    small_ref[...] = jnp.zeros_like(small_ref)
+    head_at = at_ref[0] * heads + row_at
+    by_head = [
+        dot(boxes, ((place_lane == head_at + k * 64) & (row_at < heads)).astype(bf16), ((0,), (0,)))
+        for k in range(2)
+    ]
     model = table.shape[1]
-    rest = model - small_width
-    sums = sums_ref[...]
-    share = model // docs
+    edges = list(range(0, model, small_width)) + [model]
+    rest = edges[-1] - edges[-2]
+    lane = slice(rest, rest + lanes)
+    line = (len(edges) - 2) * per
+    count = lanes // 2 // docs
     for chunk in range(docs):
-        small_ref[chunk, 0:per, :] = table[chunk * per : (chunk + 1) * per, :small_width].astype(f32)
-        small_ref[chunk, per : 2 * per, 0:rest] = (
-            table[chunk * per : (chunk + 1) * per, small_width:].astype(f32)
+        own = slice(chunk * per, (chunk + 1) * per)
+        for k, (first, end) in enumerate(zip(edges[:-1], edges[1:])):
+            small_ref[chunk, k * per : (k + 1) * per, : end - first] = table[own, first:end].astype(f32)
+        for k in range(4):
+            small_ref[chunk, line + k : line + k + 1, lane] = (
+                sums_ref[k : k + 1, chunk * lanes : (chunk + 1) * lanes]
+            )
+            first = (chunk * blocks + k) * lanes
+            where = first // model
+            small_ref[chunk, line + 4 + k : line + 5 + k, lane] = (
+                sums_ref[4 + where : 5 + where, first - where * model : first - where * model + lanes]
+            )
+        begin = chunk * count
+        small_ref[chunk, line + 8 : line + 8 + count, lane] = (
+            by_head[0][begin : begin + count, :] + by_head[1][64 + begin : 64 + begin + count, :]
         )
-        for at in range(4):
-            small_ref[chunk, per + at : per + at + 1, rest : rest + share] = (
-                sums[at : at + 1, chunk * share : (chunk + 1) * share]
-            )
-        bin_at = chunk * blocks * share
-        for at in range(blocks):
-            first = bin_at + at * share
-            line, first = first // model, first % model
-            small_ref[chunk, per + at : per + at + 1, rest + share : rest + 2 * share] = (
-                sums[4 + line : 5 + line, first : first + share]
-            )
-        count = lanes // 2 // docs
-        for axis in range(2):
-            begin = axis * 64 + chunk * count
-            lane = rest + (2 + axis) * share
-            small_ref[chunk, per : per + count, lane : lane + lanes] = boxes[begin : begin + count, :]
-
-
-def scores_grad_call(at, pieces, qkv, probs, relkq, row, col, w_query, w_key, sums, docs):
+
+
+def scores_grad_call(half, at, pieces, qkv, probs, relkq, row, col, after, docs=0, extra=()):
     rows = blocks * lanes
-    heads = probs.shape[0]
-    model = w_query.shape[0]
-    width = model // blocks
+    heads = probs.shape[0] // 2
+    width = qkv.shape[1] // 3
+    part = width // 2
+    model = width * blocks
     buckets = relkq.shape[0]
     column = pl.BlockSpec((model, width), lambda i, at: (0, at[0]))
-    return pl.pallas_call(
-        scores_grad_kernel,
-        out_shape=(
-            jax.ShapeDtypeStruct((rows + buckets, 3 * width), bf16),
+    grads = jax.ShapeDtypeStruct((rows + buckets, 3 * part), bf16)
+    box_shape = (16, lanes)
+    scratch = [
+        pltpu.VMEM((rows, part), bf16),
+        pltpu.VMEM((heads, rows, rows), bf16),
+        pltpu.VMEM((buckets, 2 * part), f32),
+    ]
+    extra_specs = []
+    if half == 1:
+        shapes = (
+            grads,
+            jax.ShapeDtypeStruct((lanes, 3 * width), bf16),
             jax.ShapeDtypeStruct((lanes, 3 * width), bf16),
             jax.ShapeDtypeStruct((2, lanes, 3 * width), bf16),
-            jax.ShapeDtypeStruct((docs, 2 * buckets // docs, 3 * width), f32),
-        ),
+            jax.ShapeDtypeStruct((docs, 3 * buckets // docs, 3 * part), f32),
+        )
+        extra_specs = [column, column, full((8, model)), full(grads.shape), full(box_shape)]
+        scratch = scratch + [pltpu.VMEM(box_shape, f32)]
+    else:
+        shapes = (grads, jax.ShapeDtypeStruct(box_shape, f32))
+    return pl.pallas_call(
+        functools.partial(scores_grad_kernel, half, len(after)),
+        out_shape=shapes,
         grid_spec=pltpu.PrefetchScalarGridSpec(
             num_scalar_prefetch=1,
             grid=(1,),
-            in_specs=[rows_of(piece) for piece in pieces]
+            in_specs=[rows_of(piece, (lanes, part), lambda i, at: half) for piece in pieces]
             + [
                 full((rows, 3 * width)),
-                full((heads, rows, rows)),
+                pl.BlockSpec((heads, rows, rows), lambda i, at: (half, 0, 0)),
                 full((buckets, 2 * width)),
                 full((8, rows)),
                 full((rows, 8)),
-                column,
-                column,
-                full((8, model)),
-            ],
-            out_specs=[
-                full((rows + buckets, 3 * width)),
-                full((lanes, 3 * width)),
-                full((2, lanes, 3 * width)),
-                full((docs, 2 * buckets // docs, 3 * width)),
-            ],
-            scratch_shapes=[
-                pltpu.VMEM((rows, width), bf16),
-                pltpu.VMEM((heads, rows, rows), bf16),
-                pltpu.VMEM((buckets, 2 * width), f32),
-                pltpu.VMEM((16, lanes), f32),
-            ],
+            ]
+            + extra_specs
+            + [pl.BlockSpec(memory_space=pl.ANY)] * len(after),
+            out_specs=[full(shape.shape) for shape in shapes],
+            scratch_shapes=scratch,
         ),
         compiler_params=params(56),
-        cost_estimate=pl.CostEstimate(
-            flops=2 * 10**10, transcendentals=0, bytes_accessed=8 << 20
-        ),
+        cost_estimate=cost(15),
         name="scores_grad",
-    )(at, *map(array_of, pieces), qkv, probs, relkq, row, col, w_query, w_key, sums)
-
-
-def weight_grad_call(at, lefts, rights, bits, extra=None, right_column=0, right_width=None, name="weight_grad"):
+    )(at, *map(array_of, pieces), qkv, probs, relkq, row, col, *extra, *after)
+
+
+def weight_grad_call(at, lefts, rights, bits, extra=None, after=(), right_width=None, name="weight_grad"):
     count = 1 << len(bits)
     model = array_of(lefts[0]).shape[-1]
     chunk = lanes
@@ -1241,7 +1293,7 @@
         right_refs, refs = refs[:pieces], refs[pieces:]
         if extra is not None:
             extra_refs, refs = refs[:per], refs[per:]
-        keep_ref, send_ref, right_all = refs
+        keep_ref, send_ref, right_all = refs[len(after) :]
         step = pl.program_id(0)
 
         @pl.when(step == 0)
@@ -1274,7 +1326,7 @@
             )
             operands.append(array_of(handle))
     for handle in rights:
-        column = handle[2] if isinstance(handle, tuple) and len(handle) == 3 else right_column
+        column = handle[2] if isinstance(handle, tuple) and len(handle) == 3 else 0
         handle = handle[:2] if isinstance(handle, tuple) and handle[1] is not None else array_of(handle)
         in_specs.append(rows_of(handle, (lanes, width), lambda i, at, column=column: column))
         operands.append(array_of(handle))
@@ -1286,6 +1338,8 @@
                 )
             )
             operands.append(extra)
+    in_specs += [pl.BlockSpec(memory_space=pl.ANY)] * len(after)
+    operands += list(after)
     shape = jax.ShapeDtypeStruct((count // 2, chunk + tail, width), bf16)
     block = (per, chunk + tail, width)
     return pl.pallas_call(
@@ -1302,16 +1356,13 @@
             scratch_shapes=[pltpu.VMEM((pieces * lanes, width), bf16)],
         ),
         compiler_params=params(40),
-        cost_estimate=pl.CostEstimate(
-            flops=2 * pieces * lanes * model * width,
-            transcendentals=0,
-            bytes_accessed=2 * (pieces * lanes + model) * (model + width),
-        ),
+        cost_estimate=cost(4),
         name=name,
     )(at, *operands)
 
 
-def tokens_grad_kernel(at_ref, d0, d1, d2, d3, resid_ref, wq_ref, wk_ref, wv_ref, out_ref):
+def tokens_grad_kernel(at_ref, d0, d1, d2, d3, resid_ref, wq_ref, wk_ref, wv_ref, *refs):
+    out_ref = refs[-1]
     step = pl.program_id(0)
     width = wq_ref.shape[1]
 
@@ -1331,7 +1382,7 @@
             out_ref[...] = total
 
 
-def tokens_grad_call(at, pieces, resid, w_query, w_key, w_value):
+def tokens_grad_call(at, pieces, resid, w_query, w_key, w_value, after):
     rows, model = resid.shape
     width = model // blocks
     tile = (rows, 3 * width)
@@ -1348,33 +1399,128 @@
             num_scalar_prefetch=1,
             grid=(blocks,),
             in_specs=[rows_of(piece, tile) for piece in pieces]
-            + [full((rows, model)), weight, weight, weight],
+            + [full((rows, model)), weight, weight, weight]
+            + [pl.BlockSpec(memory_space=pl.ANY)] * len(after),
             out_specs=full((rows, model)),
         ),
         compiler_params=params(40),
-        cost_estimate=pl.CostEstimate(
-            flops=8 * 10**8, transcendentals=0, bytes_accessed=8 << 20
+        cost_estimate=cost(4),
+        name="tokens_grad",
+    )(at, *map(array_of, pieces), resid, w_query, w_key, w_value, *after)
+
+
+def parts_kernel(fields, at_ref, *refs):
+    step = pl.program_id(0)
+    parts, outs = refs[: blocks * fields], refs[blocks * fields :]
+    for field in range(fields):
+        for at in range(blocks):
+
+            @pl.when(step == at)
+            def _(part=parts[field * blocks + at], out=outs[field]):
+                out[...] = part[...].astype(f32)
+
+
+def parts_call(at, fields, name):
+    in_specs, operands, shapes, out_specs = [], [], [], []
+    for parts, axis in fields:
+        rows, width = parts[0].shape
+        in_specs += [full((rows, width))] * blocks
+        operands += list(parts)
+        shape = (rows * blocks, width) if axis == 0 else (rows, width * blocks)
+        shapes.append(jax.ShapeDtypeStruct(shape, f32))
+
+        def index(i, at, axis=axis):
+            spot = jnp.bitwise_xor(at[0], i)
+            return (spot, 0) if axis == 0 else (0, spot)
+
+        out_specs.append(pl.BlockSpec((rows, width), index))
+    return pl.pallas_call(
+        functools.partial(parts_kernel, len(fields)),
+        out_shape=tuple(shapes),
+        grid_spec=pltpu.PrefetchScalarGridSpec(
+            num_scalar_prefetch=1, grid=(blocks,), in_specs=in_specs, out_specs=out_specs
         ),
-        name="tokens_grad",
-    )(at, *map(array_of, pieces), resid, w_query, w_key, w_value)
-
-
-def halve_chunks(keep, send, bits):
-    for place, bit in enumerate(bits):
-        came = swap(send, "docs", bit)
+        compiler_params=params(40),
+        cost_estimate=cost(2),
+        name=name,
+    )(at, *operands)
+
+
+def last_kernel(at_ref, *refs):
+    step = pl.program_id(0)
+    firsts, seconds, outs = refs[:blocks], refs[blocks : 2 * blocks], refs[2 * blocks : 2 * blocks + 3]
+    rel_ref, norm_ref, bin_ref, box_ref = refs[2 * blocks + 3 :]
+    for at in range(blocks):
+
+        @pl.when(step == at)
+        def _(first=firsts[at], second=seconds[at]):
+            for k, out in enumerate(outs):
+                span = slice(k * lanes, (k + 1) * lanes)
+                out[:, :lanes] = first[:, span].astype(f32)
+                out[:, lanes:] = second[:lanes, span].astype(f32)
+
+    @pl.when(step == 0)
+    def _():
+        total = seconds[0][lanes:, :].astype(f32)
+        for second in seconds[1:]:
+            total = total + second[lanes:, :].astype(f32)
+        rows = rel_ref.shape[0]
+        width = total.shape[1]
+        for k in range(3):
+            end = min((k + 1) * width, rel_ref.shape[1])
+            rel_ref[:, k * width : end] = total[k * rows : (k + 1) * rows, : end - k * width]
+        rest = total[2 * rows :, width - lanes :]
+        norm_ref[...] = rest[:4]
+        bin_ref[...] = rest[4:8]
+        box_ref[...] = rest[8:16]
+
+
+def last_call(at, firsts, seconds, buckets, model):
+    rows = blocks * lanes // blocks
+    wide = jax.ShapeDtypeStruct((lanes, model), f32)
+    column = pl.BlockSpec((lanes, model // blocks), lambda i, at: (0, jnp.bitwise_xor(at[0], i)))
+    return pl.pallas_call(
+        last_kernel,
+        out_shape=(wide, wide, wide)
+        + tuple(jax.ShapeDtypeStruct(shape, f32) for shape in ((buckets, model), (4, lanes), (4, lanes), (8, lanes))),
+        grid_spec=pltpu.PrefetchScalarGridSpec(
+            num_scalar_prefetch=1,
+            grid=(blocks,),
+            in_specs=[full(part.shape) for part in firsts + seconds],
+            out_specs=[column] * 3 + [full((buckets, model)), full((4, lanes)), full((4, lanes)), full((8, lanes))],
+        ),
+        compiler_params=params(40),
+        cost_estimate=cost(2),
+        name="last",
+    )(at, *firsts, *seconds)
+
+
+class Halving:
+    def __init__(self, halves, bits):
+        self.keep, self.send = halves
+        self.bits = list(bits)
+        self.step()
+
+    def step(self):
+        self.came = swap(self.send, "docs", self.bits.pop(0))
+
+    def add(self):
+        keep, came = self.keep, self.came
         total = lambda part: (keep[part].astype(f32) + came[part].astype(f32)).astype(bf16)
+        if not self.bits:
+            self.keep = self.send = total(slice(None))[0]
+            return self.keep
         middle = keep.shape[0] // 2
-        if place + 1 < len(bits):
-            send = total(slice(middle, None))
-            keep = total(slice(0, middle))
-        else:
-            keep = total(slice(None))
-    return keep[0]
-
-
-def across_core(own, core, far):
-    came_far = swap(far, "blk", 2)
-    return came_far
+        self.send = total(slice(middle, None))
+        self.keep = total(slice(0, middle))
+        sent = self.send
+        self.step()
+        return sent
+
+    def finish(self):
+        while self.keep.ndim == 3:
+            self.add()
+        return self.keep
 
 
 def shards_tiles(
@@ -1424,78 +1570,96 @@
         line(ln1_gain), line(ln1_bias), w_in, line(b_in), docs,
     )
     got_far1 = swap(far1, "blk", 2)
+    block_out, mix, grad_ffn, above = down_call(
+        act, w_down, normed1, cotangent[0],
+        line(ln1_gain), line(ln1_bias), line(ln2_gain), line(ln2_bias), units // docs,
+    )
+    ffn_far = swap(grad_ffn, "blk", 2)
     (
-        block_out, ga_own, ga_core, ga_far, grad_resid, far2, core2, up_own,
-        far3, core3, gattn_own, sums,
-    ) = down_call(
-        spot, act, w_down, slope, w_in, w_out, normed1, inverse1, cotangent[0], attended,
-        line(ln1_gain), line(ln1_bias), line(ln2_gain), line(ln2_bias), units // docs,
-    )
-    came_far = swap(ga_far, "blk", 2)
-    got_far2 = swap(far2, "blk", 2)
-    got_core1, got_both1 = swap(core1, "blk", 1), swap(got_far1, "blk", 1)
+        ga_own, ga_core, ga_far, grad_resid, up_far, up_core, up_own, far3, core3, gattn_own, sums,
+    ) = back_call(
+        spot, w_down, slope, w_in, w_out, normed1, inverse1, mix, grad_ffn, attended,
+        line(ln1_gain), above, units // docs,
+    )
+    came_far = swap(ordered(ga_far, ffn_far), "blk", 2)
+    got_core1, got_both1 = swap(core1, "blk", 1), swap(ordered(got_far1, ga_own), "blk", 1)
+    ffn_core, ffn_both = swap(grad_ffn, "blk", 1), swap(ordered(ffn_far, ga_own), "blk", 1)
+    act_all = [act_own, (got_far1, 1), (got_core1, 1), (got_both1, 2)]
+    gffn_all = [grad_ffn, ffn_far, ffn_core, ffn_both]
+    down_halves = weight_grad_call(spot, act_all, gffn_all, bits, after=[ga_own], name="grad_down")
+    down_sum = Halving(down_halves, bits)
+
     came_core = swap(ga_core, "blk", 1)
     came_both = swap(came_far, "blk", 1)
-    dqkv, dq_core, dq_far, small = scores_grad_call(
-        spot, (ga_own, (came_far, 0), came_core, (came_both, 1)), qkv, probs, relkq, row, col,
-        w_query, w_key, sums, docs,
-    )
-    got_core2, got_both2 = swap(core2, "blk", 1), swap(got_far2, "blk", 1)
-    got_far3 = swap(far3, "blk", 2)
-    got_core3, got_both3 = swap(core3, "blk", 1), swap(got_far3, "blk", 1)
-
+    ga_all = (ga_own, (came_far, 0), came_core, (came_both, 1))
+    up_far_got = swap(ordered(up_far, came_far), "blk", 2)
+    first_grads, first_boxes = scores_grad_call(
+        0, spot, ga_all, qkv, probs, relkq, row, col, [down_halves[0]]
+    )
+
+    up_core_got, up_both_got = swap(up_core, "blk", 1), swap(ordered(up_far_got, first_grads), "blk", 1)
     hidden_all = [(far1, 0), (got_far1, 0), (got_core1, 0), (got_both1, 0)]
-    act_all = [act_own, (got_far1, 1), (got_core1, 1), (got_both1, 2)]
-    gffn_all = [(far2, 0), (got_far2, 0), (got_core2, 0), (got_both2, 0)]
-    up_all = [up_own, (got_far2, 1), (got_core2, 1), (got_both2, 2)]
+    up_all = [up_own, (up_far_got, 0), up_core_got, (up_both_got, 1)]
+    got_far3 = swap(ordered(far3, first_grads), "blk", 2)
+    in_halves = weight_grad_call(spot, hidden_all, up_all, other, after=[first_grads], name="grad_in")
+    in_sum = Halving(in_halves, other)
+    down_sent = down_sum.add()
+    lefts = list(xs) + [rel_table]
+
+    def rows_by_piece(grads):
+        return [(grads.reshape(blocks + 1, lanes, -1), t) for t in range(blocks + 1)]
+
+    first_halves = weight_grad_call(
+        spot, lefts, rows_by_piece(first_grads), bits, after=[in_halves[0], down_sent], name="grad_qkv"
+    )
+    first_sum = Halving(first_halves, bits)
+    second_grads, dq_own, dq_core, dq_far, small = scores_grad_call(
+        1, spot, ga_all, qkv, probs, relkq, row, col, [first_halves[0]], docs,
+        (w_query, w_key, sums, first_grads, first_boxes),
+    )
+    down_sent = down_sum.add()
+    second_halves = weight_grad_call(
+        spot, lefts, rows_by_piece(second_grads), other, extra=small, after=[down_sent],
+        name="grad_qkv",
+    )
+    second_sum = Halving(second_halves, other)
+    got_core3, got_both3 = swap(core3, "blk", 1), swap(ordered(got_far3, second_grads), "blk", 1)
     att_all = [far3, got_far3, got_core3, got_both3]
     per = model // width
     gattn_all = [
         gattn_own, (got_far3, None, per), (got_core3, None, per), (got_both3, None, per + 1),
     ]
-
-    down_part = halve_chunks(*weight_grad_call(spot, act_all, gffn_all, bits, name="grad_down"), bits)
-    in_part = halve_chunks(*weight_grad_call(spot, hidden_all, up_all, other, name="grad_in"), other)
-    out_part = halve_chunks(
-        *weight_grad_call(spot, att_all, gattn_all, bits, right_width=width, name="grad_out"), bits
-    )
-    dq_rows = dqkv.reshape(blocks + 1, lanes, 3 * width)
-    rights = [(dq_rows, t) for t in range(blocks + 1)]
-    qkv_part = halve_chunks(
-        *weight_grad_call(spot, list(xs) + [rel_table], rights, bits, extra=small, name="grad_qkv"), bits
-    )
-
-    came_far = swap(dq_far, "blk", 2)
-    came_core = swap(dq_core, "blk", 1)
-    came_both = swap(came_far, "blk", 1)
+    out_halves = weight_grad_call(
+        spot, att_all, gattn_all, bits, right_width=width, after=[second_halves[0]], name="grad_out"
+    )
+    out_sum = Halving(out_halves, bits)
+    dq_far_got = swap(dq_far, "blk", 2)
+    dq_core_got, dq_both_got = swap(dq_core, "blk", 1), swap(dq_far_got, "blk", 1)
+    in_sent = in_sum.add()
+    first_sent = first_sum.add()
+    out_sent = out_sum.add()
+    down_part = down_sum.finish()
     grad_tokens = tokens_grad_call(
-        spot, ((dq_rows, 0), (came_far, 0), came_core, (came_both, 1)), grad_resid, w_query, w_key, w_value
-    )
+        spot, (dq_own, (dq_far_got, 0), dq_core_got, (dq_both_got, 1)), grad_resid,
+        w_query, w_key, w_value, [out_halves[0], in_sent, first_sent, out_sent, down_part],
+    )
+    in_part = in_sum.finish()
+    first_part = first_sum.finish()
+    out_part = out_sum.finish()
+    second_part = second_sum.finish()
 
     def whole(part):
         far = swap(part, "blk", 2)
-        parts = [part, swap(part, "blk", 1), far, swap(far, "blk", 1)]
-        return by_place(parts, place)
-
-    grad_w_down = jnp.concatenate(whole(down_part), axis=0).astype(f32)
-    grad_w_in = jnp.concatenate(whole(in_part), axis=1).astype(f32)
-    grad_w_out = jnp.concatenate(whole(out_part), axis=1).astype(f32)
-    pieces = whole(qkv_part)
-    grads = [
-        jnp.concatenate(
-            [piece[:lanes, at * width : (at + 1) * width] for piece in pieces], axis=1
-        ).astype(f32)
-        for at in range(3)
-    ]
-    total = sum(piece[lanes:].astype(f32) for piece in pieces)
-    buckets = rel_table.shape[0] // docs
-    rest = model - 3 * width
-    rel_out = jnp.concatenate([total[:buckets], total[buckets:, :rest]], axis=1)
-    norms = [total[buckets + k, rest : rest + lanes] for k in range(4)]
-    b_in_out = total[buckets : buckets + blocks, rest + lanes : rest + 2 * lanes].reshape(-1)
-    box_rows = boxes // docs
-    xb = total[buckets : buckets + box_rows, rest + 2 * lanes : rest + 2 * lanes + heads]
-    yb = total[buckets : buckets + box_rows, rest + 3 * lanes : rest + 3 * lanes + heads]
+        return (part, swap(part, "blk", 1), far, swap(far, "blk", 1))
+
+    grad_w_down, grad_w_in, grad_w_out = parts_call(
+        spot, ((whole(down_part), 0), (whole(in_part), 1), (whole(out_part), 1)), "gather_parts"
+    )
+    *grads, rel_out, norms, b_in_out, both_boxes = last_call(
+        spot, whole(first_part), whole(second_part), rel_table.shape[0] // docs, model
+    )
+    b_in_out = b_in_out.reshape(-1)
+    xb, yb = both_boxes[:, :heads], both_boxes[:, 64 : 64 + heads]
     return (
         block_out[None], grad_tokens[None], norms[0], norms[1], grads[0], grads[1], grads[2], grad_w_out,
         rel_out, xb, yb, norms[2], norms[3], grad_w_in, b_in_out, grad_w_down,

time: 314 us -> 265 us (0.84)
  waiting for transfers between devices: 129 us -> 86.8 us
  local copies, waits for them, and re-layouts: 23.1 us -> 7.01 us
  Pallas kernels: 107 us -> 117 us
  other arithmetic: 15.9 us -> 10.6 us
  starting transfers between devices: 37 us -> 40.8 us
    ppermute x48 -> x57, waiting for transfers between devices: 129 us -> 86.8 us  [swap(): return lax.ppermute(array, axis, [(i, i ^ by) for i in range(count)])]
    pallas_call x1 -> x5, Pallas kernels: 30.2 us -> 55.3 us  [the longest x2 36.2 us: scores_grad_call(): pl.pallas_call(functools.partial(scores_grad_kernel, half, len(after)), o...]
    pallas_call x1, Pallas kernels: 20.3 us -> 3.98 us  [down_call(): pl.pallas_call(down_kernel, out_shape=(jax.ShapeDtypeStruct((rows, model)...]
    unnamed x104 -> x84, local copies, waits for them, and re-layouts: 21.2 us -> 5.74 us
    ppermute x48 -> x57, starting transfers between devices: 37 us -> 40.8 us  [swap(): return lax.ppermute(array, axis, [(i, i ^ by) for i in range(count)])]
    convert_element_type x14 -> x10, other arithmetic: 8.42 us -> 5.66 us  [add(): (keep[part].astype(f32) + came[part].astype(f32)).astype(bf16)]
    pallas_call x4 -> x5, Pallas kernels: 15.4 us -> 16.7 us  [weight_grad_call(): pl.pallas_call(kernel, out_shape=(shape, shape), grid_spec=pltpu.Prefetch...]
  transfers between devices with their start and end apart: 48 -> 57, of which waited for: 21 -> 19; matrix products, arithmetic and copies ran while one was open for 5% -> 4% of each run, Pallas kernels for 5% -> 30%
where the time goes in v1:
time: 265 us; the launch traced here: 264 us
  Pallas kernels  117 us (44%)
  waiting for transfers between devices  86.8 us (33%)
  starting transfers between devices  40.8 us (15%)
  other arithmetic  10.6 us (4%)
  local copies, waits for them, and re-layouts  7.01 us (3%)
    ppermute x57, waiting for transfers between devices, swap(): return lax.ppermute(array, axis, [(i, i ^ by) for i in range(count)])  86.8 us
    ppermute x57, starting transfers between devices, swap(): return lax.ppermute(array, axis, [(i, i ^ by) for i in range(count)])  40.8 us
    pallas_call x2, Pallas kernels, scores_grad_call(): pl.pallas_call(functools.partial(scores_grad_kernel, half, len(after)), o...  36.2 us
    pallas_call x1, Pallas kernels, scores_call(): pl.pallas_call(scores_kernel, out_shape=(jax.ShapeDtypeStruct((lanes, wid...  26.5 us
    pallas_call x5, Pallas kernels, weight_grad_call(): pl.pallas_call(kernel, out_shape=(shape, shape), grid_spec=pltpu.Prefetch...  16.7 us
    pallas_call x1, Pallas kernels, back_call(): pl.pallas_call(back_kernel, out_shape=(jax.ShapeDtypeStruct((rows, width)...  13.5 us
    pallas_call x1, Pallas kernels, up_call(): pl.pallas_call(up_kernel, out_shape=(jax.ShapeDtypeStruct((3, rows, model...  9.36 us
    unnamed x84, local copies, waits for them, and re-layouts  5.74 us
  transfers between devices with their start and end apart: 57, of which 19 were waited for; matrix products, arithmetic and copies ran while one was open for 4% of the time, Pallas kernels for 30%

profile of v1, /device:TPU:0, one launch (start us, length us, event | category | flops | bytes accessed | tf_op | source)
XLA Modules:
  0.0 264.1 jit_solution(7641998683235454822)
XLA Ops:
  0.6 3.0 %collective-permute-start = (bf16[128,1024]{1,0:T(8,128)(2,1)}, bf16[128,1024]{1,0:T(8,128)(2,1)S(1)}, u32[]{:S(2)}, u32[]{:S(2)}) collective-permute-start(bf16[128,1024]{1,0:T(8,128)(2,1)} %bitcast.52), channel_id=1, source_target_pairs={{0,16},{8,24},{16,0},{24,8},{1,17},{9,25},{17,1},{25,9},{2,18},{10... | collective-permute-start | bytes 786440 | tf_op jit(solution)/shard_map/ppermute | solution.py:309
  4.4 5.7 %collective-permute-done.x1.refs_2_.refs_3_ = bf16[128,1024]{1,0:T(8,128)(2,1)S(1)} collective-permute-done((bf16[128,1024]{1,0:T(8,128)(2,1)}, bf16[128,1024]{1,0:T(8,128)(2,1)S(1)}, u32[]{:S(2)}, u32[]{:S(2)}) %collective-permute-start) | collective-permute-done | bytes 262176 | tf_op jit(solution)/shard_map/ppermute | solution.py:309
  17.6 26.5 %scores.1 = (bf16[128,256]{1,0:T(8,128)(2,1)}, bf16[128,256]{1,0:T(8,128)(2,1)}, bf16[2,128,256]{2,1,0:T(8,128)(2,1)}, bf16[4,512,512]{2,1,0:T(8,128)(2,1)}, bf1...) custom-call(s32[2]{0:T(128)} %pad_add_fusion.1.at_ref, ...), custom_call_target="tpu_custom_call" | custom-call | flops 7500000256 | tf_op jit(solution)/shard_map/scores/pallas_call | solution.py:725
  45.4 4.6 %collective-permute-done.6.a1 = bf16[2,128,256]{2,1,0:T(8,128)(2,1)S(1)} collective-permute-done((bf16[2,128,256]{2,1,0:T(8,128)(2,1)}, bf16[2,128,256]{2,1,0:T(8,128)(2,1)S(1)}, u32[]{:S(2)}, u32[]{:S(2)}) %collective-permute-start.6) | collective-permute-done | bytes 131104 | tf_op jit(solution)/shard_map/ppermute | solution.py:309
  52.5 9.4 %up.1 = (bf16[3,128,1024]{2,1,0:T(8,128)(2,1)S(1)}, bf16[2,128,1024]{2,1,0:T(8,128)(2,1)S(1)}, bf16[128,1024]{1,0:T(8,128)(2,1)S(1)}, bf16[128,4096]{1,0:T(8,128...) custom-call(s32[2]{0:T(128)S(1)} %pad_add_fusion.at_ref.refs_0_, ...), custom_call_target="tpu_custom_call" | custom-call | flops 2700000000 | tf_op jit(solution)/shard_map/up/pallas_call | solution.py:812
  63.1 4.0 %down.1 = (bf16[128,1024]{1,0:T(8,128)(2,1)}, f32[128,1024]{1,0:T(8,128)S(1)}, bf16[128,1024]{1,0:T(8,128)(2,1)S(1)}, f32[8,1024]{1,0:T(8,128)S(1)}) custom-call(bf16[128,4096]{1,0:T(8,128)(2,1)S(1)} %get-tuple-element.84.act_ref, bf16[4096,1024]{1,0:T(8,128)(2,1)S(1)} %copy-done, f32[128,1024]{1,0:T(8,128)S(1)} %get-tuple-element.85.normed_ref, ...), custom_call_target="tpu_custom_call" | custom-call | flops 2400000000 | tf_op jit(solution)/shard_map/down/pallas_call | solution.py:893
  67.1 13.5 %back.1 = (bf16[128,256]{1,0:T(8,128)(2,1)S(1)}, bf16[128,256]{1,0:T(8,128)(2,1)S(1)}, bf16[2,128,256]{2,1,0:T(8,128)(2,1)S(1)}, f32[128,1024]{1,0:T(8,128)S(1)}...) custom-call(s32[2]{0:T(128)S(1)} %pad_add_fusion.at_ref.refs_0_, ...), custom_call_target="tpu_custom_call" | custom-call | flops 3600000000 | tf_op jit(solution)/shard_map/back/pallas_call | solution.py:976
  83.4 7.1 %collective-permute-done.9.refs_9_ = bf16[128,1024]{1,0:T(8,128)(2,1)S(1)} collective-permute-done((bf16[128,1024]{1,0:T(8,128)(2,1)S(1)}, bf16[128,1024]{1,0:T(8,128)(2,1)S(1)}, u32[]{:S(2)}, u32[]{:S(2)}) %collective-permute-start.9) | collective-permute-done | bytes 262176 | tf_op jit(solution)/shard_map/ppermute | solution.py:309
  91.6 4.8 %collective-permute-done.10.refs_2_ = bf16[2,128,256]{2,1,0:T(8,128)(2,1)S(1)} collective-permute-done((bf16[2,128,256]{2,1,0:T(8,128)(2,1)S(1)}, bf16[2,128,256]{2,1,0:T(8,128)(2,1)S(1)}, u32[]{:S(2)}, u32[]{:S(2)}) %collective-permute-start.10) | collective-permute-done | bytes 131104 | tf_op jit(solution)/shard_map/ppermute | solution.py:309
  98.1 4.3 %grad_down.1 = (bf16[4,128,1024]{2,1,0:T(8,128)(2,1)S(1)}, bf16[4,128,1024]{2,1,0:T(8,128)(2,1)}) custom-call(s32[2]{0:T(128)S(1)} %pad_add_fusion.at_ref.refs_0_, bf16[128,1024]{1,0:T(8,128)(2,1)S(1)} %get-tuple-element.103.refs_0_.refs_1_, bf16[128,1024]{1,0:T(8,128)(2,1)S(1)} %get-tuple-element.103.refs_0_.refs_1_, ...), custom_call_target="tpu_custom_call" | custom-call | flops 1200000000 | tf_op jit(solution)/shard_map/grad_down/pallas_call | solution.py:1345
  105.5 17.5 %scores_grad.2 = (bf16[640,384]{1,0:T(8,128)(2,1)}, f32[16,128]{1,0:T(8,128)}) custom-call(s32[2]{0:T(128)} %copy-done.25, bf16[128,256]{1,0:T(8,128)(2,1)} %copy-done.23, bf16[2,128,256]{2,1,0:T(8,128)(2,1)} %copy-done.36, bf16[128,256]{1,0:T(8,128)(2,1)} %copy-done.38, bf16[2,128,256]{2,1,0:T(8,128)(2,1)} %copy-done.37, ...), custom_call_target="tpu_custom_call" | custom-call | flops 4499999744 | tf_op jit(solution)/shard_map/scores_grad/pallas_call | solution.py:1245
  126.8 3.4 %grad_in.1 = (bf16[4,128,1024]{2,1,0:T(8,128)(2,1)S(1)}, bf16[4,128,1024]{2,1,0:T(8,128)(2,1)S(1)}) custom-call(s32[2]{0:T(128)S(1)} %copy-done.26, bf16[3,128,1024]{2,1,0:T(8,128)(2,1)S(1)} %get-tuple-element.104.refs_0_.refs_1_, bf16[3,128,1024]{2,1,0:T(8,128)(2,1)S(1)} %get-tuple-element.104.refs_0_.refs_1_, ...), custom_call_target="tpu_custom_call" | custom-call | flops 1200000000 | tf_op jit(solution)/shard_map/grad_in/pallas_call | solution.py:1345
  134.0 3.2 %grad_qkv.2 = (bf16[4,128,384]{2,1,0:T(8,128)(2,1)S(1)}, bf16[4,128,384]{2,1,0:T(8,128)(2,1)S(1)}) custom-call(s32[2]{0:T(128)S(1)} %copy-done.26, bf16[128,1024]{1,0:T(8,128)(2,1)S(1)} %bitcast.56, bf16[128,1024]{1,0:T(8,128)(2,1)S(1)} %bitcast.57, bf16[128,1024]{1,0:T(8,128)(2,1)S(1)} %copy-done.8, bf16[128,1024]{1,0:T(8,128)(2,1)S(1)} %copy-done.8, ...), custom_call_target="tpu_custom_call" | custom-call | flops 1200000000 | tf_op jit(solution)/shard_map/grad_qkv/pallas_call | solution.py:1345
  138.5 18.7 %scores_grad.3 = (bf16[640,384]{1,0:T(8,128)(2,1)}, bf16[128,768]{1,0:T(8,128)(2,1)}, bf16[128,768]{1,0:T(8,128)(2,1)}, bf16[2,128,768]{2,1,0:T(8,128)(2,1)}, f32[8,48,384]{2,1,0:T(8,128)}) custom-call(s32[2]{0:T(128)} %copy-done.25, bf16[128,256]{1,0:T(8,128)(2,1)} %copy-done.23, bf16[2,128,256]{2,1,0:T(8,128)(2,1)} %copy-done.36, ...), custom_call_target="tpu_custom_call" | custom-call | flops 4499999744 | tf_op jit(solution)/shard_map/scores_grad/pallas_call | solution.py:1245
  159.4 7.5 %collective-permute-done.28 = bf16[2,128,1024]{2,1,0:T(8,128)(2,1)} collective-permute-done((bf16[2,128,1024]{2,1,0:T(8,128)(2,1)S(1)}, bf16[2,128,1024]{2,1,0:T(8,128)(2,1)}, u32[]{:S(2)}, u32[]{:S(2)}) %collective-permute-start.28) | collective-permute-done | bytes 524320 | tf_op jit(solution)/shard_map/ppermute | solution.py:309
  169.5 3.3 %grad_qkv.3 = (bf16[4,176,384]{2,1,0:T(8,128)(2,1)S(1)}, bf16[4,176,384]{2,1,0:T(8,128)(2,1)S(1)}) custom-call(s32[2]{0:T(128)S(1)} %copy-done.27, bf16[128,1024]{1,0:T(8,128)(2,1)S(1)} %bitcast.58, bf16[128,1024]{1,0:T(8,128)(2,1)S(1)} %bitcast.59, bf16[128,1024]{1,0:T(8,128)(2,1)S(1)} %copy-done.8, bf16[128,1024]{1,0:T(8,128)(2,1)S(1)} %copy-done.8, ...), custom_call_target="tpu_custom_call" | custom-call | flops 1200000000 | tf_op jit(solution)/shard_map/grad_qkv/pallas_call | solution.py:1345
  181.1 14.5 %collective-permute-done.34 = bf16[1,128,384]{2,1,0:T(8,128)(2,1)S(1)} collective-permute-done((bf16[1,128,384]{2,1,0:T(8,128)(2,1)S(1)}, bf16[1,128,384]{2,1,0:T(8,128)(2,1)S(1)}, u32[]{:S(2)}, u32[]{:S(2)}) %collective-permute-start.34) | collective-permute-done | bytes 98336 | tf_op jit(solution)/shard_map/ppermute | solution.py:309
  201.2 3.5 %collective-permute-done.31 = bf16[4,128,256]{2,1,0:T(8,128)(2,1)S(1)} collective-permute-done((bf16[4,128,256]{2,1,0:T(8,128)(2,1)S(1)}, bf16[4,128,256]{2,1,0:T(8,128)(2,1)S(1)}, u32[]{:S(2)}, u32[]{:S(2)}) %collective-permute-start.31) | collective-permute-done | bytes 262176 | tf_op jit(solution)/shard_map/ppermute | solution.py:309
  205.4 10.6 %collective-permute-done.47 = bf16[2,128,1024]{2,1,0:T(8,128)(2,1)S(1)} collective-permute-done((bf16[2,128,1024]{2,1,0:T(8,128)(2,1)S(1)}, bf16[2,128,1024]{2,1,0:T(8,128)(2,1)S(1)}, u32[]{:S(2)}, u32[]{:S(2)}) %collective-permute-start.47) | collective-permute-done | bytes 524320 | tf_op jit(solution)/shard_map/ppermute | solution.py:309
  220.0 3.4 %collective-permute-start.48 = (bf16[1,128,1024]{2,1,0:T(8,128)(2,1)S(1)}, bf16[1,128,1024]{2,1,0:T(8,128)(2,1)S(1)}, u32[]{:S(2)}, u32[]{:S(2)}) collective-permute-start(bf16[1,128,1024]{2,1,0:T(8,128)(2,1)S(1)} %add_convert_fusion.7), channel_id=1, source_target_pairs={{0,4},{1,5},{2,6},{3,7},{4,0},{5,1},{6,2},{7,3},{8,12},{9,13},{10,... | collective-permute-start | bytes 786440 | tf_op jit(solution)/shard_map/ppermute | solution.py:309
  225.7 13.9 %collective-permute-done.40 = bf16[1,176,384]{2,1,0:T(8,128)(2,1)S(1)} collective-permute-done((bf16[1,176,384]{2,1,0:T(8,128)(2,1)S(1)}, bf16[1,176,384]{2,1,0:T(8,128)(2,1)S(1)}, u32[]{:S(2)}, u32[]{:S(2)}) %collective-permute-start.40) | collective-permute-done | bytes 135200 | tf_op jit(solution)/shard_map/ppermute | solution.py:309
  247.2 5.2 %tokens_grad.1 = f32[128,1024]{1,0:T(8,128)} custom-call(s32[2]{0:T(128)S(1)} %copy-done.27, bf16[128,768]{1,0:T(8,128)(2,1)S(1)} %copy-done.22, bf16[2,128,768]{2,1,0:T(8,128)(2,1)S(1)} %collective-permute-done.22.d1, bf16[128,768]{1,0:T(8,128)(2,1)S(1)} %collective-permute-done.23.d2, bf16[2,128,768]{2,1,0:T(8,128)(2,1)S(1)} %collective-permute-done.24.d3, ...), custom_call_target="tpu_custom_call" | custom-call | flops 1200000000 | tf_op jit(solution)/shard_map/tokens_grad/pallas_call | solution.py:1395
  255.5 3.0 %collective-permute-done.55.refs_10_ = bf16[128,256]{1,0:T(8,128)(2,1)S(1)} collective-permute-done((bf16[128,256]{1,0:T(8,128)(2,1)S(1)}, bf16[128,256]{1,0:T(8,128)(2,1)S(1)}, u32[]{:S(2)}, u32[]{:S(2)}) %collective-permute-start.55) | collective-permute-done | bytes 65568 | tf_op jit(solution)/shard_map/ppermute | solution.py:309
  260.9 3.2 %gather_parts.1 = (f32[512,1024]{1,0:T(8,128)}, f32[128,4096]{1,0:T(8,128)}, f32[128,1024]{1,0:T(8,128)}) custom-call(s32[2]{0:T(128)S(1)} %copy-done.27, bf16[128,1024]{1,0:T(8,128)(2,1)S(1)} %fusion.refs_4_.refs_0_, bf16[128,1024]{1,0:T(8,128)(2,1)S(1)} %collective-permute-done.44.refs_1_, bf16[128,1024]{1,0:T(8,128)(2,1)S(1)} %collective-permute-done.45.refs_2_, ...), custom_call_target="tpu_custom_call" | custom-call | flops 600000000 | tf_op jit(solution)/shard_map/gather_parts/pallas_call | solution.py:1437
  (212 shorter events, 68.5 us)
Async XLA Ops:
  61.9 19.9 %collective-permute-start.13 = (bf16[3,128,1024]{2,1,0:T(8,128)(2,1)S(1)}, bf16[3,128,1024]{2,1,0:T(8,128)(2,1)S(1)}, u32[]{:S(2)}, u32[]{:S(2)}) collective-permute-start(bf16[3,128,1024]{2,1,0:T(8,128)(2,1)S(1)} %get-tuple-element.104.refs_0_.refs_1_), channel_id=1, source_target_pairs={{0,16},{8,24},{16,0},{24,8},{1,17},{9,25},{17,1},{25,9},{2,18},{10... | collective-permute-start | bytes 2359304 | tf_op jit(solution)/shard_map/ppermute | solution.py:309
  81.8 16.3 %collective-permute-start.15 = (bf16[3,128,1024]{2,1,0:T(8,128)(2,1)S(1)}, bf16[3,128,1024]{2,1,0:T(8,128)(2,1)S(1)}, u32[]{:S(2)}, u32[]{:S(2)}) collective-permute-start(bf16[3,128,1024]{2,1,0:T(8,128)(2,1)S(1)} %collective-permute-done.13.refs_2_.refs_3_), channel_id=1, source_target_pairs={{0,8},{8,0},{16,24},{24,16},{1,9},{9,1},{17,25},{25,17},{2,10},{10... | collective-permute-start | bytes 2359304 | tf_op jit(solution)/shard_map/ppermute | solution.py:309
  82.9 15.2 %collective-permute-start.14 = (bf16[2,128,1024]{2,1,0:T(8,128)(2,1)S(1)}, bf16[2,128,1024]{2,1,0:T(8,128)(2,1)S(1)}, u32[]{:S(2)}, u32[]{:S(2)}) collective-permute-start(bf16[2,128,1024]{2,1,0:T(8,128)(2,1)S(1)} %get-tuple-element.105), channel_id=1, source_target_pairs={{0,8},{8,0},{16,24},{24,16},{1,9},{9,1},{17,25},{25,17},{2,10},{10... | collective-permute-start | bytes 1572872 | tf_op jit(solution)/shard_map/ppermute | solution.py:309
  83.1 13.3 %collective-permute-start.16 = (bf16[128,1024]{1,0:T(8,128)(2,1)S(1)}, bf16[128,1024]{1,0:T(8,128)(2,1)S(1)}, u32[]{:S(2)}, u32[]{:S(2)}) collective-permute-start(bf16[128,1024]{1,0:T(8,128)(2,1)S(1)} %get-tuple-element.90.ffn_ref.refs_8_), channel_id=1, source_target_pairs={{0,8},{8,0},{16,24},{24,16},{1,9},{9,1},{17,25},{25,17},{2,10},{10... | collective-permute-start | bytes 786440 | tf_op jit(solution)/shard_map/ppermute | solution.py:309
  96.9 26.1 %collective-permute-start.18 = (bf16[2,128,1024]{2,1,0:T(8,128)(2,1)S(1)}, bf16[2,128,1024]{2,1,0:T(8,128)(2,1)S(1)}, u32[]{:S(2)}, u32[]{:S(2)}) collective-permute-start(bf16[2,128,1024]{2,1,0:T(8,128)(2,1)S(1)} %get-tuple-element.113), channel_id=1, source_target_pairs={{0,16},{8,24},{16,0},{24,8},{1,17},{9,25},{17,1},{25,9},{2,18},{10... | collective-permute-start | bytes 1572872 | tf_op jit(solution)/shard_map/ppermute | solution.py:309
  103.3 28.6 %collective-permute-start.21 = (bf16[4,128,1024]{2,1,0:T(8,128)(2,1)}, bf16[4,128,1024]{2,1,0:T(8,128)(2,1)}, u32[]{:S(2)}, u32[]{:S(2)}) collective-permute-start(bf16[4,128,1024]{2,1,0:T(8,128)(2,1)} %get-tuple-element.117), channel_id=1, source_target_pairs={{0,1},{1,0},{2,3},{3,2},{4,5},{5,4},{6,7},{7,6},{8,9},{9,8},{10,11... | collective-permute-start | bytes 3145736 | tf_op jit(solution)/shard_map/ppermute | solution.py:309
  123.6 49.2 %collective-permute-start.26 = (bf16[128,1280]{1,0:T(8,128)(2,1)}, bf16[128,1280]{1,0:T(8,128)(2,1)S(1)}, u32[]{:S(2)}, u32[]{:S(2)}) collective-permute-start(bf16[128,1280]{1,0:T(8,128)(2,1)} %get-tuple-element.125), channel_id=1, source_target_pairs={{0,8},{8,0},{16,24},{24,16},{1,9},{9,1},{17,25},{25,17},{2,10},{10... | collective-permute-start | bytes 983048 | tf_op jit(solution)/shard_map/ppermute | solution.py:309
  123.6 33.6 %collective-permute-start.25 = (bf16[128,1536]{1,0:T(8,128)(2,1)S(1)}, bf16[128,1536]{1,0:T(8,128)(2,1)S(1)}, u32[]{:S(2)}, u32[]{:S(2)}) collective-permute-start(bf16[128,1536]{1,0:T(8,128)(2,1)S(1)} %get-tuple-element.124.refs_0_.refs_1_), channel_id=1, source_target_pairs={{0,16},{8,24},{16,0},{24,8},{1,17},{9,25},{17,1},{25,9},{2,18},{10... | collective-permute-start | bytes 1179656 | tf_op jit(solution)/shard_map/ppermute | solution.py:309
  130.3 48.8 %collective-permute-start.29 = (bf16[4,128,1024]{2,1,0:T(8,128)(2,1)S(1)}, bf16[4,128,1024]{2,1,0:T(8,128)(2,1)}, u32[]{:S(2)}, u32[]{:S(2)}) collective-permute-start(bf16[4,128,1024]{2,1,0:T(8,128)(2,1)S(1)} %get-tuple-element.132), channel_id=1, source_target_pairs={{0,2},{1,3},{2,0},{3,1},{4,6},{5,7},{6,4},{7,5},{8,10},{9,11},{10,... | collective-permute-start | bytes 3145736 | tf_op jit(solution)/shard_map/ppermute | solution.py:309
  133.5 33.4 %collective-permute-start.28 = (bf16[2,128,1024]{2,1,0:T(8,128)(2,1)S(1)}, bf16[2,128,1024]{2,1,0:T(8,128)(2,1)}, u32[]{:S(2)}, u32[]{:S(2)}) collective-permute-start(bf16[2,128,1024]{2,1,0:T(8,128)(2,1)S(1)} %get-tuple-element.149.refs_16_), channel_id=1, source_target_pairs={{0,2},{1,3},{2,0},{3,1},{4,6},{5,7},{6,4},{7,5},{8,10},{9,11},{10,... | collective-permute-start | bytes 1572872 | tf_op jit(solution)/shard_map/ppermute | solution.py:309
  138.0 19.3 %collective-permute-start.30 = (bf16[4,128,384]{2,1,0:T(8,128)(2,1)S(1)}, bf16[4,128,384]{2,1,0:T(8,128)(2,1)}, u32[]{:S(2)}, u32[]{:S(2)}) collective-permute-start(bf16[4,128,384]{2,1,0:T(8,128)(2,1)S(1)} %get-tuple-element.133), channel_id=1, source_target_pairs={{0,1},{1,0},{2,3},{3,2},{4,5},{5,4},{6,7},{7,6},{8,9},{9,8},{10,11... | collective-permute-start | bytes 1179656 | tf_op jit(solution)/shard_map/ppermute | solution.py:309
  157.2 16.1 %collective-permute-start.27 = (bf16[128,1536]{1,0:T(8,128)(2,1)S(1)}, bf16[128,1536]{1,0:T(8,128)(2,1)S(1)}, u32[]{:S(2)}, u32[]{:S(2)}) collective-permute-start(bf16[128,1536]{1,0:T(8,128)(2,1)S(1)} %collective-permute-done.25.refs_2_.refs_3_.refs_9_), channel_id=1, source_target_pairs={{0,8},{8,0},{16,24},{24,16},{1,9},{9,1},{17,25},{25,17},{2,10},{10... | collective-permute-start | bytes 1179656 | tf_op jit(solution)/shard_map/ppermute | solution.py:309
  157.3 15.6 %collective-permute-start.22 = (bf16[2,128,768]{2,1,0:T(8,128)(2,1)}, bf16[2,128,768]{2,1,0:T(8,128)(2,1)S(1)}, u32[]{:S(2)}, u32[]{:S(2)}) collective-permute-start(bf16[2,128,768]{2,1,0:T(8,128)(2,1)} %get-tuple-element.120), channel_id=1, source_target_pairs={{0,16},{8,24},{16,0},{24,8},{1,17},{9,25},{17,1},{25,9},{2,18},{10... | collective-permute-start | bytes 1179656 | tf_op jit(solution)/shard_map/ppermute | solution.py:309
  172.8 66.8 %collective-permute-start.23 = (bf16[128,768]{1,0:T(8,128)(2,1)S(1)}, bf16[128,768]{1,0:T(8,128)(2,1)S(1)}, u32[]{:S(2)}, u32[]{:S(2)}) collective-permute-start(bf16[128,768]{1,0:T(8,128)(2,1)S(1)} %copy-done.35), channel_id=1, source_target_pairs={{0,8},{8,0},{16,24},{24,16},{1,9},{9,1},{17,25},{25,17},{2,10},{10... | collective-permute-start | bytes 589832 | tf_op jit(solution)/shard_map/ppermute | solution.py:309
  172.9 69.1 %collective-permute-start.24 = (bf16[2,128,768]{2,1,0:T(8,128)(2,1)S(1)}, bf16[2,128,768]{2,1,0:T(8,128)(2,1)S(1)}, u32[]{:S(2)}, u32[]{:S(2)}) collective-permute-start(bf16[2,128,768]{2,1,0:T(8,128)(2,1)S(1)} %collective-permute-done.22.d1), channel_id=1, source_target_pairs={{0,8},{8,0},{16,24},{24,16},{1,9},{9,1},{17,25},{25,17},{2,10},{10... | collective-permute-start | bytes 1179656 | tf_op jit(solution)/shard_map/ppermute | solution.py:309
  173.4 22.7 %collective-permute-start.32 = (bf16[1,128,1024]{2,1,0:T(8,128)(2,1)S(1)}, bf16[1,128,1024]{2,1,0:T(8,128)(2,1)S(1)}, u32[]{:S(2)}, u32[]{:S(2)}) collective-permute-start(bf16[1,128,1024]{2,1,0:T(8,128)(2,1)S(1)} %add_convert_fusion.11.refs_17_), channel_id=1, source_target_pairs={{0,4},{1,5},{2,6},{3,7},{4,0},{5,1},{6,2},{7,3},{8,12},{9,13},{10,... | collective-permute-start | bytes 786440 | tf_op jit(solution)/shard_map/ppermute | solution.py:309
  178.5 21.7 %collective-permute-start.38 = (bf16[4,176,384]{2,1,0:T(8,128)(2,1)S(1)}, bf16[4,176,384]{2,1,0:T(8,128)(2,1)S(1)}, u32[]{:S(2)}, u32[]{:S(2)}) collective-permute-start(bf16[4,176,384]{2,1,0:T(8,128)(2,1)S(1)} %get-tuple-element.135), channel_id=1, source_target_pairs={{0,2},{1,3},{2,0},{3,1},{4,6},{5,7},{6,4},{7,5},{8,10},{9,11},{10,... | collective-permute-start | bytes 1622024 | tf_op jit(solution)/shard_map/ppermute | solution.py:309
  179.1 16.5 %collective-permute-start.34 = (bf16[1,128,384]{2,1,0:T(8,128)(2,1)S(1)}, bf16[1,128,384]{2,1,0:T(8,128)(2,1)S(1)}, u32[]{:S(2)}, u32[]{:S(2)}) collective-permute-start(bf16[1,128,384]{2,1,0:T(8,128)(2,1)S(1)} %add_convert_fusion.20), channel_id=1, source_target_pairs={{0,4},{1,5},{2,6},{3,7},{4,0},{5,1},{6,2},{7,3},{8,12},{9,13},{10,... | collective-permute-start | bytes 294920 | tf_op jit(solution)/shard_map/ppermute | solution.py:309
  196.1 19.9 %collective-permute-start.47 = (bf16[2,128,1024]{2,1,0:T(8,128)(2,1)S(1)}, bf16[2,128,1024]{2,1,0:T(8,128)(2,1)S(1)}, u32[]{:S(2)}, u32[]{:S(2)}) collective-permute-start(bf16[2,128,1024]{2,1,0:T(8,128)(2,1)S(1)} %get-tuple-element.147.refs_1_), channel_id=1, source_target_pairs={{0,1},{1,0},{2,3},{3,2},{4,5},{5,4},{6,7},{7,6},{8,9},{9,8},{10,11... | collective-permute-start | bytes 1572872 | tf_op jit(solution)/shard_map/ppermute | solution.py:309
  200.2 40.6 %collective-permute-start.36 = (bf16[128,384]{1,0:T(8,128)(2,1)S(1)}, bf16[128,384]{1,0:T(8,128)(2,1)S(1)}, u32[]{:S(2)}, u32[]{:S(2)}) collective-permute-start(bf16[128,384]{1,0:T(8,128)(2,1)S(1)} %fusion.3.refs_0_), channel_id=1, source_target_pairs={{0,16},{8,24},{16,0},{24,8},{1,17},{9,25},{17,1},{25,9},{2,18},{10... | collective-permute-start | bytes 294920 | tf_op jit(solution)/shard_map/ppermute | solution.py:309
  204.8 15.2 %collective-permute-start.39 = (bf16[2,176,384]{2,1,0:T(8,128)(2,1)S(1)}, bf16[2,176,384]{2,1,0:T(8,128)(2,1)S(1)}, u32[]{:S(2)}, u32[]{:S(2)}) collective-permute-start(bf16[2,176,384]{2,1,0:T(8,128)(2,1)S(1)} %get-tuple-element.151), channel_id=1, source_target_pairs={{0,1},{1,0},{2,3},{3,2},{4,5},{5,4},{6,7},{7,6},{8,9},{9,8},{10,11... | collective-permute-start | bytes 811016 | tf_op jit(solution)/shard_map/ppermute | solution.py:309
  220.0 19.7 %collective-permute-start.48 = (bf16[1,128,1024]{2,1,0:T(8,128)(2,1)S(1)}, bf16[1,128,1024]{2,1,0:T(8,128)(2,1)S(1)}, u32[]{:S(2)}, u32[]{:S(2)}) collective-permute-start(bf16[1,128,1024]{2,1,0:T(8,128)(2,1)S(1)} %add_convert_fusion.7), channel_id=1, source_target_pairs={{0,4},{1,5},{2,6},{3,7},{4,0},{5,1},{6,2},{7,3},{8,12},{9,13},{10,... | collective-permute-start | bytes 786440 | tf_op jit(solution)/shard_map/ppermute | solution.py:309
  223.5 16.1 %collective-permute-start.40 = (bf16[1,176,384]{2,1,0:T(8,128)(2,1)S(1)}, bf16[1,176,384]{2,1,0:T(8,128)(2,1)S(1)}, u32[]{:S(2)}, u32[]{:S(2)}) collective-permute-start(bf16[1,176,384]{2,1,0:T(8,128)(2,1)S(1)} %add_convert_fusion.15), channel_id=1, source_target_pairs={{0,4},{1,5},{2,6},{3,7},{4,0},{5,1},{6,2},{7,3},{8,12},{9,13},{10,... | collective-permute-start | bytes 405512 | tf_op jit(solution)/shard_map/ppermute | solution.py:309
  242.0 16.4 %collective-permute-start.50 = (bf16[128,1024]{1,0:T(8,128)(2,1)S(1)}, bf16[128,1024]{1,0:T(8,128)(2,1)S(1)}, u32[]{:S(2)}, u32[]{:S(2)}) collective-permute-start(bf16[128,1024]{1,0:T(8,128)(2,1)S(1)} %fusion.1.refs_4_), channel_id=1, source_target_pairs={{0,16},{8,24},{16,0},{24,8},{1,17},{9,25},{17,1},{25,9},{2,18},{10... | collective-permute-start | bytes 786440 | tf_op jit(solution)/shard_map/ppermute | solution.py:309
  (75 other events, 851.4 us)

commit v2 on v1

--- a/solution.py
+++ b/solution.py
@@ -635,7 +635,8 @@
 
 def scores_kernel(
     at_ref, x0, x1, x2, x3, i0, i1, i2, i3, wq_ref, wk_ref, wv_ref, rel_ref, tab_ref,
-    own_ref, core_ref, far_ref, probs_ref, qkv_ref, relkq_ref, row_ref, col_ref, key_rel,
+    own_ref, core_ref, far_ref, probs_ref, qkv_ref, relkq_ref, row_ref, col_ref,
+    key_rel, queries, keys_t, values, rel_keys_t, sector_hot,
 ):
     scale = 1.0 / math.sqrt(192.0)
     step = pl.program_id(0)
@@ -649,16 +650,26 @@
         for t, (x_ref, i_ref) in enumerate(zip((x0, x1, x2, x3), (i0, i1, i2, i3))):
             span = slice(t * lanes, (t + 1) * lanes)
             for at, w_ref in enumerate((wq_ref, wk_ref, wv_ref)):
-                qkv_ref[span, at * width : (at + 1) * width] = dot(
-                    x_ref[...], w_ref[...]
-                ).astype(bf16)
+                part = dot(x_ref[...], w_ref[...]).astype(bf16)
+                qkv_ref[span, at * width : (at + 1) * width] = part
+                if at == 1:
+                    keys_t[:, span] = part.astype(f32).T.astype(bf16)
+                else:
+                    for h in range(heads):
+                        (queries, None, values)[at][h, span, :] = part[:, h * size : (h + 1) * size]
             first = jnp.bitwise_xor(at_ref[0], slots[t]) * lanes
             slot = first + lax.broadcasted_iota(jnp.int32, (8, lanes), 1)
             kind = lax.broadcasted_iota(jnp.int32, (8, lanes), 0)
             ints = jnp.where(kind == 3, (slot < at_ref[1]).astype(jnp.int32), i_ref[...])
             row_ref[:, span] = ints
             col_ref[span, :] = ints.astype(f32).T.astype(jnp.int32)
-        relkq_ref[:, :width] = dot(rel_ref[...], wk_ref[...]).astype(bf16)
+        sector = lax.broadcasted_iota(jnp.int32, (32, rows), 0)
+        for k in range(2):
+            hot = (jnp.right_shift(row_ref[1 + k : 2 + k, :], 5) == sector).astype(f32).astype(bf16)
+            sector_hot[k * 32 : (k + 1) * 32, :] = hot
+        rel_keys = dot(rel_ref[...], wk_ref[...])
+        relkq_ref[:, :width] = rel_keys.astype(bf16)
+        rel_keys_t[...] = rel_keys.T.astype(bf16)
         relkq_ref[:, width:] = dot(rel_ref[...], wq_ref[...]).astype(bf16)
         for h in range(heads):
             cols = slice(width + h * size, width + (h + 1) * size)
@@ -671,43 +682,46 @@
     cx_i = col_ref[here, 1:2]
     cy_i = col_ref[here, 2:3]
     own_row = row_ref[0:1, here]
-    ahead, mirror, across, vertical = [], [], [], []
+    lane = lax.broadcasted_iota(jnp.int32, (lanes, lanes), 1)
+    on_x = jnp.bitwise_and(jnp.right_shift(lane, 5), 1) == 0
+    seek = (
+        jnp.where(on_x, jnp.right_shift(cx_i, 5), jnp.right_shift(cy_i, 5) + 64)
+        + 32
+        - jnp.bitwise_and(lane, 31)
+        - (lane >= 64).astype(jnp.int32)
+    )
+    short_x = jnp.bitwise_and(cx_i, 31) < jnp.bitwise_and(row_ref[1:2, :], 31)
+    short_y = jnp.bitwise_and(cy_i, 31) < jnp.bitwise_and(row_ref[2:3, :], 31)
+    ahead, mirror = [], []
     for t in range(blocks):
         span = slice(t * lanes, (t + 1) * lanes)
         ahead.append(ahead_of(pos_i, row_ref[0:1, span]))
         mirror.append(ahead_of(col_ref[span, 0:1], own_row))
-        across.append(jnp.clip(jnp.right_shift(cx_i - row_ref[1:2, span], 5), -32, 31) + 32)
-        vertical.append(jnp.clip(jnp.right_shift(cy_i - row_ref[2:3, span], 5), -32, 31) + 96)
     valid = row_ref[3:4, :] > 0
     attended = []
     for h in range(heads):
         cols = slice(h * size, (h + 1) * size)
-        query = qkv_ref[here, cols]
-        rel_scores = (
-            dot(query, relkq_ref[:, cols], ((1,), (1,))).astype(bf16).astype(f32)
-        )
+        query = queries[h, here, :]
+        rel_scores = dot(query, rel_keys_t[cols, :]).astype(bf16).astype(f32)
         table = jnp.broadcast_to(tab_ref[0, h : h + 1, :], (lanes, lanes))
-        pieces = []
+        by_sector = pick(table, seek).astype(bf16)
+        content = dot(query, keys_t[cols, :])
+        plain_x = dot(by_sector[:, 0:32], sector_hot[0:32, :])
+        plain_y = dot(by_sector[:, 32:64], sector_hot[32:64, :])
+        less_x = dot(by_sector[:, 64:96], sector_hot[0:32, :])
+        less_y = dot(by_sector[:, 96:128], sector_hot[32:64, :])
+        bias = jnp.where(short_x, less_x, plain_x) + jnp.where(short_y, less_y, plain_y)
+        moved = []
         for t in range(blocks):
             span = slice(t * lanes, (t + 1) * lanes)
-            content = dot(
-                query, qkv_ref[span, width + h * size : width + (h + 1) * size], ((1,), (1,))
-            )
-            mirrored = pick(key_rel[h, span, :], mirror[t]).T
-            bias = pick(table, across[t]) + pick(table, vertical[t])
-            pieces.append(
-                scale * (content + pick(rel_scores, ahead[t]) + mirrored) + bias
-            )
-        scores = jnp.where(valid, jnp.concatenate(pieces, axis=1), mask_value)
+            moved.append(pick(rel_scores, ahead[t]) + pick(key_rel[h, span, :], mirror[t]).T)
+        scores = scale * (content + jnp.concatenate(moved, axis=1)) + bias
+        scores = jnp.where(valid, scores, mask_value)
         top = jnp.max(scores, axis=1, keepdims=True)
         raised = jnp.exp(scores - top)
         probs = (raised * (1.0 / jnp.sum(raised, axis=1, keepdims=True))).astype(bf16)
         probs_ref[h] = probs
-        attended.append(
-            dot(
-                probs, qkv_ref[:, 2 * width + h * size : 2 * width + (h + 1) * size]
-            ).astype(bf16)
-        )
+        attended.append(dot(probs, values[h]).astype(bf16))
     attended = jnp.concatenate(attended, axis=1)
     for t, target in enumerate((own_ref, far_ref.at[0], core_ref, far_ref.at[1])):
 
@@ -756,7 +770,14 @@
                 full((8, rows)),
                 full((rows, 8)),
             ],
-            scratch_shapes=[pltpu.VMEM((heads, rows, lanes), f32)],
+            scratch_shapes=[
+                pltpu.VMEM((heads, rows, lanes), f32),
+                pltpu.VMEM((heads, rows, width // heads), bf16),
+                pltpu.VMEM((width, rows), bf16),
+                pltpu.VMEM((heads, rows, width // heads), bf16),
+                pltpu.VMEM((width, buckets), bf16),
+                pltpu.VMEM((64, rows), bf16),
+            ],
         ),
         compiler_params=params(56),
         cost_estimate=cost(25),
@@ -942,9 +963,11 @@
     @pl.when(step == steps - 1)
     def _():
         upown_ref[...] = grad_up[0]
-        upcore_ref[...] = grad_up[1]
-        upfar_ref[0] = grad_up[2]
-        upfar_ref[1] = grad_up[3]
+        upcore_ref[0] = ffn_ref[...]
+        upcore_ref[1] = grad_up[1]
+        upfar_ref[0] = ffn_ref[...]
+        upfar_ref[1] = grad_up[2]
+        upfar_ref[2] = grad_up[3]
         grad = total[...]
         normed = normed_ref[...]
         sums_ref[0:1, :] = jnp.sum(grad * normed, axis=0, keepdims=True)
@@ -980,8 +1003,8 @@
             jax.ShapeDtypeStruct((rows, width), bf16),
             jax.ShapeDtypeStruct((2, rows, width), bf16),
             jax.ShapeDtypeStruct((rows, model), f32),
+            jax.ShapeDtypeStruct((3, rows, model), bf16),
             jax.ShapeDtypeStruct((2, rows, model), bf16),
-            jax.ShapeDtypeStruct((rows, model), bf16),
             jax.ShapeDtypeStruct((rows, model), bf16),
             jax.ShapeDtypeStruct((rows, model + 2 * width), bf16),
             jax.ShapeDtypeStruct((rows, model + width), bf16),
@@ -1009,8 +1032,8 @@
                 full((rows, width)),
                 full((2, rows, width)),
                 full((rows, model)),
+                full((3, rows, model)),
                 full((2, rows, model)),
-                full((rows, model)),
                 full((rows, model)),
                 full((rows, model + 2 * width)),
                 full((rows, model + width)),
@@ -1267,98 +1290,114 @@
     )(at, *map(array_of, pieces), qkv, probs, relkq, row, col, *extra, *after)
 
 
-def weight_grad_call(at, lefts, rights, bits, extra=None, after=(), right_width=None, name="weight_grad"):
-    count = 1 << len(bits)
-    model = array_of(lefts[0]).shape[-1]
+def weight_grads_call(at, wholes, after=(), name="weight_grads"):
+    count = 1 << len(wholes[0][1])
     chunk = lanes
-    width = right_width or array_of(rights[0]).shape[-1]
-    pieces = len(lefts)
-    tail = 0 if extra is None else extra.shape[1]
     per = 2
     steps = count // per
     half = steps // 2
 
-    def offset(p):
-        total = 0
-        for place, bit in enumerate(bits):
-            total = total + jnp.bitwise_and(jnp.right_shift(p, len(bits) - 1 - place), 1) * bit
-        return total
-
-    def chunk_of(i, at, which):
-        p = lax.rem(i + half, steps) * per + which
-        return jnp.bitwise_xor(at[1], offset(p))
+    def chunk_of(bits, which):
+        def index(i, at):
+            p = lax.rem(i + half, steps) * per + which
+            total = 0
+            for place, bit in enumerate(bits):
+                total = total + jnp.bitwise_and(jnp.right_shift(p, len(bits) - 1 - place), 1) * bit
+            return jnp.bitwise_xor(at[1], total)
+
+        return index
 
     def kernel(at_ref, *refs):
-        left_refs, refs = refs[: pieces * per], refs[pieces * per :]
-        right_refs, refs = refs[:pieces], refs[pieces:]
-        if extra is not None:
-            extra_refs, refs = refs[:per], refs[per:]
-        keep_ref, send_ref, right_all = refs[len(after) :]
+        refs = list(refs)
+        take = lambda number: [refs.pop(0) for _ in range(number)]
+        ins = []
+        for groups, bits, extra in wholes:
+            sides = [(take(len(lefts) * per), take(len(rights))) for lefts, rights, _ in groups]
+            ins.append((sides, take(per) if extra is not None else []))
+        take(len(after))
+        outs = [take(2) for _ in wholes]
         step = pl.program_id(0)
-
-        @pl.when(step == 0)
-        def _():
-            for at, ref in enumerate(right_refs):
-                right_all[at * lanes : (at + 1) * lanes, :] = ref[...]
-
-        left = jnp.concatenate(
-            [
-                jnp.concatenate([left_refs[at * per + which][...] for which in range(per)], axis=1)
-                for at in range(pieces)
-            ],
-            axis=0,
-        )
-        result = dot(left, right_all[...], ((0,), (0,))).astype(bf16)
-        for target, mine in ((send_ref, step < half), (keep_ref, step >= half)):
-
-            @pl.when(mine)
-            def _(target=target):
+        for (sides, extras), (keep_ref, send_ref) in zip(ins, outs):
+            results = []
+            for own, right_refs in sides:
+                right_all = refs.pop(0)
+
+                @pl.when(step == 0)
+                def _(right_refs=right_refs, right_all=right_all):
+                    for k, ref in enumerate(right_refs):
+                        right_all[k * lanes : (k + 1) * lanes, :] = ref[...]
+
+                left = jnp.concatenate(
+                    [
+                        jnp.concatenate([own[k + which][...] for which in range(per)], axis=1)
+                        for k in range(0, len(own), per)
+                    ],
+                    axis=0,
+                )
+                results.append(dot(left, right_all[...], ((0,), (0,))).astype(bf16))
+            for target, mine in ((send_ref, step < half), (keep_ref, step >= half)):
+
+                @pl.when(mine)
+                def _(target=target, results=results, extras=extras):
+                    for which in range(per):
+                        first = 0
+                        for result in results:
+                            end = first + result.shape[1]
+                            target[which, :chunk, first:end] = (
+                                result[which * chunk : (which + 1) * chunk, :]
+                            )
+                            first = end
+                        if extras:
+                            target[which, chunk:, :] = extras[which][...].astype(bf16)
+
+    in_specs, operands, scratch, shapes, out_specs = [], [], [], [], []
+    for groups, bits, extra in wholes:
+        total_width = sum(width for _, _, width in groups)
+        tail = 0 if extra is None else extra.shape[1]
+        for lefts, rights, width in groups:
+            for handle in lefts:
                 for which in range(per):
-                    target[which, :chunk, :] = result[which * chunk : (which + 1) * chunk, :]
-                    if extra is not None:
-                        target[which, chunk:, :] = extra_refs[which][...].astype(bf16)
-
-    in_specs, operands = [], []
-    for handle in lefts:
-        for which in range(per):
-            in_specs.append(
-                rows_of(handle, (lanes, chunk), lambda i, at, which=which: chunk_of(i, at, which))
-            )
-            operands.append(array_of(handle))
-    for handle in rights:
-        column = handle[2] if isinstance(handle, tuple) and len(handle) == 3 else 0
-        handle = handle[:2] if isinstance(handle, tuple) and handle[1] is not None else array_of(handle)
-        in_specs.append(rows_of(handle, (lanes, width), lambda i, at, column=column: column))
-        operands.append(array_of(handle))
-    if extra is not None:
-        for which in range(per):
+                    in_specs.append(rows_of(handle, (lanes, chunk), chunk_of(bits, which)))
+                    operands.append(array_of(handle))
+            for handle in rights:
+                column = handle[2] if isinstance(handle, tuple) and len(handle) == 3 else 0
+                handle = (
+                    handle[:2] if isinstance(handle, tuple) and handle[1] is not None else array_of(handle)
+                )
+                in_specs.append(rows_of(handle, (lanes, width), lambda i, at, column=column: column))
+                operands.append(array_of(handle))
+            scratch.append(pltpu.VMEM((len(rights) * lanes, width), bf16))
+        for which in range(per if extra is not None else 0):
+            index = chunk_of(bits, which)
             in_specs.append(
                 pl.BlockSpec(
-                    (None, tail, width), lambda i, at, which=which: (chunk_of(i, at, which), 0, 0)
+                    (None, tail, total_width), lambda i, at, index=index: (index(i, at), 0, 0)
                 )
             )
             operands.append(extra)
+        shapes += [jax.ShapeDtypeStruct((count // 2, chunk + tail, total_width), bf16)] * 2
+        block = (per, chunk + tail, total_width)
+        out_specs += [
+            pl.BlockSpec(block, lambda i, at: (jnp.maximum(i - half, 0), 0, 0)),
+            pl.BlockSpec(block, lambda i, at: (jnp.minimum(i, half - 1), 0, 0)),
+        ]
     in_specs += [pl.BlockSpec(memory_space=pl.ANY)] * len(after)
     operands += list(after)
-    shape = jax.ShapeDtypeStruct((count // 2, chunk + tail, width), bf16)
-    block = (per, chunk + tail, width)
-    return pl.pallas_call(
+    out = pl.pallas_call(
         kernel,
-        out_shape=(shape, shape),
+        out_shape=tuple(shapes),
         grid_spec=pltpu.PrefetchScalarGridSpec(
             num_scalar_prefetch=1,
             grid=(steps,),
             in_specs=in_specs,
-            out_specs=[
-                pl.BlockSpec(block, lambda i, at: (jnp.maximum(i - half, 0), 0, 0)),
-                pl.BlockSpec(block, lambda i, at: (jnp.minimum(i, half - 1), 0, 0)),
-            ],
-            scratch_shapes=[pltpu.VMEM((pieces * lanes, width), bf16)],
+            out_specs=out_specs,
+            scratch_shapes=scratch,
         ),
-        compiler_params=params(40),
-        cost_estimate=cost(4),
+        compiler_params=params(48),
+        cost_estimate=cost(4 * len(wholes)),
         name=name,
     )(at, *operands)
+    return [tuple(out[k : k + 2]) for k in range(0, len(out), 2)]
 
 
 def tokens_grad_kernel(at_ref, d0, d1, d2, d3, resid_ref, wq_ref, wk_ref, wv_ref, *refs):
@@ -1449,7 +1488,7 @@
 def last_kernel(at_ref, *refs):
     step = pl.program_id(0)
     firsts, seconds, outs = refs[:blocks], refs[blocks : 2 * blocks], refs[2 * blocks : 2 * blocks + 3]
-    rel_ref, norm_ref, bin_ref, box_ref = refs[2 * blocks + 3 :]
+    wout_ref, rel_ref, norm_ref, bin_ref, box_ref = refs[2 * blocks + 3 :]
     for at in range(blocks):
 
         @pl.when(step == at)
@@ -1458,6 +1497,7 @@
                 span = slice(k * lanes, (k + 1) * lanes)
                 out[:, :lanes] = first[:, span].astype(f32)
                 out[:, lanes:] = second[:lanes, span].astype(f32)
+            wout_ref[...] = first[:, 3 * lanes :].astype(f32)
 
     @pl.when(step == 0)
     def _():
@@ -1476,18 +1516,17 @@
 
 
 def last_call(at, firsts, seconds, buckets, model):
-    rows = blocks * lanes // blocks
     wide = jax.ShapeDtypeStruct((lanes, model), f32)
     column = pl.BlockSpec((lanes, model // blocks), lambda i, at: (0, jnp.bitwise_xor(at[0], i)))
     return pl.pallas_call(
         last_kernel,
-        out_shape=(wide, wide, wide)
+        out_shape=(wide, wide, wide, wide)
         + tuple(jax.ShapeDtypeStruct(shape, f32) for shape in ((buckets, model), (4, lanes), (4, lanes), (8, lanes))),
         grid_spec=pltpu.PrefetchScalarGridSpec(
             num_scalar_prefetch=1,
             grid=(blocks,),
             in_specs=[full(part.shape) for part in firsts + seconds],
-            out_specs=[column] * 3 + [full((buckets, model)), full((4, lanes)), full((4, lanes)), full((8, lanes))],
+            out_specs=[column] * 4 + [full((buckets, model)), full((4, lanes)), full((4, lanes)), full((8, lanes))],
         ),
         compiler_params=params(40),
         cost_estimate=cost(2),
@@ -1504,8 +1543,10 @@
     def step(self):
         self.came = swap(self.send, "docs", self.bits.pop(0))
 
-    def add(self):
+    def add(self, *before):
         keep, came = self.keep, self.came
+        if before:
+            came = ordered(came, *before)
         total = lambda part: (keep[part].astype(f32) + came[part].astype(f32)).astype(bf16)
         if not self.bits:
             self.keep = self.send = total(slice(None))[0]
@@ -1516,11 +1557,6 @@
         sent = self.send
         self.step()
         return sent
-
-    def finish(self):
-        while self.keep.ndim == 3:
-            self.add()
-        return self.keep
 
 
 def shards_tiles(
@@ -1551,7 +1587,7 @@
     )
     ints_far = swap(own_ints, "blk", 2)
     x_core, ints_core = swap(x_own, "blk", 1), swap(own_ints, "blk", 1)
-    x_both, ints_both = swap(x_far, "blk", 1), swap(ints_far, "blk", 1)
+    x_both, ints_both = swap(ordered(x_far, ints_far), "blk", 1), swap(ints_far, "blk", 1)
     xs = (x_own, x_far, x_core, x_both)
     tables = jnp.concatenate([xbias_table.T, ybias_table.T], axis=1).astype(f32)
     tables = tables.reshape(blocks, heads // blocks, 2 * boxes)
@@ -1574,89 +1610,97 @@
         act, w_down, normed1, cotangent[0],
         line(ln1_gain), line(ln1_bias), line(ln2_gain), line(ln2_bias), units // docs,
     )
-    ffn_far = swap(grad_ffn, "blk", 2)
     (
         ga_own, ga_core, ga_far, grad_resid, up_far, up_core, up_own, far3, core3, gattn_own, sums,
     ) = back_call(
         spot, w_down, slope, w_in, w_out, normed1, inverse1, mix, grad_ffn, attended,
         line(ln1_gain), above, units // docs,
     )
-    came_far = swap(ordered(ga_far, ffn_far), "blk", 2)
-    got_core1, got_both1 = swap(core1, "blk", 1), swap(ordered(got_far1, ga_own), "blk", 1)
-    ffn_core, ffn_both = swap(grad_ffn, "blk", 1), swap(ordered(ffn_far, ga_own), "blk", 1)
-    act_all = [act_own, (got_far1, 1), (got_core1, 1), (got_both1, 2)]
-    gffn_all = [grad_ffn, ffn_far, ffn_core, ffn_both]
-    down_halves = weight_grad_call(spot, act_all, gffn_all, bits, after=[ga_own], name="grad_down")
-    down_sum = Halving(down_halves, bits)
-
+    came_far = swap(ordered(ga_far, got_far1), "blk", 2)
     came_core = swap(ga_core, "blk", 1)
     came_both = swap(came_far, "blk", 1)
     ga_all = (ga_own, (came_far, 0), came_core, (came_both, 1))
-    up_far_got = swap(ordered(up_far, came_far), "blk", 2)
+    got_far2 = swap(ordered(up_far, came_far), "blk", 2)
     first_grads, first_boxes = scores_grad_call(
-        0, spot, ga_all, qkv, probs, relkq, row, col, [down_halves[0]]
-    )
-
-    up_core_got, up_both_got = swap(up_core, "blk", 1), swap(ordered(up_far_got, first_grads), "blk", 1)
+        0, spot, ga_all, qkv, probs, relkq, row, col, []
+    )
+
+    got_core1, got_both1 = swap(core1, "blk", 1), swap(ordered(got_far1, came_far), "blk", 1)
+    got_core2, got_both2 = swap(up_core, "blk", 1), swap(ordered(got_far2, first_grads), "blk", 1)
+    got_far3 = swap(ordered(far3, got_far2), "blk", 2)
     hidden_all = [(far1, 0), (got_far1, 0), (got_core1, 0), (got_both1, 0)]
-    up_all = [up_own, (up_far_got, 0), up_core_got, (up_both_got, 1)]
-    got_far3 = swap(ordered(far3, first_grads), "blk", 2)
-    in_halves = weight_grad_call(spot, hidden_all, up_all, other, after=[first_grads], name="grad_in")
-    in_sum = Halving(in_halves, other)
-    down_sent = down_sum.add()
+    act_all = [act_own, (got_far1, 1), (got_core1, 1), (got_both1, 2)]
+    gffn_all = [grad_ffn, (got_far2, 0), (got_core2, 0), (got_both2, 0)]
+    up_all = [up_own, (got_far2, 1), (got_core2, 1), (got_both2, 2)]
+    down_halves, in_halves = weight_grads_call(
+        spot,
+        [([(act_all, gffn_all, model)], bits, None), ([(hidden_all, up_all, model)], other, None)],
+        after=[first_grads], name="grad_down_in",
+    )
+    down_sum, in_sum = Halving(down_halves, bits), Halving(in_halves, other)
     lefts = list(xs) + [rel_table]
 
     def rows_by_piece(grads):
         return [(grads.reshape(blocks + 1, lanes, -1), t) for t in range(blocks + 1)]
 
-    first_halves = weight_grad_call(
-        spot, lefts, rows_by_piece(first_grads), bits, after=[in_halves[0], down_sent], name="grad_qkv"
-    )
-    first_sum = Halving(first_halves, bits)
-    second_grads, dq_own, dq_core, dq_far, small = scores_grad_call(
-        1, spot, ga_all, qkv, probs, relkq, row, col, [first_halves[0]], docs,
-        (w_query, w_key, sums, first_grads, first_boxes),
-    )
-    down_sent = down_sum.add()
-    second_halves = weight_grad_call(
-        spot, lefts, rows_by_piece(second_grads), other, extra=small, after=[down_sent],
-        name="grad_qkv",
-    )
-    second_sum = Halving(second_halves, other)
-    got_core3, got_both3 = swap(core3, "blk", 1), swap(ordered(got_far3, second_grads), "blk", 1)
+    got_core3, got_both3 = swap(core3, "blk", 1), swap(ordered(got_far3, in_halves[0]), "blk", 1)
     att_all = [far3, got_far3, got_core3, got_both3]
     per = model // width
     gattn_all = [
         gattn_own, (got_far3, None, per), (got_core3, None, per), (got_both3, None, per + 1),
     ]
-    out_halves = weight_grad_call(
-        spot, att_all, gattn_all, bits, right_width=width, after=[second_halves[0]], name="grad_out"
-    )
-    out_sum = Halving(out_halves, bits)
-    dq_far_got = swap(dq_far, "blk", 2)
+    first_groups = [(lefts, rows_by_piece(first_grads), 3 * width // 2), (att_all, gattn_all, width)]
+    (first_halves,) = weight_grads_call(
+        spot, [(first_groups, other, None)], after=[in_halves[0]], name="grad_qkv_out"
+    )
+    first_sum = Halving(first_halves, other)
+    second_grads, dq_own, dq_core, dq_far, small = scores_grad_call(
+        1, spot, ga_all, qkv, probs, relkq, row, col, [first_halves[0]], docs,
+        (w_query, w_key, sums, first_grads, first_boxes),
+    )
+    done = down_sum.add(second_grads)
+    done = in_sum.add(done)
+    second_groups = [(lefts, rows_by_piece(second_grads), 3 * width // 2)]
+    (second_halves,) = weight_grads_call(
+        spot, [(second_groups, bits, small)], after=[done], name="grad_qkv"
+    )
+    second_sum = Halving(second_halves, bits)
+    dq_far_got = ordered(swap(dq_far, "blk", 2), second_halves[0])
     dq_core_got, dq_both_got = swap(dq_core, "blk", 1), swap(dq_far_got, "blk", 1)
-    in_sent = in_sum.add()
-    first_sent = first_sum.add()
-    out_sent = out_sum.add()
-    down_part = down_sum.finish()
     grad_tokens = tokens_grad_call(
         spot, (dq_own, (dq_far_got, 0), dq_core_got, (dq_both_got, 1)), grad_resid,
-        w_query, w_key, w_value, [out_halves[0], in_sent, first_sent, out_sent, down_part],
-    )
-    in_part = in_sum.finish()
-    first_part = first_sum.finish()
-    out_part = out_sum.finish()
-    second_part = second_sum.finish()
+        w_query, w_key, w_value, [second_halves[0]],
+    )
 
     def whole(part):
         far = swap(part, "blk", 2)
-        return (part, swap(part, "blk", 1), far, swap(far, "blk", 1))
-
-    grad_w_down, grad_w_in, grad_w_out = parts_call(
-        spot, ((whole(down_part), 0), (whole(in_part), 1), (whole(out_part), 1)), "gather_parts"
-    )
-    *grads, rel_out, norms, b_in_out, both_boxes = last_call(
-        spot, whole(first_part), whole(second_part), rel_table.shape[0] // docs, model
+        return [part, swap(part, "blk", 1), far, far]
+
+    def both(parts, *before):
+        far = ordered(parts[2], *before)
+        return (parts[0], parts[1], far, swap(far, "blk", 1))
+
+    done = down_sum.add(grad_tokens)
+    done = in_sum.add(done)
+    done = second_sum.add(done)
+    done = first_sum.add(done)
+    done = down_sum.add(done)
+    down_all = whole(done)
+    done = second_sum.add(done)
+    done = in_sum.add(done)
+    in_all = whole(done)
+    done = first_sum.add(done)
+    done = second_sum.add(done)
+    second_all = whole(done)
+    done = first_sum.add(done)
+    first_all = whole(done)
+    down_all, in_all = both(down_all, done), both(in_all, done)
+    second_all, first_all = both(second_all, done), both(first_all, done)
+    grad_w_down, grad_w_in = parts_call(
+        spot, ((down_all, 0), (in_all, 1)), "gather_parts"
+    )
+    *grads, grad_w_out, rel_out, norms, b_in_out, both_boxes = last_call(
+        spot, first_all, second_all, rel_table.shape[0] // docs, model
     )
     b_in_out = b_in_out.reshape(-1)
     xb, yb = both_boxes[:, :heads], both_boxes[:, 64 : 64 + heads]

time: 265 us -> 228 us (0.86)
  waiting for transfers between devices: 86.8 us -> 56.2 us
  Pallas kernels: 117 us -> 110 us
  other arithmetic: 10.6 us -> 5.13 us
  local copies, waits for them, and re-layouts: 7.01 us -> 11.7 us
    ppermute x57 -> x48, waiting for transfers between devices: 86.8 us -> 56.2 us  [swap(): return lax.ppermute(array, axis, [(i, i ^ by) for i in range(count)])]
    pallas_call x1, Pallas kernels: 26.5 us -> 19.8 us  [scores_call(): pl.pallas_call(scores_kernel, out_shape=(jax.ShapeDtypeStruct((lanes, wid...]
    unnamed x84 -> x104, local copies, waits for them, and re-layouts: 5.74 us -> 10.5 us
    convert_element_type x10 -> x8, other arithmetic: 5.66 us -> 1.28 us  [add(): (keep[part].astype(f32) + came[part].astype(f32)).astype(bf16)]
    ppermute x57 -> x48, starting transfers between devices: 40.8 us -> 42.6 us  [swap(): return lax.ppermute(array, axis, [(i, i ^ by) for i in range(count)])]
    pallas_call x6 -> x4, Pallas kernels: 19 us -> 19.7 us  [the longest x3 17.1 us: weight_grads_call(): pl.pallas_call(kernel, out_shape=tuple(shapes), grid_spec=pltpu.PrefetchS...]
  transfers between devices with their start and end apart: 57 -> 48, of which waited for: 19 -> 17; matrix products, arithmetic and copies ran while one was open for 4% -> 2% of each run, Pallas kernels for 30% -> 34%
where the time goes in v2:
time: 228 us; the launch traced here: 227 us
  Pallas kernels  110 us (48%)
  waiting for transfers between devices  56.2 us (25%)
  starting transfers between devices  42.6 us (19%)
  local copies, waits for them, and re-layouts  11.7 us (5%)
  other arithmetic  5.13 us (2%)
    ppermute x48, waiting for transfers between devices, swap(): return lax.ppermute(array, axis, [(i, i ^ by) for i in range(count)])  56.2 us
    ppermute x48, starting transfers between devices, swap(): return lax.ppermute(array, axis, [(i, i ^ by) for i in range(count)])  42.6 us
    pallas_call x2, Pallas kernels, scores_grad_call(): pl.pallas_call(functools.partial(scores_grad_kernel, half, len(after)), o...  36 us
    pallas_call x1, Pallas kernels, scores_call(): pl.pallas_call(scores_kernel, out_shape=(jax.ShapeDtypeStruct((lanes, wid...  19.8 us
    pallas_call x3, Pallas kernels, weight_grads_call(): pl.pallas_call(kernel, out_shape=tuple(shapes), grid_spec=pltpu.PrefetchS...  17.1 us
    pallas_call x1, Pallas kernels, back_call(): pl.pallas_call(back_kernel, out_shape=(jax.ShapeDtypeStruct((rows, width)...  12.8 us
    unnamed x104, local copies, waits for them, and re-layouts  10.5 us
    pallas_call x1, Pallas kernels, up_call(): pl.pallas_call(up_kernel, out_shape=(jax.ShapeDtypeStruct((3, rows, model...  9.38 us
  transfers between devices with their start and end apart: 48, of which 17 were waited for; matrix products, arithmetic and copies ran while one was open for 2% of the time, Pallas kernels for 34%

profile of v2, /device:TPU:0, one launch (start us, length us, event | category | flops | bytes accessed | tf_op | source)
XLA Modules:
  0.0 227.0 jit_solution(10940623704950455381)
XLA Ops:
  0.6 3.0 %collective-permute-start = (bf16[128,1024]{1,0:T(8,128)(2,1)}, bf16[128,1024]{1,0:T(8,128)(2,1)S(1)}, u32[]{:S(2)}, u32[]{:S(2)}) collective-permute-start(bf16[128,1024]{1,0:T(8,128)(2,1)} %bitcast.50), channel_id=1, source_target_pairs={{0,16},{8,24},{16,0},{24,8},{1,17},{9,25},{17,1},{25,9},{2,18},{10... | collective-permute-start | bytes 786440 | tf_op jit(solution)/shard_map/ppermute | solution.py:309
  5.3 5.0 %collective-permute-done.2.i1 = s32[8,128]{1,0:T(8,128)S(1)} collective-permute-done((s32[8,128]{1,0:T(8,128)S(1)}, s32[8,128]{1,0:T(8,128)S(1)}, u32[]{:S(2)}, u32[]{:S(2)}) %collective-permute-start.2) | collective-permute-done | bytes 4128 | tf_op jit(solution)/shard_map/ppermute | solution.py:309
  15.5 19.8 %scores.1 = (bf16[128,256]{1,0:T(8,128)(2,1)}, bf16[128,256]{1,0:T(8,128)(2,1)}, bf16[2,128,256]{2,1,0:T(8,128)(2,1)}, bf16[4,512,512]{2,1,0:T(8,128)(2,1)}, bf1...) custom-call(s32[2]{0:T(128)} %pad_add_fusion.1.at_ref, ...), custom_call_target="tpu_custom_call" | custom-call | flops 7500000256 | tf_op jit(solution)/shard_map/scores/pallas_call | solution.py:739
  37.0 4.0 %collective-permute-done.6.a1 = bf16[2,128,256]{2,1,0:T(8,128)(2,1)S(1)} collective-permute-done((bf16[2,128,256]{2,1,0:T(8,128)(2,1)}, bf16[2,128,256]{2,1,0:T(8,128)(2,1)S(1)}, u32[]{:S(2)}, u32[]{:S(2)}) %collective-permute-start.6) | collective-permute-done | bytes 131104 | tf_op jit(solution)/shard_map/ppermute | solution.py:309
  43.6 9.4 %up.1 = (bf16[3,128,1024]{2,1,0:T(8,128)(2,1)S(1)}, bf16[2,128,1024]{2,1,0:T(8,128)(2,1)S(1)}, bf16[128,1024]{1,0:T(8,128)(2,1)S(1)}, bf16[128,4096]{1,0:T(8,128...) custom-call(s32[2]{0:T(128)S(1)} %pad_add_fusion.at_ref.refs_0_, ...), custom_call_target="tpu_custom_call" | custom-call | flops 2700000000 | tf_op jit(solution)/shard_map/up/pallas_call | solution.py:833
  55.5 4.0 %down.1 = (bf16[128,1024]{1,0:T(8,128)(2,1)}, f32[128,1024]{1,0:T(8,128)S(1)}, bf16[128,1024]{1,0:T(8,128)(2,1)S(1)}, f32[8,1024]{1,0:T(8,128)S(1)}) custom-call(bf16[128,4096]{1,0:T(8,128)(2,1)S(1)} %get-tuple-element.100.act_ref, bf16[4096,1024]{1,0:T(8,128)(2,1)S(1)} %copy-done, f32[128,1024]{1,0:T(8,128)S(1)} %get-tuple-element.101.normed_ref, ...), custom_call_target="tpu_custom_call" | custom-call | flops 2400000000 | tf_op jit(solution)/shard_map/down/pallas_call | solution.py:914
  59.5 12.8 %back.1 = (bf16[128,256]{1,0:T(8,128)(2,1)S(1)}, bf16[128,256]{1,0:T(8,128)(2,1)S(1)}, bf16[2,128,256]{2,1,0:T(8,128)(2,1)S(1)}, f32[128,1024]{1,0:T(8,128)S(1)}...) custom-call(s32[2]{0:T(128)S(1)} %pad_add_fusion.at_ref.refs_0_, ...), custom_call_target="tpu_custom_call" | custom-call | flops 3600000000 | tf_op jit(solution)/shard_map/back/pallas_call | solution.py:999
  76.1 5.2 %collective-permute-done.10.refs_2_ = bf16[2,128,256]{2,1,0:T(8,128)(2,1)S(1)} collective-permute-done((bf16[2,128,256]{2,1,0:T(8,128)(2,1)S(1)}, bf16[2,128,256]{2,1,0:T(8,128)(2,1)S(1)}, u32[]{:S(2)}, u32[]{:S(2)}) %collective-permute-start.10) | collective-permute-done | bytes 131104 | tf_op jit(solution)/shard_map/ppermute | solution.py:309
  83.7 17.4 %scores_grad.2 = (bf16[640,384]{1,0:T(8,128)(2,1)}, f32[16,128]{1,0:T(8,128)}) custom-call(s32[2]{0:T(128)} %copy-done.28, bf16[128,256]{1,0:T(8,128)(2,1)} %copy-done.41, bf16[2,128,256]{2,1,0:T(8,128)(2,1)} %copy-done.46, bf16[128,256]{1,0:T(8,128)(2,1)} %copy-done.48, bf16[2,128,256]{2,1,0:T(8,128)(2,1)} %copy-done.47, ...), custom_call_target="tpu_custom_call" | custom-call | flops 4499999744 | tf_op jit(solution)/shard_map/scores_grad/pallas_call | solution.py:1268
  105.9 8.4 %grad_down_in.1 = (bf16[4,128,1024]{2,1,0:T(8,128)(2,1)}, bf16[4,128,1024]{2,1,0:T(8,128)(2,1)}, bf16[4,128,1024]{2,1,0:T(8,128)(2,1)}, bf16[4,128,1024]{2,1,0:T(8,128)(2,1)}) custom-call(s32[2]{0:T(128)S(1)} %copy-done.29, bf16[128,1024]{1,0:T(8,128)(2,1)S(1)} %get-tuple-element.127.refs_0_.refs_1_, ...), custom_call_target="tpu_custom_call" | custom-call | flops 2400000000 | tf_op jit(solution)/shard_map/grad_down_in/pallas_call | solution.py:1386
  119.5 5.5 %grad_qkv_out.1 = (bf16[4,128,640]{2,1,0:T(8,128)(2,1)S(1)}, bf16[4,128,640]{2,1,0:T(8,128)(2,1)S(1)}) custom-call(s32[2]{0:T(128)S(1)} %copy-done.29, bf16[128,1024]{1,0:T(8,128)(2,1)S(1)} %bitcast.54, bf16[128,1024]{1,0:T(8,128)(2,1)S(1)} %bitcast.55, bf16[128,1024]{1,0:T(8,128)(2,1)S(1)} %copy-done.10, bf16[128,1024]{1,0:T(8,128)(2,1)S(1)} %copy-done.10, ...), custom_call_target="tpu_custom_call" | custom-call | flops 1200000000 | tf_op jit(solution)/shard_map/grad_qkv_out/pallas_call | solution.py:1386
  125.9 18.7 %scores_grad.3 = (bf16[640,384]{1,0:T(8,128)(2,1)}, bf16[128,768]{1,0:T(8,128)(2,1)}, bf16[128,768]{1,0:T(8,128)(2,1)}, bf16[2,128,768]{2,1,0:T(8,128)(2,1)}, f32[8,48,384]{2,1,0:T(8,128)}) custom-call(s32[2]{0:T(128)} %copy-done.28, bf16[128,256]{1,0:T(8,128)(2,1)} %copy-done.41, bf16[2,128,256]{2,1,0:T(8,128)(2,1)} %copy-done.46, ...), custom_call_target="tpu_custom_call" | custom-call | flops 4499999744 | tf_op jit(solution)/shard_map/scores_grad/pallas_call | solution.py:1268
  148.6 3.3 %grad_qkv.1 = (bf16[4,176,384]{2,1,0:T(8,128)(2,1)S(1)}, bf16[4,176,384]{2,1,0:T(8,128)(2,1)S(1)}) custom-call(s32[2]{0:T(128)S(1)} %copy-done.30, bf16[128,1024]{1,0:T(8,128)(2,1)S(1)} %bitcast.56, bf16[128,1024]{1,0:T(8,128)(2,1)S(1)} %bitcast.57, bf16[128,1024]{1,0:T(8,128)(2,1)S(1)} %copy-done.10, bf16[128,1024]{1,0:T(8,128)(2,1)S(1)} %copy-done.10, ...), custom_call_target="tpu_custom_call" | custom-call | flops 1200000000 | tf_op jit(solution)/shard_map/grad_qkv/pallas_call | solution.py:1386
  151.9 4.1 %collective-permute-done.21.d1 = bf16[2,128,768]{2,1,0:T(8,128)(2,1)S(1)} collective-permute-done((bf16[2,128,768]{2,1,0:T(8,128)(2,1)}, bf16[2,128,768]{2,1,0:T(8,128)(2,1)S(1)}, u32[]{:S(2)}, u32[]{:S(2)}) %collective-permute-start.21) | collective-permute-done | bytes 393248 | tf_op jit(solution)/shard_map/ppermute | solution.py:309
  160.1 5.0 %tokens_grad.1 = f32[128,1024]{1,0:T(8,128)} custom-call(s32[2]{0:T(128)S(1)} %copy-done.30, bf16[128,768]{1,0:T(8,128)(2,1)S(1)} %copy-done.25, bf16[2,128,768]{2,1,0:T(8,128)(2,1)S(1)} %collective-permute-done.21.d1, bf16[128,768]{1,0:T(8,128)(2,1)S(1)} %collective-permute-done.24.d2, bf16[2,128,768]{2,1,0:T(8,128)(2,1)S(1)} %collective-permute-done.25.d3, ...), custom_call_target="tpu_custom_call" | custom-call | flops 1200000000 | tf_op jit(solution)/shard_map/tokens_grad/pallas_call | solution.py:1434
  167.8 3.5 %collective-permute-done.28 = bf16[2,128,1024]{2,1,0:T(8,128)(2,1)S(1)} collective-permute-done((bf16[2,128,1024]{2,1,0:T(8,128)(2,1)S(1)}, bf16[2,128,1024]{2,1,0:T(8,128)(2,1)S(1)}, u32[]{:S(2)}, u32[]{:S(2)}) %collective-permute-start.28) | collective-permute-done | bytes 524320 | tf_op jit(solution)/shard_map/ppermute | solution.py:309
  171.3 2.7 %collective-permute-start.31 = (bf16[1,128,1024]{2,1,0:T(8,128)(2,1)S(1)}, bf16[1,128,1024]{2,1,0:T(8,128)(2,1)S(1)}, u32[]{:S(2)}, u32[]{:S(2)}) collective-permute-start(bf16[1,128,1024]{2,1,0:T(8,128)(2,1)S(1)} %add_convert_fusion.12), channel_id=1, source_target_pairs={{0,4},{1,5},{2,6},{3,7},{4,0},{5,1},{6,2},{7,3},{8,12},{9,13},{10,... | collective-permute-start | bytes 786440 | tf_op jit(solution)/shard_map/ppermute | solution.py:309
  174.0 7.9 %collective-permute-done.27 = bf16[4,176,384]{2,1,0:T(8,128)(2,1)S(1)} collective-permute-done((bf16[4,176,384]{2,1,0:T(8,128)(2,1)S(1)}, bf16[4,176,384]{2,1,0:T(8,128)(2,1)S(1)}, u32[]{:S(2)}, u32[]{:S(2)}) %collective-permute-start.27) | collective-permute-done | bytes 540704 | tf_op jit(solution)/shard_map/ppermute | solution.py:309
  186.1 6.3 %collective-permute-done.32 = bf16[2,176,384]{2,1,0:T(8,128)(2,1)S(1)} collective-permute-done((bf16[2,176,384]{2,1,0:T(8,128)(2,1)S(1)}, bf16[2,176,384]{2,1,0:T(8,128)(2,1)S(1)}, u32[]{:S(2)}, u32[]{:S(2)}) %collective-permute-start.32) | collective-permute-done | bytes 270368 | tf_op jit(solution)/shard_map/ppermute | solution.py:309
  192.4 3.5 %collective-permute-start.35 = (bf16[1,176,384]{2,1,0:T(8,128)(2,1)S(1)}, bf16[1,176,384]{2,1,0:T(8,128)(2,1)S(1)}, u32[]{:S(2)}, u32[]{:S(2)}) collective-permute-start(bf16[1,176,384]{2,1,0:T(8,128)(2,1)S(1)} %add_convert_fusion.19), channel_id=1, source_target_pairs={{0,4},{1,5},{2,6},{3,7},{4,0},{5,1},{6,2},{7,3},{8,12},{9,13},{10,... | collective-permute-start | bytes 405512 | tf_op jit(solution)/shard_map/ppermute | solution.py:309
  198.2 6.3 %collective-permute-done.35 = bf16[1,176,384]{2,1,0:T(8,128)(2,1)S(1)} collective-permute-done((bf16[1,176,384]{2,1,0:T(8,128)(2,1)S(1)}, bf16[1,176,384]{2,1,0:T(8,128)(2,1)S(1)}, u32[]{:S(2)}, u32[]{:S(2)}) %collective-permute-start.35) | collective-permute-done | bytes 135200 | tf_op jit(solution)/shard_map/ppermute | solution.py:309
  204.6 4.3 %collective-permute-done.34 = bf16[1,128,640]{2,1,0:T(8,128)(2,1)S(1)} collective-permute-done((bf16[1,128,640]{2,1,0:T(8,128)(2,1)S(1)}, bf16[1,128,640]{2,1,0:T(8,128)(2,1)S(1)}, u32[]{:S(2)}, u32[]{:S(2)}) %collective-permute-start.34) | collective-permute-done | bytes 163872 | tf_op jit(solution)/shard_map/ppermute | solution.py:309
  216.4 3.3 %collective-permute-done.40.refs_6_ = bf16[176,384]{1,0:T(8,128)(2,1)S(1)} collective-permute-done((bf16[176,384]{1,0:T(8,128)(2,1)S(1)}, bf16[176,384]{1,0:T(8,128)(2,1)S(1)}, u32[]{:S(2)}, u32[]{:S(2)}) %collective-permute-start.40) | collective-permute-done | bytes 135200 | tf_op jit(solution)/shard_map/ppermute | solution.py:309
  220.2 3.1 %gather_parts.1 = (f32[512,1024]{1,0:T(8,128)}, f32[128,4096]{1,0:T(8,128)}) custom-call(s32[2]{0:T(128)S(1)} %copy-done.30, bf16[128,1024]{1,0:T(8,128)(2,1)S(1)} %fusion.refs_0_, bf16[128,1024]{1,0:T(8,128)(2,1)S(1)} %collective-permute-done.42.refs_1_, bf16[128,1024]{1,0:T(8,128)(2,1)S(1)} %collective-permute-done.43.refs_2_, ...), custom_call_target="tpu_custom_call" | custom-call | flops 600000000 | tf_op jit(solution)/shard_map/gather_parts/pallas_call | solution.py:1476
  (209 shorter events, 59.2 us)
Async XLA Ops:
  0.6 9.6 %collective-permute-start = (bf16[128,1024]{1,0:T(8,128)(2,1)}, bf16[128,1024]{1,0:T(8,128)(2,1)S(1)}, u32[]{:S(2)}, u32[]{:S(2)}) collective-permute-start(bf16[128,1024]{1,0:T(8,128)(2,1)} %bitcast.50), channel_id=1, source_target_pairs={{0,16},{8,24},{16,0},{24,8},{1,17},{9,25},{17,1},{25,9},{2,18},{10... | collective-permute-start | bytes 786440 | tf_op jit(solution)/shard_map/ppermute | solution.py:309
  5.2 8.9 %collective-permute-start.1 = (bf16[128,1024]{1,0:T(8,128)(2,1)}, bf16[128,1024]{1,0:T(8,128)(2,1)S(1)}, u32[]{:S(2)}, u32[]{:S(2)}) collective-permute-start(bf16[128,1024]{1,0:T(8,128)(2,1)} %bitcast.51), channel_id=1, source_target_pairs={{0,8},{8,0},{16,24},{24,16},{1,9},{9,1},{17,25},{25,17},{2,10},{10... | collective-permute-start | bytes 786440 | tf_op jit(solution)/shard_map/ppermute | solution.py:309
  53.8 22.1 %collective-permute-start.9 = (bf16[3,128,1024]{2,1,0:T(8,128)(2,1)S(1)}, bf16[3,128,1024]{2,1,0:T(8,128)(2,1)S(1)}, u32[]{:S(2)}, u32[]{:S(2)}) collective-permute-start(bf16[3,128,1024]{2,1,0:T(8,128)(2,1)S(1)} %get-tuple-element.111.refs_12_.refs_13_), channel_id=1, source_target_pairs={{0,16},{8,24},{16,0},{24,8},{1,17},{9,25},{17,1},{25,9},{2,18},{10... | collective-permute-start | bytes 2359304 | tf_op jit(solution)/shard_map/ppermute | solution.py:309
  81.3 19.8 %collective-permute-start.13 = (bf16[3,128,1024]{2,1,0:T(8,128)(2,1)S(1)}, bf16[3,128,1024]{2,1,0:T(8,128)(2,1)S(1)}, u32[]{:S(2)}, u32[]{:S(2)}) collective-permute-start(bf16[3,128,1024]{2,1,0:T(8,128)(2,1)S(1)} %get-tuple-element.124), channel_id=1, source_target_pairs={{0,16},{8,24},{16,0},{24,8},{1,17},{9,25},{17,1},{25,9},{2,18},{10... | collective-permute-start | bytes 2359304 | tf_op jit(solution)/shard_map/ppermute | solution.py:309
  82.1 22.8 %collective-permute-start.17 = (bf16[3,128,1024]{2,1,0:T(8,128)(2,1)S(1)}, bf16[3,128,1024]{2,1,0:T(8,128)(2,1)S(1)}, u32[]{:S(2)}, u32[]{:S(2)}) collective-permute-start(bf16[3,128,1024]{2,1,0:T(8,128)(2,1)S(1)} %collective-permute-done.9.refs_2_.refs_3_.refs_14_.refs_15_), channel_id=1, source_target_pairs={{0,8},{8,0},{16,24},{24,16},{1,9},{9,1},{17,25},{25,17},{2,10},{10... | collective-permute-start | bytes 2359304 | tf_op jit(solution)/shard_map/ppermute | solution.py:309
  101.9 14.2 %collective-permute-start.14 = (bf16[128,1536]{1,0:T(8,128)(2,1)S(1)}, bf16[128,1536]{1,0:T(8,128)(2,1)S(1)}, u32[]{:S(2)}, u32[]{:S(2)}) collective-permute-start(bf16[128,1536]{1,0:T(8,128)(2,1)S(1)} %get-tuple-element.125.refs_15_.refs_16_), channel_id=1, source_target_pairs={{0,16},{8,24},{16,0},{24,8},{1,17},{9,25},{17,1},{25,9},{2,18},{10... | collective-permute-start | bytes 1179656 | tf_op jit(solution)/shard_map/ppermute | solution.py:309
  114.3 31.8 %collective-permute-start.23 = (bf16[4,128,1024]{2,1,0:T(8,128)(2,1)}, bf16[4,128,1024]{2,1,0:T(8,128)(2,1)S(1)}, u32[]{:S(2)}, u32[]{:S(2)}) collective-permute-start(bf16[4,128,1024]{2,1,0:T(8,128)(2,1)} %get-tuple-element.143), channel_id=1, source_target_pairs={{0,1},{1,0},{2,3},{3,2},{4,5},{5,4},{6,7},{7,6},{8,9},{9,8},{10,11... | collective-permute-start | bytes 3145736 | tf_op jit(solution)/shard_map/ppermute | solution.py:309
  116.6 31.6 %collective-permute-start.22 = (bf16[4,128,1024]{2,1,0:T(8,128)(2,1)}, bf16[4,128,1024]{2,1,0:T(8,128)(2,1)S(1)}, u32[]{:S(2)}, u32[]{:S(2)}) collective-permute-start(bf16[4,128,1024]{2,1,0:T(8,128)(2,1)} %get-tuple-element.141), channel_id=1, source_target_pairs={{0,2},{1,3},{2,0},{3,1},{4,6},{5,7},{6,4},{7,5},{8,10},{9,11},{10,... | collective-permute-start | bytes 3145736 | tf_op jit(solution)/shard_map/ppermute | solution.py:309
  144.6 11.4 %collective-permute-start.21 = (bf16[2,128,768]{2,1,0:T(8,128)(2,1)}, bf16[2,128,768]{2,1,0:T(8,128)(2,1)S(1)}, u32[]{:S(2)}, u32[]{:S(2)}) collective-permute-start(bf16[2,128,768]{2,1,0:T(8,128)(2,1)} %get-tuple-element.138), channel_id=1, source_target_pairs={{0,16},{8,24},{16,0},{24,8},{1,17},{9,25},{17,1},{25,9},{2,18},{10... | collective-permute-start | bytes 1179656 | tf_op jit(solution)/shard_map/ppermute | solution.py:309
  146.5 18.6 %collective-permute-start.29 = (bf16[2,128,1024]{2,1,0:T(8,128)(2,1)S(1)}, bf16[2,128,1024]{2,1,0:T(8,128)(2,1)S(1)}, u32[]{:S(2)}, u32[]{:S(2)}) collective-permute-start(bf16[2,128,1024]{2,1,0:T(8,128)(2,1)S(1)} %get-tuple-element.177), channel_id=1, source_target_pairs={{0,2},{1,3},{2,0},{3,1},{4,6},{5,7},{6,4},{7,5},{8,10},{9,11},{10,... | collective-permute-start | bytes 1572872 | tf_op jit(solution)/shard_map/ppermute | solution.py:309
  156.5 14.8 %collective-permute-start.28 = (bf16[2,128,1024]{2,1,0:T(8,128)(2,1)S(1)}, bf16[2,128,1024]{2,1,0:T(8,128)(2,1)S(1)}, u32[]{:S(2)}, u32[]{:S(2)}) collective-permute-start(bf16[2,128,1024]{2,1,0:T(8,128)(2,1)S(1)} %get-tuple-element.179.refs_17_), channel_id=1, source_target_pairs={{0,1},{1,0},{2,3},{3,2},{4,5},{5,4},{6,7},{7,6},{8,9},{9,8},{10,11... | collective-permute-start | bytes 1572872 | tf_op jit(solution)/shard_map/ppermute | solution.py:309
  156.7 26.9 %collective-permute-start.26 = (bf16[4,128,640]{2,1,0:T(8,128)(2,1)S(1)}, bf16[4,128,640]{2,1,0:T(8,128)(2,1)S(1)}, u32[]{:S(2)}, u32[]{:S(2)}) collective-permute-start(bf16[4,128,640]{2,1,0:T(8,128)(2,1)S(1)} %get-tuple-element.150), channel_id=1, source_target_pairs={{0,2},{1,3},{2,0},{3,1},{4,6},{5,7},{6,4},{7,5},{8,10},{9,11},{10,... | collective-permute-start | bytes 1966088 | tf_op jit(solution)/shard_map/ppermute | solution.py:309
  158.6 23.3 %collective-permute-start.27 = (bf16[4,176,384]{2,1,0:T(8,128)(2,1)S(1)}, bf16[4,176,384]{2,1,0:T(8,128)(2,1)S(1)}, u32[]{:S(2)}, u32[]{:S(2)}) collective-permute-start(bf16[4,176,384]{2,1,0:T(8,128)(2,1)S(1)} %get-tuple-element.151), channel_id=1, source_target_pairs={{0,1},{1,0},{2,3},{3,2},{4,5},{5,4},{6,7},{7,6},{8,9},{9,8},{10,11... | collective-permute-start | bytes 1622024 | tf_op jit(solution)/shard_map/ppermute | solution.py:309
  165.2 19.3 %collective-permute-start.33 = (bf16[1,128,1024]{2,1,0:T(8,128)(2,1)S(1)}, bf16[1,128,1024]{2,1,0:T(8,128)(2,1)S(1)}, u32[]{:S(2)}, u32[]{:S(2)}) collective-permute-start(bf16[1,128,1024]{2,1,0:T(8,128)(2,1)S(1)} %add_convert_fusion.13), channel_id=1, source_target_pairs={{0,4},{1,5},{2,6},{3,7},{4,0},{5,1},{6,2},{7,3},{8,12},{9,13},{10,... | collective-permute-start | bytes 786440 | tf_op jit(solution)/shard_map/ppermute | solution.py:309
  171.3 24.6 %collective-permute-start.31 = (bf16[1,128,1024]{2,1,0:T(8,128)(2,1)S(1)}, bf16[1,128,1024]{2,1,0:T(8,128)(2,1)S(1)}, u32[]{:S(2)}, u32[]{:S(2)}) collective-permute-start(bf16[1,128,1024]{2,1,0:T(8,128)(2,1)S(1)} %add_convert_fusion.12), channel_id=1, source_target_pairs={{0,4},{1,5},{2,6},{3,7},{4,0},{5,1},{6,2},{7,3},{8,12},{9,13},{10,... | collective-permute-start | bytes 786440 | tf_op jit(solution)/shard_map/ppermute | solution.py:309
  182.0 10.3 %collective-permute-start.32 = (bf16[2,176,384]{2,1,0:T(8,128)(2,1)S(1)}, bf16[2,176,384]{2,1,0:T(8,128)(2,1)S(1)}, u32[]{:S(2)}, u32[]{:S(2)}) collective-permute-start(bf16[2,176,384]{2,1,0:T(8,128)(2,1)S(1)} %get-tuple-element.183), channel_id=1, source_target_pairs={{0,2},{1,3},{2,0},{3,1},{4,6},{5,7},{6,4},{7,5},{8,10},{9,11},{10,... | collective-permute-start | bytes 811016 | tf_op jit(solution)/shard_map/ppermute | solution.py:309
  183.9 14.2 %collective-permute-start.30 = (bf16[2,128,640]{2,1,0:T(8,128)(2,1)S(1)}, bf16[2,128,640]{2,1,0:T(8,128)(2,1)S(1)}, u32[]{:S(2)}, u32[]{:S(2)}) collective-permute-start(bf16[2,128,640]{2,1,0:T(8,128)(2,1)S(1)} %get-tuple-element.180), channel_id=1, source_target_pairs={{0,1},{1,0},{2,3},{3,2},{4,5},{5,4},{6,7},{7,6},{8,9},{9,8},{10,11... | collective-permute-start | bytes 983048 | tf_op jit(solution)/shard_map/ppermute | solution.py:309
  184.6 26.9 %collective-permute-start.43 = (bf16[128,1024]{1,0:T(8,128)(2,1)S(1)}, bf16[128,1024]{1,0:T(8,128)(2,1)S(1)}, u32[]{:S(2)}, u32[]{:S(2)}) collective-permute-start(bf16[128,1024]{1,0:T(8,128)(2,1)S(1)} %fusion.refs_0_), channel_id=1, source_target_pairs={{0,16},{8,24},{16,0},{24,8},{1,17},{9,25},{17,1},{25,9},{2,18},{10... | collective-permute-start | bytes 786440 | tf_op jit(solution)/shard_map/ppermute | solution.py:309
  192.4 12.1 %collective-permute-start.35 = (bf16[1,176,384]{2,1,0:T(8,128)(2,1)S(1)}, bf16[1,176,384]{2,1,0:T(8,128)(2,1)S(1)}, u32[]{:S(2)}, u32[]{:S(2)}) collective-permute-start(bf16[1,176,384]{2,1,0:T(8,128)(2,1)S(1)} %add_convert_fusion.19), channel_id=1, source_target_pairs={{0,4},{1,5},{2,6},{3,7},{4,0},{5,1},{6,2},{7,3},{8,12},{9,13},{10,... | collective-permute-start | bytes 405512 | tf_op jit(solution)/shard_map/ppermute | solution.py:309
  196.1 15.4 %collective-permute-start.46 = (bf16[128,1024]{1,0:T(8,128)(2,1)S(1)}, bf16[128,1024]{1,0:T(8,128)(2,1)S(1)}, u32[]{:S(2)}, u32[]{:S(2)}) collective-permute-start(bf16[128,1024]{1,0:T(8,128)(2,1)S(1)} %fusion.1.refs_4_), channel_id=1, source_target_pairs={{0,16},{8,24},{16,0},{24,8},{1,17},{9,25},{17,1},{25,9},{2,18},{10... | collective-permute-start | bytes 786440 | tf_op jit(solution)/shard_map/ppermute | solution.py:309
  198.1 10.7 %collective-permute-start.34 = (bf16[1,128,640]{2,1,0:T(8,128)(2,1)S(1)}, bf16[1,128,640]{2,1,0:T(8,128)(2,1)S(1)}, u32[]{:S(2)}, u32[]{:S(2)}) collective-permute-start(bf16[1,128,640]{2,1,0:T(8,128)(2,1)S(1)} %add_convert_fusion.15), channel_id=1, source_target_pairs={{0,4},{1,5},{2,6},{3,7},{4,0},{5,1},{6,2},{7,3},{8,12},{9,13},{10,... | collective-permute-start | bytes 491528 | tf_op jit(solution)/shard_map/ppermute | solution.py:309
  211.0 8.6 %collective-permute-start.45 = (bf16[128,1024]{1,0:T(8,128)(2,1)S(1)}, bf16[128,1024]{1,0:T(8,128)(2,1)S(1)}, u32[]{:S(2)}, u32[]{:S(2)}) collective-permute-start(bf16[128,1024]{1,0:T(8,128)(2,1)S(1)} %fusion.1.refs_4_), channel_id=1, source_target_pairs={{0,8},{8,0},{16,24},{24,16},{1,9},{9,1},{17,25},{25,17},{2,10},{10... | collective-permute-start | bytes 786440 | tf_op jit(solution)/shard_map/ppermute | solution.py:309
  211.5 8.7 %collective-permute-start.44 = (bf16[128,1024]{1,0:T(8,128)(2,1)S(1)}, bf16[128,1024]{1,0:T(8,128)(2,1)S(1)}, u32[]{:S(2)}, u32[]{:S(2)}) collective-permute-start(bf16[128,1024]{1,0:T(8,128)(2,1)S(1)} %collective-permute-done.43.refs_2_), channel_id=1, source_target_pairs={{0,8},{8,0},{16,24},{24,16},{1,9},{9,1},{17,25},{25,17},{2,10},{10... | collective-permute-start | bytes 786440 | tf_op jit(solution)/shard_map/ppermute | solution.py:309
  211.5 8.7 %collective-permute-start.47 = (bf16[128,1024]{1,0:T(8,128)(2,1)S(1)}, bf16[128,1024]{1,0:T(8,128)(2,1)S(1)}, u32[]{:S(2)}, u32[]{:S(2)}) collective-permute-start(bf16[128,1024]{1,0:T(8,128)(2,1)S(1)} %collective-permute-done.46.refs_6_), channel_id=1, source_target_pairs={{0,8},{8,0},{16,24},{24,16},{1,9},{9,1},{17,25},{25,17},{2,10},{10... | collective-permute-start | bytes 786440 | tf_op jit(solution)/shard_map/ppermute | solution.py:309
  (76 other events, 575.3 us)

commit v3 on v2

--- a/solution.py
+++ b/solution.py
@@ -619,6 +619,10 @@
     return lax.optimization_barrier((array,) + before)[0]
 
 
+def in_hbm(array):
+    return pltpu.with_memory_space_constraint(array, pltpu.HBM)
+
+
 def params(limit):
     return pltpu.CompilerParams(vmem_limit_bytes=limit << 20)
 
@@ -742,11 +746,11 @@
             jax.ShapeDtypeStruct((lanes, width), bf16),
             jax.ShapeDtypeStruct((lanes, width), bf16),
             jax.ShapeDtypeStruct((2, lanes, width), bf16),
-            jax.ShapeDtypeStruct((heads, rows, rows), bf16),
-            jax.ShapeDtypeStruct((rows, 3 * width), bf16),
-            jax.ShapeDtypeStruct((buckets, 2 * width), bf16),
-            jax.ShapeDtypeStruct((8, rows), jnp.int32),
-            jax.ShapeDtypeStruct((rows, 8), jnp.int32),
+            pltpu.HBM((heads, rows, rows), bf16),
+            pltpu.HBM((rows, 3 * width), bf16),
+            pltpu.HBM((buckets, 2 * width), bf16),
+            pltpu.HBM((8, rows), jnp.int32),
+            pltpu.HBM((rows, 8), jnp.int32),
         ),
         grid_spec=pltpu.PrefetchScalarGridSpec(
             num_scalar_prefetch=1,
@@ -779,7 +783,7 @@
                 pltpu.VMEM((64, rows), bf16),
             ],
         ),
-        compiler_params=params(56),
+        compiler_params=params(18),
         cost_estimate=cost(25),
         name="scores",
     )(
@@ -810,8 +814,6 @@
         inverse_ref[...] = jnp.broadcast_to(inverse, inverse_ref.shape)
         hidden = (normed * gain_ref[...] + bias_ref[...]).astype(bf16)
         hidden_low[...] = hidden
-        far_ref[0] = hidden
-        core_ref[0] = hidden
 
     value, slope = gelu_parts(dot(hidden_low[...], win_ref[...]) + bin_ref[...])
     value = value.astype(bf16)
@@ -819,7 +821,7 @@
     slope_ref[...] = slope.astype(bf16)
     strip = tile // blocks
     here = pl.ds(pl.multiple_of(step * strip, strip), strip)
-    for t, target in enumerate((own_ref, far_ref.at[1], core_ref.at[1], far_ref.at[2])):
+    for t, target in enumerate((own_ref, far_ref.at[0], core_ref, far_ref.at[1])):
         first = pl.multiple_of(jnp.bitwise_xor(at_ref[0], slots[t]) * strip, strip)
         target[:, here] = act_ref[:, pl.ds(first, strip)]
 
@@ -833,13 +835,14 @@
     return pl.pallas_call(
         up_kernel,
         out_shape=(
-            jax.ShapeDtypeStruct((3, rows, model), bf16),
-            jax.ShapeDtypeStruct((2, rows, model), bf16),
+            jax.ShapeDtypeStruct((2, rows, quarter), bf16),
+            jax.ShapeDtypeStruct((rows, quarter), bf16),
             jax.ShapeDtypeStruct((rows, quarter), bf16),
             jax.ShapeDtypeStruct((rows, units), bf16),
             jax.ShapeDtypeStruct((rows, units), bf16),
             jax.ShapeDtypeStruct((rows, model), f32),
             jax.ShapeDtypeStruct((rows, lanes), f32),
+            jax.ShapeDtypeStruct((rows, model), bf16),
             jax.ShapeDtypeStruct((rows, model), bf16),
         ),
         grid_spec=pltpu.PrefetchScalarGridSpec(
@@ -855,18 +858,18 @@
                 pl.BlockSpec((1, tile), column),
             ],
             out_specs=[
-                full((3, rows, model)),
-                full((2, rows, model)),
+                full((2, rows, quarter)),
+                full((rows, quarter)),
                 full((rows, quarter)),
                 pl.BlockSpec((rows, tile), column),
                 pl.BlockSpec((rows, tile), column),
                 full((rows, model)),
                 full((rows, lanes)),
                 full((rows, model)),
+                full((rows, model)),
             ],
-            scratch_shapes=[pltpu.VMEM((rows, model), bf16)],
         ),
-        compiler_params=params(40),
+        compiler_params=params(18),
         cost_estimate=cost(9),
         name="up",
     )(at, *map(array_of, pieces), x_own, w_out, gain, bias, w_in, b_in)
@@ -928,7 +931,7 @@
         ]
         + [full((1, model))] * 4,
         out_specs=[full((rows, model))] * 3 + [full((8, model))],
-        compiler_params=params(40),
+        compiler_params=params(18),
         cost_estimate=cost(8),
         name="down",
     )(act, w_down, normed, cotangent, gain1, bias1, gain2, bias2)
@@ -936,7 +939,7 @@
 
 def back_kernel(
     at_ref, wdown_ref, slope_ref, win_ref, wout_ref, normed_ref, inverse_ref, mix_ref, ffn_ref,
-    attended_ref, gain1_ref, above_ref,
+    attended_ref, gain1_ref, above_ref, hidden_ref,
     own_ref, core_ref, far_ref, resid_ref, upfar_ref, upcore_ref, upown_ref,
     outfar_ref, outcore_ref, outown_ref, sums_ref,
     total, grad_up,
@@ -963,9 +966,9 @@
     @pl.when(step == steps - 1)
     def _():
         upown_ref[...] = grad_up[0]
-        upcore_ref[0] = ffn_ref[...]
+        upcore_ref[0] = hidden_ref[...]
         upcore_ref[1] = grad_up[1]
-        upfar_ref[0] = ffn_ref[...]
+        upfar_ref[0] = hidden_ref[...]
         upfar_ref[1] = grad_up[2]
         upfar_ref[2] = grad_up[3]
         grad = total[...]
@@ -991,7 +994,7 @@
 
 
 def back_call(
-    at, w_down, slope, w_in, w_out, normed, inverse, mix, grad_ffn, attended, gain1, above, tile,
+    at, w_down, slope, w_in, w_out, normed, inverse, mix, grad_ffn, attended, gain1, above, hidden, tile,
 ):
     rows, units = slope.shape
     model = w_out.shape[0]
@@ -1026,6 +1029,7 @@
                 full((rows, model)),
                 full((1, model)),
                 full((8, model)),
+                full((rows, model)),
             ],
             out_specs=[
                 full((rows, width)),
@@ -1045,10 +1049,10 @@
                 pltpu.VMEM((blocks, rows, model), bf16),
             ],
         ),
-        compiler_params=params(40),
+        compiler_params=params(18),
         cost_estimate=cost(12),
         name="back",
-    )(at, w_down, slope, w_in, w_out, normed, inverse, mix, grad_ffn, attended, gain1, above)
+    )(at, w_down, slope, w_in, w_out, normed, inverse, mix, grad_ffn, attended, gain1, above, hidden)
 
 
 def scores_grad_kernel(half, held, *refs):
@@ -1265,8 +1269,9 @@
         scratch = scratch + [pltpu.VMEM(box_shape, f32)]
     else:
         shapes = (grads, jax.ShapeDtypeStruct(box_shape, f32))
+    at = ordered(at, *after) if after else at
     return pl.pallas_call(
-        functools.partial(scores_grad_kernel, half, len(after)),
+        functools.partial(scores_grad_kernel, half, 0),
         out_shape=shapes,
         grid_spec=pltpu.PrefetchScalarGridSpec(
             num_scalar_prefetch=1,
@@ -1279,15 +1284,14 @@
                 full((8, rows)),
                 full((rows, 8)),
             ]
-            + extra_specs
-            + [pl.BlockSpec(memory_space=pl.ANY)] * len(after),
+            + extra_specs,
             out_specs=[full(shape.shape) for shape in shapes],
             scratch_shapes=scratch,
         ),
-        compiler_params=params(56),
+        compiler_params=params(18),
         cost_estimate=cost(15),
         name="scores_grad",
-    )(at, *map(array_of, pieces), qkv, probs, relkq, row, col, *extra, *after)
+    )(at, *map(array_of, pieces), qkv, probs, relkq, row, col, *extra)
 
 
 def weight_grads_call(at, wholes, after=(), name="weight_grads"):
@@ -1314,7 +1318,6 @@
         for groups, bits, extra in wholes:
             sides = [(take(len(lefts) * per), take(len(rights))) for lefts, rights, _ in groups]
             ins.append((sides, take(per) if extra is not None else []))
-        take(len(after))
         outs = [take(2) for _ in wholes]
         step = pl.program_id(0)
         for (sides, extras), (keep_ref, send_ref) in zip(ins, outs):
@@ -1381,8 +1384,7 @@
             pl.BlockSpec(block, lambda i, at: (jnp.maximum(i - half, 0), 0, 0)),
             pl.BlockSpec(block, lambda i, at: (jnp.minimum(i, half - 1), 0, 0)),
         ]
-    in_specs += [pl.BlockSpec(memory_space=pl.ANY)] * len(after)
-    operands += list(after)
+    at = ordered(at, *after) if after else at
     out = pl.pallas_call(
         kernel,
         out_shape=tuple(shapes),
@@ -1393,8 +1395,8 @@
             out_specs=out_specs,
             scratch_shapes=scratch,
         ),
-        compiler_params=params(48),
-        cost_estimate=cost(4 * len(wholes)),
+        compiler_params=params(18),
+        cost_estimate=cost(0.01),
         name=name,
     )(at, *operands)
     return [tuple(out[k : k + 2]) for k in range(0, len(out), 2)]
@@ -1431,6 +1433,7 @@
         return (0, jnp.bitwise_xor(at[0], offset))
 
     weight = pl.BlockSpec((model, width), column)
+    at = ordered(at, *after) if after else at
     return pl.pallas_call(
         tokens_grad_kernel,
         out_shape=jax.ShapeDtypeStruct((rows, model), f32),
@@ -1438,14 +1441,13 @@
             num_scalar_prefetch=1,
             grid=(blocks,),
             in_specs=[rows_of(piece, tile) for piece in pieces]
-            + [full((rows, model)), weight, weight, weight]
-            + [pl.BlockSpec(memory_space=pl.ANY)] * len(after),
+            + [full((rows, model)), weight, weight, weight],
             out_specs=full((rows, model)),
         ),
-        compiler_params=params(40),
+        compiler_params=params(18),
         cost_estimate=cost(4),
         name="tokens_grad",
-    )(at, *map(array_of, pieces), resid, w_query, w_key, w_value, *after)
+    )(at, *map(array_of, pieces), resid, w_query, w_key, w_value)
 
 
 def parts_kernel(fields, at_ref, *refs):
@@ -1479,7 +1481,7 @@
         grid_spec=pltpu.PrefetchScalarGridSpec(
             num_scalar_prefetch=1, grid=(blocks,), in_specs=in_specs, out_specs=out_specs
         ),
-        compiler_params=params(40),
+        compiler_params=params(18),
         cost_estimate=cost(2),
         name=name,
     )(at, *operands)
@@ -1528,7 +1530,7 @@
             in_specs=[full(part.shape) for part in firsts + seconds],
             out_specs=[column] * 4 + [full((buckets, model)), full((4, lanes)), full((4, lanes)), full((8, lanes))],
         ),
-        compiler_params=params(40),
+        compiler_params=params(18),
         cost_estimate=cost(2),
         name="last",
     )(at, *firsts, *seconds)
@@ -1574,6 +1576,7 @@
     bits = bits_of(docs)
     other = [bits[1], bits[0]] + bits[2:]
     x_own = tokens[0]
+    w_query, w_key, w_value = in_hbm(w_query), in_hbm(w_key), in_hbm(w_value)
 
     x_far = swap(x_own, "blk", 2)
     own_ints = jnp.concatenate(
@@ -1588,7 +1591,7 @@
     ints_far = swap(own_ints, "blk", 2)
     x_core, ints_core = swap(x_own, "blk", 1), swap(own_ints, "blk", 1)
     x_both, ints_both = swap(ordered(x_far, ints_far), "blk", 1), swap(ints_far, "blk", 1)
-    xs = (x_own, x_far, x_core, x_both)
+    xs = tuple(map(in_hbm, (x_own, x_far, x_core, x_both)))
     tables = jnp.concatenate([xbias_table.T, ybias_table.T], axis=1).astype(f32)
     tables = tables.reshape(blocks, heads // blocks, 2 * boxes)
     at = jnp.stack([place.astype(jnp.int32), lengths[0]])
@@ -1601,7 +1604,7 @@
     came_core = swap(att_core, "blk", 1)
     came_both = swap(came_far, "blk", 1)
     line = lambda vector: vector.reshape(1, -1)
-    far1, core1, act_own, act, slope, normed1, inverse1, attended = up_call(
+    far1, core1, act_own, act, slope, normed1, inverse1, attended, hidden = up_call(
         spot, (att_own, (came_far, 0), came_core, (came_both, 1)), x_own, w_out,
         line(ln1_gain), line(ln1_bias), w_in, line(b_in), docs,
     )
@@ -1614,30 +1617,33 @@
         ga_own, ga_core, ga_far, grad_resid, up_far, up_core, up_own, far3, core3, gattn_own, sums,
     ) = back_call(
         spot, w_down, slope, w_in, w_out, normed1, inverse1, mix, grad_ffn, attended,
-        line(ln1_gain), above, units // docs,
-    )
-    came_far = swap(ordered(ga_far, got_far1), "blk", 2)
+        line(ln1_gain), above, hidden, units // docs,
+    )
+    came_far = swap(ga_far, "blk", 2)
     came_core = swap(ga_core, "blk", 1)
     came_both = swap(came_far, "blk", 1)
     ga_all = (ga_own, (came_far, 0), came_core, (came_both, 1))
+    ffn_far = swap(grad_ffn, "blk", 2)
+    got_core1, got_both1 = swap(core1, "blk", 1), swap(ordered(got_far1, ga_own), "blk", 1)
+    ffn_core, ffn_both = swap(grad_ffn, "blk", 1), swap(ordered(ffn_far, ga_own), "blk", 1)
+    act_all = [act_own, (got_far1, 0), got_core1, (got_both1, 1)]
+    gffn_all = [grad_ffn, ffn_far, ffn_core, ffn_both]
+    (down_halves,) = weight_grads_call(
+        spot, [([(act_all, gffn_all, model)], bits, None)], after=[ga_own], name="grad_down"
+    )
+    down_sum = Halving(down_halves, bits)
     got_far2 = swap(ordered(up_far, came_far), "blk", 2)
     first_grads, first_boxes = scores_grad_call(
-        0, spot, ga_all, qkv, probs, relkq, row, col, []
-    )
-
-    got_core1, got_both1 = swap(core1, "blk", 1), swap(ordered(got_far1, came_far), "blk", 1)
+        0, spot, ga_all, qkv, probs, relkq, row, col, [down_halves[0]]
+    )
     got_core2, got_both2 = swap(up_core, "blk", 1), swap(ordered(got_far2, first_grads), "blk", 1)
     got_far3 = swap(ordered(far3, got_far2), "blk", 2)
-    hidden_all = [(far1, 0), (got_far1, 0), (got_core1, 0), (got_both1, 0)]
-    act_all = [act_own, (got_far1, 1), (got_core1, 1), (got_both1, 2)]
-    gffn_all = [grad_ffn, (got_far2, 0), (got_core2, 0), (got_both2, 0)]
+    hidden_all = [hidden, (got_far2, 0), (got_core2, 0), (got_both2, 0)]
     up_all = [up_own, (got_far2, 1), (got_core2, 1), (got_both2, 2)]
-    down_halves, in_halves = weight_grads_call(
-        spot,
-        [([(act_all, gffn_all, model)], bits, None), ([(hidden_all, up_all, model)], other, None)],
-        after=[first_grads], name="grad_down_in",
-    )
-    down_sum, in_sum = Halving(down_halves, bits), Halving(in_halves, other)
+    (in_halves,) = weight_grads_call(
+        spot, [([(hidden_all, up_all, model)], bits, None)], after=[first_grads], name="grad_in"
+    )
+    in_sum = Halving(in_halves, bits)
     lefts = list(xs) + [rel_table]
 
     def rows_by_piece(grads):
@@ -1649,9 +1655,10 @@
     gattn_all = [
         gattn_own, (got_far3, None, per), (got_core3, None, per), (got_both3, None, per + 1),
     ]
+    done = down_sum.add(in_halves[0])
     first_groups = [(lefts, rows_by_piece(first_grads), 3 * width // 2), (att_all, gattn_all, width)]
     (first_halves,) = weight_grads_call(
-        spot, [(first_groups, other, None)], after=[in_halves[0]], name="grad_qkv_out"
+        spot, [(first_groups, other, None)], after=[in_halves[0], done], name="grad_qkv_out"
     )
     first_sum = Halving(first_halves, other)
     second_grads, dq_own, dq_core, dq_far, small = scores_grad_call(
@@ -1667,40 +1674,34 @@
     second_sum = Halving(second_halves, bits)
     dq_far_got = ordered(swap(dq_far, "blk", 2), second_halves[0])
     dq_core_got, dq_both_got = swap(dq_core, "blk", 1), swap(dq_far_got, "blk", 1)
+    done = first_sum.add(second_halves[0])
     grad_tokens = tokens_grad_call(
         spot, (dq_own, (dq_far_got, 0), dq_core_got, (dq_both_got, 1)), grad_resid,
-        w_query, w_key, w_value, [second_halves[0]],
-    )
-
-    def whole(part):
+        w_query, w_key, w_value, [done],
+    )
+
+    def whole(part, *before):
         far = swap(part, "blk", 2)
-        return [part, swap(part, "blk", 1), far, far]
-
-    def both(parts, *before):
-        far = ordered(parts[2], *before)
-        return (parts[0], parts[1], far, swap(far, "blk", 1))
-
-    done = down_sum.add(grad_tokens)
-    done = in_sum.add(done)
+        held = ordered(far, *before) if before else far
+        return (part, swap(part, "blk", 1), far, swap(held, "blk", 1))
+
+    done = in_sum.add(grad_tokens)
     done = second_sum.add(done)
+    done = down_sum.add(done)
+    down_part = done
     done = first_sum.add(done)
-    done = down_sum.add(done)
-    down_all = whole(done)
     done = second_sum.add(done)
     done = in_sum.add(done)
-    in_all = whole(done)
+    in_part = done
     done = first_sum.add(done)
+    first_part = done
     done = second_sum.add(done)
-    second_all = whole(done)
-    done = first_sum.add(done)
-    first_all = whole(done)
-    down_all, in_all = both(down_all, done), both(in_all, done)
-    second_all, first_all = both(second_all, done), both(first_all, done)
+    second_part = done
     grad_w_down, grad_w_in = parts_call(
-        spot, ((down_all, 0), (in_all, 1)), "gather_parts"
+        spot, ((whole(down_part, done), 0), (whole(in_part, done), 1)), "gather_parts"
     )
     *grads, grad_w_out, rel_out, norms, b_in_out, both_boxes = last_call(
-        spot, first_all, second_all, rel_table.shape[0] // docs, model
+        spot, whole(first_part, grad_w_down), whole(second_part, grad_w_down), rel_table.shape[0] // docs, model
     )
     b_in_out = b_in_out.reshape(-1)
     xb, yb = both_boxes[:, :heads], both_boxes[:, 64 : 64 + heads]

time: 228 us -> 204 us (0.89)
  Pallas kernels: 110 us -> 99.2 us
  starting transfers between devices: 42.6 us -> 32.6 us
  local copies, waits for them, and re-layouts: 11.7 us -> 6.36 us
  waiting for transfers between devices: 56.2 us -> 59.8 us
    ppermute x48 -> x51, starting transfers between devices: 42.6 us -> 32.6 us  [swap(): return lax.ppermute(array, axis, [(i, i ^ by) for i in range(count)])]
    pallas_call x3, Pallas kernels: 45.4 us -> 37.7 us  [the longest x2 31.3 us: scores_grad_call(): pl.pallas_call(functools.partial(scores_grad_kernel, half, 0), out_shape=...]
    unnamed x104 -> x40, local copies, waits for them, and re-layouts: 10.5 us -> 5.09 us
    ppermute x48 -> x51, waiting for transfers between devices: 56.2 us -> 59.8 us  [swap(): return lax.ppermute(array, axis, [(i, i ^ by) for i in range(count)])]
    pallas_call x1, Pallas kernels: 12.8 us -> 9.64 us  [back_call(): pl.pallas_call(back_kernel, out_shape=(jax.ShapeDtypeStruct((rows, width)...]
    pallas_call x3 -> x4, Pallas kernels: 17.1 us -> 16.7 us  [weight_grads_call(): pl.pallas_call(kernel, out_shape=tuple(shapes), grid_spec=pltpu.PrefetchS...]
  transfers between devices with their start and end apart: 48 -> 51, of which waited for: 17 -> 20; matrix products, arithmetic and copies ran while one was open for 2% -> 2% of each run, Pallas kernels for 34% -> 35%
where the time goes in v3:
time: 204 us
  Pallas kernels  99.2 us (49%)
  waiting for transfers between devices  59.8 us (29%)
  starting transfers between devices  32.6 us (16%)
  local copies, waits for them, and re-layouts  6.36 us (3%)
  other arithmetic  4.05 us (2%)
    ppermute x51, waiting for transfers between devices, swap(): return lax.ppermute(array, axis, [(i, i ^ by) for i in range(count)])  59.8 us
    ppermute x51, starting transfers between devices, swap(): return lax.ppermute(array, axis, [(i, i ^ by) for i in range(count)])  32.6 us
    pallas_call x2, Pallas kernels, scores_grad_call(): pl.pallas_call(functools.partial(scores_grad_kernel, half, 0), out_shape=...  31.3 us
    pallas_call x1, Pallas kernels, scores_call(): pl.pallas_call(scores_kernel, out_shape=(jax.ShapeDtypeStruct((lanes, wid...  19.4 us
    pallas_call x4, Pallas kernels, weight_grads_call(): pl.pallas_call(kernel, out_shape=tuple(shapes), grid_spec=pltpu.PrefetchS...  16.7 us
    pallas_call x1, Pallas kernels, back_call(): pl.pallas_call(back_kernel, out_shape=(jax.ShapeDtypeStruct((rows, width)...  9.64 us
    pallas_call x1, Pallas kernels, up_call(): pl.pallas_call(up_kernel, out_shape=(jax.ShapeDtypeStruct((2, rows, quart...  6.35 us
    pallas_call x1, Pallas kernels, tokens_grad_call(): pl.pallas_call(tokens_grad_kernel, out_shape=jax.ShapeDtypeStruct((rows,...  6.22 us
  transfers between devices with their start and end apart: 51, of which 20 were waited for; matrix products, arithmetic and copies ran while one was open for 2% of the time, Pallas kernels for 35%

profile of v3, /device:TPU:0, one launch (start us, length us, event | category | flops | bytes accessed | tf_op | source)
XLA Modules:
  0.0 203.7 jit_solution(556370569283202896)
XLA Ops:
  0.6 3.0 %collective-permute-start = (bf16[128,1024]{1,0:T(8,128)(2,1)}, bf16[128,1024]{1,0:T(8,128)(2,1)S(1)}, u32[]{:S(2)}, u32[]{:S(2)}) collective-permute-start(bf16[128,1024]{1,0:T(8,128)(2,1)} %bitcast.50), channel_id=1, source_target_pairs={{0,16},{8,24},{16,0},{24,8},{1,17},{9,25},{17,1},{25,9},{2,18},{10... | collective-permute-start | bytes 786440 | tf_op jit(solution)/shard_map/ppermute | solution.py:309
  5.2 5.1 %collective-permute-done.2.i1 = s32[8,128]{1,0:T(8,128)S(1)} collective-permute-done((s32[8,128]{1,0:T(8,128)S(1)}, s32[8,128]{1,0:T(8,128)S(1)}, u32[]{:S(2)}, u32[]{:S(2)}) %collective-permute-start.2) | collective-permute-done | bytes 4128 | tf_op jit(solution)/shard_map/ppermute | solution.py:309
  15.0 19.4 %scores.1 = (bf16[128,256]{1,0:T(8,128)(2,1)S(1)}, bf16[128,256]{1,0:T(8,128)(2,1)S(1)}, bf16[2,128,256]{2,1,0:T(8,128)(2,1)S(1)}, bf16[4,512,512]{2,1,0:T(8,128...) custom-call(s32[2]{0:T(128)S(1)} %pad_add_fusion.1.at_ref, ...), custom_call_target="tpu_custom_call" | custom-call | flops 7500000256 | tf_op jit(solution)/shard_map/scores/pallas_call | solution.py:743
  36.1 3.8 %collective-permute-done.6.a1 = bf16[2,128,256]{2,1,0:T(8,128)(2,1)S(1)} collective-permute-done((bf16[2,128,256]{2,1,0:T(8,128)(2,1)S(1)}, bf16[2,128,256]{2,1,0:T(8,128)(2,1)S(1)}, u32[]{:S(2)}, u32[]{:S(2)}) %collective-permute-start.6) | collective-permute-done | bytes 131104 | tf_op jit(solution)/shard_map/ppermute | solution.py:309
  41.5 3.4 %copy-done = bf16[1024,4096]{1,0:T(8,128)(2,1)S(1)} copy-done((bf16[1024,4096]{1,0:T(8,128)(2,1)S(1)}, bf16[1024,4096]{1,0:T(8,128)(2,1)}, u32[]{:S(2)}) %copy-start) | copy-done | bytes 8388632
  44.9 6.3 %up.1 = (bf16[2,128,1024]{2,1,0:T(8,128)(2,1)S(1)}, bf16[128,1024]{1,0:T(8,128)(2,1)S(1)}, bf16[128,1024]{1,0:T(8,128)(2,1)S(1)}, bf16[128,4096]{1,0:T(8,128)(2,...) custom-call(s32[2]{0:T(128)S(1)} %pad_add_fusion.at_ref.refs_0_, ...), custom_call_target="tpu_custom_call" | custom-call | flops 2700000000 | tf_op jit(solution)/shard_map/up/pallas_call | solution.py:835
  53.0 4.0 %down.1 = (bf16[128,1024]{1,0:T(8,128)(2,1)}, f32[128,1024]{1,0:T(8,128)S(1)}, bf16[128,1024]{1,0:T(8,128)(2,1)S(1)}, f32[8,1024]{1,0:T(8,128)S(1)}) custom-call(bf16[128,4096]{1,0:T(8,128)(2,1)S(1)} %get-tuple-element.108.act_ref, bf16[4096,1024]{1,0:T(8,128)(2,1)S(1)} %copy-done.2, f32[128,1024]{1,0:T(8,128)S(1)} %get-tuple-element.109.normed_ref, ...), custom_call_target="tpu_custom_call" | custom-call | flops 2400000000 | tf_op jit(solution)/shard_map/down/pallas_call | solution.py:917
  57.3 9.6 %back.1 = (bf16[128,256]{1,0:T(8,128)(2,1)S(1)}, bf16[128,256]{1,0:T(8,128)(2,1)S(1)}, bf16[2,128,256]{2,1,0:T(8,128)(2,1)S(1)}, f32[128,1024]{1,0:T(8,128)S(1)}...) custom-call(s32[2]{0:T(128)S(1)} %pad_add_fusion.at_ref.refs_0_, ...), custom_call_target="tpu_custom_call" | custom-call | flops 3600000000 | tf_op jit(solution)/shard_map/back/pallas_call | solution.py:1002
  69.0 4.8 %collective-permute-done.15.refs_2_ = bf16[2,128,256]{2,1,0:T(8,128)(2,1)S(1)} collective-permute-done((bf16[2,128,256]{2,1,0:T(8,128)(2,1)S(1)}, bf16[2,128,256]{2,1,0:T(8,128)(2,1)S(1)}, u32[]{:S(2)}, u32[]{:S(2)}) %collective-permute-start.15) | collective-permute-done | bytes 131104 | tf_op jit(solution)/shard_map/ppermute | solution.py:309
  77.5 3.4 %grad_down.1 = (bf16[4,128,1024]{2,1,0:T(8,128)(2,1)S(1)}, bf16[4,128,1024]{2,1,0:T(8,128)(2,1)S(1)}) custom-call(s32[2]{0:T(128)S(1)} %pad_add_fusion.at_ref.refs_0_, bf16[128,1024]{1,0:T(8,128)(2,1)S(1)} %get-tuple-element.120.refs_0_.refs_1_, bf16[128,1024]{1,0:T(8,128)(2,1)S(1)} %get-tuple-element.120.refs_0_.refs_1_, ...), custom_call_target="tpu_custom_call" | custom-call | flops 3000000 | tf_op jit(solution)/shard_map/grad_down/pallas_call | solution.py:1388
  82.6 14.9 %scores_grad.2 = (bf16[640,384]{1,0:T(8,128)(2,1)S(1)}, f32[16,128]{1,0:T(8,128)S(1)}) custom-call(s32[2]{0:T(128)S(1)} %pad_add_fusion.at_ref.refs_0_, bf16[128,256]{1,0:T(8,128)(2,1)S(1)} %get-tuple-element.118.refs_1_, bf16[2,128,256]{2,1,0:T(8,128)(2,1)S(1)} %collective-permute-done.15.refs_2_, bf16[128,256]{1,0:T(8,128)(2,1)S(1)} %collective-permute-done.16.refs_3_, ...), custom_call_target="tpu_custom_call" | custom-call | flops 4499999744 | tf_op jit(solution)/shard_map/scores_grad/pallas_call | solution.py:1273
  100.6 3.4 %grad_in.1 = (bf16[4,128,1024]{2,1,0:T(8,128)(2,1)S(1)}, bf16[4,128,1024]{2,1,0:T(8,128)(2,1)S(1)}) custom-call(s32[2]{0:T(128)S(1)} %pad_add_fusion.at_ref.refs_0_, bf16[128,1024]{1,0:T(8,128)(2,1)S(1)} %get-tuple-element.117.hidden_ref.refs_0_.refs_1_, bf16[128,1024]{1,0:T(8,128)(2,1)S(1)} %get-tuple-element.117.hidden_ref.refs_0_.refs_1_, ...), custom_call_target="tpu_custom_call" | custom-call | flops 3000000 | tf_op jit(solution)/shard_map/grad_in/pallas_call | solution.py:1388
  104.1 5.1 %collective-permute-done.22.refs_17_.refs_18_.refs_24_ = bf16[128,1536]{1,0:T(8,128)(2,1)S(1)} collective-permute-done((bf16[128,1536]{1,0:T(8,128)(2,1)S(1)}, bf16[128,1536]{1,0:T(8,128)(2,1)S(1)}, u32[]{:S(2)}, u32[]{:S(2)}) %collective-permute-start.22) | collective-permute-done | bytes 393248 | tf_op jit(solution)/shard_map/ppermute | solution.py:309
  112.0 5.8 %grad_qkv_out.1 = (bf16[4,128,640]{2,1,0:T(8,128)(2,1)S(1)}, bf16[4,128,640]{2,1,0:T(8,128)(2,1)S(1)}) custom-call(s32[2]{0:T(128)S(1)} %pad_add_fusion.at_ref.refs_0_, bf16[128,1024]{1,0:T(8,128)(2,1)} %bitcast.53, bf16[128,1024]{1,0:T(8,128)(2,1)} %bitcast.54, bf16[128,1024]{1,0:T(8,128)(2,1)} %copy-done.18, bf16[128,1024]{1,0:T(8,128)(2,1)} %copy-done.18, ...), custom_call_target="tpu_custom_call" | custom-call | flops 3000000 | tf_op jit(solution)/shard_map/grad_qkv_out/pallas_call | solution.py:1388
  118.8 16.5 %scores_grad.3 = (bf16[640,384]{1,0:T(8,128)(2,1)S(1)}, bf16[128,768]{1,0:T(8,128)(2,1)S(1)}, bf16[128,768]{1,0:T(8,128)(2,1)S(1)}, bf16[2,128,768]{2,1,0:T(8,128)(2,1)S(1)}, f32[8,48,384]{2,1,0:T(8,128)S(1)}) custom-call(s32[2]{0:T(128)S(1)} %pad_add_fusion.at_ref.refs_0_, bf16[128,256]{1,0:T(8,128)(2,1)S(1)} %get-tuple-element.118.refs_1_, ...), custom_call_target="tpu_custom_call" | custom-call | flops 4499999744 | tf_op jit(solution)/shard_map/scores_grad/pallas_call | solution.py:1273
  137.5 4.0 %grad_qkv.1 = (bf16[4,176,384]{2,1,0:T(8,128)(2,1)S(1)}, bf16[4,176,384]{2,1,0:T(8,128)(2,1)S(1)}) custom-call(s32[2]{0:T(128)S(1)} %pad_add_fusion.at_ref.refs_0_, bf16[128,1024]{1,0:T(8,128)(2,1)} %bitcast.55, bf16[128,1024]{1,0:T(8,128)(2,1)} %bitcast.56, bf16[128,1024]{1,0:T(8,128)(2,1)} %copy-done.18, bf16[128,1024]{1,0:T(8,128)(2,1)} %copy-done.18, ...), custom_call_target="tpu_custom_call" | custom-call | flops 3000000 | tf_op jit(solution)/shard_map/grad_qkv/pallas_call | solution.py:1388
  141.5 4.7 %collective-permute-done.28.d1 = bf16[2,128,768]{2,1,0:T(8,128)(2,1)S(1)} collective-permute-done((bf16[2,128,768]{2,1,0:T(8,128)(2,1)S(1)}, bf16[2,128,768]{2,1,0:T(8,128)(2,1)S(1)}, u32[]{:S(2)}, u32[]{:S(2)}) %collective-permute-start.28) | collective-permute-done | bytes 393248 | tf_op jit(solution)/shard_map/ppermute | solution.py:309
  151.6 6.2 %tokens_grad.1 = f32[128,1024]{1,0:T(8,128)} custom-call(s32[2]{0:T(128)S(1)} %pad_add_fusion.at_ref.refs_0_, bf16[128,768]{1,0:T(8,128)(2,1)S(1)} %get-tuple-element.164.d0, bf16[2,128,768]{2,1,0:T(8,128)(2,1)S(1)} %collective-permute-done.28.d1, bf16[128,768]{1,0:T(8,128)(2,1)S(1)} %collective-permute-done.29.d2, ...), custom_call_target="tpu_custom_call" | custom-call | flops 1200000000 | tf_op jit(solution)/shard_map/tokens_grad/pallas_call | solution.py:1437
  158.7 5.8 %collective-permute-done.33 = bf16[4,176,384]{2,1,0:T(8,128)(2,1)S(1)} collective-permute-done((bf16[4,176,384]{2,1,0:T(8,128)(2,1)S(1)}, bf16[4,176,384]{2,1,0:T(8,128)(2,1)S(1)}, u32[]{:S(2)}, u32[]{:S(2)}) %collective-permute-start.33) | collective-permute-done | bytes 540704 | tf_op jit(solution)/shard_map/ppermute | solution.py:309
  170.7 7.6 %collective-permute-done.37 = bf16[2,176,384]{2,1,0:T(8,128)(2,1)S(1)} collective-permute-done((bf16[2,176,384]{2,1,0:T(8,128)(2,1)S(1)}, bf16[2,176,384]{2,1,0:T(8,128)(2,1)S(1)}, u32[]{:S(2)}, u32[]{:S(2)}) %collective-permute-start.37) | collective-permute-done | bytes 270368 | tf_op jit(solution)/shard_map/ppermute | solution.py:309
  178.7 3.0 %collective-permute-done.35 = bf16[1,128,640]{2,1,0:T(8,128)(2,1)S(1)} collective-permute-done((bf16[1,128,640]{2,1,0:T(8,128)(2,1)S(1)}, bf16[1,128,640]{2,1,0:T(8,128)(2,1)S(1)}, u32[]{:S(2)}, u32[]{:S(2)}) %collective-permute-start.35) | collective-permute-done | bytes 163872 | tf_op jit(solution)/shard_map/ppermute | solution.py:309
  183.0 2.6 %collective-permute-done.42 = bf16[1,176,384]{2,1,0:T(8,128)(2,1)S(1)} collective-permute-done((bf16[1,176,384]{2,1,0:T(8,128)(2,1)S(1)}, bf16[1,176,384]{2,1,0:T(8,128)(2,1)S(1)}, u32[]{:S(2)}, u32[]{:S(2)}) %collective-permute-start.42) | collective-permute-done | bytes 135200 | tf_op jit(solution)/shard_map/ppermute | solution.py:309
  185.7 3.4 %collective-permute-done.45.refs_6_ = bf16[128,1024]{1,0:T(8,128)(2,1)S(1)} collective-permute-done((bf16[128,1024]{1,0:T(8,128)(2,1)S(1)}, bf16[128,1024]{1,0:T(8,128)(2,1)S(1)}, u32[]{:S(2)}, u32[]{:S(2)}) %collective-permute-start.45) | collective-permute-done | bytes 262176 | tf_op jit(solution)/shard_map/ppermute | solution.py:309
  191.1 3.1 %gather_parts.1 = (f32[512,1024]{1,0:T(8,128)}, f32[128,4096]{1,0:T(8,128)}) custom-call(s32[2]{0:T(128)S(1)} %pad_add_fusion.at_ref.refs_0_, bf16[128,1024]{1,0:T(8,128)(2,1)S(1)} %fusion.refs_0_, bf16[128,1024]{1,0:T(8,128)(2,1)S(1)} %collective-permute-done.40.refs_1_, bf16[128,1024]{1,0:T(8,128)(2,1)S(1)} %collective-permute-done.41.refs_2_, ...), custom_call_target="tpu_custom_call" | custom-call | flops 600000000 | tf_op jit(solution)/shard_map/gather_parts/pallas_call | solution.py:1478
  (152 shorter events, 52.9 us)
Async XLA Ops:
  0.6 9.6 %collective-permute-start = (bf16[128,1024]{1,0:T(8,128)(2,1)}, bf16[128,1024]{1,0:T(8,128)(2,1)S(1)}, u32[]{:S(2)}, u32[]{:S(2)}) collective-permute-start(bf16[128,1024]{1,0:T(8,128)(2,1)} %bitcast.50), channel_id=1, source_target_pairs={{0,16},{8,24},{16,0},{24,8},{1,17},{9,25},{17,1},{25,9},{2,18},{10... | collective-permute-start | bytes 786440 | tf_op jit(solution)/shard_map/ppermute | solution.py:309
  5.2 8.2 %collective-permute-start.1 = (bf16[128,1024]{1,0:T(8,128)(2,1)}, bf16[128,1024]{1,0:T(8,128)(2,1)S(1)}, u32[]{:S(2)}, u32[]{:S(2)}) collective-permute-start(bf16[128,1024]{1,0:T(8,128)(2,1)} %bitcast.51), channel_id=1, source_target_pairs={{0,8},{8,0},{16,24},{24,16},{1,9},{9,1},{17,25},{25,17},{2,10},{10... | collective-permute-start | bytes 786440 | tf_op jit(solution)/shard_map/ppermute | solution.py:309
  51.2 15.8 %collective-permute-start.9 = (bf16[2,128,1024]{2,1,0:T(8,128)(2,1)S(1)}, bf16[2,128,1024]{2,1,0:T(8,128)(2,1)S(1)}, u32[]{:S(2)}, u32[]{:S(2)}) collective-permute-start(bf16[2,128,1024]{2,1,0:T(8,128)(2,1)S(1)} %get-tuple-element.121), channel_id=1, source_target_pairs={{0,16},{8,24},{16,0},{24,8},{1,17},{9,25},{17,1},{25,9},{2,18},{10... | collective-permute-start | bytes 1572872 | tf_op jit(solution)/shard_map/ppermute | solution.py:309
  57.0 18.6 %collective-permute-start.12 = (bf16[128,1024]{1,0:T(8,128)(2,1)S(1)}, bf16[128,1024]{1,0:T(8,128)(2,1)S(1)}, u32[]{:S(2)}, u32[]{:S(2)}) collective-permute-start(bf16[128,1024]{1,0:T(8,128)(2,1)S(1)} %get-tuple-element.114.ffn_ref.refs_8_), channel_id=1, source_target_pairs={{0,16},{8,24},{16,0},{24,8},{1,17},{9,25},{17,1},{25,9},{2,18},{10... | collective-permute-start | bytes 786440 | tf_op jit(solution)/shard_map/ppermute | solution.py:309
  67.0 10.5 %collective-permute-start.11 = (bf16[2,128,1024]{2,1,0:T(8,128)(2,1)S(1)}, bf16[2,128,1024]{2,1,0:T(8,128)(2,1)S(1)}, u32[]{:S(2)}, u32[]{:S(2)}) collective-permute-start(bf16[2,128,1024]{2,1,0:T(8,128)(2,1)S(1)} %collective-permute-done.9.refs_2_.refs_3_), channel_id=1, source_target_pairs={{0,8},{8,0},{16,24},{24,16},{1,9},{9,1},{17,25},{25,17},{2,10},{10... | collective-permute-start | bytes 1572872 | tf_op jit(solution)/shard_map/ppermute | solution.py:309
  73.9 23.7 %collective-permute-start.18 = (bf16[3,128,1024]{2,1,0:T(8,128)(2,1)S(1)}, bf16[3,128,1024]{2,1,0:T(8,128)(2,1)S(1)}, u32[]{:S(2)}, u32[]{:S(2)}) collective-permute-start(bf16[3,128,1024]{2,1,0:T(8,128)(2,1)S(1)} %get-tuple-element.137), channel_id=1, source_target_pairs={{0,16},{8,24},{16,0},{24,8},{1,17},{9,25},{17,1},{25,9},{2,18},{10... | collective-permute-start | bytes 2359304 | tf_op jit(solution)/shard_map/ppermute | solution.py:309
  81.0 28.9 %collective-permute-start.21 = (bf16[4,128,1024]{2,1,0:T(8,128)(2,1)S(1)}, bf16[4,128,1024]{2,1,0:T(8,128)(2,1)S(1)}, u32[]{:S(2)}, u32[]{:S(2)}) collective-permute-start(bf16[4,128,1024]{2,1,0:T(8,128)(2,1)S(1)} %get-tuple-element.142), channel_id=1, source_target_pairs={{0,1},{1,0},{2,3},{3,2},{4,5},{5,4},{6,7},{7,6},{8,9},{9,8},{10,11... | collective-permute-start | bytes 3145736 | tf_op jit(solution)/shard_map/ppermute | solution.py:309
  98.1 11.1 %collective-permute-start.22 = (bf16[128,1536]{1,0:T(8,128)(2,1)S(1)}, bf16[128,1536]{1,0:T(8,128)(2,1)S(1)}, u32[]{:S(2)}, u32[]{:S(2)}) collective-permute-start(bf16[128,1536]{1,0:T(8,128)(2,1)S(1)} %get-tuple-element.146.refs_15_.refs_16_), channel_id=1, source_target_pairs={{0,16},{8,24},{16,0},{24,8},{1,17},{9,25},{17,1},{25,9},{2,18},{10... | collective-permute-start | bytes 1179656 | tf_op jit(solution)/shard_map/ppermute | solution.py:309
  109.2 26.7 %collective-permute-start.26 = (bf16[4,128,1024]{2,1,0:T(8,128)(2,1)S(1)}, bf16[4,128,1024]{2,1,0:T(8,128)(2,1)S(1)}, u32[]{:S(2)}, u32[]{:S(2)}) collective-permute-start(bf16[4,128,1024]{2,1,0:T(8,128)(2,1)S(1)} %get-tuple-element.152), channel_id=1, source_target_pairs={{0,1},{1,0},{2,3},{3,2},{4,5},{5,4},{6,7},{7,6},{8,9},{9,8},{10,11... | collective-permute-start | bytes 3145736 | tf_op jit(solution)/shard_map/ppermute | solution.py:309
  110.3 25.5 %collective-permute-start.27 = (bf16[2,128,1024]{2,1,0:T(8,128)(2,1)S(1)}, bf16[2,128,1024]{2,1,0:T(8,128)(2,1)S(1)}, u32[]{:S(2)}, u32[]{:S(2)}) collective-permute-start(bf16[2,128,1024]{2,1,0:T(8,128)(2,1)S(1)} %get-tuple-element.195), channel_id=1, source_target_pairs={{0,2},{1,3},{2,0},{3,1},{4,6},{5,7},{6,4},{7,5},{8,10},{9,11},{10,... | collective-permute-start | bytes 1572872 | tf_op jit(solution)/shard_map/ppermute | solution.py:309
  117.8 31.5 %collective-permute-start.25 = (bf16[4,128,640]{2,1,0:T(8,128)(2,1)S(1)}, bf16[4,128,640]{2,1,0:T(8,128)(2,1)S(1)}, u32[]{:S(2)}, u32[]{:S(2)}) collective-permute-start(bf16[4,128,640]{2,1,0:T(8,128)(2,1)S(1)} %get-tuple-element.151), channel_id=1, source_target_pairs={{0,2},{1,3},{2,0},{3,1},{4,6},{5,7},{6,4},{7,5},{8,10},{9,11},{10,... | collective-permute-start | bytes 1966088 | tf_op jit(solution)/shard_map/ppermute | solution.py:309
  135.3 11.0 %collective-permute-start.28 = (bf16[2,128,768]{2,1,0:T(8,128)(2,1)S(1)}, bf16[2,128,768]{2,1,0:T(8,128)(2,1)S(1)}, u32[]{:S(2)}, u32[]{:S(2)}) collective-permute-start(bf16[2,128,768]{2,1,0:T(8,128)(2,1)S(1)} %get-tuple-element.165), channel_id=1, source_target_pairs={{0,16},{8,24},{16,0},{24,8},{1,17},{9,25},{17,1},{25,9},{2,18},{10... | collective-permute-start | bytes 1179656 | tf_op jit(solution)/shard_map/ppermute | solution.py:309
  136.3 21.5 %collective-permute-start.34 = (bf16[2,128,1024]{2,1,0:T(8,128)(2,1)S(1)}, bf16[2,128,1024]{2,1,0:T(8,128)(2,1)S(1)}, u32[]{:S(2)}, u32[]{:S(2)}) collective-permute-start(bf16[2,128,1024]{2,1,0:T(8,128)(2,1)S(1)} %get-tuple-element.193), channel_id=1, source_target_pairs={{0,2},{1,3},{2,0},{3,1},{4,6},{5,7},{6,4},{7,5},{8,10},{9,11},{10,... | collective-permute-start | bytes 1572872 | tf_op jit(solution)/shard_map/ppermute | solution.py:309
  146.8 20.3 %collective-permute-start.32 = (bf16[1,128,1024]{2,1,0:T(8,128)(2,1)S(1)}, bf16[1,128,1024]{2,1,0:T(8,128)(2,1)S(1)}, u32[]{:S(2)}, u32[]{:S(2)}) collective-permute-start(bf16[1,128,1024]{2,1,0:T(8,128)(2,1)S(1)} %add_convert_fusion.13), channel_id=1, source_target_pairs={{0,4},{1,5},{2,6},{3,7},{4,0},{5,1},{6,2},{7,3},{8,12},{9,13},{10,... | collective-permute-start | bytes 786440 | tf_op jit(solution)/shard_map/ppermute | solution.py:309
  149.3 15.2 %collective-permute-start.33 = (bf16[4,176,384]{2,1,0:T(8,128)(2,1)S(1)}, bf16[4,176,384]{2,1,0:T(8,128)(2,1)S(1)}, u32[]{:S(2)}, u32[]{:S(2)}) collective-permute-start(bf16[4,176,384]{2,1,0:T(8,128)(2,1)S(1)} %get-tuple-element.169), channel_id=1, source_target_pairs={{0,1},{1,0},{2,3},{3,2},{4,5},{5,4},{6,7},{7,6},{8,9},{9,8},{10,11... | collective-permute-start | bytes 1622024 | tf_op jit(solution)/shard_map/ppermute | solution.py:309
  151.0 19.2 %collective-permute-start.31 = (bf16[2,128,640]{2,1,0:T(8,128)(2,1)S(1)}, bf16[2,128,640]{2,1,0:T(8,128)(2,1)S(1)}, u32[]{:S(2)}, u32[]{:S(2)}) collective-permute-start(bf16[2,128,640]{2,1,0:T(8,128)(2,1)S(1)} %get-tuple-element.197), channel_id=1, source_target_pairs={{0,1},{1,0},{2,3},{3,2},{4,5},{5,4},{6,7},{7,6},{8,9},{9,8},{10,11... | collective-permute-start | bytes 983048 | tf_op jit(solution)/shard_map/ppermute | solution.py:309
  157.9 20.6 %collective-permute-start.36 = (bf16[1,128,1024]{2,1,0:T(8,128)(2,1)S(1)}, bf16[1,128,1024]{2,1,0:T(8,128)(2,1)S(1)}, u32[]{:S(2)}, u32[]{:S(2)}) collective-permute-start(bf16[1,128,1024]{2,1,0:T(8,128)(2,1)S(1)} %add_convert_fusion.11), channel_id=1, source_target_pairs={{0,4},{1,5},{2,6},{3,7},{4,0},{5,1},{6,2},{7,3},{8,12},{9,13},{10,... | collective-permute-start | bytes 786440 | tf_op jit(solution)/shard_map/ppermute | solution.py:309
  164.7 13.7 %collective-permute-start.37 = (bf16[2,176,384]{2,1,0:T(8,128)(2,1)S(1)}, bf16[2,176,384]{2,1,0:T(8,128)(2,1)S(1)}, u32[]{:S(2)}, u32[]{:S(2)}) collective-permute-start(bf16[2,176,384]{2,1,0:T(8,128)(2,1)S(1)} %get-tuple-element.199), channel_id=1, source_target_pairs={{0,2},{1,3},{2,0},{3,1},{4,6},{5,7},{6,4},{7,5},{8,10},{9,11},{10,... | collective-permute-start | bytes 811016 | tf_op jit(solution)/shard_map/ppermute | solution.py:309
  167.2 22.2 %collective-permute-start.40 = (bf16[128,1024]{1,0:T(8,128)(2,1)S(1)}, bf16[128,1024]{1,0:T(8,128)(2,1)S(1)}, u32[]{:S(2)}, u32[]{:S(2)}) collective-permute-start(bf16[128,1024]{1,0:T(8,128)(2,1)S(1)} %fusion.refs_0_), channel_id=1, source_target_pairs={{0,8},{8,0},{16,24},{24,16},{1,9},{9,1},{17,25},{25,17},{2,10},{10... | collective-permute-start | bytes 786440 | tf_op jit(solution)/shard_map/ppermute | solution.py:309
  167.3 18.3 %collective-permute-start.41 = (bf16[128,1024]{1,0:T(8,128)(2,1)S(1)}, bf16[128,1024]{1,0:T(8,128)(2,1)S(1)}, u32[]{:S(2)}, u32[]{:S(2)}) collective-permute-start(bf16[128,1024]{1,0:T(8,128)(2,1)S(1)} %fusion.refs_0_), channel_id=1, source_target_pairs={{0,16},{8,24},{16,0},{24,8},{1,17},{9,25},{17,1},{25,9},{2,18},{10... | collective-permute-start | bytes 786440 | tf_op jit(solution)/shard_map/ppermute | solution.py:309
  170.3 11.4 %collective-permute-start.35 = (bf16[1,128,640]{2,1,0:T(8,128)(2,1)S(1)}, bf16[1,128,640]{2,1,0:T(8,128)(2,1)S(1)}, u32[]{:S(2)}, u32[]{:S(2)}) collective-permute-start(bf16[1,128,640]{2,1,0:T(8,128)(2,1)S(1)} %add_convert_fusion.15), channel_id=1, source_target_pairs={{0,4},{1,5},{2,6},{3,7},{4,0},{5,1},{6,2},{7,3},{8,12},{9,13},{10,... | collective-permute-start | bytes 491528 | tf_op jit(solution)/shard_map/ppermute | solution.py:309
  178.6 12.5 %collective-permute-start.44 = (bf16[128,1024]{1,0:T(8,128)(2,1)S(1)}, bf16[128,1024]{1,0:T(8,128)(2,1)S(1)}, u32[]{:S(2)}, u32[]{:S(2)}) collective-permute-start(bf16[128,1024]{1,0:T(8,128)(2,1)S(1)} %fusion.1.refs_4_), channel_id=1, source_target_pairs={{0,8},{8,0},{16,24},{24,16},{1,9},{9,1},{17,25},{25,17},{2,10},{10... | collective-permute-start | bytes 786440 | tf_op jit(solution)/shard_map/ppermute | solution.py:309
  189.4 9.2 %collective-permute-start.49 = (bf16[176,384]{1,0:T(8,128)(2,1)S(1)}, bf16[176,384]{1,0:T(8,128)(2,1)S(1)}, u32[]{:S(2)}, u32[]{:S(2)}) collective-permute-start(bf16[176,384]{1,0:T(8,128)(2,1)S(1)} %fusion.3.refs_4_), channel_id=1, source_target_pairs={{0,16},{8,24},{16,0},{24,8},{1,17},{9,25},{17,1},{25,9},{2,18},{10... | collective-permute-start | bytes 405512 | tf_op jit(solution)/shard_map/ppermute | solution.py:309
  191.1 7.5 %collective-permute-start.38 = (bf16[128,640]{1,0:T(8,128)(2,1)S(1)}, bf16[128,640]{1,0:T(8,128)(2,1)S(1)}, u32[]{:S(2)}, u32[]{:S(2)}) collective-permute-start(bf16[128,640]{1,0:T(8,128)(2,1)S(1)} %fusion.2.refs_0_), channel_id=1, source_target_pairs={{0,8},{8,0},{16,24},{24,16},{1,9},{9,1},{17,25},{25,17},{2,10},{10... | collective-permute-start | bytes 491528 | tf_op jit(solution)/shard_map/ppermute | solution.py:309
  (47 other events, 323.4 us)

commit v4 on v3

--- a/solution.py
+++ b/solution.py
@@ -1064,116 +1064,115 @@
         refs = refs[5:]
     refs = refs[held:]
     if last:
-        dqkv_ref, own_ref, core_ref, far_ref, small_ref, ga_ref, ds_ref, drel, box_sums = refs
+        dqkv_ref, own_ref, core_ref, far_ref, small_ref, ga_ref, ds_ref, drel, own_qkv, box_sums = refs
     else:
-        dqkv_ref, box_sums, ga_ref, ds_ref, drel = refs
+        dqkv_ref, box_sums, ga_ref, ds_ref, drel, own_qkv = refs
     scale = 1.0 / math.sqrt(192.0)
     rows = blocks * lanes
     width = qkv_ref.shape[1] // 3
     part = width // 2
     heads = probs_ref.shape[0]
     size = part // heads
-    span_width = 3 * lanes
+    short = lanes // 2
     for t, piece in enumerate((g0, g1, g2, g3)):
         ga_ref[t * lanes : (t + 1) * lanes, :] = piece[...]
+    for k in range(3):
+        for h in range(heads):
+            first = k * width + half * part + h * size
+            own_qkv[k * heads + h] = qkv_ref[:, first : first + size]
     drel[...] = jnp.zeros_like(drel)
     box_sums[...] = jnp.zeros_like(box_sums)
-    window = lax.broadcasted_iota(jnp.int32, (rows, span_width), 1)
+    window = lax.broadcasted_iota(jnp.int32, (rows, 2 * lanes), 1)
     bucket = lax.broadcasted_iota(jnp.int32, (lanes, lanes), 1)
     label = lax.broadcasted_iota(jnp.int32, (rows, lanes), 1)
     all_pos = col_ref[:, 0:1]
     all_x, all_y = col_ref[:, 1:2], col_ref[:, 2:3]
     sector_x, sector_y = jnp.right_shift(all_x, 5), jnp.right_shift(all_y, 5)
-    hot_x = (label == sector_x).astype(bf16)
-    hot_y = (label == sector_y + 64).astype(bf16)
-    hot_both = ((label == sector_x) | (label == sector_y + 64)).astype(bf16)
-
-    def histogram(sums, total, at, base_row):
-        first = at - base_row + (lanes - 1) - bucket
-        low = jnp.bitwise_and(first, lanes - 1)
-        group = jnp.right_shift(first, 7)
-        found = jnp.where(
-            group == 0,
-            pick(sums[:, :lanes], low),
-            jnp.where(
-                group == 1,
-                pick(sums[:, lanes : 2 * lanes], low),
-                pick(sums[:, 2 * lanes :], low),
-            ),
-        )
-        found = jnp.where(bucket == 0, total, found)
-        later = jnp.where(bucket == lanes - 1, 0.0, pltpu.roll(found, lanes - 1, 1))
-        return found - later
+    hot_x = (label == sector_x).astype(f32).astype(bf16)
+    hot_y = (label == sector_y + 64).astype(f32).astype(bf16)
+    hot_both = hot_x + hot_y
+
+    def shares(grads, start):
+        found = []
+        for u in range(2):
+            at = col_ref[pl.ds(pl.multiple_of(start + u * short, short), short), 0:1]
+            base = jnp.min(at, axis=0, keepdims=True)
+            below = (all_pos <= base - 63 + window) | (window == 2 * lanes - 1)
+            stacked = jnp.concatenate([g[u * short : (u + 1) * short, :] for g in grads], axis=0)
+            sums = dot(stacked, below.astype(f32).astype(bf16))
+            first = at - base + (lanes - 1) - bucket[:short]
+            first = jnp.concatenate([first] * heads, axis=0)
+            low = jnp.bitwise_and(first, lanes - 1)
+            value = jnp.where(
+                first < lanes, pick(sums[:, :lanes], low), pick(sums[:, lanes:], low)
+            )
+            value = jnp.where(bucket == 0, sums[:, 2 * lanes - 1 :], value)
+            later = jnp.where(bucket == lanes - 1, 0.0, pltpu.roll(value, lanes - 1, 1))
+            found.append(scale * (value - later))
+        return [
+            jnp.concatenate([f[h * short : (h + 1) * short, :] for f in found], axis=0).astype(bf16)
+            for h in range(heads)
+        ]
 
     def by_rows(ib, carry):
-        here = pl.ds(pl.multiple_of(ib * lanes, lanes), lanes)
-        pos_i = col_ref[here, 0:1]
+        start = ib * lanes
+        here = pl.ds(pl.multiple_of(start, lanes), lanes)
         cx_i, cy_i = col_ref[here, 1:2], col_ref[here, 2:3]
-        base = jnp.min(pos_i, axis=0, keepdims=True)
-        below = (all_pos <= base - 63 + window).astype(bf16)
         short_x = jnp.bitwise_and(cx_i, 31) < jnp.bitwise_and(row_ref[1:2, :], 31)
         short_y = jnp.bitwise_and(cy_i, 31) < jnp.bitwise_and(row_ref[2:3, :], 31)
+        short_x = short_x.astype(f32).astype(bf16)
+        short_y = short_y.astype(f32).astype(bf16)
         step_x = jnp.right_shift(cx_i, 5) + 32 - bucket
         step_y = jnp.right_shift(cy_i, 5) + 32 - (bucket - 64)
         in_x = (bucket < 64) & (step_x >= 0) & (step_x < 32)
         in_y = (bucket >= 64) & (step_y >= 0) & (step_y < 32)
         seek = jnp.where(in_x, step_x, jnp.where(in_y, step_y + 64, 0))
         inside = in_x | in_y
+        grads = []
         for h in range(heads):
+            probs = probs_ref[h, here, :].astype(f32)
+            gained = dot(ga_ref[here, h * size : (h + 1) * size], own_qkv[2 * heads + h], ((1,), (1,)))
+            row_dots = jnp.sum(probs * gained, axis=1, keepdims=True)
+            grad = (probs * (gained - row_dots)).astype(bf16)
+            ds_ref[h, here, :] = grad
+            grads.append(grad)
+        rels = shares(grads, start)
+        for h, (grad, rel) in enumerate(zip(grads, rels)):
+            gcols = slice(h * size, (h + 1) * size)
+            kgcols = slice(half * part + h * size, half * part + (h + 1) * size)
+            dqkv_ref[here, gcols] = (
+                scale * dot(grad, own_qkv[heads + h]) + dot(rel, relkq_ref[:, kgcols])
+            ).astype(bf16)
+            drel[:, gcols] += dot(rel, own_qkv[h, here, :], ((0,), (0,)))
+        stacked = jnp.concatenate(grads, axis=0)
+        plain = dot(stacked, hot_both)
+        less = dot(jnp.concatenate([g * short_x for g in grads], axis=0), hot_x) + dot(
+            jnp.concatenate([g * short_y for g in grads], axis=0), hot_y
+        )
+        for h in range(heads):
+            span = slice(h * lanes, (h + 1) * lanes)
+            own_plain = jnp.where(inside, pick(plain[span, :], seek), 0.0)
+            own_less = jnp.where(inside, pick(less[span, :], seek), 0.0)
+            box_sums[h : h + 1, :] += jnp.sum(own_plain, axis=0, keepdims=True)
+            box_sums[8 + h : 9 + h, :] += jnp.sum(own_less, axis=0, keepdims=True)
+        return carry
+
+    lax.fori_loop(0, blocks, by_rows, 0)
+
+    def by_columns(jb, carry):
+        start = jb * lanes
+        here = pl.ds(pl.multiple_of(start, lanes), lanes)
+        grads = [ds_ref[h, :, here].T for h in range(heads)]
+        mirrors = shares(grads, start)
+        for h, (grad, mirror) in enumerate(zip(grads, mirrors)):
             gcols = slice(h * size, (h + 1) * size)
             kgcols = slice(part + h * size, part + (h + 1) * size)
             vgcols = slice(2 * part + h * size, 2 * part + (h + 1) * size)
-            cols, kcols, vcols = (
-                slice(k * width + half * part + h * size, k * width + half * part + (h + 1) * size)
-                for k in range(3)
-            )
-            probs = probs_ref[h, here, :].astype(f32)
-            gained = dot(ga_ref[here, gcols], qkv_ref[:, vcols], ((1,), (1,)))
-            row_dots = jnp.sum(probs * gained, axis=1, keepdims=True)
-            grad = (probs * (gained - row_dots)).astype(bf16)
-            ds_ref[h, here, :] = grad
-            exact = grad.astype(f32)
-            total = jnp.sum(exact, axis=1, keepdims=True)
-            rel = histogram(dot(grad, below), total, pos_i, base)
-            rel = (scale * rel).astype(bf16)
-            dqkv_ref[here, gcols] = (
-                scale * dot(grad, qkv_ref[:, kcols]) + dot(rel, relkq_ref[:, cols])
+            kcols = slice(width + half * part + h * size, width + half * part + (h + 1) * size)
+            dqkv_ref[here, kgcols] = (
+                scale * dot(grad, own_qkv[h]) + dot(mirror, relkq_ref[:, kcols])
             ).astype(bf16)
-            drel[:, gcols] += dot(rel, qkv_ref[here, cols], ((0,), (0,)))
-            grad_x = jnp.where(short_x, exact, 0.0).astype(bf16)
-            grad_y = jnp.where(short_y, exact, 0.0).astype(bf16)
-            plain = dot(grad, hot_both)
-            less = dot(grad_x, hot_x) + dot(grad_y, hot_y)
-            plain = jnp.where(inside, pick(plain, seek), 0.0)
-            less = jnp.where(inside, pick(less, seek), 0.0)
-            box_sums[h : h + 1, :] += jnp.sum(plain, axis=0, keepdims=True)
-            box_sums[8 + h : 9 + h, :] += jnp.sum(less, axis=0, keepdims=True)
-        return carry
-
-    lax.fori_loop(0, blocks, by_rows, 0)
-
-    def by_columns(jb, carry):
-        here = pl.ds(pl.multiple_of(jb * lanes, lanes), lanes)
-        pos_j = col_ref[here, 0:1]
-        base = jnp.min(pos_j, axis=0, keepdims=True)
-        below = (all_pos <= base - 63 + window).astype(bf16)
-        for h in range(heads):
-            gcols = slice(h * size, (h + 1) * size)
-            kgcols = slice(part + h * size, part + (h + 1) * size)
-            vgcols = slice(2 * part + h * size, 2 * part + (h + 1) * size)
-            cols, kcols, vcols = (
-                slice(k * width + half * part + h * size, k * width + half * part + (h + 1) * size)
-                for k in range(3)
-            )
-            grad = ds_ref[h, :, here]
-            total = dot(grad, jnp.ones((rows, lanes), bf16), ((0,), (0,)))
-            sums = dot(grad, below, ((0,), (0,)))
-            mirror = (scale * histogram(sums, total, pos_j, base)).astype(bf16)
-            dqkv_ref[here, kgcols] = (
-                scale * dot(grad, qkv_ref[:, cols], ((0,), (0,)))
-                + dot(mirror, relkq_ref[:, kcols])
-            ).astype(bf16)
-            drel[:, kgcols] += dot(mirror, qkv_ref[here, kcols], ((0,), (0,)))
+            drel[:, kgcols] += dot(mirror, own_qkv[heads + h, here, :], ((0,), (0,)))
             dqkv_ref[here, vgcols] = dot(
                 probs_ref[h, :, here], ga_ref[:, gcols], ((0,), (0,))
             ).astype(bf16)
@@ -1255,6 +1254,7 @@
         pltpu.VMEM((rows, part), bf16),
         pltpu.VMEM((heads, rows, rows), bf16),
         pltpu.VMEM((buckets, 2 * part), f32),
+        pltpu.VMEM((3 * heads, rows, part // heads), bf16),
     ]
     extra_specs = []
     if half == 1:
@@ -1490,7 +1490,8 @@
 def last_kernel(at_ref, *refs):
     step = pl.program_id(0)
     firsts, seconds, outs = refs[:blocks], refs[blocks : 2 * blocks], refs[2 * blocks : 2 * blocks + 3]
-    wout_ref, rel_ref, norm_ref, bin_ref, box_ref = refs[2 * blocks + 3 :]
+    wout_ref, rel_ref, *small_refs = refs[2 * blocks + 3 :]
+    norm_refs, (bin_ref, xbox_ref, ybox_ref) = small_refs[:4], small_refs[4:]
     for at in range(blocks):
 
         @pl.when(step == at)
@@ -1512,23 +1513,27 @@
             end = min((k + 1) * width, rel_ref.shape[1])
             rel_ref[:, k * width : end] = total[k * rows : (k + 1) * rows, : end - k * width]
         rest = total[2 * rows :, width - lanes :]
-        norm_ref[...] = rest[:4]
-        bin_ref[...] = rest[4:8]
-        box_ref[...] = rest[8:16]
-
-
-def last_call(at, firsts, seconds, buckets, model):
+        for k in range(4):
+            norm_refs[k][...] = rest[k]
+            bin_ref[k * lanes : (k + 1) * lanes] = rest[4 + k]
+        heads = xbox_ref.shape[1]
+        xbox_ref[...] = rest[8:16, :heads]
+        ybox_ref[...] = rest[8:16, 64 : 64 + heads]
+
+
+def last_call(at, firsts, seconds, buckets, model, heads):
     wide = jax.ShapeDtypeStruct((lanes, model), f32)
+    small_shapes = ((buckets, model),) + ((lanes,),) * 4 + ((blocks * lanes,), (8, heads), (8, heads))
     column = pl.BlockSpec((lanes, model // blocks), lambda i, at: (0, jnp.bitwise_xor(at[0], i)))
     return pl.pallas_call(
         last_kernel,
         out_shape=(wide, wide, wide, wide)
-        + tuple(jax.ShapeDtypeStruct(shape, f32) for shape in ((buckets, model), (4, lanes), (4, lanes), (8, lanes))),
+        + tuple(jax.ShapeDtypeStruct(shape, f32) for shape in small_shapes),
         grid_spec=pltpu.PrefetchScalarGridSpec(
             num_scalar_prefetch=1,
             grid=(blocks,),
             in_specs=[full(part.shape) for part in firsts + seconds],
-            out_specs=[column] * 4 + [full((buckets, model)), full((4, lanes)), full((4, lanes)), full((8, lanes))],
+            out_specs=[column] * 4 + [full(shape) for shape in small_shapes],
         ),
         compiler_params=params(18),
         cost_estimate=cost(2),
@@ -1606,7 +1611,7 @@
     line = lambda vector: vector.reshape(1, -1)
     far1, core1, act_own, act, slope, normed1, inverse1, attended, hidden = up_call(
         spot, (att_own, (came_far, 0), came_core, (came_both, 1)), x_own, w_out,
-        line(ln1_gain), line(ln1_bias), w_in, line(b_in), docs,
+        line(ln1_gain), line(ln1_bias), in_hbm(w_in), line(b_in), docs,
     )
     got_far1 = swap(far1, "blk", 2)
     block_out, mix, grad_ffn, above = down_call(
@@ -1656,9 +1661,10 @@
         gattn_own, (got_far3, None, per), (got_core3, None, per), (got_both3, None, per + 1),
     ]
     done = down_sum.add(in_halves[0])
+    early = [done]
     first_groups = [(lefts, rows_by_piece(first_grads), 3 * width // 2), (att_all, gattn_all, width)]
     (first_halves,) = weight_grads_call(
-        spot, [(first_groups, other, None)], after=[in_halves[0], done], name="grad_qkv_out"
+        spot, [(first_groups, other, None)], after=[in_halves[0]] + early, name="grad_qkv_out"
     )
     first_sum = Halving(first_halves, other)
     second_grads, dq_own, dq_core, dq_far, small = scores_grad_call(
@@ -1672,9 +1678,9 @@
         spot, [(second_groups, bits, small)], after=[done], name="grad_qkv"
     )
     second_sum = Halving(second_halves, bits)
+    done = first_sum.add(second_halves[0])
     dq_far_got = ordered(swap(dq_far, "blk", 2), second_halves[0])
     dq_core_got, dq_both_got = swap(dq_core, "blk", 1), swap(dq_far_got, "blk", 1)
-    done = first_sum.add(second_halves[0])
     grad_tokens = tokens_grad_call(
         spot, (dq_own, (dq_far_got, 0), dq_core_got, (dq_both_got, 1)), grad_resid,
         w_query, w_key, w_value, [done],
@@ -1700,11 +1706,10 @@
     grad_w_down, grad_w_in = parts_call(
         spot, ((whole(down_part, done), 0), (whole(in_part, done), 1)), "gather_parts"
     )
-    *grads, grad_w_out, rel_out, norms, b_in_out, both_boxes = last_call(
-        spot, whole(first_part, grad_w_down), whole(second_part, grad_w_down), rel_table.shape[0] // docs, model
-    )
-    b_in_out = b_in_out.reshape(-1)
-    xb, yb = both_boxes[:, :heads], both_boxes[:, 64 : 64 + heads]
+    *grads, grad_w_out, rel_out, n0, n1, n2, n3, b_in_out, xb, yb = last_call(
+        spot, whole(first_part, grad_w_down), whole(second_part, grad_w_down), rel_table.shape[0] // docs, model, heads
+    )
+    norms = (n0, n1, n2, n3)
     return (
         block_out[None], grad_tokens[None], norms[0], norms[1], grads[0], grads[1], grads[2], grad_w_out,
         rel_out, xb, yb, norms[2], norms[3], grad_w_in, b_in_out, grad_w_down,

time: 204 us -> 196 us (0.961)
  local copies, waits for them, and re-layouts: 6.36 us -> 1.8 us
  Pallas kernels: 99.2 us -> 96 us
    pallas_call x2, Pallas kernels: 31.3 us -> 24.8 us  [scores_grad_call(): pl.pallas_call(functools.partial(scores_grad_kernel, half, 0), out_shape=...]
    unnamed x40 -> x38, local copies, waits for them, and re-layouts: 5.09 us -> 1.72 us
    pallas_call x1, Pallas kernels: 6.35 us -> 9.35 us  [up_call(): pl.pallas_call(up_kernel, out_shape=(jax.ShapeDtypeStruct((2, rows, quart...]
  transfers between devices with their start and end apart: 51 -> 51, of which waited for: 20 -> 21; matrix products, arithmetic and copies ran while one was open for 2% -> 2% of each run, Pallas kernels for 35% -> 33%
where the time goes in v4:
time: 196 us; the launch traced here: 195 us
  Pallas kernels  96 us (49%)
  waiting for transfers between devices  57.8 us (29%)
  starting transfers between devices  33.9 us (17%)
  other arithmetic  4.04 us (2%)
    ppermute x51, waiting for transfers between devices, swap(): return lax.ppermute(array, axis, [(i, i ^ by) for i in range(count)])  57.8 us
    ppermute x51, starting transfers between devices, swap(): return lax.ppermute(array, axis, [(i, i ^ by) for i in range(count)])  33.9 us
    pallas_call x2, Pallas kernels, scores_grad_call(): pl.pallas_call(functools.partial(scores_grad_kernel, half, 0), out_shape=...  24.8 us
    pallas_call x1, Pallas kernels, scores_call(): pl.pallas_call(scores_kernel, out_shape=(jax.ShapeDtypeStruct((lanes, wid...  19.4 us
    pallas_call x4, Pallas kernels, weight_grads_call(): pl.pallas_call(kernel, out_shape=tuple(shapes), grid_spec=pltpu.PrefetchS...  16.9 us
    pallas_call x1, Pallas kernels, back_call(): pl.pallas_call(back_kernel, out_shape=(jax.ShapeDtypeStruct((rows, width)...  9.65 us
    pallas_call x1, Pallas kernels, up_call(): pl.pallas_call(up_kernel, out_shape=(jax.ShapeDtypeStruct((2, rows, quart...  9.35 us
    pallas_call x1, Pallas kernels, tokens_grad_call(): pl.pallas_call(tokens_grad_kernel, out_shape=jax.ShapeDtypeStruct((rows,...  6.22 us
  transfers between devices with their start and end apart: 51, of which 21 were waited for; matrix products, arithmetic and copies ran while one was open for 2% of the time, Pallas kernels for 33%

profile of v4, /device:TPU:0, one launch (start us, length us, event | category | flops | bytes accessed | tf_op | source)
XLA Modules:
  0.0 195.5 jit_solution(6618449999933487785)
XLA Ops:
  0.6 3.0 %collective-permute-start = (bf16[128,1024]{1,0:T(8,128)(2,1)}, bf16[128,1024]{1,0:T(8,128)(2,1)S(1)}, u32[]{:S(2)}, u32[]{:S(2)}) collective-permute-start(bf16[128,1024]{1,0:T(8,128)(2,1)} %bitcast.41), channel_id=1, source_target_pairs={{0,16},{8,24},{16,0},{24,8},{1,17},{9,25},{17,1},{25,9},{2,18},{10... | collective-permute-start | bytes 786440 | tf_op jit(solution)/shard_map/ppermute | solution.py:309
  5.2 5.1 %collective-permute-done.2.i1 = s32[8,128]{1,0:T(8,128)S(1)} collective-permute-done((s32[8,128]{1,0:T(8,128)S(1)}, s32[8,128]{1,0:T(8,128)S(1)}, u32[]{:S(2)}, u32[]{:S(2)}) %collective-permute-start.2) | collective-permute-done | bytes 4128 | tf_op jit(solution)/shard_map/ppermute | solution.py:309
  15.0 19.4 %scores.1 = (bf16[128,256]{1,0:T(8,128)(2,1)S(1)}, bf16[128,256]{1,0:T(8,128)(2,1)S(1)}, bf16[2,128,256]{2,1,0:T(8,128)(2,1)S(1)}, bf16[4,512,512]{2,1,0:T(8,128...) custom-call(s32[2]{0:T(128)S(1)} %pad_add_fusion.1.at_ref, ...), custom_call_target="tpu_custom_call" | custom-call | flops 7500000256 | tf_op jit(solution)/shard_map/scores/pallas_call | solution.py:743
  36.1 3.8 %collective-permute-done.6.a1 = bf16[2,128,256]{2,1,0:T(8,128)(2,1)S(1)} collective-permute-done((bf16[2,128,256]{2,1,0:T(8,128)(2,1)S(1)}, bf16[2,128,256]{2,1,0:T(8,128)(2,1)S(1)}, u32[]{:S(2)}, u32[]{:S(2)}) %collective-permute-start.6) | collective-permute-done | bytes 131104 | tf_op jit(solution)/shard_map/ppermute | solution.py:309
  41.5 9.3 %up.1 = (bf16[2,128,1024]{2,1,0:T(8,128)(2,1)S(1)}, bf16[128,1024]{1,0:T(8,128)(2,1)S(1)}, bf16[128,1024]{1,0:T(8,128)(2,1)S(1)}, bf16[128,4096]{1,0:T(8,128)(2,...) custom-call(s32[2]{0:T(128)S(1)} %pad_add_fusion.at_ref.refs_0_, ...), custom_call_target="tpu_custom_call" | custom-call | flops 2700000000 | tf_op jit(solution)/shard_map/up/pallas_call | solution.py:835
  52.7 4.0 %down.1 = (bf16[128,1024]{1,0:T(8,128)(2,1)}, f32[128,1024]{1,0:T(8,128)S(1)}, bf16[128,1024]{1,0:T(8,128)(2,1)S(1)}, f32[8,1024]{1,0:T(8,128)S(1)}) custom-call(bf16[128,4096]{1,0:T(8,128)(2,1)S(1)} %get-tuple-element.112.act_ref, bf16[4096,1024]{1,0:T(8,128)(2,1)S(1)} %copy-done.1, f32[128,1024]{1,0:T(8,128)S(1)} %get-tuple-element.113.normed_ref, ...), custom_call_target="tpu_custom_call" | custom-call | flops 2400000000 | tf_op jit(solution)/shard_map/down/pallas_call | solution.py:917
  57.0 9.7 %back.1 = (bf16[128,256]{1,0:T(8,128)(2,1)S(1)}, bf16[128,256]{1,0:T(8,128)(2,1)S(1)}, bf16[2,128,256]{2,1,0:T(8,128)(2,1)S(1)}, f32[128,1024]{1,0:T(8,128)S(1)}...) custom-call(s32[2]{0:T(128)S(1)} %pad_add_fusion.at_ref.refs_0_, ...), custom_call_target="tpu_custom_call" | custom-call | flops 3600000000 | tf_op jit(solution)/shard_map/back/pallas_call | solution.py:1002
  68.7 4.8 %collective-permute-done.15.refs_2_ = bf16[2,128,256]{2,1,0:T(8,128)(2,1)S(1)} collective-permute-done((bf16[2,128,256]{2,1,0:T(8,128)(2,1)S(1)}, bf16[2,128,256]{2,1,0:T(8,128)(2,1)S(1)}, u32[]{:S(2)}, u32[]{:S(2)}) %collective-permute-start.15) | collective-permute-done | bytes 131104 | tf_op jit(solution)/shard_map/ppermute | solution.py:309
  77.2 3.4 %grad_down.1 = (bf16[4,128,1024]{2,1,0:T(8,128)(2,1)S(1)}, bf16[4,128,1024]{2,1,0:T(8,128)(2,1)S(1)}) custom-call(s32[2]{0:T(128)S(1)} %pad_add_fusion.at_ref.refs_0_, bf16[128,1024]{1,0:T(8,128)(2,1)S(1)} %get-tuple-element.124.refs_0_.refs_1_, bf16[128,1024]{1,0:T(8,128)(2,1)S(1)} %get-tuple-element.124.refs_0_.refs_1_, ...), custom_call_target="tpu_custom_call" | custom-call | flops 3000000 | tf_op jit(solution)/shard_map/grad_down/pallas_call | solution.py:1388
  82.3 11.6 %scores_grad.2 = (bf16[640,384]{1,0:T(8,128)(2,1)S(1)}, f32[16,128]{1,0:T(8,128)S(1)}) custom-call(s32[2]{0:T(128)S(1)} %pad_add_fusion.at_ref.refs_0_, bf16[128,256]{1,0:T(8,128)(2,1)S(1)} %get-tuple-element.122.refs_1_, bf16[2,128,256]{2,1,0:T(8,128)(2,1)S(1)} %collective-permute-done.15.refs_2_, bf16[128,256]{1,0:T(8,128)(2,1)S(1)} %collective-permute-done.16.refs_3_, ...), custom_call_target="tpu_custom_call" | custom-call | flops 4499999744 | tf_op jit(solution)/shard_map/scores_grad/pallas_call | solution.py:1273
  97.0 3.6 %grad_in.1 = (bf16[4,128,1024]{2,1,0:T(8,128)(2,1)S(1)}, bf16[4,128,1024]{2,1,0:T(8,128)(2,1)S(1)}) custom-call(s32[2]{0:T(128)S(1)} %pad_add_fusion.at_ref.refs_0_, bf16[128,1024]{1,0:T(8,128)(2,1)S(1)} %get-tuple-element.121.hidden_ref.refs_0_.refs_1_, bf16[128,1024]{1,0:T(8,128)(2,1)S(1)} %get-tuple-element.121.hidden_ref.refs_0_.refs_1_, ...), custom_call_target="tpu_custom_call" | custom-call | flops 3000000 | tf_op jit(solution)/shard_map/grad_in/pallas_call | solution.py:1388
  100.6 4.9 %collective-permute-done.22.refs_17_.refs_18_.refs_24_ = bf16[128,1536]{1,0:T(8,128)(2,1)S(1)} collective-permute-done((bf16[128,1536]{1,0:T(8,128)(2,1)S(1)}, bf16[128,1536]{1,0:T(8,128)(2,1)S(1)}, u32[]{:S(2)}, u32[]{:S(2)}) %collective-permute-start.22) | collective-permute-done | bytes 393248 | tf_op jit(solution)/shard_map/ppermute | solution.py:309
  108.3 5.8 %grad_qkv_out.1 = (bf16[4,128,640]{2,1,0:T(8,128)(2,1)S(1)}, bf16[4,128,640]{2,1,0:T(8,128)(2,1)S(1)}) custom-call(s32[2]{0:T(128)S(1)} %pad_add_fusion.at_ref.refs_0_, bf16[128,1024]{1,0:T(8,128)(2,1)} %bitcast.44, bf16[128,1024]{1,0:T(8,128)(2,1)} %bitcast.45, bf16[128,1024]{1,0:T(8,128)(2,1)} %copy-done.17, bf16[128,1024]{1,0:T(8,128)(2,1)} %copy-done.17, ...), custom_call_target="tpu_custom_call" | custom-call | flops 3000000 | tf_op jit(solution)/shard_map/grad_qkv_out/pallas_call | solution.py:1388
  115.1 13.3 %scores_grad.3 = (bf16[640,384]{1,0:T(8,128)(2,1)S(1)}, bf16[128,768]{1,0:T(8,128)(2,1)S(1)}, bf16[128,768]{1,0:T(8,128)(2,1)S(1)}, bf16[2,128,768]{2,1,0:T(8,128)(2,1)S(1)}, f32[8,48,384]{2,1,0:T(8,128)S(1)}) custom-call(s32[2]{0:T(128)S(1)} %pad_add_fusion.at_ref.refs_0_, bf16[128,256]{1,0:T(8,128)(2,1)S(1)} %get-tuple-element.122.refs_1_, ...), custom_call_target="tpu_custom_call" | custom-call | flops 4499999744 | tf_op jit(solution)/shard_map/scores_grad/pallas_call | solution.py:1273
  133.2 4.0 %grad_qkv.1 = (bf16[4,176,384]{2,1,0:T(8,128)(2,1)S(1)}, bf16[4,176,384]{2,1,0:T(8,128)(2,1)S(1)}) custom-call(s32[2]{0:T(128)S(1)} %pad_add_fusion.at_ref.refs_0_, bf16[128,1024]{1,0:T(8,128)(2,1)} %bitcast.46, bf16[128,1024]{1,0:T(8,128)(2,1)} %bitcast.47, bf16[128,1024]{1,0:T(8,128)(2,1)} %copy-done.17, bf16[128,1024]{1,0:T(8,128)(2,1)} %copy-done.17, ...), custom_call_target="tpu_custom_call" | custom-call | flops 3000000 | tf_op jit(solution)/shard_map/grad_qkv/pallas_call | solution.py:1388
  139.9 2.6 %collective-permute-start.32 = (bf16[1,128,1024]{2,1,0:T(8,128)(2,1)S(1)}, bf16[1,128,1024]{2,1,0:T(8,128)(2,1)S(1)}, u32[]{:S(2)}, u32[]{:S(2)}) collective-permute-start(bf16[1,128,1024]{2,1,0:T(8,128)(2,1)S(1)} %add_convert_fusion.13), channel_id=1, source_target_pairs={{0,4},{1,5},{2,6},{3,7},{4,0},{5,1},{6,2},{7,3},{8,12},{9,13},{10,... | collective-permute-start | bytes 786440 | tf_op jit(solution)/shard_map/ppermute | solution.py:309
  144.8 6.2 %tokens_grad.1 = f32[128,1024]{1,0:T(8,128)} custom-call(s32[2]{0:T(128)S(1)} %pad_add_fusion.at_ref.refs_0_, bf16[128,768]{1,0:T(8,128)(2,1)S(1)} %get-tuple-element.168.d0, bf16[2,128,768]{2,1,0:T(8,128)(2,1)S(1)} %collective-permute-done.28.d1, bf16[128,768]{1,0:T(8,128)(2,1)S(1)} %collective-permute-done.29.d2, ...), custom_call_target="tpu_custom_call" | custom-call | flops 1200000000 | tf_op jit(solution)/shard_map/tokens_grad/pallas_call | solution.py:1437
  151.9 5.8 %collective-permute-done.33 = bf16[4,176,384]{2,1,0:T(8,128)(2,1)S(1)} collective-permute-done((bf16[4,176,384]{2,1,0:T(8,128)(2,1)S(1)}, bf16[4,176,384]{2,1,0:T(8,128)(2,1)S(1)}, u32[]{:S(2)}, u32[]{:S(2)}) %collective-permute-start.33) | collective-permute-done | bytes 540704 | tf_op jit(solution)/shard_map/ppermute | solution.py:309
  163.9 8.5 %collective-permute-done.37 = bf16[2,176,384]{2,1,0:T(8,128)(2,1)S(1)} collective-permute-done((bf16[2,176,384]{2,1,0:T(8,128)(2,1)S(1)}, bf16[2,176,384]{2,1,0:T(8,128)(2,1)S(1)}, u32[]{:S(2)}, u32[]{:S(2)}) %collective-permute-start.37) | collective-permute-done | bytes 270368 | tf_op jit(solution)/shard_map/ppermute | solution.py:309
  172.8 2.7 %collective-permute-done.35 = bf16[1,128,640]{2,1,0:T(8,128)(2,1)S(1)} collective-permute-done((bf16[1,128,640]{2,1,0:T(8,128)(2,1)S(1)}, bf16[1,128,640]{2,1,0:T(8,128)(2,1)S(1)}, u32[]{:S(2)}, u32[]{:S(2)}) %collective-permute-start.35) | collective-permute-done | bytes 163872 | tf_op jit(solution)/shard_map/ppermute | solution.py:309
  176.5 2.4 %collective-permute-done.42 = bf16[1,176,384]{2,1,0:T(8,128)(2,1)S(1)} collective-permute-done((bf16[1,176,384]{2,1,0:T(8,128)(2,1)S(1)}, bf16[1,176,384]{2,1,0:T(8,128)(2,1)S(1)}, u32[]{:S(2)}, u32[]{:S(2)}) %collective-permute-start.42) | collective-permute-done | bytes 135200 | tf_op jit(solution)/shard_map/ppermute | solution.py:309
  179.0 2.8 %collective-permute-done.45.refs_6_ = bf16[128,1024]{1,0:T(8,128)(2,1)S(1)} collective-permute-done((bf16[128,1024]{1,0:T(8,128)(2,1)S(1)}, bf16[128,1024]{1,0:T(8,128)(2,1)S(1)}, u32[]{:S(2)}, u32[]{:S(2)}) %collective-permute-start.45) | collective-permute-done | bytes 262176 | tf_op jit(solution)/shard_map/ppermute | solution.py:309
  183.9 3.1 %gather_parts.1 = (f32[512,1024]{1,0:T(8,128)}, f32[128,4096]{1,0:T(8,128)}) custom-call(s32[2]{0:T(128)S(1)} %pad_add_fusion.at_ref.refs_0_, bf16[128,1024]{1,0:T(8,128)(2,1)S(1)} %fusion.refs_0_, bf16[128,1024]{1,0:T(8,128)(2,1)S(1)} %collective-permute-done.40.refs_1_, bf16[128,1024]{1,0:T(8,128)(2,1)S(1)} %collective-permute-done.41.refs_2_, ...), custom_call_target="tpu_custom_call" | custom-call | flops 600000000 | tf_op jit(solution)/shard_map/gather_parts/pallas_call | solution.py:1478
  192.7 2.6 %last.1 = (f32[128,1024]{1,0:T(8,128)}, f32[128,1024]{1,0:T(8,128)}, f32[128,1024]{1,0:T(8,128)}, f32[128,1024]{1,0:T(8,128)}, f32[16,1024]{1,0:T(8,128)}, /*ind...) custom-call(s32[2]{0:T(128)S(1)} %pad_add_fusion.at_ref.refs_0_, ...), custom_call_target="tpu_custom_call" | custom-call | flops 600000000 | tf_op jit(solution)/shard_map/last/pallas_call | solution.py:1528
  (148 shorter events, 51.2 us)
Async XLA Ops:
  0.6 9.6 %collective-permute-start = (bf16[128,1024]{1,0:T(8,128)(2,1)}, bf16[128,1024]{1,0:T(8,128)(2,1)S(1)}, u32[]{:S(2)}, u32[]{:S(2)}) collective-permute-start(bf16[128,1024]{1,0:T(8,128)(2,1)} %bitcast.41), channel_id=1, source_target_pairs={{0,16},{8,24},{16,0},{24,8},{1,17},{9,25},{17,1},{25,9},{2,18},{10... | collective-permute-start | bytes 786440 | tf_op jit(solution)/shard_map/ppermute | solution.py:309
  5.2 8.2 %collective-permute-start.1 = (bf16[128,1024]{1,0:T(8,128)(2,1)}, bf16[128,1024]{1,0:T(8,128)(2,1)S(1)}, u32[]{:S(2)}, u32[]{:S(2)}) collective-permute-start(bf16[128,1024]{1,0:T(8,128)(2,1)} %bitcast.42), channel_id=1, source_target_pairs={{0,8},{8,0},{16,24},{24,16},{1,9},{9,1},{17,25},{25,17},{2,10},{10... | collective-permute-start | bytes 786440 | tf_op jit(solution)/shard_map/ppermute | solution.py:309
  50.9 15.8 %collective-permute-start.9 = (bf16[2,128,1024]{2,1,0:T(8,128)(2,1)S(1)}, bf16[2,128,1024]{2,1,0:T(8,128)(2,1)S(1)}, u32[]{:S(2)}, u32[]{:S(2)}) collective-permute-start(bf16[2,128,1024]{2,1,0:T(8,128)(2,1)S(1)} %get-tuple-element.125), channel_id=1, source_target_pairs={{0,16},{8,24},{16,0},{24,8},{1,17},{9,25},{17,1},{25,9},{2,18},{10... | collective-permute-start | bytes 1572872 | tf_op jit(solution)/shard_map/ppermute | solution.py:309
  56.7 18.6 %collective-permute-start.12 = (bf16[128,1024]{1,0:T(8,128)(2,1)S(1)}, bf16[128,1024]{1,0:T(8,128)(2,1)S(1)}, u32[]{:S(2)}, u32[]{:S(2)}) collective-permute-start(bf16[128,1024]{1,0:T(8,128)(2,1)S(1)} %get-tuple-element.118.ffn_ref.refs_8_), channel_id=1, source_target_pairs={{0,16},{8,24},{16,0},{24,8},{1,17},{9,25},{17,1},{25,9},{2,18},{10... | collective-permute-start | bytes 786440 | tf_op jit(solution)/shard_map/ppermute | solution.py:309
  66.6 10.5 %collective-permute-start.11 = (bf16[2,128,1024]{2,1,0:T(8,128)(2,1)S(1)}, bf16[2,128,1024]{2,1,0:T(8,128)(2,1)S(1)}, u32[]{:S(2)}, u32[]{:S(2)}) collective-permute-start(bf16[2,128,1024]{2,1,0:T(8,128)(2,1)S(1)} %collective-permute-done.9.refs_2_.refs_3_), channel_id=1, source_target_pairs={{0,8},{8,0},{16,24},{24,16},{1,9},{9,1},{17,25},{25,17},{2,10},{10... | collective-permute-start | bytes 1572872 | tf_op jit(solution)/shard_map/ppermute | solution.py:309
  73.5 20.3 %collective-permute-start.18 = (bf16[3,128,1024]{2,1,0:T(8,128)(2,1)S(1)}, bf16[3,128,1024]{2,1,0:T(8,128)(2,1)S(1)}, u32[]{:S(2)}, u32[]{:S(2)}) collective-permute-start(bf16[3,128,1024]{2,1,0:T(8,128)(2,1)S(1)} %get-tuple-element.141), channel_id=1, source_target_pairs={{0,16},{8,24},{16,0},{24,8},{1,17},{9,25},{17,1},{25,9},{2,18},{10... | collective-permute-start | bytes 2359304 | tf_op jit(solution)/shard_map/ppermute | solution.py:309
  80.7 25.6 %collective-permute-start.21 = (bf16[4,128,1024]{2,1,0:T(8,128)(2,1)S(1)}, bf16[4,128,1024]{2,1,0:T(8,128)(2,1)S(1)}, u32[]{:S(2)}, u32[]{:S(2)}) collective-permute-start(bf16[4,128,1024]{2,1,0:T(8,128)(2,1)S(1)} %get-tuple-element.146), channel_id=1, source_target_pairs={{0,1},{1,0},{2,3},{3,2},{4,5},{5,4},{6,7},{7,6},{8,9},{9,8},{10,11... | collective-permute-start | bytes 3145736 | tf_op jit(solution)/shard_map/ppermute | solution.py:309
  94.4 11.1 %collective-permute-start.22 = (bf16[128,1536]{1,0:T(8,128)(2,1)S(1)}, bf16[128,1536]{1,0:T(8,128)(2,1)S(1)}, u32[]{:S(2)}, u32[]{:S(2)}) collective-permute-start(bf16[128,1536]{1,0:T(8,128)(2,1)S(1)} %get-tuple-element.150.refs_15_.refs_16_), channel_id=1, source_target_pairs={{0,16},{8,24},{16,0},{24,8},{1,17},{9,25},{17,1},{25,9},{2,18},{10... | collective-permute-start | bytes 1179656 | tf_op jit(solution)/shard_map/ppermute | solution.py:309
  105.6 25.6 %collective-permute-start.26 = (bf16[4,128,1024]{2,1,0:T(8,128)(2,1)S(1)}, bf16[4,128,1024]{2,1,0:T(8,128)(2,1)S(1)}, u32[]{:S(2)}, u32[]{:S(2)}) collective-permute-start(bf16[4,128,1024]{2,1,0:T(8,128)(2,1)S(1)} %get-tuple-element.156), channel_id=1, source_target_pairs={{0,1},{1,0},{2,3},{3,2},{4,5},{5,4},{6,7},{7,6},{8,9},{9,8},{10,11... | collective-permute-start | bytes 3145736 | tf_op jit(solution)/shard_map/ppermute | solution.py:309
  106.7 23.0 %collective-permute-start.27 = (bf16[2,128,1024]{2,1,0:T(8,128)(2,1)S(1)}, bf16[2,128,1024]{2,1,0:T(8,128)(2,1)S(1)}, u32[]{:S(2)}, u32[]{:S(2)}) collective-permute-start(bf16[2,128,1024]{2,1,0:T(8,128)(2,1)S(1)} %get-tuple-element.203), channel_id=1, source_target_pairs={{0,2},{1,3},{2,0},{3,1},{4,6},{5,7},{6,4},{7,5},{8,10},{9,11},{10,... | collective-permute-start | bytes 1572872 | tf_op jit(solution)/shard_map/ppermute | solution.py:309
  114.1 28.4 %collective-permute-start.25 = (bf16[4,128,640]{2,1,0:T(8,128)(2,1)S(1)}, bf16[4,128,640]{2,1,0:T(8,128)(2,1)S(1)}, u32[]{:S(2)}, u32[]{:S(2)}) collective-permute-start(bf16[4,128,640]{2,1,0:T(8,128)(2,1)S(1)} %get-tuple-element.155), channel_id=1, source_target_pairs={{0,2},{1,3},{2,0},{3,1},{4,6},{5,7},{6,4},{7,5},{8,10},{9,11},{10,... | collective-permute-start | bytes 1966088 | tf_op jit(solution)/shard_map/ppermute | solution.py:309
  128.4 11.0 %collective-permute-start.28 = (bf16[2,128,768]{2,1,0:T(8,128)(2,1)S(1)}, bf16[2,128,768]{2,1,0:T(8,128)(2,1)S(1)}, u32[]{:S(2)}, u32[]{:S(2)}) collective-permute-start(bf16[2,128,768]{2,1,0:T(8,128)(2,1)S(1)} %get-tuple-element.169), channel_id=1, source_target_pairs={{0,16},{8,24},{16,0},{24,8},{1,17},{9,25},{17,1},{25,9},{2,18},{10... | collective-permute-start | bytes 1179656 | tf_op jit(solution)/shard_map/ppermute | solution.py:309
  131.5 19.5 %collective-permute-start.34 = (bf16[2,128,1024]{2,1,0:T(8,128)(2,1)S(1)}, bf16[2,128,1024]{2,1,0:T(8,128)(2,1)S(1)}, u32[]{:S(2)}, u32[]{:S(2)}) collective-permute-start(bf16[2,128,1024]{2,1,0:T(8,128)(2,1)S(1)} %get-tuple-element.201), channel_id=1, source_target_pairs={{0,2},{1,3},{2,0},{3,1},{4,6},{5,7},{6,4},{7,5},{8,10},{9,11},{10,... | collective-permute-start | bytes 1572872 | tf_op jit(solution)/shard_map/ppermute | solution.py:309
  139.9 20.3 %collective-permute-start.32 = (bf16[1,128,1024]{2,1,0:T(8,128)(2,1)S(1)}, bf16[1,128,1024]{2,1,0:T(8,128)(2,1)S(1)}, u32[]{:S(2)}, u32[]{:S(2)}) collective-permute-start(bf16[1,128,1024]{2,1,0:T(8,128)(2,1)S(1)} %add_convert_fusion.13), channel_id=1, source_target_pairs={{0,4},{1,5},{2,6},{3,7},{4,0},{5,1},{6,2},{7,3},{8,12},{9,13},{10,... | collective-permute-start | bytes 786440 | tf_op jit(solution)/shard_map/ppermute | solution.py:309
  142.5 15.2 %collective-permute-start.33 = (bf16[4,176,384]{2,1,0:T(8,128)(2,1)S(1)}, bf16[4,176,384]{2,1,0:T(8,128)(2,1)S(1)}, u32[]{:S(2)}, u32[]{:S(2)}) collective-permute-start(bf16[4,176,384]{2,1,0:T(8,128)(2,1)S(1)} %get-tuple-element.173), channel_id=1, source_target_pairs={{0,1},{1,0},{2,3},{3,2},{4,5},{5,4},{6,7},{7,6},{8,9},{9,8},{10,11... | collective-permute-start | bytes 1622024 | tf_op jit(solution)/shard_map/ppermute | solution.py:309
  144.2 19.2 %collective-permute-start.31 = (bf16[2,128,640]{2,1,0:T(8,128)(2,1)S(1)}, bf16[2,128,640]{2,1,0:T(8,128)(2,1)S(1)}, u32[]{:S(2)}, u32[]{:S(2)}) collective-permute-start(bf16[2,128,640]{2,1,0:T(8,128)(2,1)S(1)} %get-tuple-element.205), channel_id=1, source_target_pairs={{0,1},{1,0},{2,3},{3,2},{4,5},{5,4},{6,7},{7,6},{8,9},{9,8},{10,11... | collective-permute-start | bytes 983048 | tf_op jit(solution)/shard_map/ppermute | solution.py:309
  151.1 21.5 %collective-permute-start.36 = (bf16[1,128,1024]{2,1,0:T(8,128)(2,1)S(1)}, bf16[1,128,1024]{2,1,0:T(8,128)(2,1)S(1)}, u32[]{:S(2)}, u32[]{:S(2)}) collective-permute-start(bf16[1,128,1024]{2,1,0:T(8,128)(2,1)S(1)} %add_convert_fusion.11), channel_id=1, source_target_pairs={{0,4},{1,5},{2,6},{3,7},{4,0},{5,1},{6,2},{7,3},{8,12},{9,13},{10,... | collective-permute-start | bytes 786440 | tf_op jit(solution)/shard_map/ppermute | solution.py:309
  157.8 14.6 %collective-permute-start.37 = (bf16[2,176,384]{2,1,0:T(8,128)(2,1)S(1)}, bf16[2,176,384]{2,1,0:T(8,128)(2,1)S(1)}, u32[]{:S(2)}, u32[]{:S(2)}) collective-permute-start(bf16[2,176,384]{2,1,0:T(8,128)(2,1)S(1)} %get-tuple-element.207), channel_id=1, source_target_pairs={{0,2},{1,3},{2,0},{3,1},{4,6},{5,7},{6,4},{7,5},{8,10},{9,11},{10,... | collective-permute-start | bytes 811016 | tf_op jit(solution)/shard_map/ppermute | solution.py:309
  160.3 23.1 %collective-permute-start.40 = (bf16[128,1024]{1,0:T(8,128)(2,1)S(1)}, bf16[128,1024]{1,0:T(8,128)(2,1)S(1)}, u32[]{:S(2)}, u32[]{:S(2)}) collective-permute-start(bf16[128,1024]{1,0:T(8,128)(2,1)S(1)} %fusion.refs_0_), channel_id=1, source_target_pairs={{0,8},{8,0},{16,24},{24,16},{1,9},{9,1},{17,25},{25,17},{2,10},{10... | collective-permute-start | bytes 786440 | tf_op jit(solution)/shard_map/ppermute | solution.py:309
  160.4 18.6 %collective-permute-start.41 = (bf16[128,1024]{1,0:T(8,128)(2,1)S(1)}, bf16[128,1024]{1,0:T(8,128)(2,1)S(1)}, u32[]{:S(2)}, u32[]{:S(2)}) collective-permute-start(bf16[128,1024]{1,0:T(8,128)(2,1)S(1)} %fusion.refs_0_), channel_id=1, source_target_pairs={{0,16},{8,24},{16,0},{24,8},{1,17},{9,25},{17,1},{25,9},{2,18},{10... | collective-permute-start | bytes 786440 | tf_op jit(solution)/shard_map/ppermute | solution.py:309
  163.5 12.0 %collective-permute-start.35 = (bf16[1,128,640]{2,1,0:T(8,128)(2,1)S(1)}, bf16[1,128,640]{2,1,0:T(8,128)(2,1)S(1)}, u32[]{:S(2)}, u32[]{:S(2)}) collective-permute-start(bf16[1,128,640]{2,1,0:T(8,128)(2,1)S(1)} %add_convert_fusion.15), channel_id=1, source_target_pairs={{0,4},{1,5},{2,6},{3,7},{4,0},{5,1},{6,2},{7,3},{8,12},{9,13},{10,... | collective-permute-start | bytes 491528 | tf_op jit(solution)/shard_map/ppermute | solution.py:309
  172.7 11.2 %collective-permute-start.44 = (bf16[128,1024]{1,0:T(8,128)(2,1)S(1)}, bf16[128,1024]{1,0:T(8,128)(2,1)S(1)}, u32[]{:S(2)}, u32[]{:S(2)}) collective-permute-start(bf16[128,1024]{1,0:T(8,128)(2,1)S(1)} %fusion.1.refs_4_), channel_id=1, source_target_pairs={{0,8},{8,0},{16,24},{24,16},{1,9},{9,1},{17,25},{25,17},{2,10},{10... | collective-permute-start | bytes 786440 | tf_op jit(solution)/shard_map/ppermute | solution.py:309
  183.4 7.9 %collective-permute-start.49 = (bf16[176,384]{1,0:T(8,128)(2,1)S(1)}, bf16[176,384]{1,0:T(8,128)(2,1)S(1)}, u32[]{:S(2)}, u32[]{:S(2)}) collective-permute-start(bf16[176,384]{1,0:T(8,128)(2,1)S(1)} %fusion.3.refs_4_), channel_id=1, source_target_pairs={{0,16},{8,24},{16,0},{24,8},{1,17},{9,25},{17,1},{25,9},{2,18},{10... | collective-permute-start | bytes 405512 | tf_op jit(solution)/shard_map/ppermute | solution.py:309
  183.8 7.5 %collective-permute-start.38 = (bf16[128,640]{1,0:T(8,128)(2,1)S(1)}, bf16[128,640]{1,0:T(8,128)(2,1)S(1)}, u32[]{:S(2)}, u32[]{:S(2)}) collective-permute-start(bf16[128,640]{1,0:T(8,128)(2,1)S(1)} %fusion.2.refs_0_), channel_id=1, source_target_pairs={{0,8},{8,0},{16,24},{24,16},{1,9},{9,1},{17,25},{25,17},{2,10},{10... | collective-permute-start | bytes 491528 | tf_op jit(solution)/shard_map/ppermute | solution.py:309
  (46 other events, 329.6 us)

commit v5 on v4

--- a/solution.py
+++ b/solution.py
@@ -1662,6 +1662,7 @@
     ]
     done = down_sum.add(in_halves[0])
     early = [done]
+    early = [done]
     first_groups = [(lefts, rows_by_piece(first_grads), 3 * width // 2), (att_all, gattn_all, width)]
     (first_halves,) = weight_grads_call(
         spot, [(first_groups, other, None)], after=[in_halves[0]] + early, name="grad_qkv_out"
@@ -1696,9 +1697,9 @@
     done = down_sum.add(done)
     down_part = done
     done = first_sum.add(done)
-    done = second_sum.add(done)
     done = in_sum.add(done)
     in_part = done
+    done = second_sum.add(done)
     done = first_sum.add(done)
     first_part = done
     done = second_sum.add(done)

time: 196 us -> 196 us (level)
  transfers between devices with their start and end apart: 51 -> 51, of which waited for: 21 -> 20; matrix products, arithmetic and copies ran while one was open for 2% -> 2% of each run, Pallas kernels for 33% -> 33%
where the time goes in v5:
time: 196 us; the launch traced here: 195 us
  Pallas kernels  96 us (49%)
  waiting for transfers between devices  56.8 us (29%)
  starting transfers between devices  34.7 us (18%)
  other arithmetic  4.04 us (2%)
    ppermute x51, waiting for transfers between devices, swap(): return lax.ppermute(array, axis, [(i, i ^ by) for i in range(count)])  56.8 us
    ppermute x51, starting transfers between devices, swap(): return lax.ppermute(array, axis, [(i, i ^ by) for i in range(count)])  34.7 us
    pallas_call x2, Pallas kernels, scores_grad_call(): pl.pallas_call(functools.partial(scores_grad_kernel, half, 0), out_shape=...  24.8 us
    pallas_call x1, Pallas kernels, scores_call(): pl.pallas_call(scores_kernel, out_shape=(jax.ShapeDtypeStruct((lanes, wid...  19.4 us
    pallas_call x4, Pallas kernels, weight_grads_call(): pl.pallas_call(kernel, out_shape=tuple(shapes), grid_spec=pltpu.PrefetchS...  16.9 us
    pallas_call x1, Pallas kernels, back_call(): pl.pallas_call(back_kernel, out_shape=(jax.ShapeDtypeStruct((rows, width)...  9.65 us
    pallas_call x1, Pallas kernels, up_call(): pl.pallas_call(up_kernel, out_shape=(jax.ShapeDtypeStruct((2, rows, quart...  9.35 us
    pallas_call x1, Pallas kernels, tokens_grad_call(): pl.pallas_call(tokens_grad_kernel, out_shape=jax.ShapeDtypeStruct((rows,...  6.22 us
  transfers between devices with their start and end apart: 51, of which 20 were waited for; matrix products, arithmetic and copies ran while one was open for 2% of the time, Pallas kernels for 33%

profile of v5, /device:TPU:0, one launch (start us, length us, event | category | flops | bytes accessed | tf_op | source)
XLA Modules:
  0.0 195.2 jit_solution(6460608229077168377)
XLA Ops:
  0.6 3.0 %collective-permute-start = (bf16[128,1024]{1,0:T(8,128)(2,1)}, bf16[128,1024]{1,0:T(8,128)(2,1)S(1)}, u32[]{:S(2)}, u32[]{:S(2)}) collective-permute-start(bf16[128,1024]{1,0:T(8,128)(2,1)} %bitcast.41), channel_id=1, source_target_pairs={{0,16},{8,24},{16,0},{24,8},{1,17},{9,25},{17,1},{25,9},{2,18},{10... | collective-permute-start | bytes 786440 | tf_op jit(solution)/shard_map/ppermute | solution.py:309
  5.2 5.1 %collective-permute-done.2.i1 = s32[8,128]{1,0:T(8,128)S(1)} collective-permute-done((s32[8,128]{1,0:T(8,128)S(1)}, s32[8,128]{1,0:T(8,128)S(1)}, u32[]{:S(2)}, u32[]{:S(2)}) %collective-permute-start.2) | collective-permute-done | bytes 4128 | tf_op jit(solution)/shard_map/ppermute | solution.py:309
  15.0 19.4 %scores.1 = (bf16[128,256]{1,0:T(8,128)(2,1)S(1)}, bf16[128,256]{1,0:T(8,128)(2,1)S(1)}, bf16[2,128,256]{2,1,0:T(8,128)(2,1)S(1)}, bf16[4,512,512]{2,1,0:T(8,128...) custom-call(s32[2]{0:T(128)S(1)} %pad_add_fusion.1.at_ref, ...), custom_call_target="tpu_custom_call" | custom-call | flops 7500000256 | tf_op jit(solution)/shard_map/scores/pallas_call | solution.py:743
  36.1 3.8 %collective-permute-done.6.a1 = bf16[2,128,256]{2,1,0:T(8,128)(2,1)S(1)} collective-permute-done((bf16[2,128,256]{2,1,0:T(8,128)(2,1)S(1)}, bf16[2,128,256]{2,1,0:T(8,128)(2,1)S(1)}, u32[]{:S(2)}, u32[]{:S(2)}) %collective-permute-start.6) | collective-permute-done | bytes 131104 | tf_op jit(solution)/shard_map/ppermute | solution.py:309
  41.5 9.3 %up.1 = (bf16[2,128,1024]{2,1,0:T(8,128)(2,1)S(1)}, bf16[128,1024]{1,0:T(8,128)(2,1)S(1)}, bf16[128,1024]{1,0:T(8,128)(2,1)S(1)}, bf16[128,4096]{1,0:T(8,128)(2,...) custom-call(s32[2]{0:T(128)S(1)} %pad_add_fusion.at_ref.refs_0_, ...), custom_call_target="tpu_custom_call" | custom-call | flops 2700000000 | tf_op jit(solution)/shard_map/up/pallas_call | solution.py:835
  52.7 4.0 %down.1 = (bf16[128,1024]{1,0:T(8,128)(2,1)}, f32[128,1024]{1,0:T(8,128)S(1)}, bf16[128,1024]{1,0:T(8,128)(2,1)S(1)}, f32[8,1024]{1,0:T(8,128)S(1)}) custom-call(bf16[128,4096]{1,0:T(8,128)(2,1)S(1)} %get-tuple-element.112.act_ref, bf16[4096,1024]{1,0:T(8,128)(2,1)S(1)} %copy-done.1, f32[128,1024]{1,0:T(8,128)S(1)} %get-tuple-element.113.normed_ref, ...), custom_call_target="tpu_custom_call" | custom-call | flops 2400000000 | tf_op jit(solution)/shard_map/down/pallas_call | solution.py:917
  57.0 9.7 %back.1 = (bf16[128,256]{1,0:T(8,128)(2,1)S(1)}, bf16[128,256]{1,0:T(8,128)(2,1)S(1)}, bf16[2,128,256]{2,1,0:T(8,128)(2,1)S(1)}, f32[128,1024]{1,0:T(8,128)S(1)}...) custom-call(s32[2]{0:T(128)S(1)} %pad_add_fusion.at_ref.refs_0_, ...), custom_call_target="tpu_custom_call" | custom-call | flops 3600000000 | tf_op jit(solution)/shard_map/back/pallas_call | solution.py:1002
  68.7 4.8 %collective-permute-done.15.refs_2_ = bf16[2,128,256]{2,1,0:T(8,128)(2,1)S(1)} collective-permute-done((bf16[2,128,256]{2,1,0:T(8,128)(2,1)S(1)}, bf16[2,128,256]{2,1,0:T(8,128)(2,1)S(1)}, u32[]{:S(2)}, u32[]{:S(2)}) %collective-permute-start.15) | collective-permute-done | bytes 131104 | tf_op jit(solution)/shard_map/ppermute | solution.py:309
  77.2 3.4 %grad_down.1 = (bf16[4,128,1024]{2,1,0:T(8,128)(2,1)S(1)}, bf16[4,128,1024]{2,1,0:T(8,128)(2,1)S(1)}) custom-call(s32[2]{0:T(128)S(1)} %pad_add_fusion.at_ref.refs_0_, bf16[128,1024]{1,0:T(8,128)(2,1)S(1)} %get-tuple-element.124.refs_0_.refs_1_, bf16[128,1024]{1,0:T(8,128)(2,1)S(1)} %get-tuple-element.124.refs_0_.refs_1_, ...), custom_call_target="tpu_custom_call" | custom-call | flops 3000000 | tf_op jit(solution)/shard_map/grad_down/pallas_call | solution.py:1388
  82.3 11.6 %scores_grad.2 = (bf16[640,384]{1,0:T(8,128)(2,1)S(1)}, f32[16,128]{1,0:T(8,128)S(1)}) custom-call(s32[2]{0:T(128)S(1)} %pad_add_fusion.at_ref.refs_0_, bf16[128,256]{1,0:T(8,128)(2,1)S(1)} %get-tuple-element.122.refs_1_, bf16[2,128,256]{2,1,0:T(8,128)(2,1)S(1)} %collective-permute-done.15.refs_2_, bf16[128,256]{1,0:T(8,128)(2,1)S(1)} %collective-permute-done.16.refs_3_, ...), custom_call_target="tpu_custom_call" | custom-call | flops 4499999744 | tf_op jit(solution)/shard_map/scores_grad/pallas_call | solution.py:1273
  97.0 3.6 %grad_in.1 = (bf16[4,128,1024]{2,1,0:T(8,128)(2,1)S(1)}, bf16[4,128,1024]{2,1,0:T(8,128)(2,1)S(1)}) custom-call(s32[2]{0:T(128)S(1)} %pad_add_fusion.at_ref.refs_0_, bf16[128,1024]{1,0:T(8,128)(2,1)S(1)} %get-tuple-element.121.hidden_ref.refs_0_.refs_1_, bf16[128,1024]{1,0:T(8,128)(2,1)S(1)} %get-tuple-element.121.hidden_ref.refs_0_.refs_1_, ...), custom_call_target="tpu_custom_call" | custom-call | flops 3000000 | tf_op jit(solution)/shard_map/grad_in/pallas_call | solution.py:1388
  100.6 4.9 %collective-permute-done.22.refs_17_.refs_18_.refs_24_ = bf16[128,1536]{1,0:T(8,128)(2,1)S(1)} collective-permute-done((bf16[128,1536]{1,0:T(8,128)(2,1)S(1)}, bf16[128,1536]{1,0:T(8,128)(2,1)S(1)}, u32[]{:S(2)}, u32[]{:S(2)}) %collective-permute-start.22) | collective-permute-done | bytes 393248 | tf_op jit(solution)/shard_map/ppermute | solution.py:309
  108.3 5.8 %grad_qkv_out.1 = (bf16[4,128,640]{2,1,0:T(8,128)(2,1)S(1)}, bf16[4,128,640]{2,1,0:T(8,128)(2,1)S(1)}) custom-call(s32[2]{0:T(128)S(1)} %pad_add_fusion.at_ref.refs_0_, bf16[128,1024]{1,0:T(8,128)(2,1)} %bitcast.44, bf16[128,1024]{1,0:T(8,128)(2,1)} %bitcast.45, bf16[128,1024]{1,0:T(8,128)(2,1)} %copy-done.17, bf16[128,1024]{1,0:T(8,128)(2,1)} %copy-done.17, ...), custom_call_target="tpu_custom_call" | custom-call | flops 3000000 | tf_op jit(solution)/shard_map/grad_qkv_out/pallas_call | solution.py:1388
  115.1 13.3 %scores_grad.3 = (bf16[640,384]{1,0:T(8,128)(2,1)S(1)}, bf16[128,768]{1,0:T(8,128)(2,1)S(1)}, bf16[128,768]{1,0:T(8,128)(2,1)S(1)}, bf16[2,128,768]{2,1,0:T(8,128)(2,1)S(1)}, f32[8,48,384]{2,1,0:T(8,128)S(1)}) custom-call(s32[2]{0:T(128)S(1)} %pad_add_fusion.at_ref.refs_0_, bf16[128,256]{1,0:T(8,128)(2,1)S(1)} %get-tuple-element.122.refs_1_, ...), custom_call_target="tpu_custom_call" | custom-call | flops 4499999744 | tf_op jit(solution)/shard_map/scores_grad/pallas_call | solution.py:1273
  133.2 4.0 %grad_qkv.1 = (bf16[4,176,384]{2,1,0:T(8,128)(2,1)S(1)}, bf16[4,176,384]{2,1,0:T(8,128)(2,1)S(1)}) custom-call(s32[2]{0:T(128)S(1)} %pad_add_fusion.at_ref.refs_0_, bf16[128,1024]{1,0:T(8,128)(2,1)} %bitcast.46, bf16[128,1024]{1,0:T(8,128)(2,1)} %bitcast.47, bf16[128,1024]{1,0:T(8,128)(2,1)} %copy-done.17, bf16[128,1024]{1,0:T(8,128)(2,1)} %copy-done.17, ...), custom_call_target="tpu_custom_call" | custom-call | flops 3000000 | tf_op jit(solution)/shard_map/grad_qkv/pallas_call | solution.py:1388
  137.2 2.2 %collective-permute-done.28.d1 = bf16[2,128,768]{2,1,0:T(8,128)(2,1)S(1)} collective-permute-done((bf16[2,128,768]{2,1,0:T(8,128)(2,1)S(1)}, bf16[2,128,768]{2,1,0:T(8,128)(2,1)S(1)}, u32[]{:S(2)}, u32[]{:S(2)}) %collective-permute-start.28) | collective-permute-done | bytes 393248 | tf_op jit(solution)/shard_map/ppermute | solution.py:309
  139.9 2.6 %collective-permute-start.32 = (bf16[1,128,1024]{2,1,0:T(8,128)(2,1)S(1)}, bf16[1,128,1024]{2,1,0:T(8,128)(2,1)S(1)}, u32[]{:S(2)}, u32[]{:S(2)}) collective-permute-start(bf16[1,128,1024]{2,1,0:T(8,128)(2,1)S(1)} %add_convert_fusion.13), channel_id=1, source_target_pairs={{0,4},{1,5},{2,6},{3,7},{4,0},{5,1},{6,2},{7,3},{8,12},{9,13},{10,... | collective-permute-start | bytes 786440 | tf_op jit(solution)/shard_map/ppermute | solution.py:309
  144.8 6.2 %tokens_grad.1 = f32[128,1024]{1,0:T(8,128)} custom-call(s32[2]{0:T(128)S(1)} %pad_add_fusion.at_ref.refs_0_, bf16[128,768]{1,0:T(8,128)(2,1)S(1)} %get-tuple-element.168.d0, bf16[2,128,768]{2,1,0:T(8,128)(2,1)S(1)} %collective-permute-done.28.d1, bf16[128,768]{1,0:T(8,128)(2,1)S(1)} %collective-permute-done.29.d2, ...), custom_call_target="tpu_custom_call" | custom-call | flops 1200000000 | tf_op jit(solution)/shard_map/tokens_grad/pallas_call | solution.py:1437
  151.9 5.8 %collective-permute-done.33 = bf16[4,176,384]{2,1,0:T(8,128)(2,1)S(1)} collective-permute-done((bf16[4,176,384]{2,1,0:T(8,128)(2,1)S(1)}, bf16[4,176,384]{2,1,0:T(8,128)(2,1)S(1)}, u32[]{:S(2)}, u32[]{:S(2)}) %collective-permute-start.33) | collective-permute-done | bytes 540704 | tf_op jit(solution)/shard_map/ppermute | solution.py:309
  163.9 2.2 %collective-permute-done.37 = bf16[1,128,1024]{2,1,0:T(8,128)(2,1)S(1)} collective-permute-done((bf16[1,128,1024]{2,1,0:T(8,128)(2,1)S(1)}, bf16[1,128,1024]{2,1,0:T(8,128)(2,1)S(1)}, u32[]{:S(2)}, u32[]{:S(2)}) %collective-permute-start.37) | collective-permute-done | bytes 262176 | tf_op jit(solution)/shard_map/ppermute | solution.py:309
  166.3 7.2 %collective-permute-done.36 = bf16[2,176,384]{2,1,0:T(8,128)(2,1)S(1)} collective-permute-done((bf16[2,176,384]{2,1,0:T(8,128)(2,1)S(1)}, bf16[2,176,384]{2,1,0:T(8,128)(2,1)S(1)}, u32[]{:S(2)}, u32[]{:S(2)}) %collective-permute-start.36) | collective-permute-done | bytes 270368 | tf_op jit(solution)/shard_map/ppermute | solution.py:309
  174.9 6.4 %collective-permute-done.42 = bf16[1,176,384]{2,1,0:T(8,128)(2,1)S(1)} collective-permute-done((bf16[1,176,384]{2,1,0:T(8,128)(2,1)S(1)}, bf16[1,176,384]{2,1,0:T(8,128)(2,1)S(1)}, u32[]{:S(2)}, u32[]{:S(2)}) %collective-permute-start.42) | collective-permute-done | bytes 135200 | tf_op jit(solution)/shard_map/ppermute | solution.py:309
  184.0 3.1 %gather_parts.1 = (f32[512,1024]{1,0:T(8,128)}, f32[128,4096]{1,0:T(8,128)}) custom-call(s32[2]{0:T(128)S(1)} %pad_add_fusion.at_ref.refs_0_, bf16[128,1024]{1,0:T(8,128)(2,1)S(1)} %fusion.refs_0_, bf16[128,1024]{1,0:T(8,128)(2,1)S(1)} %collective-permute-done.40.refs_1_, bf16[128,1024]{1,0:T(8,128)(2,1)S(1)} %collective-permute-done.41.refs_2_, ...), custom_call_target="tpu_custom_call" | custom-call | flops 600000000 | tf_op jit(solution)/shard_map/gather_parts/pallas_call | solution.py:1478
  192.4 2.6 %last.1 = (f32[128,1024]{1,0:T(8,128)}, f32[128,1024]{1,0:T(8,128)}, f32[128,1024]{1,0:T(8,128)}, f32[128,1024]{1,0:T(8,128)}, f32[16,1024]{1,0:T(8,128)}, /*ind...) custom-call(s32[2]{0:T(128)S(1)} %pad_add_fusion.at_ref.refs_0_, ...), custom_call_target="tpu_custom_call" | custom-call | flops 600000000 | tf_op jit(solution)/shard_map/last/pallas_call | solution.py:1528
  (148 shorter events, 49.3 us)
Async XLA Ops:
  0.6 9.6 %collective-permute-start = (bf16[128,1024]{1,0:T(8,128)(2,1)}, bf16[128,1024]{1,0:T(8,128)(2,1)S(1)}, u32[]{:S(2)}, u32[]{:S(2)}) collective-permute-start(bf16[128,1024]{1,0:T(8,128)(2,1)} %bitcast.41), channel_id=1, source_target_pairs={{0,16},{8,24},{16,0},{24,8},{1,17},{9,25},{17,1},{25,9},{2,18},{10... | collective-permute-start | bytes 786440 | tf_op jit(solution)/shard_map/ppermute | solution.py:309
  5.2 8.2 %collective-permute-start.1 = (bf16[128,1024]{1,0:T(8,128)(2,1)}, bf16[128,1024]{1,0:T(8,128)(2,1)S(1)}, u32[]{:S(2)}, u32[]{:S(2)}) collective-permute-start(bf16[128,1024]{1,0:T(8,128)(2,1)} %bitcast.42), channel_id=1, source_target_pairs={{0,8},{8,0},{16,24},{24,16},{1,9},{9,1},{17,25},{25,17},{2,10},{10... | collective-permute-start | bytes 786440 | tf_op jit(solution)/shard_map/ppermute | solution.py:309
  50.9 15.8 %collective-permute-start.9 = (bf16[2,128,1024]{2,1,0:T(8,128)(2,1)S(1)}, bf16[2,128,1024]{2,1,0:T(8,128)(2,1)S(1)}, u32[]{:S(2)}, u32[]{:S(2)}) collective-permute-start(bf16[2,128,1024]{2,1,0:T(8,128)(2,1)S(1)} %get-tuple-element.125), channel_id=1, source_target_pairs={{0,16},{8,24},{16,0},{24,8},{1,17},{9,25},{17,1},{25,9},{2,18},{10... | collective-permute-start | bytes 1572872 | tf_op jit(solution)/shard_map/ppermute | solution.py:309
  56.7 18.6 %collective-permute-start.12 = (bf16[128,1024]{1,0:T(8,128)(2,1)S(1)}, bf16[128,1024]{1,0:T(8,128)(2,1)S(1)}, u32[]{:S(2)}, u32[]{:S(2)}) collective-permute-start(bf16[128,1024]{1,0:T(8,128)(2,1)S(1)} %get-tuple-element.118.ffn_ref.refs_8_), channel_id=1, source_target_pairs={{0,16},{8,24},{16,0},{24,8},{1,17},{9,25},{17,1},{25,9},{2,18},{10... | collective-permute-start | bytes 786440 | tf_op jit(solution)/shard_map/ppermute | solution.py:309
  66.6 10.5 %collective-permute-start.11 = (bf16[2,128,1024]{2,1,0:T(8,128)(2,1)S(1)}, bf16[2,128,1024]{2,1,0:T(8,128)(2,1)S(1)}, u32[]{:S(2)}, u32[]{:S(2)}) collective-permute-start(bf16[2,128,1024]{2,1,0:T(8,128)(2,1)S(1)} %collective-permute-done.9.refs_2_.refs_3_), channel_id=1, source_target_pairs={{0,8},{8,0},{16,24},{24,16},{1,9},{9,1},{17,25},{25,17},{2,10},{10... | collective-permute-start | bytes 1572872 | tf_op jit(solution)/shard_map/ppermute | solution.py:309
  73.5 20.3 %collective-permute-start.18 = (bf16[3,128,1024]{2,1,0:T(8,128)(2,1)S(1)}, bf16[3,128,1024]{2,1,0:T(8,128)(2,1)S(1)}, u32[]{:S(2)}, u32[]{:S(2)}) collective-permute-start(bf16[3,128,1024]{2,1,0:T(8,128)(2,1)S(1)} %get-tuple-element.141), channel_id=1, source_target_pairs={{0,16},{8,24},{16,0},{24,8},{1,17},{9,25},{17,1},{25,9},{2,18},{10... | collective-permute-start | bytes 2359304 | tf_op jit(solution)/shard_map/ppermute | solution.py:309
  80.7 25.6 %collective-permute-start.21 = (bf16[4,128,1024]{2,1,0:T(8,128)(2,1)S(1)}, bf16[4,128,1024]{2,1,0:T(8,128)(2,1)S(1)}, u32[]{:S(2)}, u32[]{:S(2)}) collective-permute-start(bf16[4,128,1024]{2,1,0:T(8,128)(2,1)S(1)} %get-tuple-element.146), channel_id=1, source_target_pairs={{0,1},{1,0},{2,3},{3,2},{4,5},{5,4},{6,7},{7,6},{8,9},{9,8},{10,11... | collective-permute-start | bytes 3145736 | tf_op jit(solution)/shard_map/ppermute | solution.py:309
  94.4 11.1 %collective-permute-start.22 = (bf16[128,1536]{1,0:T(8,128)(2,1)S(1)}, bf16[128,1536]{1,0:T(8,128)(2,1)S(1)}, u32[]{:S(2)}, u32[]{:S(2)}) collective-permute-start(bf16[128,1536]{1,0:T(8,128)(2,1)S(1)} %get-tuple-element.150.refs_15_.refs_16_), channel_id=1, source_target_pairs={{0,16},{8,24},{16,0},{24,8},{1,17},{9,25},{17,1},{25,9},{2,18},{10... | collective-permute-start | bytes 1179656 | tf_op jit(solution)/shard_map/ppermute | solution.py:309
  105.6 25.6 %collective-permute-start.26 = (bf16[4,128,1024]{2,1,0:T(8,128)(2,1)S(1)}, bf16[4,128,1024]{2,1,0:T(8,128)(2,1)S(1)}, u32[]{:S(2)}, u32[]{:S(2)}) collective-permute-start(bf16[4,128,1024]{2,1,0:T(8,128)(2,1)S(1)} %get-tuple-element.156), channel_id=1, source_target_pairs={{0,1},{1,0},{2,3},{3,2},{4,5},{5,4},{6,7},{7,6},{8,9},{9,8},{10,11... | collective-permute-start | bytes 3145736 | tf_op jit(solution)/shard_map/ppermute | solution.py:309
  106.7 23.0 %collective-permute-start.27 = (bf16[2,128,1024]{2,1,0:T(8,128)(2,1)S(1)}, bf16[2,128,1024]{2,1,0:T(8,128)(2,1)S(1)}, u32[]{:S(2)}, u32[]{:S(2)}) collective-permute-start(bf16[2,128,1024]{2,1,0:T(8,128)(2,1)S(1)} %get-tuple-element.203), channel_id=1, source_target_pairs={{0,2},{1,3},{2,0},{3,1},{4,6},{5,7},{6,4},{7,5},{8,10},{9,11},{10,... | collective-permute-start | bytes 1572872 | tf_op jit(solution)/shard_map/ppermute | solution.py:309
  114.1 28.4 %collective-permute-start.25 = (bf16[4,128,640]{2,1,0:T(8,128)(2,1)S(1)}, bf16[4,128,640]{2,1,0:T(8,128)(2,1)S(1)}, u32[]{:S(2)}, u32[]{:S(2)}) collective-permute-start(bf16[4,128,640]{2,1,0:T(8,128)(2,1)S(1)} %get-tuple-element.155), channel_id=1, source_target_pairs={{0,2},{1,3},{2,0},{3,1},{4,6},{5,7},{6,4},{7,5},{8,10},{9,11},{10,... | collective-permute-start | bytes 1966088 | tf_op jit(solution)/shard_map/ppermute | solution.py:309
  128.4 11.0 %collective-permute-start.28 = (bf16[2,128,768]{2,1,0:T(8,128)(2,1)S(1)}, bf16[2,128,768]{2,1,0:T(8,128)(2,1)S(1)}, u32[]{:S(2)}, u32[]{:S(2)}) collective-permute-start(bf16[2,128,768]{2,1,0:T(8,128)(2,1)S(1)} %get-tuple-element.169), channel_id=1, source_target_pairs={{0,16},{8,24},{16,0},{24,8},{1,17},{9,25},{17,1},{25,9},{2,18},{10... | collective-permute-start | bytes 1179656 | tf_op jit(solution)/shard_map/ppermute | solution.py:309
  131.5 19.5 %collective-permute-start.34 = (bf16[2,128,1024]{2,1,0:T(8,128)(2,1)S(1)}, bf16[2,128,1024]{2,1,0:T(8,128)(2,1)S(1)}, u32[]{:S(2)}, u32[]{:S(2)}) collective-permute-start(bf16[2,128,1024]{2,1,0:T(8,128)(2,1)S(1)} %get-tuple-element.201), channel_id=1, source_target_pairs={{0,2},{1,3},{2,0},{3,1},{4,6},{5,7},{6,4},{7,5},{8,10},{9,11},{10,... | collective-permute-start | bytes 1572872 | tf_op jit(solution)/shard_map/ppermute | solution.py:309
  139.9 20.3 %collective-permute-start.32 = (bf16[1,128,1024]{2,1,0:T(8,128)(2,1)S(1)}, bf16[1,128,1024]{2,1,0:T(8,128)(2,1)S(1)}, u32[]{:S(2)}, u32[]{:S(2)}) collective-permute-start(bf16[1,128,1024]{2,1,0:T(8,128)(2,1)S(1)} %add_convert_fusion.13), channel_id=1, source_target_pairs={{0,4},{1,5},{2,6},{3,7},{4,0},{5,1},{6,2},{7,3},{8,12},{9,13},{10,... | collective-permute-start | bytes 786440 | tf_op jit(solution)/shard_map/ppermute | solution.py:309
  142.5 15.2 %collective-permute-start.33 = (bf16[4,176,384]{2,1,0:T(8,128)(2,1)S(1)}, bf16[4,176,384]{2,1,0:T(8,128)(2,1)S(1)}, u32[]{:S(2)}, u32[]{:S(2)}) collective-permute-start(bf16[4,176,384]{2,1,0:T(8,128)(2,1)S(1)} %get-tuple-element.173), channel_id=1, source_target_pairs={{0,1},{1,0},{2,3},{3,2},{4,5},{5,4},{6,7},{7,6},{8,9},{9,8},{10,11... | collective-permute-start | bytes 1622024 | tf_op jit(solution)/shard_map/ppermute | solution.py:309
  144.2 19.2 %collective-permute-start.31 = (bf16[2,128,640]{2,1,0:T(8,128)(2,1)S(1)}, bf16[2,128,640]{2,1,0:T(8,128)(2,1)S(1)}, u32[]{:S(2)}, u32[]{:S(2)}) collective-permute-start(bf16[2,128,640]{2,1,0:T(8,128)(2,1)S(1)} %get-tuple-element.205), channel_id=1, source_target_pairs={{0,1},{1,0},{2,3},{3,2},{4,5},{5,4},{6,7},{7,6},{8,9},{9,8},{10,11... | collective-permute-start | bytes 983048 | tf_op jit(solution)/shard_map/ppermute | solution.py:309
  151.1 15.0 %collective-permute-start.37 = (bf16[1,128,1024]{2,1,0:T(8,128)(2,1)S(1)}, bf16[1,128,1024]{2,1,0:T(8,128)(2,1)S(1)}, u32[]{:S(2)}, u32[]{:S(2)}) collective-permute-start(bf16[1,128,1024]{2,1,0:T(8,128)(2,1)S(1)} %add_convert_fusion.11), channel_id=1, source_target_pairs={{0,4},{1,5},{2,6},{3,7},{4,0},{5,1},{6,2},{7,3},{8,12},{9,13},{10,... | collective-permute-start | bytes 786440 | tf_op jit(solution)/shard_map/ppermute | solution.py:309
  157.8 15.6 %collective-permute-start.36 = (bf16[2,176,384]{2,1,0:T(8,128)(2,1)S(1)}, bf16[2,176,384]{2,1,0:T(8,128)(2,1)S(1)}, u32[]{:S(2)}, u32[]{:S(2)}) collective-permute-start(bf16[2,176,384]{2,1,0:T(8,128)(2,1)S(1)} %get-tuple-element.207), channel_id=1, source_target_pairs={{0,2},{1,3},{2,0},{3,1},{4,6},{5,7},{6,4},{7,5},{8,10},{9,11},{10,... | collective-permute-start | bytes 811016 | tf_op jit(solution)/shard_map/ppermute | solution.py:309
  160.3 23.3 %collective-permute-start.40 = (bf16[128,1024]{1,0:T(8,128)(2,1)S(1)}, bf16[128,1024]{1,0:T(8,128)(2,1)S(1)}, u32[]{:S(2)}, u32[]{:S(2)}) collective-permute-start(bf16[128,1024]{1,0:T(8,128)(2,1)S(1)} %fusion.refs_0_), channel_id=1, source_target_pairs={{0,8},{8,0},{16,24},{24,16},{1,9},{9,1},{17,25},{25,17},{2,10},{10... | collective-permute-start | bytes 786440 | tf_op jit(solution)/shard_map/ppermute | solution.py:309
  160.4 21.0 %collective-permute-start.41 = (bf16[128,1024]{1,0:T(8,128)(2,1)S(1)}, bf16[128,1024]{1,0:T(8,128)(2,1)S(1)}, u32[]{:S(2)}, u32[]{:S(2)}) collective-permute-start(bf16[128,1024]{1,0:T(8,128)(2,1)S(1)} %fusion.refs_0_), channel_id=1, source_target_pairs={{0,16},{8,24},{16,0},{24,8},{1,17},{9,25},{17,1},{25,9},{2,18},{10... | collective-permute-start | bytes 786440 | tf_op jit(solution)/shard_map/ppermute | solution.py:309
  163.5 11.3 %collective-permute-start.35 = (bf16[1,128,640]{2,1,0:T(8,128)(2,1)S(1)}, bf16[1,128,640]{2,1,0:T(8,128)(2,1)S(1)}, u32[]{:S(2)}, u32[]{:S(2)}) collective-permute-start(bf16[1,128,640]{2,1,0:T(8,128)(2,1)S(1)} %add_convert_fusion.15), channel_id=1, source_target_pairs={{0,4},{1,5},{2,6},{3,7},{4,0},{5,1},{6,2},{7,3},{8,12},{9,13},{10,... | collective-permute-start | bytes 491528 | tf_op jit(solution)/shard_map/ppermute | solution.py:309
  166.2 17.8 %collective-permute-start.44 = (bf16[128,1024]{1,0:T(8,128)(2,1)S(1)}, bf16[128,1024]{1,0:T(8,128)(2,1)S(1)}, u32[]{:S(2)}, u32[]{:S(2)}) collective-permute-start(bf16[128,1024]{1,0:T(8,128)(2,1)S(1)} %fusion.1.refs_4_), channel_id=1, source_target_pairs={{0,8},{8,0},{16,24},{24,16},{1,9},{9,1},{17,25},{25,17},{2,10},{10... | collective-permute-start | bytes 786440 | tf_op jit(solution)/shard_map/ppermute | solution.py:309
  173.4 8.0 %collective-permute-start.45 = (bf16[128,1024]{1,0:T(8,128)(2,1)S(1)}, bf16[128,1024]{1,0:T(8,128)(2,1)S(1)}, u32[]{:S(2)}, u32[]{:S(2)}) collective-permute-start(bf16[128,1024]{1,0:T(8,128)(2,1)S(1)} %fusion.1.refs_4_), channel_id=1, source_target_pairs={{0,16},{8,24},{16,0},{24,8},{1,17},{9,25},{17,1},{25,9},{2,18},{10... | collective-permute-start | bytes 786440 | tf_op jit(solution)/shard_map/ppermute | solution.py:309
  183.6 7.4 %collective-permute-start.49 = (bf16[176,384]{1,0:T(8,128)(2,1)S(1)}, bf16[176,384]{1,0:T(8,128)(2,1)S(1)}, u32[]{:S(2)}, u32[]{:S(2)}) collective-permute-start(bf16[176,384]{1,0:T(8,128)(2,1)S(1)} %fusion.3.refs_4_), channel_id=1, source_target_pairs={{0,16},{8,24},{16,0},{24,8},{1,17},{9,25},{17,1},{25,9},{2,18},{10... | collective-permute-start | bytes 405512 | tf_op jit(solution)/shard_map/ppermute | solution.py:309
  (46 other events, 327.7 us)

commit v6 on v5

--- a/solution.py
+++ b/solution.py
@@ -1596,7 +1596,7 @@
     ints_far = swap(own_ints, "blk", 2)
     x_core, ints_core = swap(x_own, "blk", 1), swap(own_ints, "blk", 1)
     x_both, ints_both = swap(ordered(x_far, ints_far), "blk", 1), swap(ints_far, "blk", 1)
-    xs = tuple(map(in_hbm, (x_own, x_far, x_core, x_both)))
+    xs = (in_hbm(x_own), x_far, x_core, x_both)
     tables = jnp.concatenate([xbias_table.T, ybias_table.T], axis=1).astype(f32)
     tables = tables.reshape(blocks, heads // blocks, 2 * boxes)
     at = jnp.stack([place.astype(jnp.int32), lengths[0]])

time: 196 us -> 196 us (level)
  transfers between devices with their start and end apart: 51 -> 51, of which waited for: 20 -> 21; matrix products, arithmetic and copies ran while one was open for 2% -> 2% of each run, Pallas kernels for 33% -> 33%
where the time goes in v6:
time: 196 us; the launch traced here: 195 us
  Pallas kernels  95.5 us (49%)
  waiting for transfers between devices  57.3 us (29%)
  starting transfers between devices  34.5 us (18%)
  other arithmetic  4.04 us (2%)
    ppermute x51, waiting for transfers between devices, swap(): return lax.ppermute(array, axis, [(i, i ^ by) for i in range(count)])  57.3 us
    ppermute x51, starting transfers between devices, swap(): return lax.ppermute(array, axis, [(i, i ^ by) for i in range(count)])  34.5 us
    pallas_call x2, Pallas kernels, scores_grad_call(): pl.pallas_call(functools.partial(scores_grad_kernel, half, 0), out_shape=...  24.8 us
    pallas_call x1, Pallas kernels, scores_call(): pl.pallas_call(scores_kernel, out_shape=(jax.ShapeDtypeStruct((lanes, wid...  19.2 us
    pallas_call x4, Pallas kernels, weight_grads_call(): pl.pallas_call(kernel, out_shape=tuple(shapes), grid_spec=pltpu.PrefetchS...  16.6 us
    pallas_call x1, Pallas kernels, back_call(): pl.pallas_call(back_kernel, out_shape=(jax.ShapeDtypeStruct((rows, width)...  9.66 us
    pallas_call x1, Pallas kernels, up_call(): pl.pallas_call(up_kernel, out_shape=(jax.ShapeDtypeStruct((2, rows, quart...  9.35 us
    pallas_call x1, Pallas kernels, tokens_grad_call(): pl.pallas_call(tokens_grad_kernel, out_shape=jax.ShapeDtypeStruct((rows,...  6.23 us
  transfers between devices with their start and end apart: 51, of which 21 were waited for; matrix products, arithmetic and copies ran while one was open for 2% of the time, Pallas kernels for 33%

profile of v6, /device:TPU:0, one launch (start us, length us, event | category | flops | bytes accessed | tf_op | source)
XLA Modules:
  0.0 195.0 jit_solution(16259817822555486574)
XLA Ops:
  0.6 3.0 %collective-permute-start = (bf16[128,1024]{1,0:T(8,128)(2,1)}, bf16[128,1024]{1,0:T(8,128)(2,1)S(1)}, u32[]{:S(2)}, u32[]{:S(2)}) collective-permute-start(bf16[128,1024]{1,0:T(8,128)(2,1)} %bitcast.41), channel_id=1, source_target_pairs={{0,16},{8,24},{16,0},{24,8},{1,17},{9,25},{17,1},{25,9},{2,18},{10... | collective-permute-start | bytes 786440 | tf_op jit(solution)/shard_map/ppermute | solution.py:309
  5.2 5.1 %collective-permute-done.2.i1 = s32[8,128]{1,0:T(8,128)S(1)} collective-permute-done((s32[8,128]{1,0:T(8,128)S(1)}, s32[8,128]{1,0:T(8,128)S(1)}, u32[]{:S(2)}, u32[]{:S(2)}) %collective-permute-start.2) | collective-permute-done | bytes 4128 | tf_op jit(solution)/shard_map/ppermute | solution.py:309
  14.3 19.2 %scores.1 = (bf16[128,256]{1,0:T(8,128)(2,1)S(1)}, bf16[128,256]{1,0:T(8,128)(2,1)S(1)}, bf16[2,128,256]{2,1,0:T(8,128)(2,1)S(1)}, bf16[4,512,512]{2,1,0:T(8,128...) custom-call(s32[2]{0:T(128)S(1)} %pad_add_fusion.1.at_ref, ...), custom_call_target="tpu_custom_call" | custom-call | flops 7500000256 | tf_op jit(solution)/shard_map/scores/pallas_call | solution.py:743
  35.9 3.8 %collective-permute-done.6.a1 = bf16[2,128,256]{2,1,0:T(8,128)(2,1)S(1)} collective-permute-done((bf16[2,128,256]{2,1,0:T(8,128)(2,1)S(1)}, bf16[2,128,256]{2,1,0:T(8,128)(2,1)S(1)}, u32[]{:S(2)}, u32[]{:S(2)}) %collective-permute-start.6) | collective-permute-done | bytes 131104 | tf_op jit(solution)/shard_map/ppermute | solution.py:309
  41.4 9.4 %up.1 = (bf16[2,128,1024]{2,1,0:T(8,128)(2,1)S(1)}, bf16[128,1024]{1,0:T(8,128)(2,1)S(1)}, bf16[128,1024]{1,0:T(8,128)(2,1)S(1)}, bf16[128,4096]{1,0:T(8,128)(2,...) custom-call(s32[2]{0:T(128)S(1)} %pad_add_fusion.at_ref.refs_0_, ...), custom_call_target="tpu_custom_call" | custom-call | flops 2700000000 | tf_op jit(solution)/shard_map/up/pallas_call | solution.py:835
  52.6 4.0 %down.1 = (bf16[128,1024]{1,0:T(8,128)(2,1)}, f32[128,1024]{1,0:T(8,128)S(1)}, bf16[128,1024]{1,0:T(8,128)(2,1)S(1)}, f32[8,1024]{1,0:T(8,128)S(1)}) custom-call(bf16[128,4096]{1,0:T(8,128)(2,1)S(1)} %get-tuple-element.112.act_ref, bf16[4096,1024]{1,0:T(8,128)(2,1)S(1)} %copy-done.1, f32[128,1024]{1,0:T(8,128)S(1)} %get-tuple-element.113.normed_ref, ...), custom_call_target="tpu_custom_call" | custom-call | flops 2400000000 | tf_op jit(solution)/shard_map/down/pallas_call | solution.py:917
  57.0 9.7 %back.1 = (bf16[128,256]{1,0:T(8,128)(2,1)S(1)}, bf16[128,256]{1,0:T(8,128)(2,1)S(1)}, bf16[2,128,256]{2,1,0:T(8,128)(2,1)S(1)}, f32[128,1024]{1,0:T(8,128)S(1)}...) custom-call(s32[2]{0:T(128)S(1)} %pad_add_fusion.at_ref.refs_0_, ...), custom_call_target="tpu_custom_call" | custom-call | flops 3600000000 | tf_op jit(solution)/shard_map/back/pallas_call | solution.py:1002
  68.6 4.8 %collective-permute-done.15.refs_2_ = bf16[2,128,256]{2,1,0:T(8,128)(2,1)S(1)} collective-permute-done((bf16[2,128,256]{2,1,0:T(8,128)(2,1)S(1)}, bf16[2,128,256]{2,1,0:T(8,128)(2,1)S(1)}, u32[]{:S(2)}, u32[]{:S(2)}) %collective-permute-start.15) | collective-permute-done | bytes 131104 | tf_op jit(solution)/shard_map/ppermute | solution.py:309
  77.1 3.4 %grad_down.1 = (bf16[4,128,1024]{2,1,0:T(8,128)(2,1)S(1)}, bf16[4,128,1024]{2,1,0:T(8,128)(2,1)S(1)}) custom-call(s32[2]{0:T(128)S(1)} %pad_add_fusion.at_ref.refs_0_, bf16[128,1024]{1,0:T(8,128)(2,1)S(1)} %get-tuple-element.124.refs_0_.refs_1_, bf16[128,1024]{1,0:T(8,128)(2,1)S(1)} %get-tuple-element.124.refs_0_.refs_1_, ...), custom_call_target="tpu_custom_call" | custom-call | flops 3000000 | tf_op jit(solution)/shard_map/grad_down/pallas_call | solution.py:1388
  82.2 11.5 %scores_grad.2 = (bf16[640,384]{1,0:T(8,128)(2,1)S(1)}, f32[16,128]{1,0:T(8,128)S(1)}) custom-call(s32[2]{0:T(128)S(1)} %pad_add_fusion.at_ref.refs_0_, bf16[128,256]{1,0:T(8,128)(2,1)S(1)} %get-tuple-element.122.refs_1_, bf16[2,128,256]{2,1,0:T(8,128)(2,1)S(1)} %collective-permute-done.15.refs_2_, bf16[128,256]{1,0:T(8,128)(2,1)S(1)} %collective-permute-done.16.refs_3_, ...), custom_call_target="tpu_custom_call" | custom-call | flops 4499999744 | tf_op jit(solution)/shard_map/scores_grad/pallas_call | solution.py:1273
  96.9 3.6 %grad_in.1 = (bf16[4,128,1024]{2,1,0:T(8,128)(2,1)S(1)}, bf16[4,128,1024]{2,1,0:T(8,128)(2,1)S(1)}) custom-call(s32[2]{0:T(128)S(1)} %pad_add_fusion.at_ref.refs_0_, bf16[128,1024]{1,0:T(8,128)(2,1)S(1)} %get-tuple-element.121.hidden_ref.refs_0_.refs_1_, bf16[128,1024]{1,0:T(8,128)(2,1)S(1)} %get-tuple-element.121.hidden_ref.refs_0_.refs_1_, ...), custom_call_target="tpu_custom_call" | custom-call | flops 3000000 | tf_op jit(solution)/shard_map/grad_in/pallas_call | solution.py:1388
  100.5 4.9 %collective-permute-done.22.refs_17_.refs_18_.refs_24_ = bf16[128,1536]{1,0:T(8,128)(2,1)S(1)} collective-permute-done((bf16[128,1536]{1,0:T(8,128)(2,1)S(1)}, bf16[128,1536]{1,0:T(8,128)(2,1)S(1)}, u32[]{:S(2)}, u32[]{:S(2)}) %collective-permute-start.22) | collective-permute-done | bytes 393248 | tf_op jit(solution)/shard_map/ppermute | solution.py:309
  108.2 5.7 %grad_qkv_out.1 = (bf16[4,128,640]{2,1,0:T(8,128)(2,1)S(1)}, bf16[4,128,640]{2,1,0:T(8,128)(2,1)S(1)}) custom-call(s32[2]{0:T(128)S(1)} %pad_add_fusion.at_ref.refs_0_, bf16[128,1024]{1,0:T(8,128)(2,1)} %bitcast.44, bf16[128,1024]{1,0:T(8,128)(2,1)} %bitcast.45, bf16[128,1024]{1,0:T(8,128)(2,1)S(1)} %collective-permute-done.x1.refs_2_.refs_3_, ...), custom_call_target="tpu_custom_call" | custom-call | flops 3000000 | tf_op jit(solution)/shard_map/grad_qkv_out/pallas_call | solution.py:1388
  115.0 13.3 %scores_grad.3 = (bf16[640,384]{1,0:T(8,128)(2,1)S(1)}, bf16[128,768]{1,0:T(8,128)(2,1)S(1)}, bf16[128,768]{1,0:T(8,128)(2,1)S(1)}, bf16[2,128,768]{2,1,0:T(8,128)(2,1)S(1)}, f32[8,48,384]{2,1,0:T(8,128)S(1)}) custom-call(s32[2]{0:T(128)S(1)} %pad_add_fusion.at_ref.refs_0_, bf16[128,256]{1,0:T(8,128)(2,1)S(1)} %get-tuple-element.122.refs_1_, ...), custom_call_target="tpu_custom_call" | custom-call | flops 4499999744 | tf_op jit(solution)/shard_map/scores_grad/pallas_call | solution.py:1273
  133.1 3.8 %grad_qkv.1 = (bf16[4,176,384]{2,1,0:T(8,128)(2,1)S(1)}, bf16[4,176,384]{2,1,0:T(8,128)(2,1)S(1)}) custom-call(s32[2]{0:T(128)S(1)} %pad_add_fusion.at_ref.refs_0_, bf16[128,1024]{1,0:T(8,128)(2,1)} %bitcast.46, bf16[128,1024]{1,0:T(8,128)(2,1)} %bitcast.47, bf16[128,1024]{1,0:T(8,128)(2,1)S(1)} %collective-permute-done.x1.refs_2_.refs_3_, ...), custom_call_target="tpu_custom_call" | custom-call | flops 3000000 | tf_op jit(solution)/shard_map/grad_qkv/pallas_call | solution.py:1388
  136.9 2.3 %collective-permute-done.28.d1 = bf16[2,128,768]{2,1,0:T(8,128)(2,1)S(1)} collective-permute-done((bf16[2,128,768]{2,1,0:T(8,128)(2,1)S(1)}, bf16[2,128,768]{2,1,0:T(8,128)(2,1)S(1)}, u32[]{:S(2)}, u32[]{:S(2)}) %collective-permute-start.28) | collective-permute-done | bytes 393248 | tf_op jit(solution)/shard_map/ppermute | solution.py:309
  139.7 2.6 %collective-permute-start.32 = (bf16[1,128,1024]{2,1,0:T(8,128)(2,1)S(1)}, bf16[1,128,1024]{2,1,0:T(8,128)(2,1)S(1)}, u32[]{:S(2)}, u32[]{:S(2)}) collective-permute-start(bf16[1,128,1024]{2,1,0:T(8,128)(2,1)S(1)} %add_convert_fusion.13), channel_id=1, source_target_pairs={{0,4},{1,5},{2,6},{3,7},{4,0},{5,1},{6,2},{7,3},{8,12},{9,13},{10,... | collective-permute-start | bytes 786440 | tf_op jit(solution)/shard_map/ppermute | solution.py:309
  144.6 6.2 %tokens_grad.1 = f32[128,1024]{1,0:T(8,128)} custom-call(s32[2]{0:T(128)S(1)} %pad_add_fusion.at_ref.refs_0_, bf16[128,768]{1,0:T(8,128)(2,1)S(1)} %get-tuple-element.168.d0, bf16[2,128,768]{2,1,0:T(8,128)(2,1)S(1)} %collective-permute-done.28.d1, bf16[128,768]{1,0:T(8,128)(2,1)S(1)} %collective-permute-done.29.d2, ...), custom_call_target="tpu_custom_call" | custom-call | flops 1200000000 | tf_op jit(solution)/shard_map/tokens_grad/pallas_call | solution.py:1437
  151.7 5.8 %collective-permute-done.33 = bf16[4,176,384]{2,1,0:T(8,128)(2,1)S(1)} collective-permute-done((bf16[4,176,384]{2,1,0:T(8,128)(2,1)S(1)}, bf16[4,176,384]{2,1,0:T(8,128)(2,1)S(1)}, u32[]{:S(2)}, u32[]{:S(2)}) %collective-permute-start.33) | collective-permute-done | bytes 540704 | tf_op jit(solution)/shard_map/ppermute | solution.py:309
  163.7 2.2 %collective-permute-done.37 = bf16[1,128,1024]{2,1,0:T(8,128)(2,1)S(1)} collective-permute-done((bf16[1,128,1024]{2,1,0:T(8,128)(2,1)S(1)}, bf16[1,128,1024]{2,1,0:T(8,128)(2,1)S(1)}, u32[]{:S(2)}, u32[]{:S(2)}) %collective-permute-start.37) | collective-permute-done | bytes 262176 | tf_op jit(solution)/shard_map/ppermute | solution.py:309
  166.1 7.2 %collective-permute-done.36 = bf16[2,176,384]{2,1,0:T(8,128)(2,1)S(1)} collective-permute-done((bf16[2,176,384]{2,1,0:T(8,128)(2,1)S(1)}, bf16[2,176,384]{2,1,0:T(8,128)(2,1)S(1)}, u32[]{:S(2)}, u32[]{:S(2)}) %collective-permute-start.36) | collective-permute-done | bytes 270368 | tf_op jit(solution)/shard_map/ppermute | solution.py:309
  174.7 6.4 %collective-permute-done.42 = bf16[1,176,384]{2,1,0:T(8,128)(2,1)S(1)} collective-permute-done((bf16[1,176,384]{2,1,0:T(8,128)(2,1)S(1)}, bf16[1,176,384]{2,1,0:T(8,128)(2,1)S(1)}, u32[]{:S(2)}, u32[]{:S(2)}) %collective-permute-start.42) | collective-permute-done | bytes 135200 | tf_op jit(solution)/shard_map/ppermute | solution.py:309
  183.8 3.1 %gather_parts.1 = (f32[512,1024]{1,0:T(8,128)}, f32[128,4096]{1,0:T(8,128)}) custom-call(s32[2]{0:T(128)S(1)} %pad_add_fusion.at_ref.refs_0_, bf16[128,1024]{1,0:T(8,128)(2,1)S(1)} %fusion.refs_0_, bf16[128,1024]{1,0:T(8,128)(2,1)S(1)} %collective-permute-done.40.refs_1_, bf16[128,1024]{1,0:T(8,128)(2,1)S(1)} %collective-permute-done.41.refs_2_, ...), custom_call_target="tpu_custom_call" | custom-call | flops 600000000 | tf_op jit(solution)/shard_map/gather_parts/pallas_call | solution.py:1478
  192.2 2.6 %last.1 = (f32[128,1024]{1,0:T(8,128)}, f32[128,1024]{1,0:T(8,128)}, f32[128,1024]{1,0:T(8,128)}, f32[128,1024]{1,0:T(8,128)}, f32[16,1024]{1,0:T(8,128)}, /*ind...) custom-call(s32[2]{0:T(128)S(1)} %pad_add_fusion.at_ref.refs_0_, ...), custom_call_target="tpu_custom_call" | custom-call | flops 600000000 | tf_op jit(solution)/shard_map/last/pallas_call | solution.py:1528
  (146 shorter events, 49.5 us)
Async XLA Ops:
  0.6 9.6 %collective-permute-start = (bf16[128,1024]{1,0:T(8,128)(2,1)}, bf16[128,1024]{1,0:T(8,128)(2,1)S(1)}, u32[]{:S(2)}, u32[]{:S(2)}) collective-permute-start(bf16[128,1024]{1,0:T(8,128)(2,1)} %bitcast.41), channel_id=1, source_target_pairs={{0,16},{8,24},{16,0},{24,8},{1,17},{9,25},{17,1},{25,9},{2,18},{10... | collective-permute-start | bytes 786440 | tf_op jit(solution)/shard_map/ppermute | solution.py:309
  5.2 8.2 %collective-permute-start.1 = (bf16[128,1024]{1,0:T(8,128)(2,1)}, bf16[128,1024]{1,0:T(8,128)(2,1)S(1)}, u32[]{:S(2)}, u32[]{:S(2)}) collective-permute-start(bf16[128,1024]{1,0:T(8,128)(2,1)} %bitcast.42), channel_id=1, source_target_pairs={{0,8},{8,0},{16,24},{24,16},{1,9},{9,1},{17,25},{25,17},{2,10},{10... | collective-permute-start | bytes 786440 | tf_op jit(solution)/shard_map/ppermute | solution.py:309
  50.8 15.9 %collective-permute-start.9 = (bf16[2,128,1024]{2,1,0:T(8,128)(2,1)S(1)}, bf16[2,128,1024]{2,1,0:T(8,128)(2,1)S(1)}, u32[]{:S(2)}, u32[]{:S(2)}) collective-permute-start(bf16[2,128,1024]{2,1,0:T(8,128)(2,1)S(1)} %get-tuple-element.125), channel_id=1, source_target_pairs={{0,16},{8,24},{16,0},{24,8},{1,17},{9,25},{17,1},{25,9},{2,18},{10... | collective-permute-start | bytes 1572872 | tf_op jit(solution)/shard_map/ppermute | solution.py:309
  56.6 18.6 %collective-permute-start.12 = (bf16[128,1024]{1,0:T(8,128)(2,1)S(1)}, bf16[128,1024]{1,0:T(8,128)(2,1)S(1)}, u32[]{:S(2)}, u32[]{:S(2)}) collective-permute-start(bf16[128,1024]{1,0:T(8,128)(2,1)S(1)} %get-tuple-element.118.ffn_ref.refs_8_), channel_id=1, source_target_pairs={{0,16},{8,24},{16,0},{24,8},{1,17},{9,25},{17,1},{25,9},{2,18},{10... | collective-permute-start | bytes 786440 | tf_op jit(solution)/shard_map/ppermute | solution.py:309
  66.6 10.4 %collective-permute-start.11 = (bf16[2,128,1024]{2,1,0:T(8,128)(2,1)S(1)}, bf16[2,128,1024]{2,1,0:T(8,128)(2,1)S(1)}, u32[]{:S(2)}, u32[]{:S(2)}) collective-permute-start(bf16[2,128,1024]{2,1,0:T(8,128)(2,1)S(1)} %collective-permute-done.9.refs_2_.refs_3_), channel_id=1, source_target_pairs={{0,8},{8,0},{16,24},{24,16},{1,9},{9,1},{17,25},{25,17},{2,10},{10... | collective-permute-start | bytes 1572872 | tf_op jit(solution)/shard_map/ppermute | solution.py:309
  73.5 20.3 %collective-permute-start.18 = (bf16[3,128,1024]{2,1,0:T(8,128)(2,1)S(1)}, bf16[3,128,1024]{2,1,0:T(8,128)(2,1)S(1)}, u32[]{:S(2)}, u32[]{:S(2)}) collective-permute-start(bf16[3,128,1024]{2,1,0:T(8,128)(2,1)S(1)} %get-tuple-element.141), channel_id=1, source_target_pairs={{0,16},{8,24},{16,0},{24,8},{1,17},{9,25},{17,1},{25,9},{2,18},{10... | collective-permute-start | bytes 2359304 | tf_op jit(solution)/shard_map/ppermute | solution.py:309
  80.6 25.6 %collective-permute-start.21 = (bf16[4,128,1024]{2,1,0:T(8,128)(2,1)S(1)}, bf16[4,128,1024]{2,1,0:T(8,128)(2,1)S(1)}, u32[]{:S(2)}, u32[]{:S(2)}) collective-permute-start(bf16[4,128,1024]{2,1,0:T(8,128)(2,1)S(1)} %get-tuple-element.146), channel_id=1, source_target_pairs={{0,1},{1,0},{2,3},{3,2},{4,5},{5,4},{6,7},{7,6},{8,9},{9,8},{10,11... | collective-permute-start | bytes 3145736 | tf_op jit(solution)/shard_map/ppermute | solution.py:309
  94.4 11.1 %collective-permute-start.22 = (bf16[128,1536]{1,0:T(8,128)(2,1)S(1)}, bf16[128,1536]{1,0:T(8,128)(2,1)S(1)}, u32[]{:S(2)}, u32[]{:S(2)}) collective-permute-start(bf16[128,1536]{1,0:T(8,128)(2,1)S(1)} %get-tuple-element.150.refs_15_.refs_16_), channel_id=1, source_target_pairs={{0,16},{8,24},{16,0},{24,8},{1,17},{9,25},{17,1},{25,9},{2,18},{10... | collective-permute-start | bytes 1179656 | tf_op jit(solution)/shard_map/ppermute | solution.py:309
  105.5 25.6 %collective-permute-start.26 = (bf16[4,128,1024]{2,1,0:T(8,128)(2,1)S(1)}, bf16[4,128,1024]{2,1,0:T(8,128)(2,1)S(1)}, u32[]{:S(2)}, u32[]{:S(2)}) collective-permute-start(bf16[4,128,1024]{2,1,0:T(8,128)(2,1)S(1)} %get-tuple-element.156), channel_id=1, source_target_pairs={{0,1},{1,0},{2,3},{3,2},{4,5},{5,4},{6,7},{7,6},{8,9},{9,8},{10,11... | collective-permute-start | bytes 3145736 | tf_op jit(solution)/shard_map/ppermute | solution.py:309
  106.6 22.9 %collective-permute-start.27 = (bf16[2,128,1024]{2,1,0:T(8,128)(2,1)S(1)}, bf16[2,128,1024]{2,1,0:T(8,128)(2,1)S(1)}, u32[]{:S(2)}, u32[]{:S(2)}) collective-permute-start(bf16[2,128,1024]{2,1,0:T(8,128)(2,1)S(1)} %get-tuple-element.203), channel_id=1, source_target_pairs={{0,2},{1,3},{2,0},{3,1},{4,6},{5,7},{6,4},{7,5},{8,10},{9,11},{10,... | collective-permute-start | bytes 1572872 | tf_op jit(solution)/shard_map/ppermute | solution.py:309
  113.9 28.4 %collective-permute-start.25 = (bf16[4,128,640]{2,1,0:T(8,128)(2,1)S(1)}, bf16[4,128,640]{2,1,0:T(8,128)(2,1)S(1)}, u32[]{:S(2)}, u32[]{:S(2)}) collective-permute-start(bf16[4,128,640]{2,1,0:T(8,128)(2,1)S(1)} %get-tuple-element.155), channel_id=1, source_target_pairs={{0,2},{1,3},{2,0},{3,1},{4,6},{5,7},{6,4},{7,5},{8,10},{9,11},{10,... | collective-permute-start | bytes 1966088 | tf_op jit(solution)/shard_map/ppermute | solution.py:309
  128.2 11.0 %collective-permute-start.28 = (bf16[2,128,768]{2,1,0:T(8,128)(2,1)S(1)}, bf16[2,128,768]{2,1,0:T(8,128)(2,1)S(1)}, u32[]{:S(2)}, u32[]{:S(2)}) collective-permute-start(bf16[2,128,768]{2,1,0:T(8,128)(2,1)S(1)} %get-tuple-element.169), channel_id=1, source_target_pairs={{0,16},{8,24},{16,0},{24,8},{1,17},{9,25},{17,1},{25,9},{2,18},{10... | collective-permute-start | bytes 1179656 | tf_op jit(solution)/shard_map/ppermute | solution.py:309
  131.4 19.5 %collective-permute-start.34 = (bf16[2,128,1024]{2,1,0:T(8,128)(2,1)S(1)}, bf16[2,128,1024]{2,1,0:T(8,128)(2,1)S(1)}, u32[]{:S(2)}, u32[]{:S(2)}) collective-permute-start(bf16[2,128,1024]{2,1,0:T(8,128)(2,1)S(1)} %get-tuple-element.201), channel_id=1, source_target_pairs={{0,2},{1,3},{2,0},{3,1},{4,6},{5,7},{6,4},{7,5},{8,10},{9,11},{10,... | collective-permute-start | bytes 1572872 | tf_op jit(solution)/shard_map/ppermute | solution.py:309
  139.7 20.0 %collective-permute-start.32 = (bf16[1,128,1024]{2,1,0:T(8,128)(2,1)S(1)}, bf16[1,128,1024]{2,1,0:T(8,128)(2,1)S(1)}, u32[]{:S(2)}, u32[]{:S(2)}) collective-permute-start(bf16[1,128,1024]{2,1,0:T(8,128)(2,1)S(1)} %add_convert_fusion.13), channel_id=1, source_target_pairs={{0,4},{1,5},{2,6},{3,7},{4,0},{5,1},{6,2},{7,3},{8,12},{9,13},{10,... | collective-permute-start | bytes 786440 | tf_op jit(solution)/shard_map/ppermute | solution.py:309
  142.3 15.2 %collective-permute-start.33 = (bf16[4,176,384]{2,1,0:T(8,128)(2,1)S(1)}, bf16[4,176,384]{2,1,0:T(8,128)(2,1)S(1)}, u32[]{:S(2)}, u32[]{:S(2)}) collective-permute-start(bf16[4,176,384]{2,1,0:T(8,128)(2,1)S(1)} %get-tuple-element.173), channel_id=1, source_target_pairs={{0,1},{1,0},{2,3},{3,2},{4,5},{5,4},{6,7},{7,6},{8,9},{9,8},{10,11... | collective-permute-start | bytes 1622024 | tf_op jit(solution)/shard_map/ppermute | solution.py:309
  144.0 19.2 %collective-permute-start.31 = (bf16[2,128,640]{2,1,0:T(8,128)(2,1)S(1)}, bf16[2,128,640]{2,1,0:T(8,128)(2,1)S(1)}, u32[]{:S(2)}, u32[]{:S(2)}) collective-permute-start(bf16[2,128,640]{2,1,0:T(8,128)(2,1)S(1)} %get-tuple-element.205), channel_id=1, source_target_pairs={{0,1},{1,0},{2,3},{3,2},{4,5},{5,4},{6,7},{7,6},{8,9},{9,8},{10,11... | collective-permute-start | bytes 983048 | tf_op jit(solution)/shard_map/ppermute | solution.py:309
  151.0 14.9 %collective-permute-start.37 = (bf16[1,128,1024]{2,1,0:T(8,128)(2,1)S(1)}, bf16[1,128,1024]{2,1,0:T(8,128)(2,1)S(1)}, u32[]{:S(2)}, u32[]{:S(2)}) collective-permute-start(bf16[1,128,1024]{2,1,0:T(8,128)(2,1)S(1)} %add_convert_fusion.11), channel_id=1, source_target_pairs={{0,4},{1,5},{2,6},{3,7},{4,0},{5,1},{6,2},{7,3},{8,12},{9,13},{10,... | collective-permute-start | bytes 786440 | tf_op jit(solution)/shard_map/ppermute | solution.py:309
  157.7 15.6 %collective-permute-start.36 = (bf16[2,176,384]{2,1,0:T(8,128)(2,1)S(1)}, bf16[2,176,384]{2,1,0:T(8,128)(2,1)S(1)}, u32[]{:S(2)}, u32[]{:S(2)}) collective-permute-start(bf16[2,176,384]{2,1,0:T(8,128)(2,1)S(1)} %get-tuple-element.207), channel_id=1, source_target_pairs={{0,2},{1,3},{2,0},{3,1},{4,6},{5,7},{6,4},{7,5},{8,10},{9,11},{10,... | collective-permute-start | bytes 811016 | tf_op jit(solution)/shard_map/ppermute | solution.py:309
  159.8 23.6 %collective-permute-start.40 = (bf16[128,1024]{1,0:T(8,128)(2,1)S(1)}, bf16[128,1024]{1,0:T(8,128)(2,1)S(1)}, u32[]{:S(2)}, u32[]{:S(2)}) collective-permute-start(bf16[128,1024]{1,0:T(8,128)(2,1)S(1)} %fusion.refs_0_), channel_id=1, source_target_pairs={{0,8},{8,0},{16,24},{24,16},{1,9},{9,1},{17,25},{25,17},{2,10},{10... | collective-permute-start | bytes 786440 | tf_op jit(solution)/shard_map/ppermute | solution.py:309
  159.9 21.2 %collective-permute-start.41 = (bf16[128,1024]{1,0:T(8,128)(2,1)S(1)}, bf16[128,1024]{1,0:T(8,128)(2,1)S(1)}, u32[]{:S(2)}, u32[]{:S(2)}) collective-permute-start(bf16[128,1024]{1,0:T(8,128)(2,1)S(1)} %fusion.refs_0_), channel_id=1, source_target_pairs={{0,16},{8,24},{16,0},{24,8},{1,17},{9,25},{17,1},{25,9},{2,18},{10... | collective-permute-start | bytes 786440 | tf_op jit(solution)/shard_map/ppermute | solution.py:309
  163.3 11.2 %collective-permute-start.35 = (bf16[1,128,640]{2,1,0:T(8,128)(2,1)S(1)}, bf16[1,128,640]{2,1,0:T(8,128)(2,1)S(1)}, u32[]{:S(2)}, u32[]{:S(2)}) collective-permute-start(bf16[1,128,640]{2,1,0:T(8,128)(2,1)S(1)} %add_convert_fusion.15), channel_id=1, source_target_pairs={{0,4},{1,5},{2,6},{3,7},{4,0},{5,1},{6,2},{7,3},{8,12},{9,13},{10,... | collective-permute-start | bytes 491528 | tf_op jit(solution)/shard_map/ppermute | solution.py:309
  166.0 17.8 %collective-permute-start.44 = (bf16[128,1024]{1,0:T(8,128)(2,1)S(1)}, bf16[128,1024]{1,0:T(8,128)(2,1)S(1)}, u32[]{:S(2)}, u32[]{:S(2)}) collective-permute-start(bf16[128,1024]{1,0:T(8,128)(2,1)S(1)} %fusion.1.refs_4_), channel_id=1, source_target_pairs={{0,8},{8,0},{16,24},{24,16},{1,9},{9,1},{17,25},{25,17},{2,10},{10... | collective-permute-start | bytes 786440 | tf_op jit(solution)/shard_map/ppermute | solution.py:309
  173.2 8.0 %collective-permute-start.45 = (bf16[128,1024]{1,0:T(8,128)(2,1)S(1)}, bf16[128,1024]{1,0:T(8,128)(2,1)S(1)}, u32[]{:S(2)}, u32[]{:S(2)}) collective-permute-start(bf16[128,1024]{1,0:T(8,128)(2,1)S(1)} %fusion.1.refs_4_), channel_id=1, source_target_pairs={{0,16},{8,24},{16,0},{24,8},{1,17},{9,25},{17,1},{25,9},{2,18},{10... | collective-permute-start | bytes 786440 | tf_op jit(solution)/shard_map/ppermute | solution.py:309
  183.5 7.3 %collective-permute-start.49 = (bf16[176,384]{1,0:T(8,128)(2,1)S(1)}, bf16[176,384]{1,0:T(8,128)(2,1)S(1)}, u32[]{:S(2)}, u32[]{:S(2)}) collective-permute-start(bf16[176,384]{1,0:T(8,128)(2,1)S(1)} %fusion.3.refs_4_), channel_id=1, source_target_pairs={{0,16},{8,24},{16,0},{24,8},{1,17},{9,25},{17,1},{25,9},{2,18},{10... | collective-permute-start | bytes 405512 | tf_op jit(solution)/shard_map/ppermute | solution.py:309
  (45 other events, 326.5 us)
